TPU v7x, 32 devices: a whole 2x2x4 slice. The times are simulated.
32 devices in a mesh: head: 4 (over y, x), blk: 8 (over z, core).
Axes of the slice: x: 2, y: 2, z: 4, core: 2. Of those that a mesh axis runs over, the one named last changes fastest.
Arguments:
- tokens: bfloat16 [4096, 2048], P(('head', 'blk')), may hold values from -6 to 6
- query_weight: bfloat16 [2048, 2048], P(('head', 'blk')), may hold values from -0.125 to 0.125
- key_weight: bfloat16 [2048, 2048], P(('head', 'blk')), may hold values from -0.125 to 0.125
- value_weight: bfloat16 [2048, 2048], P(('head', 'blk')), may hold values from -0.125 to 0.125
- output_weight: bfloat16 [2048, 2048], P(('head', 'blk')), may hold values from -4 to 4
- mixing_gain: bfloat16 [2048], P(('head', 'blk')), may hold values from 0.5 to 1.5
- query_gain: bfloat16 [2048], P(('head', 'blk')), may hold values from 0.5 to 1.5
- key_gain: bfloat16 [2048], P(('head', 'blk')), may hold values from 0.5 to 1.5
- routing_gain: bfloat16 [2048], P(('head', 'blk')), may hold values from 0.5 to 1.5
- router_weight: bfloat16 [2048, 16], P(('head', 'blk')), may hold values from -0.125 to 0.125
- gate_weight: bfloat16 [16, 2048, 1024], P('blk', 'head'), may hold values from -0.125 to 0.125
- up_weight: bfloat16 [16, 2048, 1024], P('blk', 'head'), may hold values from -0.125 to 0.125
- down_weight: bfloat16 [16, 1024, 2048], P('blk', 'head'), may hold values from -3 to 3
- seq_lengths: int32 [3], replicated, may hold values from 1024 to 2048, as said below
- dealt_order: int32 [4096], replicated, may hold values from 0 to 4095, as said below
- expert_routes: int32 [4096, 8], P(('head', 'blk')), may hold values from 0 to 15, all different within a row
- slot_order: int32 [4096, 8], P(('head', 'blk')), may hold values from 0 to 1023, as said below
- cotangent: bfloat16 [4096, 2048], P(('head', 'blk')), may hold values from -6 to 6
Outputs:
- block_output: bfloat16 [4096, 2048], P(('head', 'blk'))
- tokens_grad: float32 [4096, 2048], P(('head', 'blk'))
- query_grad: float32 [2048, 2048], P(('head', 'blk'))
- key_grad: float32 [2048, 2048], P(('head', 'blk'))
- value_grad: float32 [2048, 2048], P(('head', 'blk'))
- output_grad: float32 [2048, 2048], P(('head', 'blk'))
- mixing_grad: float32 [2048], P(('head', 'blk'))
- querynorm_grad: float32 [2048], P(('head', 'blk'))
- keynorm_grad: float32 [2048], P(('head', 'blk'))
- routing_grad: float32 [2048], P(('head', 'blk'))
- router_grad: float32 [2048, 16], P(('head', 'blk'))
- gate_grad: float32 [16, 2048, 1024], P('blk', 'head')
- up_grad: float32 [16, 2048, 1024], P('blk', 'head')
- down_grad: float32 [16, 1024, 2048], P('blk', 'head')
Inputs may be any that keep to these rules, and one draw needn't show every extreme that they name: `seq_lengths`: 3 lengths summing to 4096, the largest exactly 2048. `dealt_order`: a permutation of the stream; the rows of the devices of one index of blk, taken in head order, are two runs of 256 consecutive stream tokens, runs c and 15 - c. `expert_routes`: each row names 8 different experts. `slot_order`: within each aligned block of 128 rows the entries are 0 to 1023, each once.
All inputs are finite; a program needn't handle non-finite values.
Results may differ from a plain program's by a relative error of at most 0.022.
Values may be sent and summed in bfloat16 or wider, within the bound.
No kernel may reach another device: no remote copies, remote signals or barrier semaphores. Data moves between devices by JAX's collectives and lax.ppermute only.
A program may use at most 320 MiB of HBM per device.

v0:
```python
from functools import partial
import math

import jax
import jax.numpy as jnp
import numpy as np
from jax import lax
from jax.experimental import pallas as pl
from jax.experimental.pallas import tpu as pltpu
from jax.sharding import PartitionSpec as P


HDIM = 128
TILE = 256
LOG2E = 1.4426950408889634
norm_eps = 1e-05
rope_base = 10000.0
f32 = jnp.float32
bf16 = jnp.bfloat16


def rms_factor(square_sum, width):
    return lax.rsqrt(square_sum / width + norm_eps)


def rope_tables(position, head_size):
    half = head_size // 2
    freqs = rope_base ** (-(np.arange(half, dtype=np.float64) * 2.0) / head_size)
    angles = position.astype(f32)[:, None] * jnp.asarray(freqs.astype(np.float32))[None, :]
    cosine = jnp.cos(angles)
    sine_part = jnp.sin(angles)
    return (
        jnp.concatenate([cosine, cosine], axis=1),
        jnp.concatenate([-sine_part, sine_part], axis=1),
    )


def column_of(pieces):
    count = len(pieces)
    rows = pieces[0].shape[1] // count
    total = pieces[0][...]
    for offset in range(1, count):
        parts = [
            pieces[offset][:, (at ^ offset) * rows : ((at ^ offset) + 1) * rows]
            for at in range(count)
        ]
        total = total + jnp.concatenate(parts, axis=1)
    return jnp.transpose(jnp.broadcast_to(total, (8, total.shape[1])))[:, :1]


def turned(value, cosine, sine_part):
    return value * cosine + pltpu.roll(value, HDIM // 2, 1) * sine_part


def rope_kernel(*refs, count, width, paired):
    squares = refs[:count]
    raw, scale, cosine, sine_part = refs[count : count + 4]
    out, factors = refs[-2:]
    factor = lax.rsqrt(column_of(squares) / width + norm_eps)
    factors[...] = jnp.broadcast_to(factor, factors.shape)
    for head in range(raw.shape[1] // HDIM):
        span = slice(head * HDIM, (head + 1) * HDIM)
        value = turned(raw[:, span] * factor * scale[:, span], cosine[...], sine_part[...])
        if paired:
            start = 2 * head * HDIM
            out[:, start : start + HDIM] = value.astype(jnp.bfloat16)
            out[:, start + HDIM : start + 2 * HDIM] = refs[count + 4][:, span]
        else:
            out[:, span] = value.astype(jnp.bfloat16)


def rope_forward(squares, raw, scale, cosine, sine_part, values, width):
    group, columns = raw.shape
    paired = values is not None
    extra = (values,) if paired else ()
    return pl.pallas_call(
        partial(rope_kernel, count=len(squares), width=width, paired=paired),
        out_shape=[
            jax.ShapeDtypeStruct((group, columns * (2 if paired else 1)), jnp.bfloat16),
            jax.ShapeDtypeStruct((group, HDIM), jnp.float32),
        ],
    )(*squares, raw, scale[None], cosine, sine_part, *extra)


def unrope_kernel(back, raw, factors, scale, cosine, sine_part, scaled, inner, gain, *, stride):
    group = raw.shape[0]
    total = jnp.zeros((group, HDIM), jnp.float32)
    for head in range(raw.shape[1] // HDIM):
        span = slice(head * HDIM, (head + 1) * HDIM)
        start = stride * head * HDIM
        grad = back[:, start : start + HDIM].astype(jnp.float32)
        turn = turned(grad, cosine[...], -sine_part[...])
        product = turn * raw[:, span]
        gain[:, span] = jnp.sum(product * factors[...], axis=0, keepdims=True)
        scaled[:, span] = turn * scale[:, span]
        total = total + product * scale[:, span]
    sums = jnp.broadcast_to(jnp.sum(total, axis=1, keepdims=True), (group, HDIM))
    inner[...] = jnp.transpose(sums)[:1, :]


def rope_backward(back, raw, factors, scale, cosine, sine_part, stride):
    group, columns = raw.shape
    return pl.pallas_call(
        partial(unrope_kernel, stride=stride),
        out_shape=[
            jax.ShapeDtypeStruct((group, columns), jnp.float32),
            jax.ShapeDtypeStruct((1, group), jnp.float32),
            jax.ShapeDtypeStruct((1, columns), jnp.float32),
        ],
    )(back, raw, factors, scale[None], cosine, sine_part)


def raw_kernel(*refs, count, width, paired):
    scaled, raw, factors = refs[count : count + 3]
    out = refs[-1]
    inner = column_of(refs[:count]) / width
    factor = factors[:, :1]
    columns = raw.shape[1]
    slope = factor * factor * factor * inner
    for head in range(columns // HDIM):
        span = slice(head * HDIM, (head + 1) * HDIM)
        out[:, span] = (factor * scaled[:, span] - raw[:, span] * slope).astype(jnp.bfloat16)
        if paired:
            start = (2 * head + 1) * HDIM
            out[:, columns + head * HDIM : columns + (head + 1) * HDIM] = refs[count + 3][
                :, start : start + HDIM
            ]


def raw_backward(inner, scaled, raw, factors, pairs_back, width):
    group, columns = raw.shape
    paired = pairs_back is not None
    extra = (pairs_back,) if paired else ()
    return pl.pallas_call(
        partial(raw_kernel, count=len(inner), width=width, paired=paired),
        out_shape=jax.ShapeDtypeStruct((group, columns * (2 if paired else 1)), jnp.bfloat16),
    )(*inner, scaled, raw, factors, *extra)


def slot_codes(routes, ordering, experts, capacity):
    expert_ids = jnp.arange(experts, dtype=jnp.int32)
    absent = jnp.int32(1 << 30)
    chosen = routes[:, :, None] == expert_ids[None, None, :]
    order = jnp.min(jnp.where(chosen, ordering[:, :, None], absent), axis=1)
    rank = jnp.sum((order[None, :, :] < order[:, None, :]).astype(jnp.int32), axis=1)
    return jnp.where((order < absent) & (rank < capacity), rank, -1)


def stream_layout(seq_lengths, stream_index):
    ends = jnp.cumsum(seq_lengths)
    starts = ends - seq_lengths
    passed = (stream_index[:, None] >= ends[None, :]).astype(jnp.int32)
    sequence = jnp.sum(passed, axis=1)
    owner = sequence[:, None] == jnp.arange(seq_lengths.shape[0], dtype=jnp.int32)[None, :]
    opening = jnp.sum(jnp.where(owner, starts[None, :], 0), axis=1)
    return (sequence, stream_index - opening)


def tile_lists(query_index, query_seq, key_index, key_seq, tile):
    query_tiles = query_index.shape[0] // tile
    key_tiles = key_index.shape[0] // tile
    query_marks = query_index.reshape(query_tiles, tile)
    query_seqs = query_seq.reshape(query_tiles, tile)
    key_marks = key_index.reshape(key_tiles, tile)
    key_seqs = key_seq.reshape(key_tiles, tile)
    early = jnp.min(key_marks, axis=1)[None, :] <= jnp.max(query_marks, axis=1)[:, None]
    above = jnp.max(key_seqs, axis=1)[None, :] >= jnp.min(query_seqs, axis=1)[:, None]
    below = jnp.min(key_seqs, axis=1)[None, :] <= jnp.max(query_seqs, axis=1)[:, None]
    live = (early & above & below).astype(jnp.int32)
    order = jnp.cumsum(live, axis=1) - 1
    numbers = jnp.arange(key_tiles, dtype=jnp.int32)
    hits = (order[:, :, None] == numbers[None, None, :]) & (live[:, :, None] > 0)
    listed = jnp.sum(jnp.where(hits, numbers[None, :, None], 0), axis=1)
    return (listed.astype(jnp.int32), jnp.sum(live, axis=1).astype(jnp.int32), live)


def spread(vector):
    return jnp.broadcast_to(vector[:, None], (vector.shape[0], 128))


def twice(value, count):
    return value if count == 1 else jnp.concatenate([value] * count, axis=1)


def forward_kernel(
    listed, counts, query, pairs, at, opening, key_at, attended, context, totals, total, acc, *, tile
):
    lanes = 128
    copies = tile // lanes
    factor = LOG2E / math.sqrt(HDIM)
    for step in range(query.shape[0] // tile):
        span = slice(step * tile, (step + 1) * tile)
        acc[...] = jnp.zeros_like(acc)
        total[...] = jnp.zeros_like(total)

        def visit(turn, carry):
            number = listed[step, turn]
            start = pl.multiple_of(number * tile, tile)
            scores = lax.dot_general(
                query[span, :],
                pairs[pl.ds(start, tile), :HDIM],
                (((1,), (1,)), ((), ())),
                preferred_element_type=jnp.float32,
            )
            marks = key_at[pl.ds(number, 1), :]
            allowed = (marks <= twice(at[span, :], copies)) & (
                marks >= twice(opening[span, :], copies)
            )
            expo = jnp.where(allowed, jnp.exp2(scores * factor), 0.0)
            partial_sum = expo[:, :lanes]
            for copy in range(1, copies):
                partial_sum = partial_sum + expo[:, copy * lanes : (copy + 1) * lanes]
            total[...] += partial_sum
            acc[...] += jnp.dot(
                expo.astype(jnp.bfloat16),
                pairs[pl.ds(start, tile), HDIM:],
                preferred_element_type=jnp.float32,
            )
            return carry

        lax.fori_loop(0, counts[step], visit, 0)
        full = jnp.sum(total[...], axis=1, keepdims=True)
        result = acc[...] / full
        attended[span, :] = result
        context[span, :] = result.astype(jnp.bfloat16)
        totals[span, :] = jnp.broadcast_to(full, (tile, lanes))


def attend_forward(queries, pairs, marks, tables, tile):
    group, columns = queries.shape
    total_rows = pairs.shape[0]
    listed, counts, _ = tables
    at, opening, key_at = marks[0], marks[1], marks[2]
    heads = columns // HDIM
    lane = lambda rows: pl.BlockSpec((rows, HDIM), lambda h, *refs: (0, h))
    wide = pl.BlockSpec((total_rows, 2 * HDIM), lambda h, *refs: (0, h))
    fixed = lambda array: pl.BlockSpec(array.shape, lambda h, *refs: (0, 0))
    return pl.pallas_call(
        partial(forward_kernel, tile=tile),
        grid_spec=pltpu.PrefetchScalarGridSpec(
            num_scalar_prefetch=2,
            grid=(heads,),
            in_specs=[
                lane(group),
                wide,
                fixed(at),
                fixed(opening),
                fixed(key_at),
            ],
            out_specs=[lane(group), lane(group), lane(group)],
            scratch_shapes=[
                pltpu.VMEM((tile, HDIM), jnp.float32),
                pltpu.VMEM((tile, HDIM), jnp.float32),
            ],
        ),
        out_shape=[
            jax.ShapeDtypeStruct((group, columns), jnp.float32),
            jax.ShapeDtypeStruct((group, columns), jnp.bfloat16),
            jax.ShapeDtypeStruct((group, columns), jnp.float32),
        ],
        name="attend_forward",
    )(listed, counts, queries, pairs, at, opening, key_at)


def backward_kernel(
    live,
    query,
    pairs,
    grad,
    attended,
    totals,
    at_row,
    opening_row,
    key_col,
    query_out,
    pairs_out,
    scaled,
    offset,
    query_acc,
    key_acc,
    value_acc,
    *,
    tile,
):
    copies = tile // 128
    steps = query.shape[0] // tile
    factor = 1.0 / math.sqrt(HDIM)
    grads = grad[...].astype(jnp.float32)
    scaled[...] = (grads / totals[...]).astype(jnp.bfloat16)
    sums = jnp.sum(grads * attended[...], axis=1, keepdims=True) / totals[...]
    offset[...] = jnp.transpose(sums)[:8, :]
    query_acc[...] = jnp.zeros_like(query_acc)

    def visit(number, carry):
        start = pl.multiple_of(number * tile, tile)
        window = pl.ds(start, tile)
        key_acc[...] = jnp.zeros_like(key_acc)
        value_acc[...] = jnp.zeros_like(value_acc)
        for step in range(steps):
            span = slice(step * tile, (step + 1) * tile)

            @pl.when(live[step, number] > 0)
            def unused():
                scores = lax.dot_general(
                    pairs[window, :HDIM],
                    query[span, :],
                    (((1,), (1,)), ((), ())),
                    preferred_element_type=jnp.float32,
                )
                marks = twice(key_col[window, :], copies)
                allowed = (marks <= at_row[:, span]) & (marks >= opening_row[:, span])
                expo = jnp.where(allowed, jnp.exp2(scores * (factor * LOG2E)), 0.0)
                inner = lax.dot_general(
                    pairs[window, HDIM:],
                    scaled[span, :],
                    (((1,), (1,)), ((), ())),
                    preferred_element_type=jnp.float32,
                )
                back = (expo * (inner - offset[0:1, span])).astype(jnp.bfloat16)
                key_acc[...] += jnp.dot(back, query[span, :], preferred_element_type=jnp.float32)
                value_acc[...] += jnp.dot(
                    expo.astype(jnp.bfloat16), scaled[span, :], preferred_element_type=jnp.float32
                )
                query_acc[span, :] += lax.dot_general(
                    back,
                    pairs[window, :HDIM],
                    (((0,), (0,)), ((), ())),
                    preferred_element_type=jnp.float32,
                )

        pairs_out[window, :HDIM] = (key_acc[...] * factor).astype(jnp.bfloat16)
        pairs_out[window, HDIM:] = value_acc[...].astype(jnp.bfloat16)
        return carry

    lax.fori_loop(0, pairs.shape[0] // tile, visit, 0)
    query_out[...] = (query_acc[...] * factor).astype(jnp.bfloat16)


def attend_backward(queries, pairs, grads, attended, totals, marks, tables, tile):
    group, columns = queries.shape
    total_rows = pairs.shape[0]
    live = tables[2]
    at_row, opening_row, key_col = marks[3], marks[4], marks[5]
    heads = columns // HDIM
    lane = lambda rows: pl.BlockSpec((rows, HDIM), lambda h, *refs: (0, h))
    wide = pl.BlockSpec((total_rows, 2 * HDIM), lambda h, *refs: (0, h))
    fixed = lambda array: pl.BlockSpec(array.shape, lambda h, *refs: (0, 0))
    return pl.pallas_call(
        partial(backward_kernel, tile=tile),
        grid_spec=pltpu.PrefetchScalarGridSpec(
            num_scalar_prefetch=1,
            grid=(heads,),
            in_specs=[
                lane(group),
                wide,
                lane(group),
                lane(group),
                lane(group),
                fixed(at_row),
                fixed(opening_row),
                fixed(key_col),
            ],
            out_specs=[lane(group), wide],
            scratch_shapes=[
                pltpu.VMEM((group, HDIM), jnp.bfloat16),
                pltpu.VMEM((8, group), jnp.float32),
                pltpu.VMEM((group, HDIM), jnp.float32),
                pltpu.VMEM((tile, HDIM), jnp.float32),
                pltpu.VMEM((tile, HDIM), jnp.float32),
            ],
        ),
        out_shape=[
            jax.ShapeDtypeStruct((group, columns), jnp.bfloat16),
            jax.ShapeDtypeStruct((total_rows, 2 * columns), jnp.bfloat16),
        ],
        name="attend_backward",
    )(live, queries, pairs, grads, attended, totals, at_row, opening_row, key_col)


def attend_marks(query_index, query_start, key_index, tile):
    return (
        spread(query_index),
        spread(query_start),
        key_index.reshape(-1, tile),
        query_index[None, :],
        query_start[None, :],
        spread(key_index),
    )


def exchange(array, offset):
    count = lax.axis_size("head")
    return lax.ppermute(array, "head", [(at, at ^ offset) for at in range(count)])


def head_pieces(array):
    return [array] + [exchange(array, offset) for offset in range(1, lax.axis_size("head"))]


def head_turn(pieces):
    return [pieces[0]] + [exchange(piece, at + 1) for at, piece in enumerate(pieces[1:])]


def add_all(pieces):
    total = pieces[0].astype(f32)
    for piece in pieces[1:]:
        total = total + piece.astype(f32)
    return total


def bit_order(turn):
    count = lax.axis_size("head").bit_length() - 1
    return [1 << ((turn + step) % count) for step in range(count)]


def gather_pieces(array, turn):
    pieces = {0: array}
    for bit in bit_order(turn):
        for offset in list(pieces):
            pieces[offset ^ bit] = exchange(pieces[offset], bit)
    return [pieces[offset] for offset in range(len(pieces))]


def scatter_pieces(pieces, turn):
    held = dict(enumerate(pieces))
    for bit in bit_order(turn):
        for offset in [item for item in held if item & bit]:
            piece = held.pop(offset).astype(bf16)
            arrived = exchange(piece, bit)
            held[offset ^ bit] = held[offset ^ bit].astype(f32) + arrived.astype(f32)
    return held[0]


def xor_order(array, axis):
    count = lax.axis_size("head")
    at = lax.axis_index("head")
    size = array.shape[axis] // count
    chunks = [
        lax.dynamic_slice_in_dim(array, (at ^ offset) * size, size, axis) for offset in range(count)
    ]
    return chunks


def xor_chunks(array, axis):
    return jnp.concatenate(xor_order(array, axis), axis=axis)


def absolute(pieces):
    at = lax.axis_index("head")
    result = []
    for place in range(len(pieces)):
        value = pieces[0]
        for offset in range(1, len(pieces)):
            value = jnp.where(at == place ^ offset, pieces[offset], value)
        result.append(value)
    return result


def move_rows(array, outer, inner, part):
    shaped = array.reshape(outer, inner, part, array.shape[1])
    return jnp.transpose(shaped, (1, 0, 2, 3)).reshape(array.shape)


def move_columns(array, outer, inner, part):
    shaped = array.reshape(array.shape[0], outer, inner, part)
    return jnp.transpose(shaped, (0, 2, 1, 3)).reshape(array.shape)


def layer(
    tokens,
    query_weight,
    key_weight,
    value_weight,
    output_weight,
    mixing_gain,
    query_gain,
    key_gain,
    routing_gain,
    router_weight,
    gate_weight,
    up_weight,
    down_weight,
    seq_lengths,
    dealt_order,
    expert_routes,
    slot_order,
    cotangent,
):
    heads_axis = lax.axis_size("head")
    blocks = lax.axis_size("blk")
    head_at = lax.axis_index("head")
    block_at = lax.axis_index("blk")
    rows, width = tokens.shape
    picks = expert_routes.shape[1]
    total_rows = dealt_order.shape[0]
    group = rows * heads_axis
    columns = width // heads_axis
    part = query_weight.shape[0]
    head_size = HDIM
    experts = router_weight.shape[1]
    local_experts = gate_weight.shape[0]
    capacity = 5 * rows * picks // (4 * experts)
    slots = blocks * capacity

    slices = [
        jnp.concatenate(chunks, axis=1)
        for chunks in zip(
            xor_order(key_weight, 1), xor_order(value_weight, 1), xor_order(query_weight, 1)
        )
    ]
    slices = head_turn(slices)
    output_rows = lax.all_gather(output_weight, "blk", axis=0, tiled=True)
    token_pieces = head_pieces(tokens)
    rows_here = jnp.stack(absolute(slices)).reshape(heads_axis * part, 3 * columns)
    pair_full = lax.all_gather(rows_here[:, : 2 * columns], "blk", axis=0, tiled=True)
    pair_full = move_rows(pair_full, blocks, heads_axis, part)
    query_full = lax.all_gather(rows_here[:, 2 * columns :], "blk", axis=0, tiled=True)
    query_full = move_rows(query_full, blocks, heads_axis, part)
    cot_all = lax.all_gather(cotangent, "blk", axis=0, tiled=True).reshape(blocks, rows, width)

    small = jnp.concatenate(
        [
            mixing_gain[:, None],
            query_gain[:, None],
            key_gain[:, None],
            routing_gain[:, None],
            router_weight,
        ],
        axis=1,
    ).reshape(1, -1)
    small = lax.all_gather(small, "blk", axis=0, tiled=True)
    small = jnp.stack(absolute(head_pieces(small))).reshape(width, 4 + experts)
    mixing_scale = small[:, 0].astype(f32)
    routing_scale = small[:, 3].astype(f32)
    query_scale = lax.dynamic_slice_in_dim(small[:, 1], head_at * columns, columns).astype(f32)
    key_scale = lax.dynamic_slice_in_dim(small[:, 2], head_at * columns, columns).astype(f32)
    router_full = small[:, 4:]
    codes = slot_codes(expert_routes, slot_order, experts, capacity)
    codes = lax.all_gather(codes, "blk", axis=0, tiled=True).reshape(blocks, rows, experts)
    codes_here = lax.dynamic_slice_in_dim(codes, block_at * local_experts, local_experts, 2)

    key_index = jnp.transpose(
        xor_chunks(dealt_order.reshape(heads_axis, blocks, rows), 0), (1, 0, 2)
    ).reshape(total_rows)
    key_seq = stream_layout(seq_lengths, key_index)[0]
    query_index = lax.dynamic_slice_in_dim(key_index, block_at * group, group)
    query_seq, query_position = stream_layout(seq_lengths, query_index)
    cosine, sine_part = rope_tables(query_position, head_size)
    tables = tile_lists(query_index, query_seq, key_index, key_seq, TILE)
    marks = attend_marks(query_index, query_index - query_position, key_index, TILE)

    gates, ups, downs = (
        [gather_pieces(weight[item], item) for item in range(local_experts)]
        for weight in (gate_weight, up_weight, down_weight)
    )

    token_group = jnp.concatenate(token_pieces, axis=0).astype(f32)
    token_factor = rms_factor(jnp.sum(token_group * token_group, axis=-1, keepdims=True), width)
    normed = (token_group * token_factor * mixing_scale).astype(bf16)
    normed_moved = move_columns(normed, heads_axis, blocks, part)
    key_raw = jnp.dot(normed, pair_full[:, :columns], preferred_element_type=f32)
    value_heads = jnp.dot(normed, pair_full[:, columns:], preferred_element_type=f32)
    value_heads = value_heads.astype(bf16)
    key_squares = head_pieces(jnp.sum(key_raw * key_raw, axis=-1)[None])
    pairs, key_factor = rope_forward(
        key_squares, key_raw, key_scale, cosine, sine_part, value_heads, width
    )
    query_raw = jnp.dot(normed, query_full, preferred_element_type=f32)
    query_squares = head_pieces(jnp.sum(query_raw * query_raw, axis=-1)[None])
    query_heads, query_factor = rope_forward(
        query_squares, query_raw, query_scale, cosine, sine_part, None, width
    )
    pairs_all = lax.all_gather(pairs, "blk", axis=0, tiled=True)
    attended, context, totals = attend_forward(query_heads, pairs_all, marks, tables, TILE)
    branch = jnp.dot(context, output_rows, preferred_element_type=f32).astype(bf16)
    branch = head_turn([branch[piece * rows : (piece + 1) * rows] for piece in range(heads_axis)])
    own_tokens = tokens.astype(f32)
    middle = own_tokens + add_all(branch)
    middle_factor = rms_factor(jnp.sum(middle * middle, axis=-1, keepdims=True), width)
    routed = (middle * middle_factor * routing_scale).astype(bf16)

    routed_all = lax.all_gather(xor_chunks(routed, 1), "blk", axis=0, tiled=True)
    probs = jax.nn.softmax(jnp.dot(routed, router_full, preferred_element_type=f32), axis=-1)
    probs_all = jax.nn.softmax(
        jnp.dot(routed_all, xor_chunks(router_full, 0), preferred_element_type=f32), axis=-1
    )
    weight_here = lax.dynamic_slice_in_dim(
        probs_all, block_at * local_experts, local_experts, 1
    ).reshape(blocks, rows, local_experts)
    routed_all = routed_all.reshape(blocks, rows, width)
    slot_ids = jnp.arange(capacity, dtype=jnp.int32)
    combined = 0.0
    incoming = 0.0
    weight_grads = []
    stores = []
    for item in range(local_experts):
        placed = codes_here[:, None, :, item] == slot_ids[None, :, None]
        place = placed.astype(bf16)
        slot_weight = jnp.sum(
            jnp.where(placed, weight_here[:, None, :, item], 0.0), axis=-1
        ).reshape(slots, 1)
        arrived = jnp.einsum("srt,std->srd", place, routed_all).reshape(slots, width)
        arrived_cot = jnp.einsum("srt,std->srd", place, cot_all).reshape(slots, width)
        gate_all = jnp.concatenate(gates[item], axis=0)
        up_all = jnp.concatenate(ups[item], axis=0)
        down_all = jnp.concatenate(downs[item], axis=0)
        gate = jnp.dot(arrived, gate_all, preferred_element_type=f32)
        upward = jnp.dot(arrived, up_all, preferred_element_type=f32)
        sigmoid = jax.nn.sigmoid(gate)
        active = xor_chunks((gate * sigmoid * upward).astype(bf16), 1)
        produced = jnp.dot(active, down_all, preferred_element_type=f32).astype(bf16)
        cot_float = arrived_cot.astype(f32)
        produced_float = produced.astype(f32)
        weighted = (slot_weight * produced_float).astype(bf16).reshape(blocks, capacity, width)
        combined = combined + jnp.einsum(
            "srt,srd->std", place, weighted, preferred_element_type=f32
        )
        slot_grad = jnp.sum(cot_float * produced_float, axis=-1).reshape(blocks, capacity, 1)
        weight_grads.append(jnp.sum(jnp.where(placed, slot_grad, 0.0), axis=1))
        produced_grad = (slot_weight * cot_float).astype(bf16)
        active_grad = xor_chunks(
            jnp.dot(produced_grad, down_all.T, preferred_element_type=f32), 1
        )
        gate_grad = (active_grad * upward * sigmoid * (1.0 + gate * (1.0 - sigmoid))).astype(bf16)
        up_grad = (active_grad * (gate * sigmoid)).astype(bf16)
        coming = jnp.dot(gate_grad, gate_all.T, preferred_element_type=f32)
        coming = coming + jnp.dot(up_grad, up_all.T, preferred_element_type=f32)
        coming = coming.astype(bf16).reshape(blocks, capacity, width)
        incoming = incoming + jnp.einsum(
            "srt,srd->std", place, coming, preferred_element_type=f32
        )
        stores.append((arrived, produced_grad, active, gate_grad, up_grad))
    routed_grad = lax.psum_scatter(
        incoming.astype(bf16).reshape(blocks * rows, width),
        "blk",
        scatter_dimension=0,
        tiled=True,
    )
    combined = lax.psum_scatter(
        combined.astype(bf16).reshape(blocks * rows, width),
        "blk",
        scatter_dimension=0,
        tiled=True,
    )
    block_output = (middle + combined.astype(f32)).astype(bf16)
    prob_grad = lax.all_to_all(
        jnp.stack(weight_grads, axis=2), "blk", split_axis=0, concat_axis=2, tiled=True
    ).reshape(rows, experts)

    def pieces_of(left, right):
        size = left.shape[1] // heads_axis
        return [
            lax.optimization_barrier(
                jnp.dot(
                    left[:, offset * size : (offset + 1) * size].T,
                    right,
                    preferred_element_type=f32,
                ).astype(bf16)
            )
            for offset in range(heads_axis)
        ]

    down_out, gate_out, up_out = (
        jnp.stack(
            [
                scatter_pieces(pieces_of(store[left], store[right]), item)
                for item, store in enumerate(stores)
            ]
        ).astype(f32)
        for left, right in ((2, 1), (0, 3), (0, 4))
    )

    logit_grad = (
        probs * (prob_grad - jnp.sum(probs * prob_grad, axis=1, keepdims=True))
    ).astype(bf16)
    router_sum = jnp.dot(routed.T, logit_grad, preferred_element_type=f32)
    routed_grad = xor_chunks(routed_grad, 1).astype(f32) + jnp.dot(
        logit_grad, router_full.T, preferred_element_type=f32
    )
    scaled = routed_grad * routing_scale
    inner = jnp.mean(scaled * middle, axis=-1, keepdims=True)
    middle_grad = (
        cotangent.astype(f32) + middle_factor * scaled - middle * (middle_factor**3 * inner)
    )
    routing_sum = jnp.sum(routed_grad * middle * middle_factor, axis=0)

    branch_grad = head_pieces(middle_grad.astype(bf16))
    branch_grad = jnp.concatenate(branch_grad, axis=0)
    context_grad = jnp.dot(branch_grad, output_rows.T, preferred_element_type=f32).astype(bf16)
    output_sum = jnp.dot(context.T, branch_grad, preferred_element_type=f32).astype(bf16)
    output_out = lax.psum_scatter(output_sum, "blk", scatter_dimension=0, tiled=True)
    query_back, pairs_back = attend_backward(
        query_heads, pairs_all, context_grad, attended, totals, marks, tables, TILE
    )
    pairs_back = lax.psum_scatter(pairs_back, "blk", scatter_dimension=0, tiled=True)
    query_scaled, query_inner, querynorm_sum = rope_backward(
        query_back, query_raw, query_factor, query_scale, cosine, sine_part, 1
    )
    query_inner = head_pieces(query_inner)
    query_raw_grad = raw_backward(query_inner, query_scaled, query_raw, query_factor, None, width)
    query_sum = jnp.dot(normed_moved.T, query_raw_grad, preferred_element_type=f32).astype(bf16)
    query_sum = lax.psum_scatter(query_sum, "blk", scatter_dimension=0, tiled=True)
    normed_part = jnp.dot(query_raw_grad, query_full.T, preferred_element_type=f32)
    key_scaled, key_inner, keynorm_sum = rope_backward(
        pairs_back, key_raw, key_factor, key_scale, cosine, sine_part, 2
    )
    key_inner = head_pieces(key_inner)
    pair_grad = raw_backward(key_inner, key_scaled, key_raw, key_factor, pairs_back, width)
    pair_sum = jnp.dot(normed_moved.T, pair_grad, preferred_element_type=f32).astype(bf16)
    pair_sum = lax.psum_scatter(pair_sum, "blk", scatter_dimension=0, tiled=True)
    normed_part = normed_part + jnp.dot(pair_grad, pair_full.T, preferred_element_type=f32)
    normed_part = normed_part.astype(bf16)
    normed_part = head_turn(
        [normed_part[piece * rows : (piece + 1) * rows] for piece in range(heads_axis)]
    )
    normed_grad = add_all(normed_part)
    own_factor = rms_factor(jnp.sum(own_tokens * own_tokens, axis=-1, keepdims=True), width)
    scaled = normed_grad * mixing_scale
    inner = jnp.mean(scaled * own_tokens, axis=-1, keepdims=True)
    tokens_grad = middle_grad + own_factor * scaled - own_tokens * (own_factor**3 * inner)
    mixing_sum = jnp.sum(normed_grad * own_tokens * own_factor, axis=0)

    def turned_back(array):
        return jnp.stack(
            [
                jnp.concatenate(absolute(list(pieces)), axis=1).astype(f32)
                for pieces in zip(
                    *(
                        [piece[:, at : at + columns] for at in range(0, piece.shape[1], columns)]
                        for piece in head_turn(xor_order(array, 0))
                    )
                )
            ]
        )

    query_out = turned_back(query_sum)[0]
    pair_out = turned_back(pair_sum)

    blank = jnp.zeros((heads_axis, columns), f32)
    query_line = lax.dynamic_update_slice(blank, querynorm_sum, (head_at, 0)).reshape(width)
    key_line = lax.dynamic_update_slice(blank, keynorm_sum, (head_at, 0)).reshape(width)
    lines = jnp.concatenate(
        [
            mixing_sum[:, None],
            query_line[:, None],
            key_line[:, None],
            routing_sum[:, None],
            router_sum,
        ],
        axis=1,
    ).reshape(heads_axis, -1)
    lines = add_all(head_turn(xor_order(lines, 0)))
    lines = lax.all_to_all(lines.reshape(blocks, -1), "blk", 0, 0, tiled=True)
    lines = jnp.sum(lines, axis=0).reshape(part, 4 + experts)
    return (
        block_output,
        tokens_grad,
        query_out,
        pair_out[0],
        pair_out[1],
        output_out.astype(f32),
        lines[:, 0],
        lines[:, 1],
        lines[:, 2],
        lines[:, 3],
        lines[:, 4:],
        gate_out,
        up_out,
        down_out,
    )


def solution(mesh):
    in_specs = (
        P(("head", "blk"), None),
        P(("head", "blk"), None),
        P(("head", "blk"), None),
        P(("head", "blk"), None),
        P(("head", "blk"), None),
        P(("head", "blk")),
        P(("head", "blk")),
        P(("head", "blk")),
        P(("head", "blk")),
        P(("head", "blk"), None),
        P("blk", "head", None),
        P("blk", "head", None),
        P("blk", "head", None),
        P(),
        P(),
        P(("head", "blk"), None),
        P(("head", "blk"), None),
        P(("head", "blk"), None),
    )
    out_specs = (
        P(("head", "blk"), None),
        P(("head", "blk"), None),
        P(("head", "blk"), None),
        P(("head", "blk"), None),
        P(("head", "blk"), None),
        P(("head", "blk"), None),
        P(("head", "blk")),
        P(("head", "blk")),
        P(("head", "blk")),
        P(("head", "blk")),
        P(("head", "blk"), None),
        P("blk", "head", None),
        P("blk", "head", None),
        P("blk", "head", None),
    )
    return jax.shard_map(layer, mesh=mesh, in_specs=in_specs, out_specs=out_specs, check_vma=False)
```

profile of v0, /device:TPU:0, one launch (start us, length us, event | category | flops | bytes accessed | tf_op | source)
XLA Modules:
  0.0 1178.9 jit_solution(17554006450359026753)
XLA Ops:
  18.1 4.7 collective-permute-done.6
  26.2 14.3 %all-gather = bf16[8,1,1280]{2,1,0:T(2,128)(2,1)S(1)} all-gather(bf16[1,1,1280]{2,1,0:T(2,128)(2,1)S(1)} %reshape.476), channel_id=1, replica_groups=mesh['head'=4,'blk'=8] {'blk'}, dimensions={0}, use_global_device_ids=true | all-gather | bytes 23040 | tf_op jit(solution)/shard_map/all_gather | solution.py:531
  54.9 5.2 collective-permute-done.2
  60.1 9.8 collective-permute-done.1
  91.5 9.8 all-gather.16.cloned.1.call-start
  120.1 66.8 %all-gather.12.cloned.1.call-done.pairs = bf16[4096,1024]{1,0:T(8,128)(2,1)} async-done(((bf16[512,1024]{1,0:T(8,128)(2,1)}), bf16[4096,1024]{1,0:T(8,128)(2,1)}) %all-gather.12.cloned.1.call-update) | async-done | bytes 8388624 | tf_op jit(solution)/shard_map/all_gather | solution.py:573
  188.5 11.3 attend_forward.1
  199.9 16.1 %all-gather.14.cloned.1.call-done = bf16[512,2048]{1,0:T(8,128)(2,1)} async-done(((bf16[64,2048]{1,0:T(8,128)(2,1)}), bf16[512,2048]{1,0:T(8,128)(2,1)}) %all-gather.14.cloned.1.call-update) | async-done | bytes 2097168 | tf_op jit(solution)/shard_map/all_gather | solution.py:512
  222.8 11.3 collective-permute-done.15
  234.1 11.5 collective-permute-done.17
  262.2 14.0 %all_gather.29 = s32[1024,16]{0,1:T(8,128)S(1)} all-gather(s32[128,16]{0,1:T(8,128)S(1)} %and_select_fusion), channel_id=1, replica_groups=mesh['head'=4,'blk'=8] {'blk'}, dimensions={0}, use_global_device_ids=true | all-gather | bytes 73728 | tf_op jit(solution)/shard_map/all_gather | solution.py:539
  279.0 22.8 %collective-permute-done.18 = bf16[512,1024]{1,0:T(8,128)(2,1)} collective-permute-done((bf16[512,1024]{1,0:T(8,128)(2,1)}, bf16[512,1024]{1,0:T(8,128)(2,1)}, u32[]{:S(2)}, u32[]{:S(2)}) %collective-permute-start.18) | collective-permute-done | bytes 1048608 | tf_op jit(solution)/shard_map/ppermute | solution.py:393
  303.3 4.7 fusion.62
  316.2 5.8 collective-permute-done.21
  329.0 4.8 fusion.45
  333.8 16.1 %collective-permute-done.22 = bf16[512,1024]{1,0:T(8,128)(2,1)S(1)} collective-permute-done((bf16[512,1024]{1,0:T(8,128)(2,1)}, bf16[512,1024]{1,0:T(8,128)(2,1)S(1)}, u32[]{:S(2)}, u32[]{:S(2)}) %collective-permute-start.22) | collective-permute-done | bytes 1048608 | tf_op jit(solution)/shard_map/ppermute | solution.py:393
  351.9 20.4 %collective-permute-done.23 = bf16[512,1024]{1,0:T(8,128)(2,1)S(1)} collective-permute-done((bf16[512,1024]{1,0:T(8,128)(2,1)}, bf16[512,1024]{1,0:T(8,128)(2,1)S(1)}, u32[]{:S(2)}, u32[]{:S(2)}) %collective-permute-start.23) | collective-permute-done | bytes 1048608 | tf_op jit(solution)/shard_map/ppermute | solution.py:393
  373.8 5.7 multiply_convert_fusion.6
  383.0 11.8 %collective-permute-done.25 = bf16[256,2048]{1,0:T(8,128)(2,1)S(1)} collective-permute-done((bf16[256,2048]{1,0:T(8,128)(2,1)S(1)}, bf16[256,2048]{1,0:T(8,128)(2,1)S(1)}, u32[]{:S(2)}, u32[]{:S(2)}) %collective-permute-start.25) | collective-permute-done | bytes 1048608 | tf_op jit(solution)/shard_map/ppermute | solution.py:393
  396.3 43.5 %collective-permute-done.26 = bf16[256,2048]{1,0:T(8,128)(2,1)S(1)} collective-permute-done((bf16[256,2048]{1,0:T(8,128)(2,1)S(1)}, bf16[256,2048]{1,0:T(8,128)(2,1)S(1)}, u32[]{:S(2)}, u32[]{:S(2)}) %collective-permute-start.26) | collective-permute-done | bytes 1048608 | tf_op jit(solution)/shard_map/ppermute | solution.py:393
  451.5 6.0 collective-permute-done.34
  459.0 7.1 collective-permute-done.29
  466.1 4.6 fusion.41
  470.7 40.2 %collective-permute-done.32 = bf16[512,1024]{1,0:T(8,128)(2,1)S(1)} collective-permute-done((bf16[512,1024]{1,0:T(8,128)(2,1)}, bf16[512,1024]{1,0:T(8,128)(2,1)S(1)}, u32[]{:S(2)}, u32[]{:S(2)}) %collective-permute-start.32) | collective-permute-done | bytes 1048608 | tf_op jit(solution)/shard_map/ppermute | solution.py:393
  511.0 6.5 multiply_convert_fusion.5
  529.0 5.4 fusion.5
  535.0 5.9 fusion.4
  540.9 7.2 fusion.38
  552.5 5.4 fusion.43
  557.9 5.1 add_convert_fusion.3
  567.2 7.5 fusion.39
  574.8 5.1 add_convert_fusion.2
  589.1 5.7 all-to-all-done
  594.8 38.2 %reduce-scatter.9.cloned.1.call-done = bf16[128,2048]{1,0:T(8,128)(2,1)} async-done(((bf16[1024,2048]{1,0:T(8,128)(2,1)}), bf16[128,2048]{1,0:T(8,128)(2,1)}) %reduce-scatter.9.cloned.1.call-update) | async-done | bytes 524304 | tf_op jit(solution)/shard_map/reduce_scatter | solution.py:633
  641.4 12.2 %collective-permute-done.38 = bf16[128,2048]{1,0:T(8,128)(2,1)S(1)} collective-permute-done((bf16[128,2048]{1,0:T(8,128)(2,1)S(1)}, bf16[128,2048]{1,0:T(8,128)(2,1)S(1)}, u32[]{:S(2)}, u32[]{:S(2)}) %collective-permute-start.38) | collective-permute-done | bytes 524320 | tf_op jit(solution)/shard_map/ppermute | solution.py:393
  653.7 8.2 collective-permute-done.37
  667.0 19.5 %attend_backward.1 = (bf16[512,512]{1,0:T(8,128)(2,1)}, bf16[4096,1024]{1,0:T(8,128)(2,1)}) custom-call(s32[2,16]{1,0:T(2,128)} %copy-done.96, bf16[512,512]{1,0:T(8,128)(2,1)} %get-tuple-element.29.query, bf16[4096,1024]{1,0:T(8,128)(2,1)} %all-gather.12.cloned.1.call-done.pairs, bf16[512,512]{1,0:T(8,128)(2,1)} %convolution_convert_fusion.30.grad, ...), custom_call_target="tpu_custom_call" | custom-call | tf_op jit(solution)/shard_map/attend_backward/pallas_call | solution.py:348
  709.2 74.3 %reduce-scatter.11.cloned.1.call-done.back.refs_7_ = bf16[512,1024]{1,0:T(8,128)(2,1)} async-done(((bf16[4096,1024]{1,0:T(8,128)(2,1)}), bf16[512,1024]{1,0:T(8,128)(2,1)}) %reduce-scatter.11.cloned.1.call-update) | async-done | bytes 1048592 | tf_op jit(solution)/shard_map/reduce_scatter | solution.py:695
  797.5 6.3 convolution_convert_fusion
  865.0 53.7 %collective-permute-done.70 = bf16[256,2048]{1,0:T(8,128)(2,1)} collective-permute-done((bf16[256,2048]{1,0:T(8,128)(2,1)}, bf16[256,2048]{1,0:T(8,128)(2,1)}, u32[]{:S(2)}, u32[]{:S(2)}) %collective-permute-start.70) | collective-permute-done | bytes 1048608 | tf_op jit(solution)/shard_map/ppermute | solution.py:393
  927.4 17.6 %collective-permute-done.73 = bf16[256,2048]{1,0:T(8,128)(2,1)S(1)} collective-permute-done((bf16[256,2048]{1,0:T(8,128)(2,1)}, bf16[256,2048]{1,0:T(8,128)(2,1)S(1)}, u32[]{:S(2)}, u32[]{:S(2)}) %collective-permute-start.73) | collective-permute-done | bytes 1048608 | tf_op jit(solution)/shard_map/ppermute | solution.py:393
  949.3 18.2 %collective-permute-done.61 = bf16[512,1024]{1,0:T(8,128)(2,1)S(1)} collective-permute-done((bf16[512,1024]{1,0:T(8,128)(2,1)S(1)}, bf16[512,1024]{1,0:T(8,128)(2,1)S(1)}, u32[]{:S(2)}, u32[]{:S(2)}) %collective-permute-start.61) | collective-permute-done | bytes 1048608 | tf_op jit(solution)/shard_map/ppermute | solution.py:393
  970.1 19.8 %collective-permute-done.72 = bf16[256,2048]{1,0:T(8,128)(2,1)S(1)} collective-permute-done((bf16[256,2048]{1,0:T(8,128)(2,1)S(1)}, bf16[256,2048]{1,0:T(8,128)(2,1)S(1)}, u32[]{:S(2)}, u32[]{:S(2)}) %collective-permute-start.72) | collective-permute-done | bytes 1048608 | tf_op jit(solution)/shard_map/ppermute | solution.py:393
  991.4 21.0 %collective-permute-done.71 = bf16[256,2048]{1,0:T(8,128)(2,1)S(1)} collective-permute-done((bf16[256,2048]{1,0:T(8,128)(2,1)S(1)}, bf16[256,2048]{1,0:T(8,128)(2,1)S(1)}, u32[]{:S(2)}, u32[]{:S(2)}) %collective-permute-start.71) | collective-permute-done | bytes 1048608 | tf_op jit(solution)/shard_map/ppermute | solution.py:393
  1018.6 38.8 %collective-permute-done.65 = bf16[512,1024]{1,0:T(8,128)(2,1)S(1)} collective-permute-done((bf16[512,1024]{1,0:T(8,128)(2,1)S(1)}, bf16[512,1024]{1,0:T(8,128)(2,1)S(1)}, u32[]{:S(2)}, u32[]{:S(2)}) %collective-permute-start.65) | collective-permute-done | bytes 1048608 | tf_op jit(solution)/shard_map/ppermute | solution.py:393
  1065.3 31.4 %collective-permute-done.59 = bf16[512,1024]{1,0:T(8,128)(2,1)S(1)} collective-permute-done((bf16[512,1024]{1,0:T(8,128)(2,1)S(1)}, bf16[512,1024]{1,0:T(8,128)(2,1)S(1)}, u32[]{:S(2)}, u32[]{:S(2)}) %collective-permute-start.59) | collective-permute-done | bytes 1048608 | tf_op jit(solution)/shard_map/ppermute | solution.py:393
  1126.3 6.1 collective-permute-done.47
  1146.3 10.1 all-to-all-start.1
  (671 shorter events, 364.8 us)
Async XLA Ops:
  7.2 65.9 %all-gather.10.cloned.1.call-start = ((), (), s32[]{:S(2)}) async-start(), calls=%async_computation.9 | async-start | bytes 4718592 | tf_op jit(solution)/shard_map/all_gather | solution.py:515
  25.7 78.8 %all-gather.8.cloned.1.call-start = ((), (), s32[]{:S(2)}) async-start(), calls=%async_computation.8 | async-start | bytes 2359296 | tf_op jit(solution)/shard_map/all_gather | solution.py:517
  48.3 138.5 %all-gather.12.cloned.1.call-start = ((), (), s32[]{:S(2)}) async-start(), calls=%async_computation.10 | async-start | bytes 9437184 | tf_op jit(solution)/shard_map/all_gather | solution.py:573
  90.4 125.6 %all-gather.14.cloned.1.call-start = ((), (), s32[]{:S(2)}) async-start(), calls=%async_computation.11 | async-start | bytes 2359296 | tf_op jit(solution)/shard_map/all_gather | solution.py:512
  90.9 212.4 %all-gather.18.cloned.1.call-start = ((), (), s32[]{:S(2)}) async-start(), calls=%async_computation.14 | async-start | bytes 4718592 | tf_op jit(solution)/shard_map/all_gather | solution.py:519
  91.5 220.0 %all-gather.16.cloned.1.call-start = ((), (), s32[]{:S(2)}) async-start(), calls=%async_computation.12 | async-start | bytes 4718592 | tf_op jit(solution)/shard_map/all_gather | solution.py:582
  250.8 382.2 %reduce-scatter.9.cloned.1.call-start = ((), (), s32[]{:S(2)}) async-start(), calls=%async_computation.15 | async-start | bytes 4718592 | tf_op jit(solution)/shard_map/reduce_scatter | solution.py:633
  252.5 129.0 %collective-permute-start.28 = (bf16[512,1024]{1,0:T(8,128)(2,1)}, bf16[512,1024]{1,0:T(8,128)(2,1)}, u32[]{:S(2)}, u32[]{:S(2)}) collective-permute-start(bf16[512,1024]{1,0:T(8,128)(2,1)} %get-tuple-element.141), channel_id=1, source_target_pairs={{0,16},{8,24},{16,0},{24,8},{1,17},{9,25},{17,1},{25,9},{2,18},{10... | collective-permute-start | bytes 3145736 | tf_op jit(solution)/shard_map/ppermute | solution.py:393
  253.0 196.4 %collective-permute-start.27 = (bf16[512,1024]{1,0:T(8,128)(2,1)}, bf16[512,1024]{1,0:T(8,128)(2,1)}, u32[]{:S(2)}, u32[]{:S(2)}) collective-permute-start(bf16[512,1024]{1,0:T(8,128)(2,1)} %get-tuple-element.141), channel_id=1, source_target_pairs={{0,8},{8,0},{16,24},{24,16},{1,9},{9,1},{17,25},{25,17},{2,10},{10... | collective-permute-start | bytes 3145736 | tf_op jit(solution)/shard_map/ppermute | solution.py:393
  254.5 60.1 %collective-permute-start.19 = (bf16[512,1024]{1,0:T(8,128)(2,1)}, bf16[512,1024]{1,0:T(8,128)(2,1)}, u32[]{:S(2)}, u32[]{:S(2)}) collective-permute-start(bf16[512,1024]{1,0:T(8,128)(2,1)} %get-tuple-element.142), channel_id=1, source_target_pairs={{0,16},{8,24},{16,0},{24,8},{1,17},{9,25},{17,1},{25,9},{2,18},{10... | collective-permute-start | bytes 3145736 | tf_op jit(solution)/shard_map/ppermute | solution.py:393
  256.0 45.9 %collective-permute-start.18 = (bf16[512,1024]{1,0:T(8,128)(2,1)}, bf16[512,1024]{1,0:T(8,128)(2,1)}, u32[]{:S(2)}, u32[]{:S(2)}) collective-permute-start(bf16[512,1024]{1,0:T(8,128)(2,1)} %get-tuple-element.142), channel_id=1, source_target_pairs={{0,8},{8,0},{16,24},{24,16},{1,9},{9,1},{17,25},{25,17},{2,10},{10... | collective-permute-start | bytes 3145736 | tf_op jit(solution)/shard_map/ppermute | solution.py:393
  258.0 64.0 %collective-permute-start.21 = (bf16[512,1024]{1,0:T(8,128)(2,1)}, bf16[512,1024]{1,0:T(8,128)(2,1)}, u32[]{:S(2)}, u32[]{:S(2)}) collective-permute-start(bf16[512,1024]{1,0:T(8,128)(2,1)} %get-tuple-element.144), channel_id=1, source_target_pairs={{0,8},{8,0},{16,24},{24,16},{1,9},{9,1},{17,25},{25,17},{2,10},{10... | collective-permute-start | bytes 3145736 | tf_op jit(solution)/shard_map/ppermute | solution.py:393
  301.9 25.7 %collective-permute-start.20 = (bf16[512,1024]{1,0:T(8,128)(2,1)}, bf16[512,1024]{1,0:T(8,128)(2,1)}, u32[]{:S(2)}, u32[]{:S(2)}) collective-permute-start(bf16[512,1024]{1,0:T(8,128)(2,1)} %collective-permute-done.18), channel_id=1, source_target_pairs={{0,16},{8,24},{16,0},{24,8},{1,17},{9,25},{17,1},{25,9},{2,18},{10... | collective-permute-start | bytes 3145736 | tf_op jit(solution)/shard_map/ppermute | solution.py:393
  314.6 35.2 %collective-permute-start.22 = (bf16[512,1024]{1,0:T(8,128)(2,1)}, bf16[512,1024]{1,0:T(8,128)(2,1)S(1)}, u32[]{:S(2)}, u32[]{:S(2)}) collective-permute-start(bf16[512,1024]{1,0:T(8,128)(2,1)} %get-tuple-element.144), channel_id=1, source_target_pairs={{0,16},{8,24},{16,0},{24,8},{1,17},{9,25},{17,1},{25,9},{2,18},{10... | collective-permute-start | bytes 3145736 | tf_op jit(solution)/shard_map/ppermute | solution.py:393
  322.0 29.3 %collective-permute-start.24 = (bf16[256,2048]{1,0:T(8,128)(2,1)S(1)}, bf16[256,2048]{1,0:T(8,128)(2,1)S(1)}, u32[]{:S(2)}, u32[]{:S(2)}) collective-permute-start(bf16[256,2048]{1,0:T(8,128)(2,1)S(1)} %copy-done.81), channel_id=1, source_target_pairs={{0,8},{8,0},{16,24},{24,16},{1,9},{9,1},{17,25},{25,17},{2,10},{10... | collective-permute-start | bytes 3145736 | tf_op jit(solution)/shard_map/ppermute | solution.py:393
  327.5 44.8 %collective-permute-start.23 = (bf16[512,1024]{1,0:T(8,128)(2,1)}, bf16[512,1024]{1,0:T(8,128)(2,1)S(1)}, u32[]{:S(2)}, u32[]{:S(2)}) collective-permute-start(bf16[512,1024]{1,0:T(8,128)(2,1)} %collective-permute-done.21), channel_id=1, source_target_pairs={{0,16},{8,24},{16,0},{24,8},{1,17},{9,25},{17,1},{25,9},{2,18},{10... | collective-permute-start | bytes 3145736 | tf_op jit(solution)/shard_map/ppermute | solution.py:393
  349.9 44.9 %collective-permute-start.25 = (bf16[256,2048]{1,0:T(8,128)(2,1)S(1)}, bf16[256,2048]{1,0:T(8,128)(2,1)S(1)}, u32[]{:S(2)}, u32[]{:S(2)}) collective-permute-start(bf16[256,2048]{1,0:T(8,128)(2,1)S(1)} %copy-done.81), channel_id=1, source_target_pairs={{0,16},{8,24},{16,0},{24,8},{1,17},{9,25},{17,1},{25,9},{2,18},{10... | collective-permute-start | bytes 3145736 | tf_op jit(solution)/shard_map/ppermute | solution.py:393
  351.3 98.7 %collective-permute-start.31 = (bf16[512,1024]{1,0:T(8,128)(2,1)}, bf16[512,1024]{1,0:T(8,128)(2,1)}, u32[]{:S(2)}, u32[]{:S(2)}) collective-permute-start(bf16[512,1024]{1,0:T(8,128)(2,1)} %get-tuple-element.143), channel_id=1, source_target_pairs={{0,16},{8,24},{16,0},{24,8},{1,17},{9,25},{17,1},{25,9},{2,18},{10... | collective-permute-start | bytes 3145736 | tf_op jit(solution)/shard_map/ppermute | solution.py:393
  372.4 67.4 %collective-permute-start.26 = (bf16[256,2048]{1,0:T(8,128)(2,1)S(1)}, bf16[256,2048]{1,0:T(8,128)(2,1)S(1)}, u32[]{:S(2)}, u32[]{:S(2)}) collective-permute-start(bf16[256,2048]{1,0:T(8,128)(2,1)S(1)} %collective-permute-done.24), channel_id=1, source_target_pairs={{0,16},{8,24},{16,0},{24,8},{1,17},{9,25},{17,1},{25,9},{2,18},{10... | collective-permute-start | bytes 3145736 | tf_op jit(solution)/shard_map/ppermute | solution.py:393
  381.5 89.2 %collective-permute-start.30 = (bf16[512,1024]{1,0:T(8,128)(2,1)}, bf16[512,1024]{1,0:T(8,128)(2,1)}, u32[]{:S(2)}, u32[]{:S(2)}) collective-permute-start(bf16[512,1024]{1,0:T(8,128)(2,1)} %get-tuple-element.143), channel_id=1, source_target_pairs={{0,8},{8,0},{16,24},{24,16},{1,9},{9,1},{17,25},{25,17},{2,10},{10... | collective-permute-start | bytes 3145736 | tf_op jit(solution)/shard_map/ppermute | solution.py:393
  394.8 62.7 %collective-permute-start.34 = (bf16[256,2048]{1,0:T(8,128)(2,1)}, bf16[256,2048]{1,0:T(8,128)(2,1)}, u32[]{:S(2)}, u32[]{:S(2)}) collective-permute-start(bf16[256,2048]{1,0:T(8,128)(2,1)} %get-tuple-element.139), channel_id=1, source_target_pairs={{0,16},{8,24},{16,0},{24,8},{1,17},{9,25},{17,1},{25,9},{2,18},{10... | collective-permute-start | bytes 3145736 | tf_op jit(solution)/shard_map/ppermute | solution.py:393
  439.8 26.3 %collective-permute-start.29 = (bf16[512,1024]{1,0:T(8,128)(2,1)}, bf16[512,1024]{1,0:T(8,128)(2,1)}, u32[]{:S(2)}, u32[]{:S(2)}) collective-permute-start(bf16[512,1024]{1,0:T(8,128)(2,1)} %collective-permute-done.28), channel_id=1, source_target_pairs={{0,8},{8,0},{16,24},{24,16},{1,9},{9,1},{17,25},{25,17},{2,10},{10... | collective-permute-start | bytes 3145736 | tf_op jit(solution)/shard_map/ppermute | solution.py:393
  449.4 78.2 %collective-permute-start.33 = (bf16[256,2048]{1,0:T(8,128)(2,1)}, bf16[256,2048]{1,0:T(8,128)(2,1)S(1)}, u32[]{:S(2)}, u32[]{:S(2)}) collective-permute-start(bf16[256,2048]{1,0:T(8,128)(2,1)} %get-tuple-element.139), channel_id=1, source_target_pairs={{0,8},{8,0},{16,24},{24,16},{1,9},{9,1},{17,25},{25,17},{2,10},{10... | collective-permute-start | bytes 3145736 | tf_op jit(solution)/shard_map/ppermute | solution.py:393
  450.0 60.9 %collective-permute-start.32 = (bf16[512,1024]{1,0:T(8,128)(2,1)}, bf16[512,1024]{1,0:T(8,128)(2,1)S(1)}, u32[]{:S(2)}, u32[]{:S(2)}) collective-permute-start(bf16[512,1024]{1,0:T(8,128)(2,1)} %collective-permute-done.31), channel_id=1, source_target_pairs={{0,8},{8,0},{16,24},{24,16},{1,9},{9,1},{17,25},{25,17},{2,10},{10... | collective-permute-start | bytes 3145736 | tf_op jit(solution)/shard_map/ppermute | solution.py:393
  457.5 70.1 %collective-permute-start.35 = (bf16[256,2048]{1,0:T(8,128)(2,1)}, bf16[256,2048]{1,0:T(8,128)(2,1)S(1)}, u32[]{:S(2)}, u32[]{:S(2)}) collective-permute-start(bf16[256,2048]{1,0:T(8,128)(2,1)} %collective-permute-done.34), channel_id=1, source_target_pairs={{0,8},{8,0},{16,24},{24,16},{1,9},{9,1},{17,25},{25,17},{2,10},{10... | collective-permute-start | bytes 3145736 | tf_op jit(solution)/shard_map/ppermute | solution.py:393
  589.0 194.6 %reduce-scatter.11.cloned.1.call-start = ((), (), s32[]{:S(2)}) async-start(), calls=%async_computation.16 | async-start | bytes 9437184 | tf_op jit(solution)/shard_map/reduce_scatter | solution.py:695
  686.5 414.1 %reduce-scatter.13.cloned.1.call-start = ((), (), s32[]{:S(2)}) async-start(), calls=%async_computation.17 | async-start | bytes 2359296 | tf_op jit(solution)/shard_map/reduce_scatter | solution.py:702
  704.8 416.5 %reduce-scatter.17.cloned.1.call-start = ((), (), s32[]{:S(2)}) async-start(), calls=%async_computation.19 | async-start | bytes 2359296 | tf_op jit(solution)/shard_map/reduce_scatter | solution.py:691
  709.1 447.3 %reduce-scatter.15.cloned.1.call-start = ((), (), s32[]{:S(2)}) async-start(), calls=%async_computation.18 | async-start | bytes 4718592 | tf_op jit(solution)/shard_map/reduce_scatter | solution.py:710
  803.8 357.9 %reduce-scatter.7.cloned.1.call-start = ((), (), s32[]{:S(2)}) async-start(), calls=%async_computation.13 | async-start | bytes 4718592 | tf_op jit(solution)/shard_map/reduce_scatter | solution.py:639
  829.6 92.3 %collective-permute-start.64 = (bf16[512,1024]{1,0:T(8,128)(2,1)}, bf16[512,1024]{1,0:T(8,128)(2,1)}, u32[]{:S(2)}, u32[]{:S(2)}) collective-permute-start(bf16[512,1024]{1,0:T(8,128)(2,1)} %convolution_convert_fusion.18), channel_id=1, source_target_pairs={{0,8},{8,0},{16,24},{24,16},{1,9},{9,1},{17,25},{25,17},{2,10},{10... | collective-permute-start | bytes 3145736 | tf_op jit(solution)/shard_map/ppermute | solution.py:393
  830.2 93.9 %collective-permute-start.58 = (bf16[512,1024]{1,0:T(8,128)(2,1)}, bf16[512,1024]{1,0:T(8,128)(2,1)}, u32[]{:S(2)}, u32[]{:S(2)}) collective-permute-start(bf16[512,1024]{1,0:T(8,128)(2,1)} %convolution_convert_fusion.26), channel_id=1, source_target_pairs={{0,8},{8,0},{16,24},{24,16},{1,9},{9,1},{17,25},{25,17},{2,10},{10... | collective-permute-start | bytes 3145736 | tf_op jit(solution)/shard_map/ppermute | solution.py:393
  831.6 136.9 %collective-permute-start.69 = (bf16[256,2048]{1,0:T(8,128)(2,1)}, bf16[256,2048]{1,0:T(8,128)(2,1)}, u32[]{:S(2)}, u32[]{:S(2)}) collective-permute-start(bf16[256,2048]{1,0:T(8,128)(2,1)} %convolution_convert_fusion.12), channel_id=1, source_target_pairs={{0,8},{8,0},{16,24},{24,16},{1,9},{9,1},{17,25},{25,17},{2,10},{10... | collective-permute-start | bytes 3145736 | tf_op jit(solution)/shard_map/ppermute | solution.py:393
  832.2 86.5 %collective-permute-start.70 = (bf16[256,2048]{1,0:T(8,128)(2,1)}, bf16[256,2048]{1,0:T(8,128)(2,1)}, u32[]{:S(2)}, u32[]{:S(2)}) collective-permute-start(bf16[256,2048]{1,0:T(8,128)(2,1)} %convolution_convert_fusion.10), channel_id=1, source_target_pairs={{0,8},{8,0},{16,24},{24,16},{1,9},{9,1},{17,25},{25,17},{2,10},{10... | collective-permute-start | bytes 3145736 | tf_op jit(solution)/shard_map/ppermute | solution.py:393
  857.2 89.7 %collective-permute-start.67 = (bf16[512,1024]{1,0:T(8,128)(2,1)}, bf16[512,1024]{1,0:T(8,128)(2,1)}, u32[]{:S(2)}, u32[]{:S(2)}) collective-permute-start(bf16[512,1024]{1,0:T(8,128)(2,1)} %convolution_convert_fusion.14), channel_id=1, source_target_pairs={{0,16},{8,24},{16,0},{24,8},{1,17},{9,25},{17,1},{25,9},{2,18},{10... | collective-permute-start | bytes 3145736 | tf_op jit(solution)/shard_map/ppermute | solution.py:393
  918.7 26.2 %collective-permute-start.73 = (bf16[256,2048]{1,0:T(8,128)(2,1)}, bf16[256,2048]{1,0:T(8,128)(2,1)S(1)}, u32[]{:S(2)}, u32[]{:S(2)}) collective-permute-start(bf16[256,2048]{1,0:T(8,128)(2,1)} %convolution_convert_fusion.6), channel_id=1, source_target_pairs={{0,16},{8,24},{16,0},{24,8},{1,17},{9,25},{17,1},{25,9},{2,18},{10... | collective-permute-start | bytes 3145736 | tf_op jit(solution)/shard_map/ppermute | solution.py:393
  921.9 45.5 %collective-permute-start.61 = (bf16[512,1024]{1,0:T(8,128)(2,1)S(1)}, bf16[512,1024]{1,0:T(8,128)(2,1)S(1)}, u32[]{:S(2)}, u32[]{:S(2)}) collective-permute-start(bf16[512,1024]{1,0:T(8,128)(2,1)S(1)} %copy-done.145), channel_id=1, source_target_pairs={{0,16},{8,24},{16,0},{24,8},{1,17},{9,25},{17,1},{25,9},{2,18},{10... | collective-permute-start | bytes 3145736 | tf_op jit(solution)/shard_map/ppermute | solution.py:393
  924.1 65.8 %collective-permute-start.72 = (bf16[256,2048]{1,0:T(8,128)(2,1)S(1)}, bf16[256,2048]{1,0:T(8,128)(2,1)S(1)}, u32[]{:S(2)}, u32[]{:S(2)}) collective-permute-start(bf16[256,2048]{1,0:T(8,128)(2,1)S(1)} %copy-done.83), channel_id=1, source_target_pairs={{0,16},{8,24},{16,0},{24,8},{1,17},{9,25},{17,1},{25,9},{2,18},{10... | collective-permute-start | bytes 3145736 | tf_op jit(solution)/shard_map/ppermute | solution.py:393
  945.0 67.4 %collective-permute-start.71 = (bf16[256,2048]{1,0:T(8,128)(2,1)S(1)}, bf16[256,2048]{1,0:T(8,128)(2,1)S(1)}, u32[]{:S(2)}, u32[]{:S(2)}) collective-permute-start(bf16[256,2048]{1,0:T(8,128)(2,1)S(1)} %add_convert_fusion.6), channel_id=1, source_target_pairs={{0,16},{8,24},{16,0},{24,8},{1,17},{9,25},{17,1},{25,9},{2,18},{10... | collective-permute-start | bytes 3145736 | tf_op jit(solution)/shard_map/ppermute | solution.py:393
  946.9 68.1 %collective-permute-start.74 = (bf16[256,2048]{1,0:T(8,128)(2,1)S(1)}, bf16[256,2048]{1,0:T(8,128)(2,1)S(1)}, u32[]{:S(2)}, u32[]{:S(2)}) collective-permute-start(bf16[256,2048]{1,0:T(8,128)(2,1)S(1)} %add_convert_fusion.5), channel_id=1, source_target_pairs={{0,8},{8,0},{16,24},{24,16},{1,9},{9,1},{17,25},{25,17},{2,10},{10... | collective-permute-start | bytes 3145736 | tf_op jit(solution)/shard_map/ppermute | solution.py:393
  967.4 49.5 %collective-permute-start.63 = (bf16[512,1024]{1,0:T(8,128)(2,1)S(1)}, bf16[512,1024]{1,0:T(8,128)(2,1)S(1)}, u32[]{:S(2)}, u32[]{:S(2)}) collective-permute-start(bf16[512,1024]{1,0:T(8,128)(2,1)S(1)} %copy-done.135), channel_id=1, source_target_pairs={{0,8},{8,0},{16,24},{24,16},{1,9},{9,1},{17,25},{25,17},{2,10},{10... | collective-permute-start | bytes 3145736 | tf_op jit(solution)/shard_map/ppermute | solution.py:393
  968.6 90.8 %collective-permute-start.66 = (bf16[512,1024]{1,0:T(8,128)(2,1)S(1)}, bf16[512,1024]{1,0:T(8,128)(2,1)S(1)}, u32[]{:S(2)}, u32[]{:S(2)}) collective-permute-start(bf16[512,1024]{1,0:T(8,128)(2,1)S(1)} %copy-done.136), channel_id=1, source_target_pairs={{0,16},{8,24},{16,0},{24,8},{1,17},{9,25},{17,1},{25,9},{2,18},{10... | collective-permute-start | bytes 3145736 | tf_op jit(solution)/shard_map/ppermute | solution.py:393
  989.9 67.4 %collective-permute-start.65 = (bf16[512,1024]{1,0:T(8,128)(2,1)S(1)}, bf16[512,1024]{1,0:T(8,128)(2,1)S(1)}, u32[]{:S(2)}, u32[]{:S(2)}) collective-permute-start(bf16[512,1024]{1,0:T(8,128)(2,1)S(1)} %add_convert_fusion.8), channel_id=1, source_target_pairs={{0,16},{8,24},{16,0},{24,8},{1,17},{9,25},{17,1},{25,9},{2,18},{10... | collective-permute-start | bytes 3145736 | tf_op jit(solution)/shard_map/ppermute | solution.py:393
  1012.4 47.8 %collective-permute-start.68 = (bf16[512,1024]{1,0:T(8,128)(2,1)S(1)}, bf16[512,1024]{1,0:T(8,128)(2,1)S(1)}, u32[]{:S(2)}, u32[]{:S(2)}) collective-permute-start(bf16[512,1024]{1,0:T(8,128)(2,1)S(1)} %add_convert_fusion.7), channel_id=1, source_target_pairs={{0,8},{8,0},{16,24},{24,16},{1,9},{9,1},{17,25},{25,17},{2,10},{10... | collective-permute-start | bytes 3145736 | tf_op jit(solution)/shard_map/ppermute | solution.py:393
  1015.0 50.3 %collective-permute-start.57 = (bf16[512,1024]{1,0:T(8,128)(2,1)S(1)}, bf16[512,1024]{1,0:T(8,128)(2,1)S(1)}, u32[]{:S(2)}, u32[]{:S(2)}) collective-permute-start(bf16[512,1024]{1,0:T(8,128)(2,1)S(1)} %copy-done.131), channel_id=1, source_target_pairs={{0,8},{8,0},{16,24},{24,16},{1,9},{9,1},{17,25},{25,17},{2,10},{10... | collective-permute-start | bytes 3145736 | tf_op jit(solution)/shard_map/ppermute | solution.py:393
  1017.0 81.7 %collective-permute-start.60 = (bf16[512,1024]{1,0:T(8,128)(2,1)S(1)}, bf16[512,1024]{1,0:T(8,128)(2,1)S(1)}, u32[]{:S(2)}, u32[]{:S(2)}) collective-permute-start(bf16[512,1024]{1,0:T(8,128)(2,1)S(1)} %copy-done.134), channel_id=1, source_target_pairs={{0,16},{8,24},{16,0},{24,8},{1,17},{9,25},{17,1},{25,9},{2,18},{10... | collective-permute-start | bytes 3145736 | tf_op jit(solution)/shard_map/ppermute | solution.py:393
  1057.3 39.4 %collective-permute-start.59 = (bf16[512,1024]{1,0:T(8,128)(2,1)S(1)}, bf16[512,1024]{1,0:T(8,128)(2,1)S(1)}, u32[]{:S(2)}, u32[]{:S(2)}) collective-permute-start(bf16[512,1024]{1,0:T(8,128)(2,1)S(1)} %add_convert_fusion.10), channel_id=1, source_target_pairs={{0,16},{8,24},{16,0},{24,8},{1,17},{9,25},{17,1},{25,9},{2,18},{10... | collective-permute-start | bytes 3145736 | tf_op jit(solution)/shard_map/ppermute | solution.py:393
  1059.4 39.2 %collective-permute-start.62 = (bf16[512,1024]{1,0:T(8,128)(2,1)S(1)}, bf16[512,1024]{1,0:T(8,128)(2,1)S(1)}, u32[]{:S(2)}, u32[]{:S(2)}) collective-permute-start(bf16[512,1024]{1,0:T(8,128)(2,1)S(1)} %add_convert_fusion.9), channel_id=1, source_target_pairs={{0,8},{8,0},{16,24},{24,16},{1,9},{9,1},{17,25},{25,17},{2,10},{10... | collective-permute-start | bytes 3145736 | tf_op jit(solution)/shard_map/ppermute | solution.py:393
  (195 other events, 3772.6 us)
Sparse Core Ops, SparseCore 0:
  25.8 47.2 all-gather.9
  75.2 27.9 all-gather.7
  105.4 81.4 all-gather.11
  188.3 27.6 all-gather.13
  217.5 46.2 all-gather.17
  265.8 45.6 all-gather.15
  583.4 49.5 reduce-scatter.8
  686.6 96.8 reduce-scatter.10
  785.8 34.4 reduce-scatter.12
  822.5 34.7 reduce-scatter.16
  859.6 48.4 reduce-scatter.14
  910.2 48.3 reduce-scatter.6
where the time goes:
time: 1190 us; the launch traced here: 1180 us
  waiting for transfers between devices  668 us (56%)
  matrix products  173 us (15%)
  starting transfers between devices  115 us (10%)
  other arithmetic  66.7 us (6%)
  local copies, waits for them, and re-layouts  62.2 us (5%)
  Pallas kernels  49.3 us (4%)
  blocking collectives  28.3 us (2%)
  between operations  16.4 us (1%)
    ppermute x75, waiting for transfers between devices, exchange(): lax.ppermute(array, 'head', [(at, at ^ offset) for at in range(count)])  461 us
    ppermute x75, starting transfers between devices, exchange(): lax.ppermute(array, 'head', [(at, at ^ offset) for at in range(count)])  91 us
    reduce_scatter x1, waiting for transfers between devices, layer(): lax.psum_scatter(pairs_back, 'blk', scatter_dimension=0, tiled=True)  74.3 us
    all_gather x1, waiting for transfers between devices, layer(): pairs_all = lax.all_gather(pairs, 'blk', axis=0, tiled=True)  66.8 us
    dot_general x24, matrix products, pieces_of(): jnp.dot(left[:, offset * size:(offset + 1) * size].T, right, preferred_el...  48.5 us
    reduce_scatter x1, waiting for transfers between devices, layer(): lax.psum_scatter(incoming.astype(bf16).reshape(blocks * rows, width), 'bl...  38.2 us
  transfers between devices with their start and end apart: 89, of which 42 were waited for; matrix products, arithmetic and copies ran while one was open for 19% of the time, Pallas kernels for 3%

commit v1 on v0

--- a/solution.py
+++ b/solution.py
@@ -135,6 +135,67 @@
         partial(raw_kernel, count=len(inner), width=width, paired=paired),
         out_shape=jax.ShapeDtypeStruct((group, columns * (2 if paired else 1)), jnp.bfloat16),
     )(*inner, scaled, raw, factors, *extra)
+
+
+def norm_kernel(*refs, count):
+    scale, out = refs[count], refs[count + 1]
+    rows, width = refs[0].shape
+    for place in range(count):
+        value = refs[place][...].astype(jnp.float32)
+        square = jnp.sum(value * value, axis=1, keepdims=True)
+        factor = lax.rsqrt(square / width + norm_eps)
+        out[place * rows : (place + 1) * rows, :] = (value * factor * scale[...]).astype(
+            jnp.bfloat16
+        )
+
+
+def norm_rows(pieces, scale):
+    rows, width = pieces[0].shape
+    return pl.pallas_call(
+        partial(norm_kernel, count=len(pieces)),
+        out_shape=jax.ShapeDtypeStruct((rows * len(pieces), width), jnp.bfloat16),
+        name="norm_rows",
+    )(*pieces, scale[None])
+
+
+def project_kernel(normed, weight, raw, square, total):
+    step = pl.program_id(0)
+
+    @pl.when(step == 0)
+    def start():
+        total[...] = jnp.zeros_like(total)
+
+    value = jnp.dot(normed[...], weight[...], preferred_element_type=jnp.float32)
+    raw[...] = value
+    for at in range(0, value.shape[1], HDIM):
+        total[...] += value[:, at : at + HDIM] * value[:, at : at + HDIM]
+
+    @pl.when(step == pl.num_programs(0) - 1)
+    def finish():
+        sums = jnp.sum(total[...], axis=1, keepdims=True)
+        square[...] = jnp.transpose(jnp.broadcast_to(sums, total.shape))[:1, :]
+
+
+def project(normed, weight, columns):
+    group, width = normed.shape
+    block = min(columns, 256)
+    return pl.pallas_call(
+        project_kernel,
+        grid=(columns // block,),
+        in_specs=[
+            pl.BlockSpec((group, width), lambda step: (0, 0)),
+            pl.BlockSpec((width, block), lambda step: (0, step)),
+        ],
+        out_specs=[
+            pl.BlockSpec((group, block), lambda step: (0, step)),
+            pl.BlockSpec((1, group), lambda step: (0, 0)),
+        ],
+        out_shape=[
+            jax.ShapeDtypeStruct((group, columns), jnp.float32),
+            jax.ShapeDtypeStruct((1, group), jnp.float32),
+        ],
+        scratch_shapes=[pltpu.VMEM((group, HDIM), jnp.float32)],
+    )(normed, weight)
 
 
 def slot_codes(routes, ordering, experts, capacity):
@@ -528,15 +589,19 @@
         ],
         axis=1,
     ).reshape(1, -1)
-    small = lax.all_gather(small, "blk", axis=0, tiled=True)
+    codes = slot_codes(expert_routes, slot_order, experts, capacity).astype(bf16)
+    sizes = small.shape[1]
+    small = lax.all_gather(
+        jnp.concatenate([small, codes.reshape(1, -1)], axis=1), "blk", axis=0, tiled=True
+    )
+    codes = small[:, sizes:].reshape(blocks, rows, experts).astype(jnp.int32)
+    small = small[:, :sizes]
     small = jnp.stack(absolute(head_pieces(small))).reshape(width, 4 + experts)
     mixing_scale = small[:, 0].astype(f32)
     routing_scale = small[:, 3].astype(f32)
     query_scale = lax.dynamic_slice_in_dim(small[:, 1], head_at * columns, columns).astype(f32)
     key_scale = lax.dynamic_slice_in_dim(small[:, 2], head_at * columns, columns).astype(f32)
     router_full = small[:, 4:]
-    codes = slot_codes(expert_routes, slot_order, experts, capacity)
-    codes = lax.all_gather(codes, "blk", axis=0, tiled=True).reshape(blocks, rows, experts)
     codes_here = lax.dynamic_slice_in_dim(codes, block_at * local_experts, local_experts, 2)
 
     key_index = jnp.transpose(
@@ -554,19 +619,17 @@
         for weight in (gate_weight, up_weight, down_weight)
     )
 
-    token_group = jnp.concatenate(token_pieces, axis=0).astype(f32)
-    token_factor = rms_factor(jnp.sum(token_group * token_group, axis=-1, keepdims=True), width)
-    normed = (token_group * token_factor * mixing_scale).astype(bf16)
+    normed = norm_rows(token_pieces, mixing_scale)
     normed_moved = move_columns(normed, heads_axis, blocks, part)
-    key_raw = jnp.dot(normed, pair_full[:, :columns], preferred_element_type=f32)
+    key_raw, key_square = project(normed, pair_full, columns)
     value_heads = jnp.dot(normed, pair_full[:, columns:], preferred_element_type=f32)
     value_heads = value_heads.astype(bf16)
-    key_squares = head_pieces(jnp.sum(key_raw * key_raw, axis=-1)[None])
+    key_squares = head_pieces(key_square)
     pairs, key_factor = rope_forward(
         key_squares, key_raw, key_scale, cosine, sine_part, value_heads, width
     )
-    query_raw = jnp.dot(normed, query_full, preferred_element_type=f32)
-    query_squares = head_pieces(jnp.sum(query_raw * query_raw, axis=-1)[None])
+    query_raw, query_square = project(normed, query_full, columns)
+    query_squares = head_pieces(query_square)
     query_heads, query_factor = rope_forward(
         query_squares, query_raw, query_scale, cosine, sine_part, None, width
     )

time: 1190 us -> 1180 us (level)
  waiting for transfers between devices: 668 us -> 685 us
  blocking collectives: 28.3 us -> 14.8 us
  Pallas kernels: 49.3 us -> 62 us
    ppermute x75, waiting for transfers between devices: 461 us -> 483 us  [exchange(): lax.ppermute(array, 'head', [(at, at ^ offset) for at in range(count)])]
    all_gather x2 -> x1, blocking collectives: 28.3 us -> 14.8 us  [layer(): lax.all_gather(jnp.concatenate([small, codes.reshape(1, -1)], axis=1), 'b...]
    pallas_call x0 -> x3, Pallas kernels: none -> 12.5 us  [the longest x2 8.94 us: project(): pl.pallas_call(project_kernel, grid=(columns // block,), in_specs=[pl.Blo...]
  transfers between devices with their start and end apart: 89 -> 89, of which waited for: 42 -> 47; matrix products, arithmetic and copies ran while one was open for 19% -> 18% of each run, Pallas kernels for 3% -> 4%
where the time goes in v1:
time: 1180 us; the launch traced here: 1170 us
  waiting for transfers between devices  685 us (58%)
  matrix products  167 us (14%)
  starting transfers between devices  106 us (9%)
  Pallas kernels  62 us (5%)
  other arithmetic  61.7 us (5%)
  local copies, waits for them, and re-layouts  61.5 us (5%)
  between operations  16.4 us (1%)
  blocking collectives  14.8 us (1%)
    ppermute x75, waiting for transfers between devices, exchange(): lax.ppermute(array, 'head', [(at, at ^ offset) for at in range(count)])  483 us
    ppermute x75, starting transfers between devices, exchange(): lax.ppermute(array, 'head', [(at, at ^ offset) for at in range(count)])  92.1 us
    reduce_scatter x1, waiting for transfers between devices, layer(): lax.psum_scatter(pairs_back, 'blk', scatter_dimension=0, tiled=True)  71.5 us
    all_gather x1, waiting for transfers between devices, layer(): pairs_all = lax.all_gather(pairs, 'blk', axis=0, tiled=True)  65.7 us
    dot_general x24, matrix products, pieces_of(): jnp.dot(left[:, offset * size:(offset + 1) * size].T, right, preferred_el...  47.2 us
    reduce_scatter x1, waiting for transfers between devices, layer(): lax.psum_scatter(incoming.astype(bf16).reshape(blocks * rows, width), 'bl...  38.3 us
  transfers between devices with their start and end apart: 89, of which 47 were waited for; matrix products, arithmetic and copies ran while one was open for 18% of the time, Pallas kernels for 4%

profile of v1, /device:TPU:0, one launch (start us, length us, event | category | flops | bytes accessed | tf_op | source)
XLA Modules:
  0.0 1174.0 jit_solution(18016633107936462856)
XLA Ops:
  18.1 4.7 collective-permute-done.6
  30.0 14.8 %all-gather = bf16[8,1,3328]{2,1,0:T(2,128)(2,1)S(1)} all-gather(bf16[1,1,3328]{2,1,0:T(2,128)(2,1)S(1)} %maximum_bitcast_fusion), channel_id=1, replica_groups=mesh['head'=4,'blk'=8] {'blk'}, dimensions={0}, use_global_device_ids=true | all-gather | bytes 59904 | tf_op jit(solution)/shard_map/all_gather | solution.py:594
  63.7 10.5 collective-permute-done.2.refs_3_
  78.6 4.9 copy.96
  83.5 4.6 shard_map.292
  121.6 65.7 %all-gather.12.cloned.1.call-done.pairs = bf16[4096,1024]{1,0:T(8,128)(2,1)} async-done(((bf16[512,1024]{1,0:T(8,128)(2,1)}), bf16[4096,1024]{1,0:T(8,128)(2,1)}) %all-gather.12.cloned.1.call-update) | async-done | bytes 8388624 | tf_op jit(solution)/shard_map/all_gather | solution.py:636
  189.0 11.4 attend_forward.1
  200.3 16.0 %all-gather.14.cloned.1.call-done = bf16[512,2048]{1,0:T(8,128)(2,1)} async-done(((bf16[64,2048]{1,0:T(8,128)(2,1)}), bf16[512,2048]{1,0:T(8,128)(2,1)}) %all-gather.14.cloned.1.call-update) | async-done | bytes 2097168 | tf_op jit(solution)/shard_map/all_gather | solution.py:573
  223.1 11.3 collective-permute-done.15
  234.4 11.6 collective-permute-done.17
  263.5 38.7 %collective-permute-done.18 = bf16[512,1024]{1,0:T(8,128)(2,1)} collective-permute-done((bf16[512,1024]{1,0:T(8,128)(2,1)}, bf16[512,1024]{1,0:T(8,128)(2,1)}, u32[]{:S(2)}, u32[]{:S(2)}) %collective-permute-start.18) | collective-permute-done | bytes 1048608 | tf_op jit(solution)/shard_map/ppermute | solution.py:454
  303.7 4.7 fusion.56
  316.6 5.7 collective-permute-done.21
  329.4 4.7 fusion.39
  334.1 16.0 %collective-permute-done.22 = bf16[512,1024]{1,0:T(8,128)(2,1)S(1)} collective-permute-done((bf16[512,1024]{1,0:T(8,128)(2,1)}, bf16[512,1024]{1,0:T(8,128)(2,1)S(1)}, u32[]{:S(2)}, u32[]{:S(2)}) %collective-permute-start.22) | collective-permute-done | bytes 1048608 | tf_op jit(solution)/shard_map/ppermute | solution.py:454
  352.1 20.4 %collective-permute-done.23 = bf16[512,1024]{1,0:T(8,128)(2,1)S(1)} collective-permute-done((bf16[512,1024]{1,0:T(8,128)(2,1)}, bf16[512,1024]{1,0:T(8,128)(2,1)S(1)}, u32[]{:S(2)}, u32[]{:S(2)}) %collective-permute-start.23) | collective-permute-done | bytes 1048608 | tf_op jit(solution)/shard_map/ppermute | solution.py:454
  374.2 5.7 multiply_convert_fusion.5
  383.4 11.6 collective-permute-done.25
  396.7 43.3 %collective-permute-done.26 = bf16[256,2048]{1,0:T(8,128)(2,1)S(1)} collective-permute-done((bf16[256,2048]{1,0:T(8,128)(2,1)S(1)}, bf16[256,2048]{1,0:T(8,128)(2,1)S(1)}, u32[]{:S(2)}, u32[]{:S(2)}) %collective-permute-start.26) | collective-permute-done | bytes 1048608 | tf_op jit(solution)/shard_map/ppermute | solution.py:454
  441.6 4.6 fusion.3
  451.9 5.9 collective-permute-done.34
  459.4 6.9 collective-permute-done.29
  466.3 4.6 fusion.35
  470.9 40.2 %collective-permute-done.32 = bf16[512,1024]{1,0:T(8,128)(2,1)S(1)} collective-permute-done((bf16[512,1024]{1,0:T(8,128)(2,1)}, bf16[512,1024]{1,0:T(8,128)(2,1)S(1)}, u32[]{:S(2)}, u32[]{:S(2)}) %collective-permute-start.32) | collective-permute-done | bytes 1048608 | tf_op jit(solution)/shard_map/ppermute | solution.py:454
  511.2 6.3 multiply_convert_fusion.4
  529.0 5.5 fusion.5
  535.0 5.9 fusion.4
  540.9 7.2 fusion.32
  552.8 5.4 fusion.37
  558.2 5.1 add_convert_fusion.3
  567.5 7.3 fusion.33
  574.8 5.1 add_convert_fusion.2
  589.2 5.7 all-to-all-done
  595.0 38.3 %reduce-scatter.9.cloned.1.call-done = bf16[128,2048]{1,0:T(8,128)(2,1)} async-done(((bf16[1024,2048]{1,0:T(8,128)(2,1)}), bf16[128,2048]{1,0:T(8,128)(2,1)}) %reduce-scatter.9.cloned.1.call-update) | async-done | bytes 524304 | tf_op jit(solution)/shard_map/reduce_scatter | solution.py:696
  641.0 12.2 %collective-permute-done.38 = bf16[128,2048]{1,0:T(8,128)(2,1)S(1)} collective-permute-done((bf16[128,2048]{1,0:T(8,128)(2,1)S(1)}, bf16[128,2048]{1,0:T(8,128)(2,1)S(1)}, u32[]{:S(2)}, u32[]{:S(2)}) %collective-permute-start.38) | collective-permute-done | bytes 524320 | tf_op jit(solution)/shard_map/ppermute | solution.py:454
  653.3 8.2 collective-permute-done.37
  666.5 19.6 %attend_backward.1 = (bf16[512,512]{1,0:T(8,128)(2,1)}, bf16[4096,1024]{1,0:T(8,128)(2,1)}) custom-call(s32[2,16]{1,0:T(2,128)} %copy-done.95, bf16[512,512]{1,0:T(8,128)(2,1)} %get-tuple-element.35.query, bf16[4096,1024]{1,0:T(8,128)(2,1)} %all-gather.12.cloned.1.call-done.pairs, bf16[512,512]{1,0:T(8,128)(2,1)} %convolution_convert_fusion.30.grad, ...), custom_call_target="tpu_custom_call" | custom-call | tf_op jit(solution)/shard_map/attend_backward/pallas_call | solution.py:409
  711.7 71.5 %reduce-scatter.11.cloned.1.call-done.back.refs_7_ = bf16[512,1024]{1,0:T(8,128)(2,1)} async-done(((bf16[4096,1024]{1,0:T(8,128)(2,1)}), bf16[512,1024]{1,0:T(8,128)(2,1)}) %reduce-scatter.11.cloned.1.call-update) | async-done | bytes 1048592 | tf_op jit(solution)/shard_map/reduce_scatter | solution.py:758
  797.1 6.3 convolution_convert_fusion
  864.2 53.7 %collective-permute-done.70 = bf16[256,2048]{1,0:T(8,128)(2,1)} collective-permute-done((bf16[256,2048]{1,0:T(8,128)(2,1)}, bf16[256,2048]{1,0:T(8,128)(2,1)}, u32[]{:S(2)}, u32[]{:S(2)}) %collective-permute-start.70) | collective-permute-done | bytes 1048608 | tf_op jit(solution)/shard_map/ppermute | solution.py:454
  926.6 17.6 %collective-permute-done.73 = bf16[256,2048]{1,0:T(8,128)(2,1)S(1)} collective-permute-done((bf16[256,2048]{1,0:T(8,128)(2,1)}, bf16[256,2048]{1,0:T(8,128)(2,1)S(1)}, u32[]{:S(2)}, u32[]{:S(2)}) %collective-permute-start.73) | collective-permute-done | bytes 1048608 | tf_op jit(solution)/shard_map/ppermute | solution.py:454
  948.5 18.2 %collective-permute-done.61 = bf16[512,1024]{1,0:T(8,128)(2,1)S(1)} collective-permute-done((bf16[512,1024]{1,0:T(8,128)(2,1)S(1)}, bf16[512,1024]{1,0:T(8,128)(2,1)S(1)}, u32[]{:S(2)}, u32[]{:S(2)}) %collective-permute-start.61) | collective-permute-done | bytes 1048608 | tf_op jit(solution)/shard_map/ppermute | solution.py:454
  969.3 19.8 %collective-permute-done.72 = bf16[256,2048]{1,0:T(8,128)(2,1)S(1)} collective-permute-done((bf16[256,2048]{1,0:T(8,128)(2,1)S(1)}, bf16[256,2048]{1,0:T(8,128)(2,1)S(1)}, u32[]{:S(2)}, u32[]{:S(2)}) %collective-permute-start.72) | collective-permute-done | bytes 1048608 | tf_op jit(solution)/shard_map/ppermute | solution.py:454
  990.6 21.0 %collective-permute-done.71 = bf16[256,2048]{1,0:T(8,128)(2,1)S(1)} collective-permute-done((bf16[256,2048]{1,0:T(8,128)(2,1)S(1)}, bf16[256,2048]{1,0:T(8,128)(2,1)S(1)}, u32[]{:S(2)}, u32[]{:S(2)}) %collective-permute-start.71) | collective-permute-done | bytes 1048608 | tf_op jit(solution)/shard_map/ppermute | solution.py:454
  1017.8 38.7 %collective-permute-done.65 = bf16[512,1024]{1,0:T(8,128)(2,1)S(1)} collective-permute-done((bf16[512,1024]{1,0:T(8,128)(2,1)S(1)}, bf16[512,1024]{1,0:T(8,128)(2,1)S(1)}, u32[]{:S(2)}, u32[]{:S(2)}) %collective-permute-start.65) | collective-permute-done | bytes 1048608 | tf_op jit(solution)/shard_map/ppermute | solution.py:454
  1064.6 31.4 %collective-permute-done.59 = bf16[512,1024]{1,0:T(8,128)(2,1)S(1)} collective-permute-done((bf16[512,1024]{1,0:T(8,128)(2,1)S(1)}, bf16[512,1024]{1,0:T(8,128)(2,1)S(1)}, u32[]{:S(2)}, u32[]{:S(2)}) %collective-permute-start.59) | collective-permute-done | bytes 1048608 | tf_op jit(solution)/shard_map/ppermute | solution.py:454
  1125.3 7.4 collective-permute-done.47
  1144.8 9.3 all-to-all-start.1
  (657 shorter events, 362.5 us)
Async XLA Ops:
  7.2 71.4 %all-gather.10.cloned.1.call-start = ((), (), s32[]{:S(2)}) async-start(), calls=%async_computation.9 | async-start | bytes 4718592 | tf_op jit(solution)/shard_map/all_gather | solution.py:576
  25.7 78.3 %all-gather.8.cloned.1.call-start = ((), (), s32[]{:S(2)}) async-start(), calls=%async_computation.8 | async-start | bytes 2359296 | tf_op jit(solution)/shard_map/all_gather | solution.py:578
  29.5 157.8 %all-gather.12.cloned.1.call-start = ((), (), s32[]{:S(2)}) async-start(), calls=%async_computation.10 | async-start | bytes 9437184 | tf_op jit(solution)/shard_map/all_gather | solution.py:636
  99.1 117.2 %all-gather.14.cloned.1.call-start = ((), (), s32[]{:S(2)}) async-start(), calls=%async_computation.11 | async-start | bytes 2359296 | tf_op jit(solution)/shard_map/all_gather | solution.py:573
  99.7 204.0 %all-gather.18.cloned.1.call-start = ((), (), s32[]{:S(2)}) async-start(), calls=%async_computation.14 | async-start | bytes 4718592 | tf_op jit(solution)/shard_map/all_gather | solution.py:580
  100.3 211.6 %all-gather.16.cloned.1.call-start = ((), (), s32[]{:S(2)}) async-start(), calls=%async_computation.12 | async-start | bytes 4718592 | tf_op jit(solution)/shard_map/all_gather | solution.py:645
  251.3 382.0 %reduce-scatter.9.cloned.1.call-start = ((), (), s32[]{:S(2)}) async-start(), calls=%async_computation.15 | async-start | bytes 4718592 | tf_op jit(solution)/shard_map/reduce_scatter | solution.py:696
  252.9 129.0 %collective-permute-start.28 = (bf16[512,1024]{1,0:T(8,128)(2,1)}, bf16[512,1024]{1,0:T(8,128)(2,1)}, u32[]{:S(2)}, u32[]{:S(2)}) collective-permute-start(bf16[512,1024]{1,0:T(8,128)(2,1)} %get-tuple-element.165), channel_id=1, source_target_pairs={{0,16},{8,24},{16,0},{24,8},{1,17},{9,25},{17,1},{25,9},{2,18},{10... | collective-permute-start | bytes 3145736 | tf_op jit(solution)/shard_map/ppermute | solution.py:454
  253.4 196.5 %collective-permute-start.27 = (bf16[512,1024]{1,0:T(8,128)(2,1)}, bf16[512,1024]{1,0:T(8,128)(2,1)}, u32[]{:S(2)}, u32[]{:S(2)}) collective-permute-start(bf16[512,1024]{1,0:T(8,128)(2,1)} %get-tuple-element.165), channel_id=1, source_target_pairs={{0,8},{8,0},{16,24},{24,16},{1,9},{9,1},{17,25},{25,17},{2,10},{10... | collective-permute-start | bytes 3145736 | tf_op jit(solution)/shard_map/ppermute | solution.py:454
  254.9 60.1 %collective-permute-start.19 = (bf16[512,1024]{1,0:T(8,128)(2,1)}, bf16[512,1024]{1,0:T(8,128)(2,1)}, u32[]{:S(2)}, u32[]{:S(2)}) collective-permute-start(bf16[512,1024]{1,0:T(8,128)(2,1)} %get-tuple-element.166), channel_id=1, source_target_pairs={{0,16},{8,24},{16,0},{24,8},{1,17},{9,25},{17,1},{25,9},{2,18},{10... | collective-permute-start | bytes 3145736 | tf_op jit(solution)/shard_map/ppermute | solution.py:454
  256.4 45.8 %collective-permute-start.18 = (bf16[512,1024]{1,0:T(8,128)(2,1)}, bf16[512,1024]{1,0:T(8,128)(2,1)}, u32[]{:S(2)}, u32[]{:S(2)}) collective-permute-start(bf16[512,1024]{1,0:T(8,128)(2,1)} %get-tuple-element.166), channel_id=1, source_target_pairs={{0,8},{8,0},{16,24},{24,16},{1,9},{9,1},{17,25},{25,17},{2,10},{10... | collective-permute-start | bytes 3145736 | tf_op jit(solution)/shard_map/ppermute | solution.py:454
  258.5 63.8 %collective-permute-start.21 = (bf16[512,1024]{1,0:T(8,128)(2,1)}, bf16[512,1024]{1,0:T(8,128)(2,1)}, u32[]{:S(2)}, u32[]{:S(2)}) collective-permute-start(bf16[512,1024]{1,0:T(8,128)(2,1)} %get-tuple-element.168), channel_id=1, source_target_pairs={{0,8},{8,0},{16,24},{24,16},{1,9},{9,1},{17,25},{25,17},{2,10},{10... | collective-permute-start | bytes 3145736 | tf_op jit(solution)/shard_map/ppermute | solution.py:454
  302.2 25.6 %collective-permute-start.20 = (bf16[512,1024]{1,0:T(8,128)(2,1)}, bf16[512,1024]{1,0:T(8,128)(2,1)}, u32[]{:S(2)}, u32[]{:S(2)}) collective-permute-start(bf16[512,1024]{1,0:T(8,128)(2,1)} %collective-permute-done.18), channel_id=1, source_target_pairs={{0,16},{8,24},{16,0},{24,8},{1,17},{9,25},{17,1},{25,9},{2,18},{10... | collective-permute-start | bytes 3145736 | tf_op jit(solution)/shard_map/ppermute | solution.py:454
  315.1 35.0 %collective-permute-start.22 = (bf16[512,1024]{1,0:T(8,128)(2,1)}, bf16[512,1024]{1,0:T(8,128)(2,1)S(1)}, u32[]{:S(2)}, u32[]{:S(2)}) collective-permute-start(bf16[512,1024]{1,0:T(8,128)(2,1)} %get-tuple-element.168), channel_id=1, source_target_pairs={{0,16},{8,24},{16,0},{24,8},{1,17},{9,25},{17,1},{25,9},{2,18},{10... | collective-permute-start | bytes 3145736 | tf_op jit(solution)/shard_map/ppermute | solution.py:454
  322.3 29.4 %collective-permute-start.24 = (bf16[256,2048]{1,0:T(8,128)(2,1)S(1)}, bf16[256,2048]{1,0:T(8,128)(2,1)S(1)}, u32[]{:S(2)}, u32[]{:S(2)}) collective-permute-start(bf16[256,2048]{1,0:T(8,128)(2,1)S(1)} %copy-done.79), channel_id=1, source_target_pairs={{0,8},{8,0},{16,24},{24,16},{1,9},{9,1},{17,25},{25,17},{2,10},{10... | collective-permute-start | bytes 3145736 | tf_op jit(solution)/shard_map/ppermute | solution.py:454
  327.7 44.8 %collective-permute-start.23 = (bf16[512,1024]{1,0:T(8,128)(2,1)}, bf16[512,1024]{1,0:T(8,128)(2,1)S(1)}, u32[]{:S(2)}, u32[]{:S(2)}) collective-permute-start(bf16[512,1024]{1,0:T(8,128)(2,1)} %collective-permute-done.21), channel_id=1, source_target_pairs={{0,16},{8,24},{16,0},{24,8},{1,17},{9,25},{17,1},{25,9},{2,18},{10... | collective-permute-start | bytes 3145736 | tf_op jit(solution)/shard_map/ppermute | solution.py:454
  350.1 44.9 %collective-permute-start.25 = (bf16[256,2048]{1,0:T(8,128)(2,1)S(1)}, bf16[256,2048]{1,0:T(8,128)(2,1)S(1)}, u32[]{:S(2)}, u32[]{:S(2)}) collective-permute-start(bf16[256,2048]{1,0:T(8,128)(2,1)S(1)} %copy-done.79), channel_id=1, source_target_pairs={{0,16},{8,24},{16,0},{24,8},{1,17},{9,25},{17,1},{25,9},{2,18},{10... | collective-permute-start | bytes 3145736 | tf_op jit(solution)/shard_map/ppermute | solution.py:454
  351.7 98.5 %collective-permute-start.31 = (bf16[512,1024]{1,0:T(8,128)(2,1)}, bf16[512,1024]{1,0:T(8,128)(2,1)}, u32[]{:S(2)}, u32[]{:S(2)}) collective-permute-start(bf16[512,1024]{1,0:T(8,128)(2,1)} %get-tuple-element.167), channel_id=1, source_target_pairs={{0,16},{8,24},{16,0},{24,8},{1,17},{9,25},{17,1},{25,9},{2,18},{10... | collective-permute-start | bytes 3145736 | tf_op jit(solution)/shard_map/ppermute | solution.py:454
  372.6 67.4 %collective-permute-start.26 = (bf16[256,2048]{1,0:T(8,128)(2,1)S(1)}, bf16[256,2048]{1,0:T(8,128)(2,1)S(1)}, u32[]{:S(2)}, u32[]{:S(2)}) collective-permute-start(bf16[256,2048]{1,0:T(8,128)(2,1)S(1)} %collective-permute-done.24), channel_id=1, source_target_pairs={{0,16},{8,24},{16,0},{24,8},{1,17},{9,25},{17,1},{25,9},{2,18},{10... | collective-permute-start | bytes 3145736 | tf_op jit(solution)/shard_map/ppermute | solution.py:454
  381.9 89.0 %collective-permute-start.30 = (bf16[512,1024]{1,0:T(8,128)(2,1)}, bf16[512,1024]{1,0:T(8,128)(2,1)}, u32[]{:S(2)}, u32[]{:S(2)}) collective-permute-start(bf16[512,1024]{1,0:T(8,128)(2,1)} %get-tuple-element.167), channel_id=1, source_target_pairs={{0,8},{8,0},{16,24},{24,16},{1,9},{9,1},{17,25},{25,17},{2,10},{10... | collective-permute-start | bytes 3145736 | tf_op jit(solution)/shard_map/ppermute | solution.py:454
  395.0 62.8 %collective-permute-start.34 = (bf16[256,2048]{1,0:T(8,128)(2,1)}, bf16[256,2048]{1,0:T(8,128)(2,1)}, u32[]{:S(2)}, u32[]{:S(2)}) collective-permute-start(bf16[256,2048]{1,0:T(8,128)(2,1)} %get-tuple-element.163), channel_id=1, source_target_pairs={{0,16},{8,24},{16,0},{24,8},{1,17},{9,25},{17,1},{25,9},{2,18},{10... | collective-permute-start | bytes 3145736 | tf_op jit(solution)/shard_map/ppermute | solution.py:454
  440.0 26.3 %collective-permute-start.29 = (bf16[512,1024]{1,0:T(8,128)(2,1)}, bf16[512,1024]{1,0:T(8,128)(2,1)}, u32[]{:S(2)}, u32[]{:S(2)}) collective-permute-start(bf16[512,1024]{1,0:T(8,128)(2,1)} %collective-permute-done.28), channel_id=1, source_target_pairs={{0,8},{8,0},{16,24},{24,16},{1,9},{9,1},{17,25},{25,17},{2,10},{10... | collective-permute-start | bytes 3145736 | tf_op jit(solution)/shard_map/ppermute | solution.py:454
  449.8 77.7 %collective-permute-start.33 = (bf16[256,2048]{1,0:T(8,128)(2,1)}, bf16[256,2048]{1,0:T(8,128)(2,1)S(1)}, u32[]{:S(2)}, u32[]{:S(2)}) collective-permute-start(bf16[256,2048]{1,0:T(8,128)(2,1)} %get-tuple-element.163), channel_id=1, source_target_pairs={{0,8},{8,0},{16,24},{24,16},{1,9},{9,1},{17,25},{25,17},{2,10},{10... | collective-permute-start | bytes 3145736 | tf_op jit(solution)/shard_map/ppermute | solution.py:454
  450.3 60.9 %collective-permute-start.32 = (bf16[512,1024]{1,0:T(8,128)(2,1)}, bf16[512,1024]{1,0:T(8,128)(2,1)S(1)}, u32[]{:S(2)}, u32[]{:S(2)}) collective-permute-start(bf16[512,1024]{1,0:T(8,128)(2,1)} %collective-permute-done.31), channel_id=1, source_target_pairs={{0,8},{8,0},{16,24},{24,16},{1,9},{9,1},{17,25},{25,17},{2,10},{10... | collective-permute-start | bytes 3145736 | tf_op jit(solution)/shard_map/ppermute | solution.py:454
  457.8 69.7 %collective-permute-start.35 = (bf16[256,2048]{1,0:T(8,128)(2,1)}, bf16[256,2048]{1,0:T(8,128)(2,1)S(1)}, u32[]{:S(2)}, u32[]{:S(2)}) collective-permute-start(bf16[256,2048]{1,0:T(8,128)(2,1)} %collective-permute-done.34), channel_id=1, source_target_pairs={{0,8},{8,0},{16,24},{24,16},{1,9},{9,1},{17,25},{25,17},{2,10},{10... | collective-permute-start | bytes 3145736 | tf_op jit(solution)/shard_map/ppermute | solution.py:454
  589.2 194.0 %reduce-scatter.11.cloned.1.call-start = ((), (), s32[]{:S(2)}) async-start(), calls=%async_computation.16 | async-start | bytes 9437184 | tf_op jit(solution)/shard_map/reduce_scatter | solution.py:758
  686.2 413.6 %reduce-scatter.13.cloned.1.call-start = ((), (), s32[]{:S(2)}) async-start(), calls=%async_computation.17 | async-start | bytes 2359296 | tf_op jit(solution)/shard_map/reduce_scatter | solution.py:765
  707.4 410.6 %reduce-scatter.17.cloned.1.call-start = ((), (), s32[]{:S(2)}) async-start(), calls=%async_computation.19 | async-start | bytes 2359296 | tf_op jit(solution)/shard_map/reduce_scatter | solution.py:754
  711.6 442.5 %reduce-scatter.15.cloned.1.call-start = ((), (), s32[]{:S(2)}) async-start(), calls=%async_computation.18 | async-start | bytes 4718592 | tf_op jit(solution)/shard_map/reduce_scatter | solution.py:773
  803.4 355.4 %reduce-scatter.7.cloned.1.call-start = ((), (), s32[]{:S(2)}) async-start(), calls=%async_computation.13 | async-start | bytes 4718592 | tf_op jit(solution)/shard_map/reduce_scatter | solution.py:702
  828.8 92.3 %collective-permute-start.64 = (bf16[512,1024]{1,0:T(8,128)(2,1)}, bf16[512,1024]{1,0:T(8,128)(2,1)}, u32[]{:S(2)}, u32[]{:S(2)}) collective-permute-start(bf16[512,1024]{1,0:T(8,128)(2,1)} %convolution_convert_fusion.18), channel_id=1, source_target_pairs={{0,8},{8,0},{16,24},{24,16},{1,9},{9,1},{17,25},{25,17},{2,10},{10... | collective-permute-start | bytes 3145736 | tf_op jit(solution)/shard_map/ppermute | solution.py:454
  829.4 94.0 %collective-permute-start.58 = (bf16[512,1024]{1,0:T(8,128)(2,1)}, bf16[512,1024]{1,0:T(8,128)(2,1)}, u32[]{:S(2)}, u32[]{:S(2)}) collective-permute-start(bf16[512,1024]{1,0:T(8,128)(2,1)} %convolution_convert_fusion.26), channel_id=1, source_target_pairs={{0,8},{8,0},{16,24},{24,16},{1,9},{9,1},{17,25},{25,17},{2,10},{10... | collective-permute-start | bytes 3145736 | tf_op jit(solution)/shard_map/ppermute | solution.py:454
  830.9 136.9 %collective-permute-start.69 = (bf16[256,2048]{1,0:T(8,128)(2,1)}, bf16[256,2048]{1,0:T(8,128)(2,1)}, u32[]{:S(2)}, u32[]{:S(2)}) collective-permute-start(bf16[256,2048]{1,0:T(8,128)(2,1)} %convolution_convert_fusion.12), channel_id=1, source_target_pairs={{0,8},{8,0},{16,24},{24,16},{1,9},{9,1},{17,25},{25,17},{2,10},{10... | collective-permute-start | bytes 3145736 | tf_op jit(solution)/shard_map/ppermute | solution.py:454
  831.4 86.5 %collective-permute-start.70 = (bf16[256,2048]{1,0:T(8,128)(2,1)}, bf16[256,2048]{1,0:T(8,128)(2,1)}, u32[]{:S(2)}, u32[]{:S(2)}) collective-permute-start(bf16[256,2048]{1,0:T(8,128)(2,1)} %convolution_convert_fusion.10), channel_id=1, source_target_pairs={{0,8},{8,0},{16,24},{24,16},{1,9},{9,1},{17,25},{25,17},{2,10},{10... | collective-permute-start | bytes 3145736 | tf_op jit(solution)/shard_map/ppermute | solution.py:454
  856.3 89.9 %collective-permute-start.67 = (bf16[512,1024]{1,0:T(8,128)(2,1)}, bf16[512,1024]{1,0:T(8,128)(2,1)}, u32[]{:S(2)}, u32[]{:S(2)}) collective-permute-start(bf16[512,1024]{1,0:T(8,128)(2,1)} %convolution_convert_fusion.14), channel_id=1, source_target_pairs={{0,16},{8,24},{16,0},{24,8},{1,17},{9,25},{17,1},{25,9},{2,18},{10... | collective-permute-start | bytes 3145736 | tf_op jit(solution)/shard_map/ppermute | solution.py:454
  917.9 26.2 %collective-permute-start.73 = (bf16[256,2048]{1,0:T(8,128)(2,1)}, bf16[256,2048]{1,0:T(8,128)(2,1)S(1)}, u32[]{:S(2)}, u32[]{:S(2)}) collective-permute-start(bf16[256,2048]{1,0:T(8,128)(2,1)} %convolution_convert_fusion.6), channel_id=1, source_target_pairs={{0,16},{8,24},{16,0},{24,8},{1,17},{9,25},{17,1},{25,9},{2,18},{10... | collective-permute-start | bytes 3145736 | tf_op jit(solution)/shard_map/ppermute | solution.py:454
  921.1 45.5 %collective-permute-start.61 = (bf16[512,1024]{1,0:T(8,128)(2,1)S(1)}, bf16[512,1024]{1,0:T(8,128)(2,1)S(1)}, u32[]{:S(2)}, u32[]{:S(2)}) collective-permute-start(bf16[512,1024]{1,0:T(8,128)(2,1)S(1)} %copy-done.138), channel_id=1, source_target_pairs={{0,16},{8,24},{16,0},{24,8},{1,17},{9,25},{17,1},{25,9},{2,18},{10... | collective-permute-start | bytes 3145736 | tf_op jit(solution)/shard_map/ppermute | solution.py:454
  923.4 65.8 %collective-permute-start.72 = (bf16[256,2048]{1,0:T(8,128)(2,1)S(1)}, bf16[256,2048]{1,0:T(8,128)(2,1)S(1)}, u32[]{:S(2)}, u32[]{:S(2)}) collective-permute-start(bf16[256,2048]{1,0:T(8,128)(2,1)S(1)} %copy-done.81), channel_id=1, source_target_pairs={{0,16},{8,24},{16,0},{24,8},{1,17},{9,25},{17,1},{25,9},{2,18},{10... | collective-permute-start | bytes 3145736 | tf_op jit(solution)/shard_map/ppermute | solution.py:454
  944.2 67.4 %collective-permute-start.71 = (bf16[256,2048]{1,0:T(8,128)(2,1)S(1)}, bf16[256,2048]{1,0:T(8,128)(2,1)S(1)}, u32[]{:S(2)}, u32[]{:S(2)}) collective-permute-start(bf16[256,2048]{1,0:T(8,128)(2,1)S(1)} %add_convert_fusion.6), channel_id=1, source_target_pairs={{0,16},{8,24},{16,0},{24,8},{1,17},{9,25},{17,1},{25,9},{2,18},{10... | collective-permute-start | bytes 3145736 | tf_op jit(solution)/shard_map/ppermute | solution.py:454
  946.1 68.1 %collective-permute-start.74 = (bf16[256,2048]{1,0:T(8,128)(2,1)S(1)}, bf16[256,2048]{1,0:T(8,128)(2,1)S(1)}, u32[]{:S(2)}, u32[]{:S(2)}) collective-permute-start(bf16[256,2048]{1,0:T(8,128)(2,1)S(1)} %add_convert_fusion.5), channel_id=1, source_target_pairs={{0,8},{8,0},{16,24},{24,16},{1,9},{9,1},{17,25},{25,17},{2,10},{10... | collective-permute-start | bytes 3145736 | tf_op jit(solution)/shard_map/ppermute | solution.py:454
  966.7 49.6 %collective-permute-start.63 = (bf16[512,1024]{1,0:T(8,128)(2,1)S(1)}, bf16[512,1024]{1,0:T(8,128)(2,1)S(1)}, u32[]{:S(2)}, u32[]{:S(2)}) collective-permute-start(bf16[512,1024]{1,0:T(8,128)(2,1)S(1)} %copy-done.128), channel_id=1, source_target_pairs={{0,8},{8,0},{16,24},{24,16},{1,9},{9,1},{17,25},{25,17},{2,10},{10... | collective-permute-start | bytes 3145736 | tf_op jit(solution)/shard_map/ppermute | solution.py:454
  967.8 90.9 %collective-permute-start.66 = (bf16[512,1024]{1,0:T(8,128)(2,1)S(1)}, bf16[512,1024]{1,0:T(8,128)(2,1)S(1)}, u32[]{:S(2)}, u32[]{:S(2)}) collective-permute-start(bf16[512,1024]{1,0:T(8,128)(2,1)S(1)} %copy-done.129), channel_id=1, source_target_pairs={{0,16},{8,24},{16,0},{24,8},{1,17},{9,25},{17,1},{25,9},{2,18},{10... | collective-permute-start | bytes 3145736 | tf_op jit(solution)/shard_map/ppermute | solution.py:454
  989.1 67.4 %collective-permute-start.65 = (bf16[512,1024]{1,0:T(8,128)(2,1)S(1)}, bf16[512,1024]{1,0:T(8,128)(2,1)S(1)}, u32[]{:S(2)}, u32[]{:S(2)}) collective-permute-start(bf16[512,1024]{1,0:T(8,128)(2,1)S(1)} %add_convert_fusion.8), channel_id=1, source_target_pairs={{0,16},{8,24},{16,0},{24,8},{1,17},{9,25},{17,1},{25,9},{2,18},{10... | collective-permute-start | bytes 3145736 | tf_op jit(solution)/shard_map/ppermute | solution.py:454
  1011.6 47.8 %collective-permute-start.68 = (bf16[512,1024]{1,0:T(8,128)(2,1)S(1)}, bf16[512,1024]{1,0:T(8,128)(2,1)S(1)}, u32[]{:S(2)}, u32[]{:S(2)}) collective-permute-start(bf16[512,1024]{1,0:T(8,128)(2,1)S(1)} %add_convert_fusion.7), channel_id=1, source_target_pairs={{0,8},{8,0},{16,24},{24,16},{1,9},{9,1},{17,25},{25,17},{2,10},{10... | collective-permute-start | bytes 3145736 | tf_op jit(solution)/shard_map/ppermute | solution.py:454
  1014.3 50.3 %collective-permute-start.57 = (bf16[512,1024]{1,0:T(8,128)(2,1)S(1)}, bf16[512,1024]{1,0:T(8,128)(2,1)S(1)}, u32[]{:S(2)}, u32[]{:S(2)}) collective-permute-start(bf16[512,1024]{1,0:T(8,128)(2,1)S(1)} %copy-done.124), channel_id=1, source_target_pairs={{0,8},{8,0},{16,24},{24,16},{1,9},{9,1},{17,25},{25,17},{2,10},{10... | collective-permute-start | bytes 3145736 | tf_op jit(solution)/shard_map/ppermute | solution.py:454
  1016.2 81.6 %collective-permute-start.60 = (bf16[512,1024]{1,0:T(8,128)(2,1)S(1)}, bf16[512,1024]{1,0:T(8,128)(2,1)S(1)}, u32[]{:S(2)}, u32[]{:S(2)}) collective-permute-start(bf16[512,1024]{1,0:T(8,128)(2,1)S(1)} %copy-done.127), channel_id=1, source_target_pairs={{0,16},{8,24},{16,0},{24,8},{1,17},{9,25},{17,1},{25,9},{2,18},{10... | collective-permute-start | bytes 3145736 | tf_op jit(solution)/shard_map/ppermute | solution.py:454
  1056.5 39.4 %collective-permute-start.59 = (bf16[512,1024]{1,0:T(8,128)(2,1)S(1)}, bf16[512,1024]{1,0:T(8,128)(2,1)S(1)}, u32[]{:S(2)}, u32[]{:S(2)}) collective-permute-start(bf16[512,1024]{1,0:T(8,128)(2,1)S(1)} %add_convert_fusion.10), channel_id=1, source_target_pairs={{0,16},{8,24},{16,0},{24,8},{1,17},{9,25},{17,1},{25,9},{2,18},{10... | collective-permute-start | bytes 3145736 | tf_op jit(solution)/shard_map/ppermute | solution.py:454
  1058.7 39.2 %collective-permute-start.62 = (bf16[512,1024]{1,0:T(8,128)(2,1)S(1)}, bf16[512,1024]{1,0:T(8,128)(2,1)S(1)}, u32[]{:S(2)}, u32[]{:S(2)}) collective-permute-start(bf16[512,1024]{1,0:T(8,128)(2,1)S(1)} %add_convert_fusion.9), channel_id=1, source_target_pairs={{0,8},{8,0},{16,24},{24,16},{1,9},{9,1},{17,25},{25,17},{2,10},{10... | collective-permute-start | bytes 3145736 | tf_op jit(solution)/shard_map/ppermute | solution.py:454
  (188 other events, 3058.6 us)
Sparse Core Ops, SparseCore 0:
  25.8 47.5 all-gather.9
  75.6 28.0 all-gather.7
  105.8 81.3 all-gather.11
  188.7 27.5 all-gather.13
  217.8 46.3 all-gather.17
  266.2 45.6 all-gather.15
  583.4 49.7 reduce-scatter.8
  686.3 96.8 reduce-scatter.10
  785.5 34.3 reduce-scatter.12
  822.0 34.8 reduce-scatter.16
  859.3 48.3 reduce-scatter.14
  909.9 48.3 reduce-scatter.6

commit v2 on v1

--- a/solution.py
+++ b/solution.py
@@ -449,6 +449,168 @@
     )
 
 
+def expert_kernel(
+    perm,
+    arrived,
+    cot,
+    weight,
+    gate_weight,
+    up_weight,
+    down_weight,
+    active,
+    gate_grad,
+    up_grad,
+    weighted,
+    inner,
+    incoming,
+    produced_grad,
+    out_acc,
+    in_acc,
+):
+    step = pl.program_id(0)
+
+    @pl.when(step == 0)
+    def start():
+        produced_grad[...] = (weight[...] * cot[...].astype(jnp.float32)).astype(jnp.bfloat16)
+
+    gate = jnp.dot(arrived[...], gate_weight[...], preferred_element_type=jnp.float32)
+    upward = jnp.dot(arrived[...], up_weight[...], preferred_element_type=jnp.float32)
+    active_grad = lax.dot_general(
+        produced_grad[...],
+        down_weight[...],
+        (((1,), (1,)), ((), ())),
+        preferred_element_type=jnp.float32,
+    )
+    sigmoid = 1.0 / (1.0 + jnp.exp(-gate))
+    silu = gate * sigmoid
+    hidden = (silu * upward).astype(jnp.bfloat16)
+    active[...] = hidden
+    gate_back = (active_grad * upward * sigmoid * (1.0 + gate * (1.0 - sigmoid))).astype(
+        jnp.bfloat16
+    )
+    up_back = (active_grad * silu).astype(jnp.bfloat16)
+    gate_grad[...] = gate_back
+    up_grad[...] = up_back
+    out_part = jnp.dot(hidden, down_weight[...], preferred_element_type=jnp.float32)
+    in_part = lax.dot_general(
+        jnp.concatenate([gate_back, up_back], axis=1),
+        jnp.concatenate([gate_weight[...], up_weight[...]], axis=1),
+        (((1,), (1,)), ((), ())),
+        preferred_element_type=jnp.float32,
+    )
+
+    @pl.when(step == 0)
+    def first():
+        out_acc[...] = out_part
+        in_acc[...] = in_part
+
+    @pl.when(step > 0)
+    def later():
+        out_acc[...] += out_part
+        in_acc[...] += in_part
+
+    @pl.when(step == pl.num_programs(0) - 1)
+    def finish():
+        produced = out_acc[...].astype(jnp.bfloat16).astype(jnp.float32)
+        weighted[...] = (weight[...] * produced).astype(jnp.bfloat16)
+        sums = jnp.sum(cot[...].astype(jnp.float32) * produced, axis=1, keepdims=True)
+        inner[...] = jnp.transpose(jnp.broadcast_to(sums, (sums.shape[0], 128)))[:8, :]
+        incoming[...] = in_acc[...].astype(jnp.bfloat16)
+
+
+def run_expert(perm, arrived, cot, weight, gate_all, up_all, down_all):
+    slots, width = arrived.shape
+    hidden = gate_all.shape[1]
+    steps = perm.shape[0]
+    chunk = hidden // steps
+    rows = pl.BlockSpec((slots, width), lambda c, perm: (0, 0))
+    natural = pl.BlockSpec((slots, chunk), lambda c, perm: (0, perm[c]))
+    turned_in = pl.BlockSpec((width, chunk), lambda c, perm: (0, perm[c]))
+    wide = jax.ShapeDtypeStruct((slots, width), jnp.bfloat16)
+    thin = jax.ShapeDtypeStruct((slots, hidden), jnp.bfloat16)
+    return pl.pallas_call(
+        expert_kernel,
+        grid_spec=pltpu.PrefetchScalarGridSpec(
+            num_scalar_prefetch=1,
+            grid=(steps,),
+            in_specs=[
+                rows,
+                rows,
+                pl.BlockSpec((slots, 1), lambda c, perm: (0, 0)),
+                turned_in,
+                turned_in,
+                pl.BlockSpec((chunk, width), lambda c, perm: (c, 0)),
+            ],
+            out_specs=[
+                pl.BlockSpec((slots, chunk), lambda c, perm: (0, c)),
+                natural,
+                natural,
+                rows,
+                pl.BlockSpec((8, slots), lambda c, perm: (0, 0)),
+                rows,
+                rows,
+            ],
+            scratch_shapes=[
+                pltpu.VMEM((slots, width), jnp.float32),
+                pltpu.VMEM((slots, width), jnp.float32),
+            ],
+        ),
+        out_shape=[
+            thin,
+            thin,
+            thin,
+            wide,
+            jax.ShapeDtypeStruct((8, slots), jnp.float32),
+            wide,
+            wide,
+        ],
+        name="run_expert",
+    )(perm, arrived, cot, weight, gate_all, up_all, down_all)
+
+
+def dispatch_kernel(codes, chosen_weights, rows, *outs, capacity, experts):
+    blocks, tokens = codes.shape[1:]
+    numbers = lax.broadcasted_iota(jnp.int32, (capacity, tokens), 0)
+    for item in range(experts):
+        for block in range(blocks):
+            placed = numbers == codes[item, block : block + 1, :]
+            span = slice(block * capacity, (block + 1) * capacity)
+            outs[item][span, :] = jnp.dot(
+                placed.astype(jnp.bfloat16),
+                rows[block * tokens : (block + 1) * tokens, :],
+                preferred_element_type=jnp.float32,
+            ).astype(jnp.bfloat16)
+
+    @pl.when(pl.program_id(0) == 0)
+    def weigh():
+        for item in range(experts):
+            for block in range(blocks):
+                placed = numbers == codes[item, block : block + 1, :]
+                span = slice(block * capacity, (block + 1) * capacity)
+                row = chosen_weights[item, block : block + 1, :]
+                outs[experts + item][span, :] = jnp.sum(
+                    jnp.where(placed, row, 0.0), axis=1, keepdims=True
+                )
+
+
+def dispatch(codes, chosen_weights, rows, capacity):
+    experts, blocks, _ = codes.shape
+    slots = blocks * capacity
+    width = rows.shape[1]
+    block = min(width, 512)
+    whole = pl.BlockSpec(codes.shape, lambda step: (0, 0, 0))
+    results = pl.pallas_call(
+        partial(dispatch_kernel, capacity=capacity, experts=experts),
+        grid=(width // block,),
+        in_specs=[whole, whole, pl.BlockSpec((rows.shape[0], block), lambda step: (0, step))],
+        out_specs=[pl.BlockSpec((slots, block), lambda step: (0, step))] * experts
+        + [pl.BlockSpec((slots, 1), lambda step: (0, 0))] * experts,
+        out_shape=[jax.ShapeDtypeStruct((slots, width), jnp.bfloat16)] * experts
+        + [jax.ShapeDtypeStruct((slots, 1), jnp.float32)] * experts,
+    )(codes, chosen_weights, rows)
+    return results[:experts], results[experts:]
+
+
 def exchange(array, offset):
     count = lax.axis_size("head")
     return lax.ppermute(array, "head", [(at, at ^ offset) for at in range(count)])
@@ -577,7 +739,7 @@
     pair_full = move_rows(pair_full, blocks, heads_axis, part)
     query_full = lax.all_gather(rows_here[:, 2 * columns :], "blk", axis=0, tiled=True)
     query_full = move_rows(query_full, blocks, heads_axis, part)
-    cot_all = lax.all_gather(cotangent, "blk", axis=0, tiled=True).reshape(blocks, rows, width)
+    cot_all = lax.all_gather(cotangent, "blk", axis=0, tiled=True)
 
     small = jnp.concatenate(
         [
@@ -650,49 +812,67 @@
     weight_here = lax.dynamic_slice_in_dim(
         probs_all, block_at * local_experts, local_experts, 1
     ).reshape(blocks, rows, local_experts)
-    routed_all = routed_all.reshape(blocks, rows, width)
     slot_ids = jnp.arange(capacity, dtype=jnp.int32)
-    combined = 0.0
-    incoming = 0.0
-    weight_grads = []
-    stores = []
-    for item in range(local_experts):
-        placed = codes_here[:, None, :, item] == slot_ids[None, :, None]
-        place = placed.astype(bf16)
-        slot_weight = jnp.sum(
-            jnp.where(placed, weight_here[:, None, :, item], 0.0), axis=-1
-        ).reshape(slots, 1)
-        arrived = jnp.einsum("srt,std->srd", place, routed_all).reshape(slots, width)
-        arrived_cot = jnp.einsum("srt,std->srd", place, cot_all).reshape(slots, width)
-        gate_all = jnp.concatenate(gates[item], axis=0)
-        up_all = jnp.concatenate(ups[item], axis=0)
-        down_all = jnp.concatenate(downs[item], axis=0)
-        gate = jnp.dot(arrived, gate_all, preferred_element_type=f32)
-        upward = jnp.dot(arrived, up_all, preferred_element_type=f32)
-        sigmoid = jax.nn.sigmoid(gate)
-        active = xor_chunks((gate * sigmoid * upward).astype(bf16), 1)
-        produced = jnp.dot(active, down_all, preferred_element_type=f32).astype(bf16)
-        cot_float = arrived_cot.astype(f32)
-        produced_float = produced.astype(f32)
-        weighted = (slot_weight * produced_float).astype(bf16).reshape(blocks, capacity, width)
-        combined = combined + jnp.einsum(
-            "srt,srd->std", place, weighted, preferred_element_type=f32
+    codes_here = jnp.transpose(codes_here, (2, 0, 1))
+    weight_here = jnp.transpose(weight_here, (2, 0, 1))
+    placed = codes_here[:, :, None, :] == slot_ids[None, None, :, None]
+    place = placed.astype(bf16)
+
+    def arrange(flat, weighed=True):
+        lots_here = weight_here if weighed else jnp.zeros(codes_here.shape, f32)
+        if capacity % 16 == 0:
+            return dispatch(codes_here, lots_here, flat, capacity)
+        shaped = flat.reshape(blocks, rows, width)
+        lots = jnp.sum(jnp.where(placed, lots_here[:, :, None, :], 0.0), axis=-1)
+        return (
+            [
+                jnp.einsum("srt,std->srd", item, shaped).reshape(slots, width)
+                for item in place
+            ],
+            [item.reshape(slots, 1) for item in lots],
         )
-        slot_grad = jnp.sum(cot_float * produced_float, axis=-1).reshape(blocks, capacity, 1)
-        weight_grads.append(jnp.sum(jnp.where(placed, slot_grad, 0.0), axis=1))
-        produced_grad = (slot_weight * cot_float).astype(bf16)
-        active_grad = xor_chunks(
-            jnp.dot(produced_grad, down_all.T, preferred_element_type=f32), 1
+
+    arrived_cot = arrange(cot_all, False)[0]
+    gate_all, up_all, down_all = (
+        [jnp.concatenate(pieces, axis=0) for pieces in group_pieces]
+        for group_pieces in (gates, ups, downs)
+    )
+    arrived, slot_weight = arrange(routed_all)
+    offsets = jnp.bitwise_xor(head_at, jnp.arange(heads_axis, dtype=jnp.int32))
+    results = [
+        run_expert(
+            offsets,
+            arrived[item],
+            arrived_cot[item],
+            slot_weight[item],
+            gate_all[item],
+            up_all[item],
+            down_all[item],
         )
-        gate_grad = (active_grad * upward * sigmoid * (1.0 + gate * (1.0 - sigmoid))).astype(bf16)
-        up_grad = (active_grad * (gate * sigmoid)).astype(bf16)
-        coming = jnp.dot(gate_grad, gate_all.T, preferred_element_type=f32)
-        coming = coming + jnp.dot(up_grad, up_all.T, preferred_element_type=f32)
-        coming = coming.astype(bf16).reshape(blocks, capacity, width)
-        incoming = incoming + jnp.einsum(
-            "srt,srd->std", place, coming, preferred_element_type=f32
+        for item in range(local_experts)
+    ]
+
+    def back_to_rows(which):
+        return sum(
+            jnp.einsum(
+                "srt,srd->std",
+                place[item],
+                results[item][which].reshape(blocks, capacity, width),
+                preferred_element_type=f32,
+            )
+            for item in range(local_experts)
         )
-        stores.append((arrived, produced_grad, active, gate_grad, up_grad))
+
+    incoming = back_to_rows(5)
+    combined = back_to_rows(3)
+    slot_grad = jnp.stack([result[4][0] for result in results])
+    slot_grad = slot_grad.reshape(local_experts, blocks, capacity, 1)
+    weight_grads = jnp.sum(jnp.where(placed, slot_grad, 0.0), axis=2)
+    weight_grads = jnp.transpose(weight_grads, (1, 2, 0))
+    stores = [
+        (arrived[item], results[item][6], results[item][0], results[item][1], results[item][2])
+        for item in range(local_experts)
+    ]
     routed_grad = lax.psum_scatter(
         incoming.astype(bf16).reshape(blocks * rows, width),
         "blk",
@@ -707,7 +887,7 @@
     )
     block_output = (middle + combined.astype(f32)).astype(bf16)
     prob_grad = lax.all_to_all(
-        jnp.stack(weight_grads, axis=2), "blk", split_axis=0, concat_axis=2, tiled=True
+        weight_grads, "blk", split_axis=0, concat_axis=2, tiled=True
     ).reshape(rows, experts)
 
     def pieces_of(left, right):

time: 1180 us -> 1100 us (0.932)
  waiting for transfers between devices: 685 us -> 589 us
  Pallas kernels: 62 us -> 138 us
  matrix products: 167 us -> 98.9 us
  other arithmetic: 61.7 us -> 77 us
  starting transfers between devices: 106 us -> 92.6 us
    ppermute x75, waiting for transfers between devices: 483 us -> 390 us  [exchange(): lax.ppermute(array, 'head', [(at, at ^ offset) for at in range(count)])]
    pallas_call x0 -> x4, Pallas kernels: none -> 75.5 us  [the longest x2 62.8 us: run_expert(): pl.pallas_call(expert_kernel, grid_spec=pltpu.PrefetchScalarGridSpec(num_...]
    dot_general x20 -> x4, matrix products: 85.3 us -> 18.3 us  [back_to_rows(): jnp.einsum('srt,srd->std', place[item], results[item][which].reshape(bloc...]
    concatenate x0 -> x6, other arithmetic: none -> 24.7 us  [layer(): jnp.concatenate(pieces, axis=0)]
    convert_element_type x4 -> x0, other arithmetic: 12.9 us -> none  [the longest x2 9.21 us: layer(): produced_grad = (slot_weight * cot_float).astype(bf16)]
  transfers between devices with their start and end apart: 89 -> 89, of which waited for: 47 -> 39; matrix products, arithmetic and copies ran while one was open for 18% -> 18% of each run, Pallas kernels for 4% -> 5%
where the time goes in v2:
time: 1100 us; the launch traced here: 1090 us
  waiting for transfers between devices  589 us (54%)
  Pallas kernels  138 us (13%)
  matrix products  98.9 us (9%)
  starting transfers between devices  92.6 us (8%)
  other arithmetic  77 us (7%)
  local copies, waits for them, and re-layouts  64.3 us (6%)
  between operations  16 us (1%)
  blocking collectives  14.8 us (1%)
    ppermute x75, waiting for transfers between devices, exchange(): lax.ppermute(array, 'head', [(at, at ^ offset) for at in range(count)])  390 us
    ppermute x75, starting transfers between devices, exchange(): lax.ppermute(array, 'head', [(at, at ^ offset) for at in range(count)])  81.5 us
    reduce_scatter x1, waiting for transfers between devices, layer(): lax.psum_scatter(pairs_back, 'blk', scatter_dimension=0, tiled=True)  74.5 us
    all_gather x1, waiting for transfers between devices, layer(): pairs_all = lax.all_gather(pairs, 'blk', axis=0, tiled=True)  66.1 us
    pallas_call x2, Pallas kernels, run_expert(): pl.pallas_call(expert_kernel, grid_spec=pltpu.PrefetchScalarGridSpec(num_...  62.8 us
    dot_general x24, matrix products, pieces_of(): jnp.dot(left[:, offset * size:(offset + 1) * size].T, right, preferred_el...  47.2 us
    reduce_scatter x1, waiting for transfers between devices, layer(): lax.psum_scatter(incoming.astype(bf16).reshape(blocks * rows, width), 'bl...  36.4 us
    concatenate x6, other arithmetic, layer(): jnp.concatenate(pieces, axis=0)  24.7 us
  transfers between devices with their start and end apart: 89, of which 39 were waited for; matrix products, arithmetic and copies ran while one was open for 18% of the time, Pallas kernels for 5%

profile of v2, /device:TPU:0, one launch (start us, length us, event | category | flops | bytes accessed | tf_op | source)
XLA Modules:
  0.0 1090.9 jit_solution(10197578026848401192)
XLA Ops:
  14.1 5.0 collective-permute-done.6
  28.4 14.8 %all-gather = bf16[8,1,3328]{2,1,0:T(2,128)(2,1)S(1)} all-gather(bf16[1,1,3328]{2,1,0:T(2,128)(2,1)S(1)} %maximum_bitcast_fusion), channel_id=1, replica_groups=mesh['head'=4,'blk'=8] {'blk'}, dimensions={0}, use_global_device_ids=true | all-gather | bytes 59904 | tf_op jit(solution)/shard_map/all_gather | solution.py:756
  57.1 4.5 collective-permute-done.refs_1_
  61.6 11.0 %collective-permute-done.1.refs_2_ = bf16[128,2048]{1,0:T(8,128)(2,1)S(1)} collective-permute-done((bf16[128,2048]{1,0:T(8,128)(2,1)S(1)}, bf16[128,2048]{1,0:T(8,128)(2,1)S(1)}, u32[]{:S(2)}, u32[]{:S(2)}) %collective-permute-start.1) | collective-permute-done | bytes 524320 | tf_op jit(solution)/shard_map/ppermute | solution.py:616
  77.3 4.9 copy.121
  82.2 4.6 shard_map.292
  105.6 4.4 shard_map.290
  119.9 66.1 %all-gather.12.cloned.1.call-done.pairs = bf16[4096,1024]{1,0:T(8,128)(2,1)} async-done(((bf16[512,1024]{1,0:T(8,128)(2,1)}), bf16[4096,1024]{1,0:T(8,128)(2,1)}) %all-gather.12.cloned.1.call-update) | async-done | bytes 8388624 | tf_op jit(solution)/shard_map/all_gather | solution.py:798
  187.6 11.4 %attend_forward.1 = (f32[512,512]{1,0:T(8,128)}, bf16[512,512]{1,0:T(8,128)(2,1)}, f32[512,512]{1,0:T(8,128)}) custom-call(s32[2,16]{1,0:T(2,128)} %select_reduce_fusion.2.listed, s32[2]{0:T(128)} %get-tuple-element.194.counts, bf16[512,512]{1,0:T(8,128)(2,1)} %get-tuple-element.55.query, bf16[4096,1024]{1,0:T(8,128)(2,1)} %all-gather.12.cloned.1.call-done.pairs, ...), custom_call_target="tpu_custom_call" | custom-call | tf_op jit(solution)/shard_map/attend_forward/pallas_call | solution.py:299
  199.0 16.0 %all-gather.14.cloned.1.call-done = bf16[512,2048]{1,0:T(8,128)(2,1)} async-done(((bf16[64,2048]{1,0:T(8,128)(2,1)}), bf16[512,2048]{1,0:T(8,128)(2,1)}) %all-gather.14.cloned.1.call-update) | async-done | bytes 2097168 | tf_op jit(solution)/shard_map/all_gather | solution.py:735
  221.8 11.3 %collective-permute-done.15 = bf16[128,2048]{1,0:T(8,128)(2,1)S(1)} collective-permute-done((bf16[128,2048]{1,0:T(8,128)(2,1)S(1)}, bf16[128,2048]{1,0:T(8,128)(2,1)S(1)}, u32[]{:S(2)}, u32[]{:S(2)}) %collective-permute-start.15) | collective-permute-done | bytes 524320 | tf_op jit(solution)/shard_map/ppermute | solution.py:616
  233.1 11.7 %collective-permute-done.16 = bf16[128,2048]{1,0:T(8,128)(2,1)S(1)} collective-permute-done((bf16[128,2048]{1,0:T(8,128)(2,1)S(1)}, bf16[128,2048]{1,0:T(8,128)(2,1)S(1)}, u32[]{:S(2)}, u32[]{:S(2)}) %collective-permute-start.16) | collective-permute-done | bytes 524320 | tf_op jit(solution)/shard_map/ppermute | solution.py:616
  256.2 18.5 %collective-permute-done.18 = bf16[512,1024]{1,0:T(8,128)(2,1)} collective-permute-done((bf16[512,1024]{1,0:T(8,128)(2,1)S(1)}, bf16[512,1024]{1,0:T(8,128)(2,1)}, u32[]{:S(2)}, u32[]{:S(2)}) %collective-permute-start.18) | collective-permute-done | bytes 1048608 | tf_op jit(solution)/shard_map/ppermute | solution.py:616
  276.8 20.4 %collective-permute-done.21 = bf16[512,1024]{1,0:T(8,128)(2,1)} collective-permute-done((bf16[512,1024]{1,0:T(8,128)(2,1)S(1)}, bf16[512,1024]{1,0:T(8,128)(2,1)}, u32[]{:S(2)}, u32[]{:S(2)}) %collective-permute-start.21) | collective-permute-done | bytes 1048608 | tf_op jit(solution)/shard_map/ppermute | solution.py:616
  299.3 20.3 %collective-permute-done.24 = bf16[256,2048]{1,0:T(8,128)(2,1)S(1)} collective-permute-done((bf16[256,2048]{1,0:T(8,128)(2,1)S(1)}, bf16[256,2048]{1,0:T(8,128)(2,1)S(1)}, u32[]{:S(2)}, u32[]{:S(2)}) %collective-permute-start.24) | collective-permute-done | bytes 1048608 | tf_op jit(solution)/shard_map/ppermute | solution.py:616
  327.3 16.0 %collective-permute-done.28 = bf16[512,1024]{1,0:T(8,128)(2,1)} collective-permute-done((bf16[512,1024]{1,0:T(8,128)(2,1)S(1)}, bf16[512,1024]{1,0:T(8,128)(2,1)}, u32[]{:S(2)}, u32[]{:S(2)}) %collective-permute-start.28) | collective-permute-done | bytes 1048608 | tf_op jit(solution)/shard_map/ppermute | solution.py:616
  350.0 15.8 %collective-permute-done.20 = bf16[512,1024]{1,0:T(8,128)(2,1)} collective-permute-done((bf16[512,1024]{1,0:T(8,128)(2,1)}, bf16[512,1024]{1,0:T(8,128)(2,1)}, u32[]{:S(2)}, u32[]{:S(2)}) %collective-permute-start.20) | collective-permute-done | bytes 1048608 | tf_op jit(solution)/shard_map/ppermute | solution.py:616
  370.4 18.0 %collective-permute-done.31 = bf16[512,1024]{1,0:T(8,128)(2,1)} collective-permute-done((bf16[512,1024]{1,0:T(8,128)(2,1)}, bf16[512,1024]{1,0:T(8,128)(2,1)}, u32[]{:S(2)}, u32[]{:S(2)}) %collective-permute-start.31) | collective-permute-done | bytes 1048608 | tf_op jit(solution)/shard_map/ppermute | solution.py:616
  389.1 21.7 %collective-permute-done.23 = bf16[512,1024]{1,0:T(8,128)(2,1)} collective-permute-done((bf16[512,1024]{1,0:T(8,128)(2,1)}, bf16[512,1024]{1,0:T(8,128)(2,1)}, u32[]{:S(2)}, u32[]{:S(2)}) %collective-permute-start.23) | collective-permute-done | bytes 1048608 | tf_op jit(solution)/shard_map/ppermute | solution.py:616
  415.0 18.3 %collective-permute-done.34 = bf16[256,2048]{1,0:T(8,128)(2,1)} collective-permute-done((bf16[256,2048]{1,0:T(8,128)(2,1)}, bf16[256,2048]{1,0:T(8,128)(2,1)}, u32[]{:S(2)}, u32[]{:S(2)}) %collective-permute-start.34) | collective-permute-done | bytes 1048608 | tf_op jit(solution)/shard_map/ppermute | solution.py:616
  434.1 19.9 %collective-permute-done.26 = bf16[256,2048]{1,0:T(8,128)(2,1)} collective-permute-done((bf16[256,2048]{1,0:T(8,128)(2,1)}, bf16[256,2048]{1,0:T(8,128)(2,1)}, u32[]{:S(2)}, u32[]{:S(2)}) %collective-permute-start.26) | collective-permute-done | bytes 1048608 | tf_op jit(solution)/shard_map/ppermute | solution.py:616
  464.7 12.9 %collective-permute-done.35 = bf16[256,2048]{1,0:T(8,128)(2,1)S(1)} collective-permute-done((bf16[256,2048]{1,0:T(8,128)(2,1)}, bf16[256,2048]{1,0:T(8,128)(2,1)S(1)}, u32[]{:S(2)}, u32[]{:S(2)}) %collective-permute-start.35) | collective-permute-done | bytes 1048608 | tf_op jit(solution)/shard_map/ppermute | solution.py:616
  477.6 7.5 pad_maximum_fusion.5.down_weight
  485.7 6.3 shard_map.295
  496.1 6.3 shard_map.294
  502.4 31.5 %run_expert.2 = (bf16[640,1024]{1,0:T(8,128)(2,1)}, bf16[640,1024]{1,0:T(8,128)(2,1)}, bf16[640,1024]{1,0:T(8,128)(2,1)}, bf16[640,2048]{1,0:T(8,128)(2,1)}, f32...) custom-call(s32[4]{0:T(128)} %iota_xor_fusion.perm, ...), custom_call_target="tpu_custom_call" | custom-call | tf_op jit(solution)/shard_map/run_expert/pallas_call | solution.py:531
  534.0 6.3 fusion.34
  540.3 31.3 %run_expert.3 = (bf16[640,1024]{1,0:T(8,128)(2,1)}, bf16[640,1024]{1,0:T(8,128)(2,1)}, bf16[640,1024]{1,0:T(8,128)(2,1)}, bf16[640,2048]{1,0:T(8,128)(2,1)}, f32...) custom-call(s32[4]{0:T(128)} %iota_xor_fusion.perm, ...), custom_call_target="tpu_custom_call" | custom-call | tf_op jit(solution)/shard_map/run_expert/pallas_call | solution.py:531
  571.6 7.5 add_convert_fusion
  585.6 5.7 all-to-all-done
  591.3 36.4 %reduce-scatter.9.cloned.1.call-done = bf16[128,2048]{1,0:T(8,128)(2,1)} async-done(((bf16[1024,2048]{1,0:T(8,128)(2,1)}), bf16[128,2048]{1,0:T(8,128)(2,1)}) %reduce-scatter.9.cloned.1.call-update) | async-done | bytes 524304 | tf_op jit(solution)/shard_map/reduce_scatter | solution.py:876
  634.5 11.3 %collective-permute-done.36 = bf16[128,2048]{1,0:T(8,128)(2,1)S(1)} collective-permute-done((bf16[128,2048]{1,0:T(8,128)(2,1)S(1)}, bf16[128,2048]{1,0:T(8,128)(2,1)S(1)}, u32[]{:S(2)}, u32[]{:S(2)}) %collective-permute-start.36) | collective-permute-done | bytes 524320 | tf_op jit(solution)/shard_map/ppermute | solution.py:616
  645.8 9.4 collective-permute-done.37
  660.5 19.6 %attend_backward.1 = (bf16[512,512]{1,0:T(8,128)(2,1)}, bf16[4096,1024]{1,0:T(8,128)(2,1)}) custom-call(s32[2,16]{1,0:T(2,128)} %copy-done.58, bf16[512,512]{1,0:T(8,128)(2,1)} %get-tuple-element.55.query, bf16[4096,1024]{1,0:T(8,128)(2,1)} %all-gather.12.cloned.1.call-done.pairs, bf16[512,512]{1,0:T(8,128)(2,1)} %convolution_convert_fusion.28.grad, ...), custom_call_target="tpu_custom_call" | custom-call | tf_op jit(solution)/shard_map/attend_backward/pallas_call | solution.py:409
  702.5 74.5 %reduce-scatter.11.cloned.1.call-done.back.refs_7_ = bf16[512,1024]{1,0:T(8,128)(2,1)} async-done(((bf16[4096,1024]{1,0:T(8,128)(2,1)}), bf16[512,1024]{1,0:T(8,128)(2,1)}) %reduce-scatter.11.cloned.1.call-update) | async-done | bytes 1048592 | tf_op jit(solution)/shard_map/reduce_scatter | solution.py:938
  791.9 5.5 convolution_convert_fusion
  860.9 9.9 collective-permute-done.64
  878.4 15.5 %collective-permute-done.58 = bf16[512,1024]{1,0:T(8,128)(2,1)S(1)} collective-permute-done((bf16[512,1024]{1,0:T(8,128)(2,1)S(1)}, bf16[512,1024]{1,0:T(8,128)(2,1)S(1)}, u32[]{:S(2)}, u32[]{:S(2)}) %collective-permute-start.58) | collective-permute-done | bytes 1048608 | tf_op jit(solution)/shard_map/ppermute | solution.py:616
  894.9 11.8 %collective-permute-done.61 = bf16[512,1024]{1,0:T(8,128)(2,1)S(1)} collective-permute-done((bf16[512,1024]{1,0:T(8,128)(2,1)S(1)}, bf16[512,1024]{1,0:T(8,128)(2,1)S(1)}, u32[]{:S(2)}, u32[]{:S(2)}) %collective-permute-start.61) | collective-permute-done | bytes 1048608 | tf_op jit(solution)/shard_map/ppermute | solution.py:616
  910.7 18.4 %collective-permute-done.71 = bf16[256,2048]{1,0:T(8,128)(2,1)S(1)} collective-permute-done((bf16[256,2048]{1,0:T(8,128)(2,1)S(1)}, bf16[256,2048]{1,0:T(8,128)(2,1)S(1)}, u32[]{:S(2)}, u32[]{:S(2)}) %collective-permute-start.71) | collective-permute-done | bytes 1048608 | tf_op jit(solution)/shard_map/ppermute | solution.py:616
  933.7 8.8 collective-permute-done.63
  943.0 31.1 %collective-permute-done.65 = bf16[512,1024]{1,0:T(8,128)(2,1)S(1)} collective-permute-done((bf16[512,1024]{1,0:T(8,128)(2,1)S(1)}, bf16[512,1024]{1,0:T(8,128)(2,1)S(1)}, u32[]{:S(2)}, u32[]{:S(2)}) %collective-permute-start.65) | collective-permute-done | bytes 1048608 | tf_op jit(solution)/shard_map/ppermute | solution.py:616
  982.0 5.4 collective-permute-done.57
  987.4 25.8 %collective-permute-done.59 = bf16[512,1024]{1,0:T(8,128)(2,1)S(1)} collective-permute-done((bf16[512,1024]{1,0:T(8,128)(2,1)S(1)}, bf16[512,1024]{1,0:T(8,128)(2,1)S(1)}, u32[]{:S(2)}, u32[]{:S(2)}) %collective-permute-start.59) | collective-permute-done | bytes 1048608 | tf_op jit(solution)/shard_map/ppermute | solution.py:616
  1021.5 4.7 fusion.70
  1042.9 5.5 collective-permute-done.46
  1061.4 6.7 all-to-all-start.1
  1073.5 4.1 fusion.7
  (553 shorter events, 320.6 us)
Async XLA Ops:
  7.2 70.1 %all-gather.10.cloned.1.call-start = ((), (), s32[]{:S(2)}) async-start(), calls=%async_computation.9 | async-start | bytes 4718592 | tf_op jit(solution)/shard_map/all_gather | solution.py:738
  24.1 78.3 %all-gather.8.cloned.1.call-start = ((), (), s32[]{:S(2)}) async-start(), calls=%async_computation.8 | async-start | bytes 2359296 | tf_op jit(solution)/shard_map/all_gather | solution.py:740
  27.9 158.1 %all-gather.12.cloned.1.call-start = ((), (), s32[]{:S(2)}) async-start(), calls=%async_computation.10 | async-start | bytes 9437184 | tf_op jit(solution)/shard_map/all_gather | solution.py:798
  48.3 24.3 %collective-permute-start.1 = (bf16[128,2048]{1,0:T(8,128)(2,1)S(1)}, bf16[128,2048]{1,0:T(8,128)(2,1)S(1)}, u32[]{:S(2)}, u32[]{:S(2)}) collective-permute-start(bf16[128,2048]{1,0:T(8,128)(2,1)S(1)} %copy-done.9), channel_id=1, source_target_pairs={{0,16},{8,24},{16,0},{24,8},{1,17},{9,25},{17,1},{25,9},{2,18},{10... | collective-permute-start | bytes 1572872 | tf_op jit(solution)/shard_map/ppermute | solution.py:616
  97.8 117.2 %all-gather.14.cloned.1.call-start = ((), (), s32[]{:S(2)}) async-start(), calls=%async_computation.11 | async-start | bytes 2359296 | tf_op jit(solution)/shard_map/all_gather | solution.py:735
  98.4 386.7 %all-gather.18.cloned.1.call-start = ((), (), s32[]{:S(2)}) async-start(), calls=%async_computation.13 | async-start | bytes 4718592 | tf_op jit(solution)/shard_map/all_gather | solution.py:742
  99.0 393.0 %all-gather.16.cloned.1.call-start = ((), (), s32[]{:S(2)}) async-start(), calls=%async_computation.12 | async-start | bytes 4718592 | tf_op jit(solution)/shard_map/all_gather | solution.py:807
  219.9 25.0 %collective-permute-start.16 = (bf16[128,2048]{1,0:T(8,128)(2,1)S(1)}, bf16[128,2048]{1,0:T(8,128)(2,1)S(1)}, u32[]{:S(2)}, u32[]{:S(2)}) collective-permute-start(bf16[128,2048]{1,0:T(8,128)(2,1)S(1)} %get-tuple-element.207), channel_id=1, source_target_pairs={{0,16},{8,24},{16,0},{24,8},{1,17},{9,25},{17,1},{25,9},{2,18},{10... | collective-permute-start | bytes 1572872 | tf_op jit(solution)/shard_map/ppermute | solution.py:616
  246.6 381.1 %reduce-scatter.9.cloned.1.call-start = ((), (), s32[]{:S(2)}) async-start(), calls=%async_computation.15 | async-start | bytes 4718592 | tf_op jit(solution)/shard_map/reduce_scatter | solution.py:876
  248.6 26.2 %collective-permute-start.18 = (bf16[512,1024]{1,0:T(8,128)(2,1)S(1)}, bf16[512,1024]{1,0:T(8,128)(2,1)}, u32[]{:S(2)}, u32[]{:S(2)}) collective-permute-start(bf16[512,1024]{1,0:T(8,128)(2,1)S(1)} %get-tuple-element.204), channel_id=1, source_target_pairs={{0,8},{8,0},{16,24},{24,16},{1,9},{9,1},{17,25},{25,17},{2,10},{10... | collective-permute-start | bytes 3145736 | tf_op jit(solution)/shard_map/ppermute | solution.py:616
  249.8 26.4 %collective-permute-start.19 = (bf16[512,1024]{1,0:T(8,128)(2,1)S(1)}, bf16[512,1024]{1,0:T(8,128)(2,1)S(1)}, u32[]{:S(2)}, u32[]{:S(2)}) collective-permute-start(bf16[512,1024]{1,0:T(8,128)(2,1)S(1)} %get-tuple-element.204), channel_id=1, source_target_pairs={{0,16},{8,24},{16,0},{24,8},{1,17},{9,25},{17,1},{25,9},{2,18},{10... | collective-permute-start | bytes 3145736 | tf_op jit(solution)/shard_map/ppermute | solution.py:616
  251.9 45.4 %collective-permute-start.21 = (bf16[512,1024]{1,0:T(8,128)(2,1)S(1)}, bf16[512,1024]{1,0:T(8,128)(2,1)}, u32[]{:S(2)}, u32[]{:S(2)}) collective-permute-start(bf16[512,1024]{1,0:T(8,128)(2,1)S(1)} %get-tuple-element.202), channel_id=1, source_target_pairs={{0,8},{8,0},{16,24},{24,16},{1,9},{9,1},{17,25},{25,17},{2,10},{10... | collective-permute-start | bytes 3145736 | tf_op jit(solution)/shard_map/ppermute | solution.py:616
  253.3 45.1 %collective-permute-start.22 = (bf16[512,1024]{1,0:T(8,128)(2,1)S(1)}, bf16[512,1024]{1,0:T(8,128)(2,1)S(1)}, u32[]{:S(2)}, u32[]{:S(2)}) collective-permute-start(bf16[512,1024]{1,0:T(8,128)(2,1)S(1)} %get-tuple-element.202), channel_id=1, source_target_pairs={{0,16},{8,24},{16,0},{24,8},{1,17},{9,25},{17,1},{25,9},{2,18},{10... | collective-permute-start | bytes 3145736 | tf_op jit(solution)/shard_map/ppermute | solution.py:616
  255.0 64.6 %collective-permute-start.24 = (bf16[256,2048]{1,0:T(8,128)(2,1)S(1)}, bf16[256,2048]{1,0:T(8,128)(2,1)S(1)}, u32[]{:S(2)}, u32[]{:S(2)}) collective-permute-start(bf16[256,2048]{1,0:T(8,128)(2,1)S(1)} %get-tuple-element.200), channel_id=1, source_target_pairs={{0,8},{8,0},{16,24},{24,16},{1,9},{9,1},{17,25},{25,17},{2,10},{10... | collective-permute-start | bytes 3145736 | tf_op jit(solution)/shard_map/ppermute | solution.py:616
  274.8 46.3 %collective-permute-start.25 = (bf16[256,2048]{1,0:T(8,128)(2,1)S(1)}, bf16[256,2048]{1,0:T(8,128)(2,1)S(1)}, u32[]{:S(2)}, u32[]{:S(2)}) collective-permute-start(bf16[256,2048]{1,0:T(8,128)(2,1)S(1)} %get-tuple-element.200), channel_id=1, source_target_pairs={{0,16},{8,24},{16,0},{24,8},{1,17},{9,25},{17,1},{25,9},{2,18},{10... | collective-permute-start | bytes 3145736 | tf_op jit(solution)/shard_map/ppermute | solution.py:616
  276.3 67.1 %collective-permute-start.28 = (bf16[512,1024]{1,0:T(8,128)(2,1)S(1)}, bf16[512,1024]{1,0:T(8,128)(2,1)}, u32[]{:S(2)}, u32[]{:S(2)}) collective-permute-start(bf16[512,1024]{1,0:T(8,128)(2,1)S(1)} %get-tuple-element.203), channel_id=1, source_target_pairs={{0,16},{8,24},{16,0},{24,8},{1,17},{9,25},{17,1},{25,9},{2,18},{10... | collective-permute-start | bytes 3145736 | tf_op jit(solution)/shard_map/ppermute | solution.py:616
  297.2 47.0 %collective-permute-start.27 = (bf16[512,1024]{1,0:T(8,128)(2,1)S(1)}, bf16[512,1024]{1,0:T(8,128)(2,1)}, u32[]{:S(2)}, u32[]{:S(2)}) collective-permute-start(bf16[512,1024]{1,0:T(8,128)(2,1)S(1)} %get-tuple-element.203), channel_id=1, source_target_pairs={{0,8},{8,0},{16,24},{24,16},{1,9},{9,1},{17,25},{25,17},{2,10},{10... | collective-permute-start | bytes 3145736 | tf_op jit(solution)/shard_map/ppermute | solution.py:616
  298.4 67.4 %collective-permute-start.20 = (bf16[512,1024]{1,0:T(8,128)(2,1)}, bf16[512,1024]{1,0:T(8,128)(2,1)}, u32[]{:S(2)}, u32[]{:S(2)}) collective-permute-start(bf16[512,1024]{1,0:T(8,128)(2,1)} %collective-permute-done.18), channel_id=1, source_target_pairs={{0,16},{8,24},{16,0},{24,8},{1,17},{9,25},{17,1},{25,9},{2,18},{10... | collective-permute-start | bytes 3145736 | tf_op jit(solution)/shard_map/ppermute | solution.py:616
  319.6 68.7 %collective-permute-start.31 = (bf16[512,1024]{1,0:T(8,128)(2,1)}, bf16[512,1024]{1,0:T(8,128)(2,1)}, u32[]{:S(2)}, u32[]{:S(2)}) collective-permute-start(bf16[512,1024]{1,0:T(8,128)(2,1)} %get-tuple-element.201), channel_id=1, source_target_pairs={{0,16},{8,24},{16,0},{24,8},{1,17},{9,25},{17,1},{25,9},{2,18},{10... | collective-permute-start | bytes 3145736 | tf_op jit(solution)/shard_map/ppermute | solution.py:616
  322.1 88.7 %collective-permute-start.23 = (bf16[512,1024]{1,0:T(8,128)(2,1)}, bf16[512,1024]{1,0:T(8,128)(2,1)}, u32[]{:S(2)}, u32[]{:S(2)}) collective-permute-start(bf16[512,1024]{1,0:T(8,128)(2,1)} %collective-permute-done.21), channel_id=1, source_target_pairs={{0,16},{8,24},{16,0},{24,8},{1,17},{9,25},{17,1},{25,9},{2,18},{10... | collective-permute-start | bytes 3145736 | tf_op jit(solution)/shard_map/ppermute | solution.py:616
  343.4 89.9 %collective-permute-start.34 = (bf16[256,2048]{1,0:T(8,128)(2,1)}, bf16[256,2048]{1,0:T(8,128)(2,1)}, u32[]{:S(2)}, u32[]{:S(2)}) collective-permute-start(bf16[256,2048]{1,0:T(8,128)(2,1)} %get-tuple-element.199), channel_id=1, source_target_pairs={{0,16},{8,24},{16,0},{24,8},{1,17},{9,25},{17,1},{25,9},{2,18},{10... | collective-permute-start | bytes 3145736 | tf_op jit(solution)/shard_map/ppermute | solution.py:616
  344.3 109.7 %collective-permute-start.26 = (bf16[256,2048]{1,0:T(8,128)(2,1)}, bf16[256,2048]{1,0:T(8,128)(2,1)}, u32[]{:S(2)}, u32[]{:S(2)}) collective-permute-start(bf16[256,2048]{1,0:T(8,128)(2,1)} %copy-done.40), channel_id=1, source_target_pairs={{0,16},{8,24},{16,0},{24,8},{1,17},{9,25},{17,1},{25,9},{2,18},{10... | collective-permute-start | bytes 3145736 | tf_op jit(solution)/shard_map/ppermute | solution.py:616
  365.9 92.0 %collective-permute-start.29 = (bf16[512,1024]{1,0:T(8,128)(2,1)}, bf16[512,1024]{1,0:T(8,128)(2,1)S(1)}, u32[]{:S(2)}, u32[]{:S(2)}) collective-permute-start(bf16[512,1024]{1,0:T(8,128)(2,1)} %collective-permute-done.28), channel_id=1, source_target_pairs={{0,8},{8,0},{16,24},{24,16},{1,9},{9,1},{17,25},{25,17},{2,10},{10... | collective-permute-start | bytes 3145736 | tf_op jit(solution)/shard_map/ppermute | solution.py:616
  388.3 72.9 %collective-permute-start.30 = (bf16[512,1024]{1,0:T(8,128)(2,1)}, bf16[512,1024]{1,0:T(8,128)(2,1)S(1)}, u32[]{:S(2)}, u32[]{:S(2)}) collective-permute-start(bf16[512,1024]{1,0:T(8,128)(2,1)} %get-tuple-element.201), channel_id=1, source_target_pairs={{0,8},{8,0},{16,24},{24,16},{1,9},{9,1},{17,25},{25,17},{2,10},{10... | collective-permute-start | bytes 3145736 | tf_op jit(solution)/shard_map/ppermute | solution.py:616
  410.8 50.5 %collective-permute-start.32 = (bf16[512,1024]{1,0:T(8,128)(2,1)}, bf16[512,1024]{1,0:T(8,128)(2,1)S(1)}, u32[]{:S(2)}, u32[]{:S(2)}) collective-permute-start(bf16[512,1024]{1,0:T(8,128)(2,1)} %collective-permute-done.31), channel_id=1, source_target_pairs={{0,8},{8,0},{16,24},{24,16},{1,9},{9,1},{17,25},{25,17},{2,10},{10... | collective-permute-start | bytes 3145736 | tf_op jit(solution)/shard_map/ppermute | solution.py:616
  433.3 31.4 %collective-permute-start.33 = (bf16[256,2048]{1,0:T(8,128)(2,1)S(1)}, bf16[256,2048]{1,0:T(8,128)(2,1)S(1)}, u32[]{:S(2)}, u32[]{:S(2)}) collective-permute-start(bf16[256,2048]{1,0:T(8,128)(2,1)S(1)} %copy-done.15), channel_id=1, source_target_pairs={{0,8},{8,0},{16,24},{24,16},{1,9},{9,1},{17,25},{25,17},{2,10},{10... | collective-permute-start | bytes 3145736 | tf_op jit(solution)/shard_map/ppermute | solution.py:616
  585.5 191.5 %reduce-scatter.11.cloned.1.call-start = ((), (), s32[]{:S(2)}) async-start(), calls=%async_computation.16 | async-start | bytes 9437184 | tf_op jit(solution)/shard_map/reduce_scatter | solution.py:938
  680.1 336.9 %reduce-scatter.13.cloned.1.call-start = ((), (), s32[]{:S(2)}) async-start(), calls=%async_computation.17 | async-start | bytes 2359296 | tf_op jit(solution)/shard_map/reduce_scatter | solution.py:945
  698.3 339.6 %reduce-scatter.17.cloned.1.call-start = ((), (), s32[]{:S(2)}) async-start(), calls=%async_computation.19 | async-start | bytes 2359296 | tf_op jit(solution)/shard_map/reduce_scatter | solution.py:934
  702.4 365.7 %reduce-scatter.15.cloned.1.call-start = ((), (), s32[]{:S(2)}) async-start(), calls=%async_computation.18 | async-start | bytes 4718592 | tf_op jit(solution)/shard_map/reduce_scatter | solution.py:953
  797.5 276.0 %reduce-scatter.7.cloned.1.call-start = ((), (), s32[]{:S(2)}) async-start(), calls=%async_computation.14 | async-start | bytes 4718592 | tf_op jit(solution)/shard_map/reduce_scatter | solution.py:882
  802.2 55.6 %collective-permute-start.70 = (bf16[256,2048]{1,0:T(8,128)(2,1)}, bf16[256,2048]{1,0:T(8,128)(2,1)}, u32[]{:S(2)}, u32[]{:S(2)}) collective-permute-start(bf16[256,2048]{1,0:T(8,128)(2,1)} %convolution_convert_fusion.8), channel_id=1, source_target_pairs={{0,8},{8,0},{16,24},{24,16},{1,9},{9,1},{17,25},{25,17},{2,10},{10... | collective-permute-start | bytes 3145736 | tf_op jit(solution)/shard_map/ppermute | solution.py:616
  806.8 101.7 %collective-permute-start.69 = (bf16[256,2048]{1,0:T(8,128)(2,1)}, bf16[256,2048]{1,0:T(8,128)(2,1)}, u32[]{:S(2)}, u32[]{:S(2)}) collective-permute-start(bf16[256,2048]{1,0:T(8,128)(2,1)} %convolution_convert_fusion.10), channel_id=1, source_target_pairs={{0,8},{8,0},{16,24},{24,16},{1,9},{9,1},{17,25},{25,17},{2,10},{10... | collective-permute-start | bytes 3145736 | tf_op jit(solution)/shard_map/ppermute | solution.py:616
  812.4 62.8 %collective-permute-start.73 = (bf16[256,2048]{1,0:T(8,128)(2,1)}, bf16[256,2048]{1,0:T(8,128)(2,1)}, u32[]{:S(2)}, u32[]{:S(2)}) collective-permute-start(bf16[256,2048]{1,0:T(8,128)(2,1)} %convolution_convert_fusion.4), channel_id=1, source_target_pairs={{0,16},{8,24},{16,0},{24,8},{1,17},{9,25},{17,1},{25,9},{2,18},{10... | collective-permute-start | bytes 3145736 | tf_op jit(solution)/shard_map/ppermute | solution.py:616
  820.1 50.7 %collective-permute-start.64 = (bf16[512,1024]{1,0:T(8,128)(2,1)}, bf16[512,1024]{1,0:T(8,128)(2,1)}, u32[]{:S(2)}, u32[]{:S(2)}) collective-permute-start(bf16[512,1024]{1,0:T(8,128)(2,1)} %convolution_convert_fusion.16), channel_id=1, source_target_pairs={{0,8},{8,0},{16,24},{24,16},{1,9},{9,1},{17,25},{25,17},{2,10},{10... | collective-permute-start | bytes 3145736 | tf_op jit(solution)/shard_map/ppermute | solution.py:616
  829.0 43.9 %collective-permute-start.67 = (bf16[512,1024]{1,0:T(8,128)(2,1)}, bf16[512,1024]{1,0:T(8,128)(2,1)}, u32[]{:S(2)}, u32[]{:S(2)}) collective-permute-start(bf16[512,1024]{1,0:T(8,128)(2,1)} %convolution_convert_fusion.12), channel_id=1, source_target_pairs={{0,16},{8,24},{16,0},{24,8},{1,17},{9,25},{17,1},{25,9},{2,18},{10... | collective-permute-start | bytes 3145736 | tf_op jit(solution)/shard_map/ppermute | solution.py:616
  857.9 51.3 %collective-permute-start.72 = (bf16[256,2048]{1,0:T(8,128)(2,1)}, bf16[256,2048]{1,0:T(8,128)(2,1)S(1)}, u32[]{:S(2)}, u32[]{:S(2)}) collective-permute-start(bf16[256,2048]{1,0:T(8,128)(2,1)} %convolution_convert_fusion.6), channel_id=1, source_target_pairs={{0,16},{8,24},{16,0},{24,8},{1,17},{9,25},{17,1},{25,9},{2,18},{10... | collective-permute-start | bytes 3145736 | tf_op jit(solution)/shard_map/ppermute | solution.py:616
  872.9 33.7 %collective-permute-start.61 = (bf16[512,1024]{1,0:T(8,128)(2,1)S(1)}, bf16[512,1024]{1,0:T(8,128)(2,1)S(1)}, u32[]{:S(2)}, u32[]{:S(2)}) collective-permute-start(bf16[512,1024]{1,0:T(8,128)(2,1)S(1)} %copy-done.95), channel_id=1, source_target_pairs={{0,16},{8,24},{16,0},{24,8},{1,17},{9,25},{17,1},{25,9},{2,18},{10... | collective-permute-start | bytes 3145736 | tf_op jit(solution)/shard_map/ppermute | solution.py:616
  875.2 53.9 %collective-permute-start.71 = (bf16[256,2048]{1,0:T(8,128)(2,1)S(1)}, bf16[256,2048]{1,0:T(8,128)(2,1)S(1)}, u32[]{:S(2)}, u32[]{:S(2)}) collective-permute-start(bf16[256,2048]{1,0:T(8,128)(2,1)S(1)} %add_convert_fusion.4), channel_id=1, source_target_pairs={{0,16},{8,24},{16,0},{24,8},{1,17},{9,25},{17,1},{25,9},{2,18},{10... | collective-permute-start | bytes 3145736 | tf_op jit(solution)/shard_map/ppermute | solution.py:616
  893.9 38.6 %collective-permute-start.74 = (bf16[256,2048]{1,0:T(8,128)(2,1)S(1)}, bf16[256,2048]{1,0:T(8,128)(2,1)S(1)}, u32[]{:S(2)}, u32[]{:S(2)}) collective-permute-start(bf16[256,2048]{1,0:T(8,128)(2,1)S(1)} %add_convert_fusion.3), channel_id=1, source_target_pairs={{0,8},{8,0},{16,24},{24,16},{1,9},{9,1},{17,25},{25,17},{2,10},{10... | collective-permute-start | bytes 3145736 | tf_op jit(solution)/shard_map/ppermute | solution.py:616
  906.6 35.8 %collective-permute-start.63 = (bf16[512,1024]{1,0:T(8,128)(2,1)S(1)}, bf16[512,1024]{1,0:T(8,128)(2,1)S(1)}, u32[]{:S(2)}, u32[]{:S(2)}) collective-permute-start(bf16[512,1024]{1,0:T(8,128)(2,1)S(1)} %copy-done.94), channel_id=1, source_target_pairs={{0,8},{8,0},{16,24},{24,16},{1,9},{9,1},{17,25},{25,17},{2,10},{10... | collective-permute-start | bytes 3145736 | tf_op jit(solution)/shard_map/ppermute | solution.py:616
  908.6 66.6 %collective-permute-start.66 = (bf16[512,1024]{1,0:T(8,128)(2,1)S(1)}, bf16[512,1024]{1,0:T(8,128)(2,1)S(1)}, u32[]{:S(2)}, u32[]{:S(2)}) collective-permute-start(bf16[512,1024]{1,0:T(8,128)(2,1)S(1)} %copy-done.93), channel_id=1, source_target_pairs={{0,16},{8,24},{16,0},{24,8},{1,17},{9,25},{17,1},{25,9},{2,18},{10... | collective-permute-start | bytes 3145736 | tf_op jit(solution)/shard_map/ppermute | solution.py:616
  909.2 64.9 %collective-permute-start.65 = (bf16[512,1024]{1,0:T(8,128)(2,1)S(1)}, bf16[512,1024]{1,0:T(8,128)(2,1)S(1)}, u32[]{:S(2)}, u32[]{:S(2)}) collective-permute-start(bf16[512,1024]{1,0:T(8,128)(2,1)S(1)} %add_convert_fusion.6), channel_id=1, source_target_pairs={{0,16},{8,24},{16,0},{24,8},{1,17},{9,25},{17,1},{25,9},{2,18},{10... | collective-permute-start | bytes 3145736 | tf_op jit(solution)/shard_map/ppermute | solution.py:616
  929.1 47.6 %collective-permute-start.68 = (bf16[512,1024]{1,0:T(8,128)(2,1)S(1)}, bf16[512,1024]{1,0:T(8,128)(2,1)S(1)}, u32[]{:S(2)}, u32[]{:S(2)}) collective-permute-start(bf16[512,1024]{1,0:T(8,128)(2,1)S(1)} %add_convert_fusion.5), channel_id=1, source_target_pairs={{0,8},{8,0},{16,24},{24,16},{1,9},{9,1},{17,25},{25,17},{2,10},{10... | collective-permute-start | bytes 3145736 | tf_op jit(solution)/shard_map/ppermute | solution.py:616
  932.6 54.8 %collective-permute-start.57 = (bf16[512,1024]{1,0:T(8,128)(2,1)S(1)}, bf16[512,1024]{1,0:T(8,128)(2,1)S(1)}, u32[]{:S(2)}, u32[]{:S(2)}) collective-permute-start(bf16[512,1024]{1,0:T(8,128)(2,1)S(1)} %copy-done.92), channel_id=1, source_target_pairs={{0,8},{8,0},{16,24},{24,16},{1,9},{9,1},{17,25},{25,17},{2,10},{10... | collective-permute-start | bytes 3145736 | tf_op jit(solution)/shard_map/ppermute | solution.py:616
  942.5 72.6 %collective-permute-start.60 = (bf16[512,1024]{1,0:T(8,128)(2,1)S(1)}, bf16[512,1024]{1,0:T(8,128)(2,1)S(1)}, u32[]{:S(2)}, u32[]{:S(2)}) collective-permute-start(bf16[512,1024]{1,0:T(8,128)(2,1)S(1)} %copy-done.91), channel_id=1, source_target_pairs={{0,16},{8,24},{16,0},{24,8},{1,17},{9,25},{17,1},{25,9},{2,18},{10... | collective-permute-start | bytes 3145736 | tf_op jit(solution)/shard_map/ppermute | solution.py:616
  974.1 39.1 %collective-permute-start.59 = (bf16[512,1024]{1,0:T(8,128)(2,1)S(1)}, bf16[512,1024]{1,0:T(8,128)(2,1)S(1)}, u32[]{:S(2)}, u32[]{:S(2)}) collective-permute-start(bf16[512,1024]{1,0:T(8,128)(2,1)S(1)} %add_convert_fusion.8), channel_id=1, source_target_pairs={{0,16},{8,24},{16,0},{24,8},{1,17},{9,25},{17,1},{25,9},{2,18},{10... | collective-permute-start | bytes 3145736 | tf_op jit(solution)/shard_map/ppermute | solution.py:616
  975.2 39.9 %collective-permute-start.62 = (bf16[512,1024]{1,0:T(8,128)(2,1)S(1)}, bf16[512,1024]{1,0:T(8,128)(2,1)S(1)}, u32[]{:S(2)}, u32[]{:S(2)}) collective-permute-start(bf16[512,1024]{1,0:T(8,128)(2,1)S(1)} %add_convert_fusion.7), channel_id=1, source_target_pairs={{0,8},{8,0},{16,24},{24,16},{1,9},{9,1},{17,25},{25,17},{2,10},{10... | collective-permute-start | bytes 3145736 | tf_op jit(solution)/shard_map/ppermute | solution.py:616
  (142 other events, 3675.6 us)
Sparse Core Ops, SparseCore 0:
  24.2 47.9 all-gather.9
  74.3 27.9 all-gather.7
  104.5 81.4 all-gather.11
  187.4 27.5 all-gather.13
  216.5 46.3 all-gather.17
  264.9 45.6 all-gather.15
  579.2 48.4 reduce-scatter.8
  680.2 96.6 reduce-scatter.10
  779.3 34.5 reduce-scatter.12
  815.9 34.6 reduce-scatter.16
  853.0 48.4 reduce-scatter.14
  903.6 48.3 reduce-scatter.6

commit v3 on v2

--- a/solution.py
+++ b/solution.py
@@ -571,15 +571,19 @@
 def dispatch_kernel(codes, chosen_weights, rows, *outs, capacity, experts):
     blocks, tokens = codes.shape[1:]
     numbers = lax.broadcasted_iota(jnp.int32, (capacity, tokens), 0)
-    for item in range(experts):
-        for block in range(blocks):
-            placed = numbers == codes[item, block : block + 1, :]
-            span = slice(block * capacity, (block + 1) * capacity)
-            outs[item][span, :] = jnp.dot(
-                placed.astype(jnp.bfloat16),
-                rows[block * tokens : (block + 1) * tokens, :],
-                preferred_element_type=jnp.float32,
-            ).astype(jnp.bfloat16)
+    for block in range(blocks):
+        span = slice(block * capacity, (block + 1) * capacity)
+        placed = [
+            (numbers == codes[item, block : block + 1, :]).astype(jnp.bfloat16)
+            for item in range(experts)
+        ]
+        found = jnp.dot(
+            jnp.concatenate(placed, axis=0),
+            rows[block * tokens : (block + 1) * tokens, :],
+            preferred_element_type=jnp.float32,
+        ).astype(jnp.bfloat16)
+        for item in range(experts):
+            outs[item][span, :] = found[item * capacity : (item + 1) * capacity, :]
 
     @pl.when(pl.program_id(0) == 0)
     def weigh():
@@ -609,6 +613,39 @@
         + [jax.ShapeDtypeStruct((slots, 1), jnp.float32)] * experts,
     )(codes, chosen_weights, rows)
     return results[:experts], results[experts:]
+
+
+def collect_kernel(codes, *refs, capacity, experts):
+    out = refs[-1]
+    blocks, tokens = codes.shape[1:]
+    numbers = lax.broadcasted_iota(jnp.int32, (capacity, tokens), 0)
+    for block in range(blocks):
+        span = slice(block * capacity, (block + 1) * capacity)
+        placed = [
+            (numbers == codes[item, block : block + 1, :]).astype(jnp.bfloat16)
+            for item in range(experts)
+        ]
+        total = lax.dot_general(
+            jnp.concatenate(placed, axis=0),
+            jnp.concatenate([refs[item][span, :] for item in range(experts)], axis=0),
+            (((0,), (0,)), ((), ())),
+            preferred_element_type=jnp.float32,
+        )
+        out[block * tokens : (block + 1) * tokens, :] = total.astype(jnp.bfloat16)
+
+
+def collect(codes, arrays, capacity):
+    experts, blocks, tokens = codes.shape
+    slots, width = arrays[0].shape
+    block = min(width, 512)
+    return pl.pallas_call(
+        partial(collect_kernel, capacity=capacity, experts=experts),
+        grid=(width // block,),
+        in_specs=[pl.BlockSpec(codes.shape, lambda step: (0, 0, 0))]
+        + [pl.BlockSpec((slots, block), lambda step: (0, step))] * experts,
+        out_specs=pl.BlockSpec((blocks * tokens, block), lambda step: (0, step)),
+        out_shape=jax.ShapeDtypeStruct((blocks * tokens, width), jnp.bfloat16),
+    )(codes, *arrays)
 
 
 def exchange(array, offset):
@@ -853,15 +890,18 @@
     ]
 
     def back_to_rows(which):
+        arrays = [result[which] for result in results]
+        if capacity % 16 == 0:
+            return collect(codes_here, arrays, capacity)
         return sum(
             jnp.einsum(
                 "srt,srd->std",
                 place[item],
-                results[item][which].reshape(blocks, capacity, width),
+                arrays[item].reshape(blocks, capacity, width),
                 preferred_element_type=f32,
             )
             for item in range(local_experts)
-        )
+        ).astype(bf16)
 
     incoming = back_to_rows(5)
     combined = back_to_rows(3)
@@ -874,13 +914,13 @@
         for item in range(local_experts)
     ]
     routed_grad = lax.psum_scatter(
-        incoming.astype(bf16).reshape(blocks * rows, width),
+        incoming.reshape(blocks * rows, width),
         "blk",
         scatter_dimension=0,
         tiled=True,
     )
     combined = lax.psum_scatter(
-        combined.astype(bf16).reshape(blocks * rows, width),
+        combined.reshape(blocks * rows, width),
         "blk",
         scatter_dimension=0,
         tiled=True,
@@ -892,24 +932,26 @@
 
     def pieces_of(left, right):
         size = left.shape[1] // heads_axis
-        return [
-            lax.optimization_barrier(
-                jnp.dot(
-                    left[:, offset * size : (offset + 1) * size].T,
-                    right,
-                    preferred_element_type=f32,
-                ).astype(bf16)
+        products = []
+        for offset in range(heads_axis):
+            product = jnp.dot(
+                left[:, offset * size : (offset + 1) * size].T,
+                right,
+                preferred_element_type=f32,
             )
-            for offset in range(heads_axis)
-        ]
+            products.append(lax.optimization_barrier(product.astype(bf16)))
+        return products
+
+    def stacked(items):
+        return jnp.stack(items).astype(f32)
 
     down_out, gate_out, up_out = (
-        jnp.stack(
+        stacked(
             [
                 scatter_pieces(pieces_of(store[left], store[right]), item)
                 for item, store in enumerate(stores)
             ]
-        ).astype(f32)
+        )
         for left, right in ((2, 1), (0, 3), (0, 4))
     )
 

time: 1100 us -> 1100 us (level)
  matrix products: 98.9 us -> 80.5 us
  Pallas kernels: 138 us -> 150 us
    dot_general x4 -> x0, matrix products: 18.3 us -> none  [back_to_rows(): jnp.einsum('srt,srd->std', place[item], results[item][which].reshape(bloc...]
    pallas_call x0 -> x2, Pallas kernels: none -> 11.9 us  [collect(): pl.pallas_call(partial(collect_kernel, capacity=capacity, experts=experts...]
  transfers between devices with their start and end apart: 89 -> 89, of which waited for: 39 -> 41; matrix products, arithmetic and copies ran while one was open for 18% -> 18% of each run, Pallas kernels for 5% -> 5%
where the time goes in v3:
time: 1100 us; the launch traced here: 1090 us
  waiting for transfers between devices  587 us (53%)
  Pallas kernels  150 us (14%)
  starting transfers between devices  92.3 us (8%)
  other arithmetic  83 us (8%)
  matrix products  80.5 us (7%)
  local copies, waits for them, and re-layouts  62.5 us (6%)
  between operations  16.1 us (1%)
  blocking collectives  14.9 us (1%)
    ppermute x75, waiting for transfers between devices, exchange(): lax.ppermute(array, 'head', [(at, at ^ offset) for at in range(count)])  387 us
    ppermute x75, starting transfers between devices, exchange(): lax.ppermute(array, 'head', [(at, at ^ offset) for at in range(count)])  81.2 us
    reduce_scatter x1, waiting for transfers between devices, layer(): lax.psum_scatter(pairs_back, 'blk', scatter_dimension=0, tiled=True)  74.6 us
    all_gather x1, waiting for transfers between devices, layer(): pairs_all = lax.all_gather(pairs, 'blk', axis=0, tiled=True)  66.2 us
    pallas_call x2, Pallas kernels, run_expert(): pl.pallas_call(expert_kernel, grid_spec=pltpu.PrefetchScalarGridSpec(num_...  62.6 us
    dot_general x24, matrix products, pieces_of(): jnp.dot(left[:, offset * size:(offset + 1) * size].T, right, preferred_el...  47.2 us
    reduce_scatter x1, waiting for transfers between devices, layer(): lax.psum_scatter(incoming.reshape(blocks * rows, width), 'blk', scatter_d...  36.3 us
    concatenate x6, other arithmetic, layer(): jnp.concatenate(pieces, axis=0)  30.9 us
  transfers between devices with their start and end apart: 89, of which 41 were waited for; matrix products, arithmetic and copies ran while one was open for 18% of the time, Pallas kernels for 5%

profile of v3, /device:TPU:0, one launch (start us, length us, event | category | flops | bytes accessed | tf_op | source)
XLA Modules:
  0.0 1085.3 jit_solution(6110876678865315143)
XLA Ops:
  14.1 5.0 collective-permute-done.6
  28.5 14.9 %all-gather = bf16[8,1,3328]{2,1,0:T(2,128)(2,1)S(1)} all-gather(bf16[1,1,3328]{2,1,0:T(2,128)(2,1)S(1)} %maximum_bitcast_fusion), channel_id=1, replica_groups=mesh['head'=4,'blk'=8] {'blk'}, dimensions={0}, use_global_device_ids=true | all-gather | bytes 59904 | tf_op jit(solution)/shard_map/all_gather | solution.py:793
  57.3 4.4 collective-permute-done.refs_1_
  61.7 11.0 %collective-permute-done.1.refs_2_ = bf16[128,2048]{1,0:T(8,128)(2,1)S(1)} collective-permute-done((bf16[128,2048]{1,0:T(8,128)(2,1)S(1)}, bf16[128,2048]{1,0:T(8,128)(2,1)S(1)}, u32[]{:S(2)}, u32[]{:S(2)}) %collective-permute-start.1) | collective-permute-done | bytes 524320 | tf_op jit(solution)/shard_map/ppermute | solution.py:653
  77.4 4.9 copy.119
  82.3 4.6 shard_map.292
  105.7 4.4 shard_map.290
  119.9 66.2 %all-gather.12.cloned.1.call-done.pairs = bf16[4096,1024]{1,0:T(8,128)(2,1)} async-done(((bf16[512,1024]{1,0:T(8,128)(2,1)}), bf16[4096,1024]{1,0:T(8,128)(2,1)}) %all-gather.12.cloned.1.call-update) | async-done | bytes 8388624 | tf_op jit(solution)/shard_map/all_gather | solution.py:835
  187.7 11.4 %attend_forward.1 = (f32[512,512]{1,0:T(8,128)}, bf16[512,512]{1,0:T(8,128)(2,1)}, f32[512,512]{1,0:T(8,128)}) custom-call(s32[2,16]{1,0:T(2,128)} %select_reduce_fusion.2.listed, s32[2]{0:T(128)} %get-tuple-element.194.counts, bf16[512,512]{1,0:T(8,128)(2,1)} %get-tuple-element.55.query, bf16[4096,1024]{1,0:T(8,128)(2,1)} %all-gather.12.cloned.1.call-done.pairs, ...), custom_call_target="tpu_custom_call" | custom-call | tf_op jit(solution)/shard_map/attend_forward/pallas_call | solution.py:299
  199.1 16.0 %all-gather.14.cloned.1.call-done = bf16[512,2048]{1,0:T(8,128)(2,1)} async-done(((bf16[64,2048]{1,0:T(8,128)(2,1)}), bf16[512,2048]{1,0:T(8,128)(2,1)}) %all-gather.14.cloned.1.call-update) | async-done | bytes 2097168 | tf_op jit(solution)/shard_map/all_gather | solution.py:772
  221.9 11.3 %collective-permute-done.15 = bf16[128,2048]{1,0:T(8,128)(2,1)S(1)} collective-permute-done((bf16[128,2048]{1,0:T(8,128)(2,1)S(1)}, bf16[128,2048]{1,0:T(8,128)(2,1)S(1)}, u32[]{:S(2)}, u32[]{:S(2)}) %collective-permute-start.15) | collective-permute-done | bytes 524320 | tf_op jit(solution)/shard_map/ppermute | solution.py:653
  233.2 11.7 %collective-permute-done.16 = bf16[128,2048]{1,0:T(8,128)(2,1)S(1)} collective-permute-done((bf16[128,2048]{1,0:T(8,128)(2,1)S(1)}, bf16[128,2048]{1,0:T(8,128)(2,1)S(1)}, u32[]{:S(2)}, u32[]{:S(2)}) %collective-permute-start.16) | collective-permute-done | bytes 524320 | tf_op jit(solution)/shard_map/ppermute | solution.py:653
  257.0 18.3 %collective-permute-done.18 = bf16[512,1024]{1,0:T(8,128)(2,1)} collective-permute-done((bf16[512,1024]{1,0:T(8,128)(2,1)S(1)}, bf16[512,1024]{1,0:T(8,128)(2,1)}, u32[]{:S(2)}, u32[]{:S(2)}) %collective-permute-start.18) | collective-permute-done | bytes 1048608 | tf_op jit(solution)/shard_map/ppermute | solution.py:653
  277.3 20.3 %collective-permute-done.21 = bf16[512,1024]{1,0:T(8,128)(2,1)S(1)} collective-permute-done((bf16[512,1024]{1,0:T(8,128)(2,1)S(1)}, bf16[512,1024]{1,0:T(8,128)(2,1)S(1)}, u32[]{:S(2)}, u32[]{:S(2)}) %collective-permute-start.21) | collective-permute-done | bytes 1048608 | tf_op jit(solution)/shard_map/ppermute | solution.py:653
  301.1 19.1 %collective-permute-done.24 = bf16[256,2048]{1,0:T(8,128)(2,1)} collective-permute-done((bf16[256,2048]{1,0:T(8,128)(2,1)}, bf16[256,2048]{1,0:T(8,128)(2,1)}, u32[]{:S(2)}, u32[]{:S(2)}) %collective-permute-start.24) | collective-permute-done | bytes 1048608 | tf_op jit(solution)/shard_map/ppermute | solution.py:653
  323.3 20.6 %collective-permute-done.28 = bf16[512,1024]{1,0:T(8,128)(2,1)} collective-permute-done((bf16[512,1024]{1,0:T(8,128)(2,1)S(1)}, bf16[512,1024]{1,0:T(8,128)(2,1)}, u32[]{:S(2)}, u32[]{:S(2)}) %collective-permute-start.28) | collective-permute-done | bytes 1048608 | tf_op jit(solution)/shard_map/ppermute | solution.py:653
  353.7 12.7 %collective-permute-done.20 = bf16[512,1024]{1,0:T(8,128)(2,1)} collective-permute-done((bf16[512,1024]{1,0:T(8,128)(2,1)}, bf16[512,1024]{1,0:T(8,128)(2,1)}, u32[]{:S(2)}, u32[]{:S(2)}) %collective-permute-start.20) | collective-permute-done | bytes 1048608 | tf_op jit(solution)/shard_map/ppermute | solution.py:653
  371.3 17.6 %collective-permute-done.31 = bf16[512,1024]{1,0:T(8,128)(2,1)} collective-permute-done((bf16[512,1024]{1,0:T(8,128)(2,1)}, bf16[512,1024]{1,0:T(8,128)(2,1)}, u32[]{:S(2)}, u32[]{:S(2)}) %collective-permute-start.31) | collective-permute-done | bytes 1048608 | tf_op jit(solution)/shard_map/ppermute | solution.py:653
  389.7 21.6 %collective-permute-done.23 = bf16[512,1024]{1,0:T(8,128)(2,1)} collective-permute-done((bf16[512,1024]{1,0:T(8,128)(2,1)}, bf16[512,1024]{1,0:T(8,128)(2,1)}, u32[]{:S(2)}, u32[]{:S(2)}) %collective-permute-start.23) | collective-permute-done | bytes 1048608 | tf_op jit(solution)/shard_map/ppermute | solution.py:653
  415.4 18.4 %collective-permute-done.34 = bf16[256,2048]{1,0:T(8,128)(2,1)} collective-permute-done((bf16[256,2048]{1,0:T(8,128)(2,1)}, bf16[256,2048]{1,0:T(8,128)(2,1)}, u32[]{:S(2)}, u32[]{:S(2)}) %collective-permute-start.34) | collective-permute-done | bytes 1048608 | tf_op jit(solution)/shard_map/ppermute | solution.py:653
  434.6 19.9 %collective-permute-done.26 = bf16[256,2048]{1,0:T(8,128)(2,1)} collective-permute-done((bf16[256,2048]{1,0:T(8,128)(2,1)}, bf16[256,2048]{1,0:T(8,128)(2,1)}, u32[]{:S(2)}, u32[]{:S(2)}) %collective-permute-start.26) | collective-permute-done | bytes 1048608 | tf_op jit(solution)/shard_map/ppermute | solution.py:653
  462.3 8.9 pad_maximum_fusion.4.up_weight
  471.2 6.9 collective-permute-done.35
  478.1 7.5 pad_maximum_fusion.5.down_weight
  486.3 6.3 shard_map.295
  496.7 6.3 shard_map.294
  503.0 31.3 %run_expert.2 = (bf16[640,1024]{1,0:T(8,128)(2,1)}, bf16[640,1024]{1,0:T(8,128)(2,1)}, bf16[640,1024]{1,0:T(8,128)(2,1)}, bf16[640,2048]{1,0:T(8,128)(2,1)}, f32...) custom-call(s32[4]{0:T(128)} %iota_xor_fusion.perm, ...), custom_call_target="tpu_custom_call" | custom-call | tf_op jit(solution)/shard_map/run_expert/pallas_call | solution.py:531
  534.3 31.3 %run_expert.3 = (bf16[640,1024]{1,0:T(8,128)(2,1)}, bf16[640,1024]{1,0:T(8,128)(2,1)}, bf16[640,1024]{1,0:T(8,128)(2,1)}, bf16[640,2048]{1,0:T(8,128)(2,1)}, f32...) custom-call(s32[4]{0:T(128)} %iota_xor_fusion.perm, ...), custom_call_target="tpu_custom_call" | custom-call | tf_op jit(solution)/shard_map/run_expert/pallas_call | solution.py:531
  565.6 5.8 shard_map.297
  577.9 5.7 all-to-all-done
  583.6 36.3 %reduce-scatter.9.cloned.1.call-done = bf16[128,2048]{1,0:T(8,128)(2,1)} async-done(((bf16[1024,2048]{1,0:T(8,128)(2,1)}), bf16[128,2048]{1,0:T(8,128)(2,1)}) %reduce-scatter.9.cloned.1.call-update) | async-done | bytes 524304 | tf_op jit(solution)/shard_map/reduce_scatter | solution.py:916
  626.8 11.3 %collective-permute-done.36 = bf16[128,2048]{1,0:T(8,128)(2,1)S(1)} collective-permute-done((bf16[128,2048]{1,0:T(8,128)(2,1)S(1)}, bf16[128,2048]{1,0:T(8,128)(2,1)S(1)}, u32[]{:S(2)}, u32[]{:S(2)}) %collective-permute-start.36) | collective-permute-done | bytes 524320 | tf_op jit(solution)/shard_map/ppermute | solution.py:653
  638.1 9.4 collective-permute-done.37
  653.0 19.6 %attend_backward.1 = (bf16[512,512]{1,0:T(8,128)(2,1)}, bf16[4096,1024]{1,0:T(8,128)(2,1)}) custom-call(s32[2,16]{1,0:T(2,128)} %copy-done.56, bf16[512,512]{1,0:T(8,128)(2,1)} %get-tuple-element.55.query, bf16[4096,1024]{1,0:T(8,128)(2,1)} %all-gather.12.cloned.1.call-done.pairs, bf16[512,512]{1,0:T(8,128)(2,1)} %convolution_convert_fusion.28.grad, ...), custom_call_target="tpu_custom_call" | custom-call | tf_op jit(solution)/shard_map/attend_backward/pallas_call | solution.py:409
  694.8 74.6 %reduce-scatter.11.cloned.1.call-done.back.refs_7_ = bf16[512,1024]{1,0:T(8,128)(2,1)} async-done(((bf16[4096,1024]{1,0:T(8,128)(2,1)}), bf16[512,1024]{1,0:T(8,128)(2,1)}) %reduce-scatter.11.cloned.1.call-update) | async-done | bytes 1048592 | tf_op jit(solution)/shard_map/reduce_scatter | solution.py:980
  784.4 5.5 convolution_convert_fusion
  845.1 6.1 shard_map.296
  854.0 9.2 collective-permute-done.64
  870.8 15.6 %collective-permute-done.58 = bf16[512,1024]{1,0:T(8,128)(2,1)S(1)} collective-permute-done((bf16[512,1024]{1,0:T(8,128)(2,1)S(1)}, bf16[512,1024]{1,0:T(8,128)(2,1)S(1)}, u32[]{:S(2)}, u32[]{:S(2)}) %collective-permute-start.58) | collective-permute-done | bytes 1048608 | tf_op jit(solution)/shard_map/ppermute | solution.py:653
  887.3 12.9 %collective-permute-done.61 = bf16[512,1024]{1,0:T(8,128)(2,1)S(1)} collective-permute-done((bf16[512,1024]{1,0:T(8,128)(2,1)S(1)}, bf16[512,1024]{1,0:T(8,128)(2,1)S(1)}, u32[]{:S(2)}, u32[]{:S(2)}) %collective-permute-start.61) | collective-permute-done | bytes 1048608 | tf_op jit(solution)/shard_map/ppermute | solution.py:653
  904.3 18.4 %collective-permute-done.71 = bf16[256,2048]{1,0:T(8,128)(2,1)S(1)} collective-permute-done((bf16[256,2048]{1,0:T(8,128)(2,1)S(1)}, bf16[256,2048]{1,0:T(8,128)(2,1)S(1)}, u32[]{:S(2)}, u32[]{:S(2)}) %collective-permute-start.71) | collective-permute-done | bytes 1048608 | tf_op jit(solution)/shard_map/ppermute | solution.py:653
  927.1 7.8 collective-permute-done.63
  935.4 32.2 %collective-permute-done.65 = bf16[512,1024]{1,0:T(8,128)(2,1)S(1)} collective-permute-done((bf16[512,1024]{1,0:T(8,128)(2,1)S(1)}, bf16[512,1024]{1,0:T(8,128)(2,1)S(1)}, u32[]{:S(2)}, u32[]{:S(2)}) %collective-permute-start.65) | collective-permute-done | bytes 1048608 | tf_op jit(solution)/shard_map/ppermute | solution.py:653
  975.5 4.3 collective-permute-done.57
  979.8 26.9 %collective-permute-done.59 = bf16[512,1024]{1,0:T(8,128)(2,1)S(1)} collective-permute-done((bf16[512,1024]{1,0:T(8,128)(2,1)S(1)}, bf16[512,1024]{1,0:T(8,128)(2,1)S(1)}, u32[]{:S(2)}, u32[]{:S(2)}) %collective-permute-start.59) | collective-permute-done | bytes 1048608 | tf_op jit(solution)/shard_map/ppermute | solution.py:653
  1015.0 4.7 fusion.68
  1035.5 6.4 collective-permute-done.46
  1055.7 6.8 all-to-all-start.1
  (550 shorter events, 316.8 us)
Async XLA Ops:
  7.2 70.2 %all-gather.10.cloned.1.call-start = ((), (), s32[]{:S(2)}) async-start(), calls=%async_computation.9 | async-start | bytes 4718592 | tf_op jit(solution)/shard_map/all_gather | solution.py:775
  24.1 78.4 %all-gather.8.cloned.1.call-start = ((), (), s32[]{:S(2)}) async-start(), calls=%async_computation.8 | async-start | bytes 2359296 | tf_op jit(solution)/shard_map/all_gather | solution.py:777
  27.9 158.1 %all-gather.12.cloned.1.call-start = ((), (), s32[]{:S(2)}) async-start(), calls=%async_computation.10 | async-start | bytes 9437184 | tf_op jit(solution)/shard_map/all_gather | solution.py:835
  48.4 24.3 %collective-permute-start.1 = (bf16[128,2048]{1,0:T(8,128)(2,1)S(1)}, bf16[128,2048]{1,0:T(8,128)(2,1)S(1)}, u32[]{:S(2)}, u32[]{:S(2)}) collective-permute-start(bf16[128,2048]{1,0:T(8,128)(2,1)S(1)} %copy-done.9), channel_id=1, source_target_pairs={{0,16},{8,24},{16,0},{24,8},{1,17},{9,25},{17,1},{25,9},{2,18},{10... | collective-permute-start | bytes 1572872 | tf_op jit(solution)/shard_map/ppermute | solution.py:653
  97.9 117.2 %all-gather.14.cloned.1.call-start = ((), (), s32[]{:S(2)}) async-start(), calls=%async_computation.11 | async-start | bytes 2359296 | tf_op jit(solution)/shard_map/all_gather | solution.py:772
  98.5 387.1 %all-gather.18.cloned.1.call-start = ((), (), s32[]{:S(2)}) async-start(), calls=%async_computation.13 | async-start | bytes 4718592 | tf_op jit(solution)/shard_map/all_gather | solution.py:779
  99.1 393.5 %all-gather.16.cloned.1.call-start = ((), (), s32[]{:S(2)}) async-start(), calls=%async_computation.12 | async-start | bytes 4718592 | tf_op jit(solution)/shard_map/all_gather | solution.py:844
  219.9 25.0 %collective-permute-start.16 = (bf16[128,2048]{1,0:T(8,128)(2,1)S(1)}, bf16[128,2048]{1,0:T(8,128)(2,1)S(1)}, u32[]{:S(2)}, u32[]{:S(2)}) collective-permute-start(bf16[128,2048]{1,0:T(8,128)(2,1)S(1)} %get-tuple-element.207), channel_id=1, source_target_pairs={{0,16},{8,24},{16,0},{24,8},{1,17},{9,25},{17,1},{25,9},{2,18},{10... | collective-permute-start | bytes 1572872 | tf_op jit(solution)/shard_map/ppermute | solution.py:653
  247.2 372.8 %reduce-scatter.9.cloned.1.call-start = ((), (), s32[]{:S(2)}) async-start(), calls=%async_computation.15 | async-start | bytes 4718592 | tf_op jit(solution)/shard_map/reduce_scatter | solution.py:916
  249.1 26.2 %collective-permute-start.18 = (bf16[512,1024]{1,0:T(8,128)(2,1)S(1)}, bf16[512,1024]{1,0:T(8,128)(2,1)}, u32[]{:S(2)}, u32[]{:S(2)}) collective-permute-start(bf16[512,1024]{1,0:T(8,128)(2,1)S(1)} %get-tuple-element.204), channel_id=1, source_target_pairs={{0,8},{8,0},{16,24},{24,16},{1,9},{9,1},{17,25},{25,17},{2,10},{10... | collective-permute-start | bytes 3145736 | tf_op jit(solution)/shard_map/ppermute | solution.py:653
  250.4 26.4 %collective-permute-start.19 = (bf16[512,1024]{1,0:T(8,128)(2,1)S(1)}, bf16[512,1024]{1,0:T(8,128)(2,1)S(1)}, u32[]{:S(2)}, u32[]{:S(2)}) collective-permute-start(bf16[512,1024]{1,0:T(8,128)(2,1)S(1)} %get-tuple-element.204), channel_id=1, source_target_pairs={{0,16},{8,24},{16,0},{24,8},{1,17},{9,25},{17,1},{25,9},{2,18},{10... | collective-permute-start | bytes 3145736 | tf_op jit(solution)/shard_map/ppermute | solution.py:653
  252.4 45.3 %collective-permute-start.21 = (bf16[512,1024]{1,0:T(8,128)(2,1)S(1)}, bf16[512,1024]{1,0:T(8,128)(2,1)S(1)}, u32[]{:S(2)}, u32[]{:S(2)}) collective-permute-start(bf16[512,1024]{1,0:T(8,128)(2,1)S(1)} %get-tuple-element.202), channel_id=1, source_target_pairs={{0,8},{8,0},{16,24},{24,16},{1,9},{9,1},{17,25},{25,17},{2,10},{10... | collective-permute-start | bytes 3145736 | tf_op jit(solution)/shard_map/ppermute | solution.py:653
  253.8 45.0 %collective-permute-start.22 = (bf16[512,1024]{1,0:T(8,128)(2,1)S(1)}, bf16[512,1024]{1,0:T(8,128)(2,1)S(1)}, u32[]{:S(2)}, u32[]{:S(2)}) collective-permute-start(bf16[512,1024]{1,0:T(8,128)(2,1)S(1)} %get-tuple-element.202), channel_id=1, source_target_pairs={{0,16},{8,24},{16,0},{24,8},{1,17},{9,25},{17,1},{25,9},{2,18},{10... | collective-permute-start | bytes 3145736 | tf_op jit(solution)/shard_map/ppermute | solution.py:653
  255.8 64.4 %collective-permute-start.24 = (bf16[256,2048]{1,0:T(8,128)(2,1)}, bf16[256,2048]{1,0:T(8,128)(2,1)}, u32[]{:S(2)}, u32[]{:S(2)}) collective-permute-start(bf16[256,2048]{1,0:T(8,128)(2,1)} %get-tuple-element.200), channel_id=1, source_target_pairs={{0,8},{8,0},{16,24},{24,16},{1,9},{9,1},{17,25},{25,17},{2,10},{10... | collective-permute-start | bytes 3145736 | tf_op jit(solution)/shard_map/ppermute | solution.py:653
  275.3 46.4 %collective-permute-start.25 = (bf16[256,2048]{1,0:T(8,128)(2,1)}, bf16[256,2048]{1,0:T(8,128)(2,1)}, u32[]{:S(2)}, u32[]{:S(2)}) collective-permute-start(bf16[256,2048]{1,0:T(8,128)(2,1)} %get-tuple-element.200), channel_id=1, source_target_pairs={{0,16},{8,24},{16,0},{24,8},{1,17},{9,25},{17,1},{25,9},{2,18},{10... | collective-permute-start | bytes 3145736 | tf_op jit(solution)/shard_map/ppermute | solution.py:653
  276.8 67.1 %collective-permute-start.28 = (bf16[512,1024]{1,0:T(8,128)(2,1)S(1)}, bf16[512,1024]{1,0:T(8,128)(2,1)}, u32[]{:S(2)}, u32[]{:S(2)}) collective-permute-start(bf16[512,1024]{1,0:T(8,128)(2,1)S(1)} %get-tuple-element.203), channel_id=1, source_target_pairs={{0,16},{8,24},{16,0},{24,8},{1,17},{9,25},{17,1},{25,9},{2,18},{10... | collective-permute-start | bytes 3145736 | tf_op jit(solution)/shard_map/ppermute | solution.py:653
  297.7 47.1 %collective-permute-start.27 = (bf16[512,1024]{1,0:T(8,128)(2,1)S(1)}, bf16[512,1024]{1,0:T(8,128)(2,1)}, u32[]{:S(2)}, u32[]{:S(2)}) collective-permute-start(bf16[512,1024]{1,0:T(8,128)(2,1)S(1)} %get-tuple-element.203), channel_id=1, source_target_pairs={{0,8},{8,0},{16,24},{24,16},{1,9},{9,1},{17,25},{25,17},{2,10},{10... | collective-permute-start | bytes 3145736 | tf_op jit(solution)/shard_map/ppermute | solution.py:653
  299.9 66.5 %collective-permute-start.20 = (bf16[512,1024]{1,0:T(8,128)(2,1)}, bf16[512,1024]{1,0:T(8,128)(2,1)}, u32[]{:S(2)}, u32[]{:S(2)}) collective-permute-start(bf16[512,1024]{1,0:T(8,128)(2,1)} %collective-permute-done.18), channel_id=1, source_target_pairs={{0,16},{8,24},{16,0},{24,8},{1,17},{9,25},{17,1},{25,9},{2,18},{10... | collective-permute-start | bytes 3145736 | tf_op jit(solution)/shard_map/ppermute | solution.py:653
  320.3 68.6 %collective-permute-start.31 = (bf16[512,1024]{1,0:T(8,128)(2,1)}, bf16[512,1024]{1,0:T(8,128)(2,1)}, u32[]{:S(2)}, u32[]{:S(2)}) collective-permute-start(bf16[512,1024]{1,0:T(8,128)(2,1)} %get-tuple-element.201), channel_id=1, source_target_pairs={{0,16},{8,24},{16,0},{24,8},{1,17},{9,25},{17,1},{25,9},{2,18},{10... | collective-permute-start | bytes 3145736 | tf_op jit(solution)/shard_map/ppermute | solution.py:653
  321.7 89.6 %collective-permute-start.23 = (bf16[512,1024]{1,0:T(8,128)(2,1)}, bf16[512,1024]{1,0:T(8,128)(2,1)}, u32[]{:S(2)}, u32[]{:S(2)}) collective-permute-start(bf16[512,1024]{1,0:T(8,128)(2,1)} %copy-done.37), channel_id=1, source_target_pairs={{0,16},{8,24},{16,0},{24,8},{1,17},{9,25},{17,1},{25,9},{2,18},{10... | collective-permute-start | bytes 3145736 | tf_op jit(solution)/shard_map/ppermute | solution.py:653
  343.9 89.9 %collective-permute-start.34 = (bf16[256,2048]{1,0:T(8,128)(2,1)}, bf16[256,2048]{1,0:T(8,128)(2,1)}, u32[]{:S(2)}, u32[]{:S(2)}) collective-permute-start(bf16[256,2048]{1,0:T(8,128)(2,1)} %get-tuple-element.199), channel_id=1, source_target_pairs={{0,16},{8,24},{16,0},{24,8},{1,17},{9,25},{17,1},{25,9},{2,18},{10... | collective-permute-start | bytes 3145736 | tf_op jit(solution)/shard_map/ppermute | solution.py:653
  344.8 109.7 %collective-permute-start.26 = (bf16[256,2048]{1,0:T(8,128)(2,1)}, bf16[256,2048]{1,0:T(8,128)(2,1)}, u32[]{:S(2)}, u32[]{:S(2)}) collective-permute-start(bf16[256,2048]{1,0:T(8,128)(2,1)} %collective-permute-done.24), channel_id=1, source_target_pairs={{0,16},{8,24},{16,0},{24,8},{1,17},{9,25},{17,1},{25,9},{2,18},{10... | collective-permute-start | bytes 3145736 | tf_op jit(solution)/shard_map/ppermute | solution.py:653
  366.4 92.5 %collective-permute-start.29 = (bf16[512,1024]{1,0:T(8,128)(2,1)}, bf16[512,1024]{1,0:T(8,128)(2,1)S(1)}, u32[]{:S(2)}, u32[]{:S(2)}) collective-permute-start(bf16[512,1024]{1,0:T(8,128)(2,1)} %collective-permute-done.28), channel_id=1, source_target_pairs={{0,8},{8,0},{16,24},{24,16},{1,9},{9,1},{17,25},{25,17},{2,10},{10... | collective-permute-start | bytes 3145736 | tf_op jit(solution)/shard_map/ppermute | solution.py:653
  388.9 73.4 %collective-permute-start.30 = (bf16[512,1024]{1,0:T(8,128)(2,1)S(1)}, bf16[512,1024]{1,0:T(8,128)(2,1)S(1)}, u32[]{:S(2)}, u32[]{:S(2)}) collective-permute-start(bf16[512,1024]{1,0:T(8,128)(2,1)S(1)} %copy-done.15), channel_id=1, source_target_pairs={{0,8},{8,0},{16,24},{24,16},{1,9},{9,1},{17,25},{25,17},{2,10},{10... | collective-permute-start | bytes 3145736 | tf_op jit(solution)/shard_map/ppermute | solution.py:653
  411.3 50.9 %collective-permute-start.32 = (bf16[512,1024]{1,0:T(8,128)(2,1)}, bf16[512,1024]{1,0:T(8,128)(2,1)S(1)}, u32[]{:S(2)}, u32[]{:S(2)}) collective-permute-start(bf16[512,1024]{1,0:T(8,128)(2,1)} %collective-permute-done.31), channel_id=1, source_target_pairs={{0,8},{8,0},{16,24},{24,16},{1,9},{9,1},{17,25},{25,17},{2,10},{10... | collective-permute-start | bytes 3145736 | tf_op jit(solution)/shard_map/ppermute | solution.py:653
  433.8 37.4 %collective-permute-start.33 = (bf16[256,2048]{1,0:T(8,128)(2,1)S(1)}, bf16[256,2048]{1,0:T(8,128)(2,1)S(1)}, u32[]{:S(2)}, u32[]{:S(2)}) collective-permute-start(bf16[256,2048]{1,0:T(8,128)(2,1)S(1)} %copy-done.16), channel_id=1, source_target_pairs={{0,8},{8,0},{16,24},{24,16},{1,9},{9,1},{17,25},{25,17},{2,10},{10... | collective-permute-start | bytes 3145736 | tf_op jit(solution)/shard_map/ppermute | solution.py:653
  577.8 191.6 %reduce-scatter.11.cloned.1.call-start = ((), (), s32[]{:S(2)}) async-start(), calls=%async_computation.16 | async-start | bytes 9437184 | tf_op jit(solution)/shard_map/reduce_scatter | solution.py:980
  672.6 337.9 %reduce-scatter.13.cloned.1.call-start = ((), (), s32[]{:S(2)}) async-start(), calls=%async_computation.17 | async-start | bytes 2359296 | tf_op jit(solution)/shard_map/reduce_scatter | solution.py:987
  690.6 338.8 %reduce-scatter.17.cloned.1.call-start = ((), (), s32[]{:S(2)}) async-start(), calls=%async_computation.19 | async-start | bytes 2359296 | tf_op jit(solution)/shard_map/reduce_scatter | solution.py:976
  694.8 367.7 %reduce-scatter.15.cloned.1.call-start = ((), (), s32[]{:S(2)}) async-start(), calls=%async_computation.18 | async-start | bytes 4718592 | tf_op jit(solution)/shard_map/reduce_scatter | solution.py:995
  790.0 277.8 %reduce-scatter.7.cloned.1.call-start = ((), (), s32[]{:S(2)}) async-start(), calls=%async_computation.14 | async-start | bytes 4718592 | tf_op jit(solution)/shard_map/reduce_scatter | solution.py:922
  794.7 107.5 %collective-permute-start.69 = (bf16[256,2048]{1,0:T(8,128)(2,1)}, bf16[256,2048]{1,0:T(8,128)(2,1)}, u32[]{:S(2)}, u32[]{:S(2)}) collective-permute-start(bf16[256,2048]{1,0:T(8,128)(2,1)} %convolution_convert_fusion.10), channel_id=1, source_target_pairs={{0,8},{8,0},{16,24},{24,16},{1,9},{9,1},{17,25},{25,17},{2,10},{10... | collective-permute-start | bytes 3145736 | tf_op jit(solution)/shard_map/ppermute | solution.py:653
  799.3 52.2 %collective-permute-start.70 = (bf16[256,2048]{1,0:T(8,128)(2,1)}, bf16[256,2048]{1,0:T(8,128)(2,1)}, u32[]{:S(2)}, u32[]{:S(2)}) collective-permute-start(bf16[256,2048]{1,0:T(8,128)(2,1)} %convolution_convert_fusion.8), channel_id=1, source_target_pairs={{0,8},{8,0},{16,24},{24,16},{1,9},{9,1},{17,25},{25,17},{2,10},{10... | collective-permute-start | bytes 3145736 | tf_op jit(solution)/shard_map/ppermute | solution.py:653
  804.7 62.9 %collective-permute-start.73 = (bf16[256,2048]{1,0:T(8,128)(2,1)}, bf16[256,2048]{1,0:T(8,128)(2,1)}, u32[]{:S(2)}, u32[]{:S(2)}) collective-permute-start(bf16[256,2048]{1,0:T(8,128)(2,1)} %convolution_convert_fusion.4), channel_id=1, source_target_pairs={{0,16},{8,24},{16,0},{24,8},{1,17},{9,25},{17,1},{25,9},{2,18},{10... | collective-permute-start | bytes 3145736 | tf_op jit(solution)/shard_map/ppermute | solution.py:653
  812.3 50.8 %collective-permute-start.64 = (bf16[512,1024]{1,0:T(8,128)(2,1)}, bf16[512,1024]{1,0:T(8,128)(2,1)}, u32[]{:S(2)}, u32[]{:S(2)}) collective-permute-start(bf16[512,1024]{1,0:T(8,128)(2,1)} %convolution_convert_fusion.16), channel_id=1, source_target_pairs={{0,8},{8,0},{16,24},{24,16},{1,9},{9,1},{17,25},{25,17},{2,10},{10... | collective-permute-start | bytes 3145736 | tf_op jit(solution)/shard_map/ppermute | solution.py:653
  821.3 44.0 %collective-permute-start.67 = (bf16[512,1024]{1,0:T(8,128)(2,1)}, bf16[512,1024]{1,0:T(8,128)(2,1)}, u32[]{:S(2)}, u32[]{:S(2)}) collective-permute-start(bf16[512,1024]{1,0:T(8,128)(2,1)} %convolution_convert_fusion.12), channel_id=1, source_target_pairs={{0,16},{8,24},{16,0},{24,8},{1,17},{9,25},{17,1},{25,9},{2,18},{10... | collective-permute-start | bytes 3145736 | tf_op jit(solution)/shard_map/ppermute | solution.py:653
  851.4 51.3 %collective-permute-start.72 = (bf16[256,2048]{1,0:T(8,128)(2,1)}, bf16[256,2048]{1,0:T(8,128)(2,1)S(1)}, u32[]{:S(2)}, u32[]{:S(2)}) collective-permute-start(bf16[256,2048]{1,0:T(8,128)(2,1)} %convolution_convert_fusion.6), channel_id=1, source_target_pairs={{0,16},{8,24},{16,0},{24,8},{1,17},{9,25},{17,1},{25,9},{2,18},{10... | collective-permute-start | bytes 3145736 | tf_op jit(solution)/shard_map/ppermute | solution.py:653
  865.4 34.8 %collective-permute-start.61 = (bf16[512,1024]{1,0:T(8,128)(2,1)S(1)}, bf16[512,1024]{1,0:T(8,128)(2,1)S(1)}, u32[]{:S(2)}, u32[]{:S(2)}) collective-permute-start(bf16[512,1024]{1,0:T(8,128)(2,1)S(1)} %copy-done.95), channel_id=1, source_target_pairs={{0,16},{8,24},{16,0},{24,8},{1,17},{9,25},{17,1},{25,9},{2,18},{10... | collective-permute-start | bytes 3145736 | tf_op jit(solution)/shard_map/ppermute | solution.py:653
  867.6 55.1 %collective-permute-start.71 = (bf16[256,2048]{1,0:T(8,128)(2,1)S(1)}, bf16[256,2048]{1,0:T(8,128)(2,1)S(1)}, u32[]{:S(2)}, u32[]{:S(2)}) collective-permute-start(bf16[256,2048]{1,0:T(8,128)(2,1)S(1)} %add_convert_fusion.2), channel_id=1, source_target_pairs={{0,16},{8,24},{16,0},{24,8},{1,17},{9,25},{17,1},{25,9},{2,18},{10... | collective-permute-start | bytes 3145736 | tf_op jit(solution)/shard_map/ppermute | solution.py:653
  886.4 39.6 %collective-permute-start.74 = (bf16[256,2048]{1,0:T(8,128)(2,1)S(1)}, bf16[256,2048]{1,0:T(8,128)(2,1)S(1)}, u32[]{:S(2)}, u32[]{:S(2)}) collective-permute-start(bf16[256,2048]{1,0:T(8,128)(2,1)S(1)} %add_convert_fusion.1), channel_id=1, source_target_pairs={{0,8},{8,0},{16,24},{24,16},{1,9},{9,1},{17,25},{25,17},{2,10},{10... | collective-permute-start | bytes 3145736 | tf_op jit(solution)/shard_map/ppermute | solution.py:653
  900.2 34.7 %collective-permute-start.63 = (bf16[512,1024]{1,0:T(8,128)(2,1)S(1)}, bf16[512,1024]{1,0:T(8,128)(2,1)S(1)}, u32[]{:S(2)}, u32[]{:S(2)}) collective-permute-start(bf16[512,1024]{1,0:T(8,128)(2,1)S(1)} %copy-done.94), channel_id=1, source_target_pairs={{0,8},{8,0},{16,24},{24,16},{1,9},{9,1},{17,25},{25,17},{2,10},{10... | collective-permute-start | bytes 3145736 | tf_op jit(solution)/shard_map/ppermute | solution.py:653
  902.2 66.6 %collective-permute-start.66 = (bf16[512,1024]{1,0:T(8,128)(2,1)S(1)}, bf16[512,1024]{1,0:T(8,128)(2,1)S(1)}, u32[]{:S(2)}, u32[]{:S(2)}) collective-permute-start(bf16[512,1024]{1,0:T(8,128)(2,1)S(1)} %copy-done.93), channel_id=1, source_target_pairs={{0,16},{8,24},{16,0},{24,8},{1,17},{9,25},{17,1},{25,9},{2,18},{10... | collective-permute-start | bytes 3145736 | tf_op jit(solution)/shard_map/ppermute | solution.py:653
  902.7 64.9 %collective-permute-start.65 = (bf16[512,1024]{1,0:T(8,128)(2,1)S(1)}, bf16[512,1024]{1,0:T(8,128)(2,1)S(1)}, u32[]{:S(2)}, u32[]{:S(2)}) collective-permute-start(bf16[512,1024]{1,0:T(8,128)(2,1)S(1)} %add_convert_fusion.4), channel_id=1, source_target_pairs={{0,16},{8,24},{16,0},{24,8},{1,17},{9,25},{17,1},{25,9},{2,18},{10... | collective-permute-start | bytes 3145736 | tf_op jit(solution)/shard_map/ppermute | solution.py:653
  922.7 47.6 %collective-permute-start.68 = (bf16[512,1024]{1,0:T(8,128)(2,1)S(1)}, bf16[512,1024]{1,0:T(8,128)(2,1)S(1)}, u32[]{:S(2)}, u32[]{:S(2)}) collective-permute-start(bf16[512,1024]{1,0:T(8,128)(2,1)S(1)} %add_convert_fusion.3), channel_id=1, source_target_pairs={{0,8},{8,0},{16,24},{24,16},{1,9},{9,1},{17,25},{25,17},{2,10},{10... | collective-permute-start | bytes 3145736 | tf_op jit(solution)/shard_map/ppermute | solution.py:653
  926.0 53.9 %collective-permute-start.57 = (bf16[512,1024]{1,0:T(8,128)(2,1)S(1)}, bf16[512,1024]{1,0:T(8,128)(2,1)S(1)}, u32[]{:S(2)}, u32[]{:S(2)}) collective-permute-start(bf16[512,1024]{1,0:T(8,128)(2,1)S(1)} %copy-done.92), channel_id=1, source_target_pairs={{0,8},{8,0},{16,24},{24,16},{1,9},{9,1},{17,25},{25,17},{2,10},{10... | collective-permute-start | bytes 3145736 | tf_op jit(solution)/shard_map/ppermute | solution.py:653
  934.9 73.7 %collective-permute-start.60 = (bf16[512,1024]{1,0:T(8,128)(2,1)S(1)}, bf16[512,1024]{1,0:T(8,128)(2,1)S(1)}, u32[]{:S(2)}, u32[]{:S(2)}) collective-permute-start(bf16[512,1024]{1,0:T(8,128)(2,1)S(1)} %copy-done.91), channel_id=1, source_target_pairs={{0,16},{8,24},{16,0},{24,8},{1,17},{9,25},{17,1},{25,9},{2,18},{10... | collective-permute-start | bytes 3145736 | tf_op jit(solution)/shard_map/ppermute | solution.py:653
  967.6 39.1 %collective-permute-start.59 = (bf16[512,1024]{1,0:T(8,128)(2,1)S(1)}, bf16[512,1024]{1,0:T(8,128)(2,1)S(1)}, u32[]{:S(2)}, u32[]{:S(2)}) collective-permute-start(bf16[512,1024]{1,0:T(8,128)(2,1)S(1)} %add_convert_fusion.6), channel_id=1, source_target_pairs={{0,16},{8,24},{16,0},{24,8},{1,17},{9,25},{17,1},{25,9},{2,18},{10... | collective-permute-start | bytes 3145736 | tf_op jit(solution)/shard_map/ppermute | solution.py:653
  968.8 39.9 %collective-permute-start.62 = (bf16[512,1024]{1,0:T(8,128)(2,1)S(1)}, bf16[512,1024]{1,0:T(8,128)(2,1)S(1)}, u32[]{:S(2)}, u32[]{:S(2)}) collective-permute-start(bf16[512,1024]{1,0:T(8,128)(2,1)S(1)} %add_convert_fusion.5), channel_id=1, source_target_pairs={{0,8},{8,0},{16,24},{24,16},{1,9},{9,1},{17,25},{25,17},{2,10},{10... | collective-permute-start | bytes 3145736 | tf_op jit(solution)/shard_map/ppermute | solution.py:653
  (142 other events, 2526.7 us)
Sparse Core Ops, SparseCore 0:
  24.2 47.8 all-gather.9
  74.3 27.9 all-gather.7
  104.5 81.4 all-gather.11
  187.5 27.5 all-gather.13
  216.6 46.3 all-gather.17
  265.0 45.6 all-gather.15
  571.6 48.3 reduce-scatter.8
  672.7 96.6 reduce-scatter.10
  771.7 34.5 reduce-scatter.12
  808.4 34.5 reduce-scatter.16
  845.3 48.5 reduce-scatter.14
  896.1 48.3 reduce-scatter.6

commit v4 on v3

--- a/solution.py
+++ b/solution.py
@@ -472,6 +472,8 @@
     @pl.when(step == 0)
     def start():
         produced_grad[...] = (weight[...] * cot[...].astype(jnp.float32)).astype(jnp.bfloat16)
+        out_acc[...] = jnp.zeros_like(out_acc)
+        in_acc[...] = jnp.zeros_like(in_acc)
 
     gate = jnp.dot(arrived[...], gate_weight[...], preferred_element_type=jnp.float32)
     upward = jnp.dot(arrived[...], up_weight[...], preferred_element_type=jnp.float32)
@@ -491,23 +493,13 @@
     up_back = (active_grad * silu).astype(jnp.bfloat16)
     gate_grad[...] = gate_back
     up_grad[...] = up_back
-    out_part = jnp.dot(hidden, down_weight[...], preferred_element_type=jnp.float32)
-    in_part = lax.dot_general(
+    out_acc[...] += jnp.dot(hidden, down_weight[...], preferred_element_type=jnp.float32)
+    in_acc[...] += lax.dot_general(
         jnp.concatenate([gate_back, up_back], axis=1),
         jnp.concatenate([gate_weight[...], up_weight[...]], axis=1),
         (((1,), (1,)), ((), ())),
         preferred_element_type=jnp.float32,
     )
-
-    @pl.when(step == 0)
-    def first():
-        out_acc[...] = out_part
-        in_acc[...] = in_part
-
-    @pl.when(step > 0)
-    def later():
-        out_acc[...] += out_part
-        in_acc[...] += in_part
 
     @pl.when(step == pl.num_programs(0) - 1)
     def finish():
@@ -811,7 +803,10 @@
     query_seq, query_position = stream_layout(seq_lengths, query_index)
     cosine, sine_part = rope_tables(query_position, head_size)
     tables = tile_lists(query_index, query_seq, key_index, key_seq, TILE)
-    marks = attend_marks(query_index, query_index - query_position, key_index, TILE)
+    marks = attend_marks(
+        query_index, query_index - query_position, key_index, TILE
+    )
+    marks = lax.optimization_barrier(marks)
 
     gates, ups, downs = (
         [gather_pieces(weight[item], item) for item in range(local_experts)]

time: 1100 us -> 1090 us (level)
  transfers between devices with their start and end apart: 89 -> 89, of which waited for: 41 -> 40; matrix products, arithmetic and copies ran while one was open for 18% -> 19% of each run, Pallas kernels for 5% -> 5%
where the time goes in v4:
time: 1090 us; the launch traced here: 1080 us
  waiting for transfers between devices  580 us (53%)
  Pallas kernels  145 us (13%)
  starting transfers between devices  92.5 us (8%)
  other arithmetic  82.7 us (8%)
  matrix products  80.3 us (7%)
  local copies, waits for them, and re-layouts  64.7 us (6%)
  between operations  16.1 us (1%)
  blocking collectives  14.9 us (1%)
    ppermute x75, waiting for transfers between devices, exchange(): lax.ppermute(array, 'head', [(at, at ^ offset) for at in range(count)])  383 us
    ppermute x75, starting transfers between devices, exchange(): lax.ppermute(array, 'head', [(at, at ^ offset) for at in range(count)])  81.1 us
    reduce_scatter x1, waiting for transfers between devices, layer(): lax.psum_scatter(pairs_back, 'blk', scatter_dimension=0, tiled=True)  73.6 us
    all_gather x1, waiting for transfers between devices, layer(): pairs_all = lax.all_gather(pairs, 'blk', axis=0, tiled=True)  62.1 us
    pallas_call x2, Pallas kernels, run_expert(): pl.pallas_call(expert_kernel, grid_spec=pltpu.PrefetchScalarGridSpec(num_...  56.9 us
    dot_general x24, matrix products, pieces_of(): jnp.dot(left[:, offset * size:(offset + 1) * size].T, right, preferred_el...  47.1 us
    reduce_scatter x1, waiting for transfers between devices, layer(): lax.psum_scatter(incoming.reshape(blocks * rows, width), 'blk', scatter_d...  36.3 us
    concatenate x6, other arithmetic, layer(): jnp.concatenate(pieces, axis=0)  31 us
  transfers between devices with their start and end apart: 89, of which 40 were waited for; matrix products, arithmetic and copies ran while one was open for 19% of the time, Pallas kernels for 5%

profile of v4, /device:TPU:0, one launch (start us, length us, event | category | flops | bytes accessed | tf_op | source)
XLA Modules:
  0.0 1075.7 jit_solution(747712723070015574)
XLA Ops:
  14.1 5.0 collective-permute-done.6
  28.5 14.9 %all-gather = bf16[8,1,3328]{2,1,0:T(2,128)(2,1)S(1)} all-gather(bf16[1,1,3328]{2,1,0:T(2,128)(2,1)S(1)} %maximum_bitcast_fusion), channel_id=1, replica_groups=mesh['head'=4,'blk'=8] {'blk'}, dimensions={0}, use_global_device_ids=true | all-gather | bytes 59904 | tf_op jit(solution)/shard_map/all_gather | solution.py:785
  57.3 4.4 collective-permute-done.refs_1_
  61.7 11.0 %collective-permute-done.1.refs_2_ = bf16[128,2048]{1,0:T(8,128)(2,1)S(1)} collective-permute-done((bf16[128,2048]{1,0:T(8,128)(2,1)S(1)}, bf16[128,2048]{1,0:T(8,128)(2,1)S(1)}, u32[]{:S(2)}, u32[]{:S(2)}) %collective-permute-start.1) | collective-permute-done | bytes 524320 | tf_op jit(solution)/shard_map/ppermute | solution.py:645
  77.4 4.9 copy.119
  82.3 4.6 shard_map.292
  110.4 4.7 shard_map.290
  123.9 62.1 %all-gather.12.cloned.1.call-done.pairs = bf16[4096,1024]{1,0:T(8,128)(2,1)} async-done(((bf16[512,1024]{1,0:T(8,128)(2,1)}), bf16[4096,1024]{1,0:T(8,128)(2,1)}) %all-gather.12.cloned.1.call-update) | async-done | bytes 8388624 | tf_op jit(solution)/shard_map/all_gather | solution.py:830
  186.0 11.4 %attend_forward.1 = (f32[512,512]{1,0:T(8,128)}, bf16[512,512]{1,0:T(8,128)(2,1)}, f32[512,512]{1,0:T(8,128)}) custom-call(s32[2,16]{1,0:T(2,128)} %select_reduce_fusion.2.listed, s32[2]{0:T(128)} %get-tuple-element.206.counts, bf16[512,512]{1,0:T(8,128)(2,1)} %get-tuple-element.61.query, bf16[4096,1024]{1,0:T(8,128)(2,1)} %all-gather.12.cloned.1.call-done.pairs, ...), custom_call_target="tpu_custom_call" | custom-call | tf_op jit(solution)/shard_map/attend_forward/pallas_call | solution.py:299
  197.3 17.7 %all-gather.14.cloned.1.call-done = bf16[512,2048]{1,0:T(8,128)(2,1)} async-done(((bf16[64,2048]{1,0:T(8,128)(2,1)}), bf16[512,2048]{1,0:T(8,128)(2,1)}) %all-gather.14.cloned.1.call-update) | async-done | bytes 2097168 | tf_op jit(solution)/shard_map/all_gather | solution.py:764
  221.8 11.3 %collective-permute-done.15 = bf16[128,2048]{1,0:T(8,128)(2,1)S(1)} collective-permute-done((bf16[128,2048]{1,0:T(8,128)(2,1)S(1)}, bf16[128,2048]{1,0:T(8,128)(2,1)S(1)}, u32[]{:S(2)}, u32[]{:S(2)}) %collective-permute-start.15) | collective-permute-done | bytes 524320 | tf_op jit(solution)/shard_map/ppermute | solution.py:645
  233.1 11.6 %collective-permute-done.16 = bf16[128,2048]{1,0:T(8,128)(2,1)S(1)} collective-permute-done((bf16[128,2048]{1,0:T(8,128)(2,1)S(1)}, bf16[128,2048]{1,0:T(8,128)(2,1)S(1)}, u32[]{:S(2)}, u32[]{:S(2)}) %collective-permute-start.16) | collective-permute-done | bytes 524320 | tf_op jit(solution)/shard_map/ppermute | solution.py:645
  256.4 18.2 %collective-permute-done.18 = bf16[512,1024]{1,0:T(8,128)(2,1)} collective-permute-done((bf16[512,1024]{1,0:T(8,128)(2,1)S(1)}, bf16[512,1024]{1,0:T(8,128)(2,1)}, u32[]{:S(2)}, u32[]{:S(2)}) %collective-permute-start.18) | collective-permute-done | bytes 1048608 | tf_op jit(solution)/shard_map/ppermute | solution.py:645
  276.7 20.3 %collective-permute-done.21 = bf16[512,1024]{1,0:T(8,128)(2,1)S(1)} collective-permute-done((bf16[512,1024]{1,0:T(8,128)(2,1)S(1)}, bf16[512,1024]{1,0:T(8,128)(2,1)S(1)}, u32[]{:S(2)}, u32[]{:S(2)}) %collective-permute-start.21) | collective-permute-done | bytes 1048608 | tf_op jit(solution)/shard_map/ppermute | solution.py:645
  300.5 19.1 %collective-permute-done.24 = bf16[256,2048]{1,0:T(8,128)(2,1)} collective-permute-done((bf16[256,2048]{1,0:T(8,128)(2,1)}, bf16[256,2048]{1,0:T(8,128)(2,1)}, u32[]{:S(2)}, u32[]{:S(2)}) %collective-permute-start.24) | collective-permute-done | bytes 1048608 | tf_op jit(solution)/shard_map/ppermute | solution.py:645
  322.7 20.6 %collective-permute-done.28 = bf16[512,1024]{1,0:T(8,128)(2,1)} collective-permute-done((bf16[512,1024]{1,0:T(8,128)(2,1)S(1)}, bf16[512,1024]{1,0:T(8,128)(2,1)}, u32[]{:S(2)}, u32[]{:S(2)}) %collective-permute-start.28) | collective-permute-done | bytes 1048608 | tf_op jit(solution)/shard_map/ppermute | solution.py:645
  353.1 12.7 %collective-permute-done.20 = bf16[512,1024]{1,0:T(8,128)(2,1)} collective-permute-done((bf16[512,1024]{1,0:T(8,128)(2,1)}, bf16[512,1024]{1,0:T(8,128)(2,1)}, u32[]{:S(2)}, u32[]{:S(2)}) %collective-permute-start.20) | collective-permute-done | bytes 1048608 | tf_op jit(solution)/shard_map/ppermute | solution.py:645
  370.7 17.6 %collective-permute-done.31 = bf16[512,1024]{1,0:T(8,128)(2,1)} collective-permute-done((bf16[512,1024]{1,0:T(8,128)(2,1)}, bf16[512,1024]{1,0:T(8,128)(2,1)}, u32[]{:S(2)}, u32[]{:S(2)}) %collective-permute-start.31) | collective-permute-done | bytes 1048608 | tf_op jit(solution)/shard_map/ppermute | solution.py:645
  389.0 21.7 %collective-permute-done.23 = bf16[512,1024]{1,0:T(8,128)(2,1)} collective-permute-done((bf16[512,1024]{1,0:T(8,128)(2,1)}, bf16[512,1024]{1,0:T(8,128)(2,1)}, u32[]{:S(2)}, u32[]{:S(2)}) %collective-permute-start.23) | collective-permute-done | bytes 1048608 | tf_op jit(solution)/shard_map/ppermute | solution.py:645
  414.8 18.4 %collective-permute-done.34 = bf16[256,2048]{1,0:T(8,128)(2,1)} collective-permute-done((bf16[256,2048]{1,0:T(8,128)(2,1)}, bf16[256,2048]{1,0:T(8,128)(2,1)}, u32[]{:S(2)}, u32[]{:S(2)}) %collective-permute-start.34) | collective-permute-done | bytes 1048608 | tf_op jit(solution)/shard_map/ppermute | solution.py:645
  434.0 19.9 %collective-permute-done.26 = bf16[256,2048]{1,0:T(8,128)(2,1)} collective-permute-done((bf16[256,2048]{1,0:T(8,128)(2,1)}, bf16[256,2048]{1,0:T(8,128)(2,1)}, u32[]{:S(2)}, u32[]{:S(2)}) %collective-permute-start.26) | collective-permute-done | bytes 1048608 | tf_op jit(solution)/shard_map/ppermute | solution.py:645
  461.6 8.9 pad_maximum_fusion.4.up_weight
  470.5 7.0 collective-permute-done.35
  477.5 7.5 pad_maximum_fusion.5.down_weight
  485.6 6.3 shard_map.295
  496.0 6.3 shard_map.294
  502.3 28.4 %run_expert.2 = (bf16[640,1024]{1,0:T(8,128)(2,1)}, bf16[640,1024]{1,0:T(8,128)(2,1)}, bf16[640,1024]{1,0:T(8,128)(2,1)}, bf16[640,2048]{1,0:T(8,128)(2,1)}, f32...) custom-call(s32[4]{0:T(128)} %iota_xor_fusion.perm, ...), custom_call_target="tpu_custom_call" | custom-call | tf_op jit(solution)/shard_map/run_expert/pallas_call | solution.py:523
  530.7 28.5 %run_expert.3 = (bf16[640,1024]{1,0:T(8,128)(2,1)}, bf16[640,1024]{1,0:T(8,128)(2,1)}, bf16[640,1024]{1,0:T(8,128)(2,1)}, bf16[640,2048]{1,0:T(8,128)(2,1)}, f32...) custom-call(s32[4]{0:T(128)} %iota_xor_fusion.perm, ...), custom_call_target="tpu_custom_call" | custom-call | tf_op jit(solution)/shard_map/run_expert/pallas_call | solution.py:523
  559.2 5.8 shard_map.297
  571.5 5.7 all-to-all-done
  577.2 36.3 %reduce-scatter.9.cloned.1.call-done = bf16[128,2048]{1,0:T(8,128)(2,1)} async-done(((bf16[1024,2048]{1,0:T(8,128)(2,1)}), bf16[128,2048]{1,0:T(8,128)(2,1)}) %reduce-scatter.9.cloned.1.call-update) | async-done | bytes 524304 | tf_op jit(solution)/shard_map/reduce_scatter | solution.py:911
  620.3 11.3 %collective-permute-done.36 = bf16[128,2048]{1,0:T(8,128)(2,1)S(1)} collective-permute-done((bf16[128,2048]{1,0:T(8,128)(2,1)S(1)}, bf16[128,2048]{1,0:T(8,128)(2,1)S(1)}, u32[]{:S(2)}, u32[]{:S(2)}) %collective-permute-start.36) | collective-permute-done | bytes 524320 | tf_op jit(solution)/shard_map/ppermute | solution.py:645
  631.6 9.4 collective-permute-done.37
  643.2 19.7 %attend_backward.1 = (bf16[512,512]{1,0:T(8,128)(2,1)}, bf16[4096,1024]{1,0:T(8,128)(2,1)}) custom-call(s32[2,16]{1,0:T(2,128)} %copy-done.53, bf16[512,512]{1,0:T(8,128)(2,1)} %get-tuple-element.61.query, bf16[4096,1024]{1,0:T(8,128)(2,1)} %all-gather.12.cloned.1.call-done.pairs, bf16[512,512]{1,0:T(8,128)(2,1)} %convolution_convert_fusion.28.grad, ...), custom_call_target="tpu_custom_call" | custom-call | tf_op jit(solution)/shard_map/attend_backward/pallas_call | solution.py:409
  686.1 73.6 %reduce-scatter.11.cloned.1.call-done.back.refs_7_ = bf16[512,1024]{1,0:T(8,128)(2,1)} async-done(((bf16[4096,1024]{1,0:T(8,128)(2,1)}), bf16[512,1024]{1,0:T(8,128)(2,1)}) %reduce-scatter.11.cloned.1.call-update) | async-done | bytes 1048592 | tf_op jit(solution)/shard_map/reduce_scatter | solution.py:975
  774.7 5.5 convolution_convert_fusion
  835.3 6.1 shard_map.296
  844.2 11.2 %collective-permute-done.64 = bf16[512,1024]{1,0:T(8,128)(2,1)} collective-permute-done((bf16[512,1024]{1,0:T(8,128)(2,1)}, bf16[512,1024]{1,0:T(8,128)(2,1)}, u32[]{:S(2)}, u32[]{:S(2)}) %collective-permute-start.64) | collective-permute-done | bytes 1048608 | tf_op jit(solution)/shard_map/ppermute | solution.py:645
  863.1 15.6 %collective-permute-done.58 = bf16[512,1024]{1,0:T(8,128)(2,1)S(1)} collective-permute-done((bf16[512,1024]{1,0:T(8,128)(2,1)S(1)}, bf16[512,1024]{1,0:T(8,128)(2,1)S(1)}, u32[]{:S(2)}, u32[]{:S(2)}) %collective-permute-start.58) | collective-permute-done | bytes 1048608 | tf_op jit(solution)/shard_map/ppermute | solution.py:645
  879.6 10.9 %collective-permute-done.61 = bf16[512,1024]{1,0:T(8,128)(2,1)S(1)} collective-permute-done((bf16[512,1024]{1,0:T(8,128)(2,1)S(1)}, bf16[512,1024]{1,0:T(8,128)(2,1)S(1)}, u32[]{:S(2)}, u32[]{:S(2)}) %collective-permute-start.61) | collective-permute-done | bytes 1048608 | tf_op jit(solution)/shard_map/ppermute | solution.py:645
  894.5 18.4 %collective-permute-done.71 = bf16[256,2048]{1,0:T(8,128)(2,1)S(1)} collective-permute-done((bf16[256,2048]{1,0:T(8,128)(2,1)S(1)}, bf16[256,2048]{1,0:T(8,128)(2,1)S(1)}, u32[]{:S(2)}, u32[]{:S(2)}) %collective-permute-start.71) | collective-permute-done | bytes 1048608 | tf_op jit(solution)/shard_map/ppermute | solution.py:645
  917.3 9.8 collective-permute-done.63
  927.7 30.2 %collective-permute-done.65 = bf16[512,1024]{1,0:T(8,128)(2,1)S(1)} collective-permute-done((bf16[512,1024]{1,0:T(8,128)(2,1)S(1)}, bf16[512,1024]{1,0:T(8,128)(2,1)S(1)}, u32[]{:S(2)}, u32[]{:S(2)}) %collective-permute-start.65) | collective-permute-done | bytes 1048608 | tf_op jit(solution)/shard_map/ppermute | solution.py:645
  965.7 6.3 collective-permute-done.57
  972.1 25.0 %collective-permute-done.59 = bf16[512,1024]{1,0:T(8,128)(2,1)S(1)} collective-permute-done((bf16[512,1024]{1,0:T(8,128)(2,1)S(1)}, bf16[512,1024]{1,0:T(8,128)(2,1)S(1)}, u32[]{:S(2)}, u32[]{:S(2)}) %collective-permute-start.59) | collective-permute-done | bytes 1048608 | tf_op jit(solution)/shard_map/ppermute | solution.py:645
  1005.5 4.6 fusion.68
  1026.9 5.5 collective-permute-done.46
  1046.1 6.8 all-to-all-start.1
  (538 shorter events, 316.9 us)
Async XLA Ops:
  7.2 70.2 %all-gather.10.cloned.1.call-start = ((), (), s32[]{:S(2)}) async-start(), calls=%async_computation.9 | async-start | bytes 4718592 | tf_op jit(solution)/shard_map/all_gather | solution.py:767
  24.1 83.1 %all-gather.8.cloned.1.call-start = ((), (), s32[]{:S(2)}) async-start(), calls=%async_computation.8 | async-start | bytes 2359296 | tf_op jit(solution)/shard_map/all_gather | solution.py:769
  27.9 158.1 %all-gather.12.cloned.1.call-start = ((), (), s32[]{:S(2)}) async-start(), calls=%async_computation.10 | async-start | bytes 9437184 | tf_op jit(solution)/shard_map/all_gather | solution.py:830
  48.4 24.3 %collective-permute-start.1 = (bf16[128,2048]{1,0:T(8,128)(2,1)S(1)}, bf16[128,2048]{1,0:T(8,128)(2,1)S(1)}, u32[]{:S(2)}, u32[]{:S(2)}) collective-permute-start(bf16[128,2048]{1,0:T(8,128)(2,1)S(1)} %copy-done.9), channel_id=1, source_target_pairs={{0,16},{8,24},{16,0},{24,8},{1,17},{9,25},{17,1},{25,9},{2,18},{10... | collective-permute-start | bytes 1572872 | tf_op jit(solution)/shard_map/ppermute | solution.py:645
  98.0 117.0 %all-gather.14.cloned.1.call-start = ((), (), s32[]{:S(2)}) async-start(), calls=%async_computation.11 | async-start | bytes 2359296 | tf_op jit(solution)/shard_map/all_gather | solution.py:764
  98.6 386.4 %all-gather.18.cloned.1.call-start = ((), (), s32[]{:S(2)}) async-start(), calls=%async_computation.13 | async-start | bytes 4718592 | tf_op jit(solution)/shard_map/all_gather | solution.py:771
  99.2 392.7 %all-gather.16.cloned.1.call-start = ((), (), s32[]{:S(2)}) async-start(), calls=%async_computation.12 | async-start | bytes 4718592 | tf_op jit(solution)/shard_map/all_gather | solution.py:839
  219.7 25.0 %collective-permute-start.16 = (bf16[128,2048]{1,0:T(8,128)(2,1)S(1)}, bf16[128,2048]{1,0:T(8,128)(2,1)S(1)}, u32[]{:S(2)}, u32[]{:S(2)}) collective-permute-start(bf16[128,2048]{1,0:T(8,128)(2,1)S(1)} %get-tuple-element.219), channel_id=1, source_target_pairs={{0,16},{8,24},{16,0},{24,8},{1,17},{9,25},{17,1},{25,9},{2,18},{10... | collective-permute-start | bytes 1572872 | tf_op jit(solution)/shard_map/ppermute | solution.py:645
  246.5 367.0 %reduce-scatter.9.cloned.1.call-start = ((), (), s32[]{:S(2)}) async-start(), calls=%async_computation.15 | async-start | bytes 4718592 | tf_op jit(solution)/shard_map/reduce_scatter | solution.py:911
  248.4 26.2 %collective-permute-start.18 = (bf16[512,1024]{1,0:T(8,128)(2,1)S(1)}, bf16[512,1024]{1,0:T(8,128)(2,1)}, u32[]{:S(2)}, u32[]{:S(2)}) collective-permute-start(bf16[512,1024]{1,0:T(8,128)(2,1)S(1)} %get-tuple-element.216), channel_id=1, source_target_pairs={{0,8},{8,0},{16,24},{24,16},{1,9},{9,1},{17,25},{25,17},{2,10},{10... | collective-permute-start | bytes 3145736 | tf_op jit(solution)/shard_map/ppermute | solution.py:645
  249.8 26.4 %collective-permute-start.19 = (bf16[512,1024]{1,0:T(8,128)(2,1)S(1)}, bf16[512,1024]{1,0:T(8,128)(2,1)S(1)}, u32[]{:S(2)}, u32[]{:S(2)}) collective-permute-start(bf16[512,1024]{1,0:T(8,128)(2,1)S(1)} %get-tuple-element.216), channel_id=1, source_target_pairs={{0,16},{8,24},{16,0},{24,8},{1,17},{9,25},{17,1},{25,9},{2,18},{10... | collective-permute-start | bytes 3145736 | tf_op jit(solution)/shard_map/ppermute | solution.py:645
  251.7 45.3 %collective-permute-start.21 = (bf16[512,1024]{1,0:T(8,128)(2,1)S(1)}, bf16[512,1024]{1,0:T(8,128)(2,1)S(1)}, u32[]{:S(2)}, u32[]{:S(2)}) collective-permute-start(bf16[512,1024]{1,0:T(8,128)(2,1)S(1)} %get-tuple-element.214), channel_id=1, source_target_pairs={{0,8},{8,0},{16,24},{24,16},{1,9},{9,1},{17,25},{25,17},{2,10},{10... | collective-permute-start | bytes 3145736 | tf_op jit(solution)/shard_map/ppermute | solution.py:645
  253.2 45.1 %collective-permute-start.22 = (bf16[512,1024]{1,0:T(8,128)(2,1)S(1)}, bf16[512,1024]{1,0:T(8,128)(2,1)S(1)}, u32[]{:S(2)}, u32[]{:S(2)}) collective-permute-start(bf16[512,1024]{1,0:T(8,128)(2,1)S(1)} %get-tuple-element.214), channel_id=1, source_target_pairs={{0,16},{8,24},{16,0},{24,8},{1,17},{9,25},{17,1},{25,9},{2,18},{10... | collective-permute-start | bytes 3145736 | tf_op jit(solution)/shard_map/ppermute | solution.py:645
  255.2 64.4 %collective-permute-start.24 = (bf16[256,2048]{1,0:T(8,128)(2,1)}, bf16[256,2048]{1,0:T(8,128)(2,1)}, u32[]{:S(2)}, u32[]{:S(2)}) collective-permute-start(bf16[256,2048]{1,0:T(8,128)(2,1)} %get-tuple-element.212), channel_id=1, source_target_pairs={{0,8},{8,0},{16,24},{24,16},{1,9},{9,1},{17,25},{25,17},{2,10},{10... | collective-permute-start | bytes 3145736 | tf_op jit(solution)/shard_map/ppermute | solution.py:645
  274.6 46.5 %collective-permute-start.25 = (bf16[256,2048]{1,0:T(8,128)(2,1)}, bf16[256,2048]{1,0:T(8,128)(2,1)}, u32[]{:S(2)}, u32[]{:S(2)}) collective-permute-start(bf16[256,2048]{1,0:T(8,128)(2,1)} %get-tuple-element.212), channel_id=1, source_target_pairs={{0,16},{8,24},{16,0},{24,8},{1,17},{9,25},{17,1},{25,9},{2,18},{10... | collective-permute-start | bytes 3145736 | tf_op jit(solution)/shard_map/ppermute | solution.py:645
  276.2 67.1 %collective-permute-start.28 = (bf16[512,1024]{1,0:T(8,128)(2,1)S(1)}, bf16[512,1024]{1,0:T(8,128)(2,1)}, u32[]{:S(2)}, u32[]{:S(2)}) collective-permute-start(bf16[512,1024]{1,0:T(8,128)(2,1)S(1)} %get-tuple-element.215), channel_id=1, source_target_pairs={{0,16},{8,24},{16,0},{24,8},{1,17},{9,25},{17,1},{25,9},{2,18},{10... | collective-permute-start | bytes 3145736 | tf_op jit(solution)/shard_map/ppermute | solution.py:645
  297.0 47.1 %collective-permute-start.27 = (bf16[512,1024]{1,0:T(8,128)(2,1)S(1)}, bf16[512,1024]{1,0:T(8,128)(2,1)}, u32[]{:S(2)}, u32[]{:S(2)}) collective-permute-start(bf16[512,1024]{1,0:T(8,128)(2,1)S(1)} %get-tuple-element.215), channel_id=1, source_target_pairs={{0,8},{8,0},{16,24},{24,16},{1,9},{9,1},{17,25},{25,17},{2,10},{10... | collective-permute-start | bytes 3145736 | tf_op jit(solution)/shard_map/ppermute | solution.py:645
  299.2 66.5 %collective-permute-start.20 = (bf16[512,1024]{1,0:T(8,128)(2,1)}, bf16[512,1024]{1,0:T(8,128)(2,1)}, u32[]{:S(2)}, u32[]{:S(2)}) collective-permute-start(bf16[512,1024]{1,0:T(8,128)(2,1)} %collective-permute-done.18), channel_id=1, source_target_pairs={{0,16},{8,24},{16,0},{24,8},{1,17},{9,25},{17,1},{25,9},{2,18},{10... | collective-permute-start | bytes 3145736 | tf_op jit(solution)/shard_map/ppermute | solution.py:645
  319.6 68.7 %collective-permute-start.31 = (bf16[512,1024]{1,0:T(8,128)(2,1)}, bf16[512,1024]{1,0:T(8,128)(2,1)}, u32[]{:S(2)}, u32[]{:S(2)}) collective-permute-start(bf16[512,1024]{1,0:T(8,128)(2,1)} %get-tuple-element.213), channel_id=1, source_target_pairs={{0,16},{8,24},{16,0},{24,8},{1,17},{9,25},{17,1},{25,9},{2,18},{10... | collective-permute-start | bytes 3145736 | tf_op jit(solution)/shard_map/ppermute | solution.py:645
  321.1 89.6 %collective-permute-start.23 = (bf16[512,1024]{1,0:T(8,128)(2,1)}, bf16[512,1024]{1,0:T(8,128)(2,1)}, u32[]{:S(2)}, u32[]{:S(2)}) collective-permute-start(bf16[512,1024]{1,0:T(8,128)(2,1)} %copy-done.37), channel_id=1, source_target_pairs={{0,16},{8,24},{16,0},{24,8},{1,17},{9,25},{17,1},{25,9},{2,18},{10... | collective-permute-start | bytes 3145736 | tf_op jit(solution)/shard_map/ppermute | solution.py:645
  343.3 89.9 %collective-permute-start.34 = (bf16[256,2048]{1,0:T(8,128)(2,1)}, bf16[256,2048]{1,0:T(8,128)(2,1)}, u32[]{:S(2)}, u32[]{:S(2)}) collective-permute-start(bf16[256,2048]{1,0:T(8,128)(2,1)} %get-tuple-element.211), channel_id=1, source_target_pairs={{0,16},{8,24},{16,0},{24,8},{1,17},{9,25},{17,1},{25,9},{2,18},{10... | collective-permute-start | bytes 3145736 | tf_op jit(solution)/shard_map/ppermute | solution.py:645
  344.1 109.8 %collective-permute-start.26 = (bf16[256,2048]{1,0:T(8,128)(2,1)}, bf16[256,2048]{1,0:T(8,128)(2,1)}, u32[]{:S(2)}, u32[]{:S(2)}) collective-permute-start(bf16[256,2048]{1,0:T(8,128)(2,1)} %collective-permute-done.24), channel_id=1, source_target_pairs={{0,16},{8,24},{16,0},{24,8},{1,17},{9,25},{17,1},{25,9},{2,18},{10... | collective-permute-start | bytes 3145736 | tf_op jit(solution)/shard_map/ppermute | solution.py:645
  365.8 92.4 %collective-permute-start.29 = (bf16[512,1024]{1,0:T(8,128)(2,1)}, bf16[512,1024]{1,0:T(8,128)(2,1)S(1)}, u32[]{:S(2)}, u32[]{:S(2)}) collective-permute-start(bf16[512,1024]{1,0:T(8,128)(2,1)} %collective-permute-done.28), channel_id=1, source_target_pairs={{0,8},{8,0},{16,24},{24,16},{1,9},{9,1},{17,25},{25,17},{2,10},{10... | collective-permute-start | bytes 3145736 | tf_op jit(solution)/shard_map/ppermute | solution.py:645
  388.2 73.3 %collective-permute-start.30 = (bf16[512,1024]{1,0:T(8,128)(2,1)S(1)}, bf16[512,1024]{1,0:T(8,128)(2,1)S(1)}, u32[]{:S(2)}, u32[]{:S(2)}) collective-permute-start(bf16[512,1024]{1,0:T(8,128)(2,1)S(1)} %copy-done.15), channel_id=1, source_target_pairs={{0,8},{8,0},{16,24},{24,16},{1,9},{9,1},{17,25},{25,17},{2,10},{10... | collective-permute-start | bytes 3145736 | tf_op jit(solution)/shard_map/ppermute | solution.py:645
  410.7 50.9 %collective-permute-start.32 = (bf16[512,1024]{1,0:T(8,128)(2,1)}, bf16[512,1024]{1,0:T(8,128)(2,1)S(1)}, u32[]{:S(2)}, u32[]{:S(2)}) collective-permute-start(bf16[512,1024]{1,0:T(8,128)(2,1)} %collective-permute-done.31), channel_id=1, source_target_pairs={{0,8},{8,0},{16,24},{24,16},{1,9},{9,1},{17,25},{25,17},{2,10},{10... | collective-permute-start | bytes 3145736 | tf_op jit(solution)/shard_map/ppermute | solution.py:645
  433.2 37.3 %collective-permute-start.33 = (bf16[256,2048]{1,0:T(8,128)(2,1)S(1)}, bf16[256,2048]{1,0:T(8,128)(2,1)S(1)}, u32[]{:S(2)}, u32[]{:S(2)}) collective-permute-start(bf16[256,2048]{1,0:T(8,128)(2,1)S(1)} %copy-done.16), channel_id=1, source_target_pairs={{0,8},{8,0},{16,24},{24,16},{1,9},{9,1},{17,25},{25,17},{2,10},{10... | collective-permute-start | bytes 3145736 | tf_op jit(solution)/shard_map/ppermute | solution.py:645
  571.4 188.3 %reduce-scatter.11.cloned.1.call-start = ((), (), s32[]{:S(2)}) async-start(), calls=%async_computation.16 | async-start | bytes 9437184 | tf_op jit(solution)/shard_map/reduce_scatter | solution.py:975
  662.9 338.1 %reduce-scatter.13.cloned.1.call-start = ((), (), s32[]{:S(2)}) async-start(), calls=%async_computation.17 | async-start | bytes 2359296 | tf_op jit(solution)/shard_map/reduce_scatter | solution.py:982
  681.8 339.7 %reduce-scatter.17.cloned.1.call-start = ((), (), s32[]{:S(2)}) async-start(), calls=%async_computation.19 | async-start | bytes 2359296 | tf_op jit(solution)/shard_map/reduce_scatter | solution.py:971
  686.0 366.9 %reduce-scatter.15.cloned.1.call-start = ((), (), s32[]{:S(2)}) async-start(), calls=%async_computation.18 | async-start | bytes 4718592 | tf_op jit(solution)/shard_map/reduce_scatter | solution.py:990
  780.2 278.0 %reduce-scatter.7.cloned.1.call-start = ((), (), s32[]{:S(2)}) async-start(), calls=%async_computation.14 | async-start | bytes 4718592 | tf_op jit(solution)/shard_map/reduce_scatter | solution.py:917
  786.9 105.4 %collective-permute-start.69 = (bf16[256,2048]{1,0:T(8,128)(2,1)}, bf16[256,2048]{1,0:T(8,128)(2,1)}, u32[]{:S(2)}, u32[]{:S(2)}) collective-permute-start(bf16[256,2048]{1,0:T(8,128)(2,1)} %convolution_convert_fusion.10), channel_id=1, source_target_pairs={{0,8},{8,0},{16,24},{24,16},{1,9},{9,1},{17,25},{25,17},{2,10},{10... | collective-permute-start | bytes 3145736 | tf_op jit(solution)/shard_map/ppermute | solution.py:645
  791.4 50.2 %collective-permute-start.70 = (bf16[256,2048]{1,0:T(8,128)(2,1)}, bf16[256,2048]{1,0:T(8,128)(2,1)}, u32[]{:S(2)}, u32[]{:S(2)}) collective-permute-start(bf16[256,2048]{1,0:T(8,128)(2,1)} %convolution_convert_fusion.8), channel_id=1, source_target_pairs={{0,8},{8,0},{16,24},{24,16},{1,9},{9,1},{17,25},{25,17},{2,10},{10... | collective-permute-start | bytes 3145736 | tf_op jit(solution)/shard_map/ppermute | solution.py:645
  794.9 64.9 %collective-permute-start.73 = (bf16[256,2048]{1,0:T(8,128)(2,1)}, bf16[256,2048]{1,0:T(8,128)(2,1)}, u32[]{:S(2)}, u32[]{:S(2)}) collective-permute-start(bf16[256,2048]{1,0:T(8,128)(2,1)} %convolution_convert_fusion.4), channel_id=1, source_target_pairs={{0,16},{8,24},{16,0},{24,8},{1,17},{9,25},{17,1},{25,9},{2,18},{10... | collective-permute-start | bytes 3145736 | tf_op jit(solution)/shard_map/ppermute | solution.py:645
  802.5 52.9 %collective-permute-start.64 = (bf16[512,1024]{1,0:T(8,128)(2,1)}, bf16[512,1024]{1,0:T(8,128)(2,1)}, u32[]{:S(2)}, u32[]{:S(2)}) collective-permute-start(bf16[512,1024]{1,0:T(8,128)(2,1)} %convolution_convert_fusion.16), channel_id=1, source_target_pairs={{0,8},{8,0},{16,24},{24,16},{1,9},{9,1},{17,25},{25,17},{2,10},{10... | collective-permute-start | bytes 3145736 | tf_op jit(solution)/shard_map/ppermute | solution.py:645
  811.6 46.0 %collective-permute-start.67 = (bf16[512,1024]{1,0:T(8,128)(2,1)}, bf16[512,1024]{1,0:T(8,128)(2,1)}, u32[]{:S(2)}, u32[]{:S(2)}) collective-permute-start(bf16[512,1024]{1,0:T(8,128)(2,1)} %convolution_convert_fusion.12), channel_id=1, source_target_pairs={{0,16},{8,24},{16,0},{24,8},{1,17},{9,25},{17,1},{25,9},{2,18},{10... | collective-permute-start | bytes 3145736 | tf_op jit(solution)/shard_map/ppermute | solution.py:645
  841.7 51.3 %collective-permute-start.72 = (bf16[256,2048]{1,0:T(8,128)(2,1)}, bf16[256,2048]{1,0:T(8,128)(2,1)S(1)}, u32[]{:S(2)}, u32[]{:S(2)}) collective-permute-start(bf16[256,2048]{1,0:T(8,128)(2,1)} %convolution_convert_fusion.6), channel_id=1, source_target_pairs={{0,16},{8,24},{16,0},{24,8},{1,17},{9,25},{17,1},{25,9},{2,18},{10... | collective-permute-start | bytes 3145736 | tf_op jit(solution)/shard_map/ppermute | solution.py:645
  857.6 32.8 %collective-permute-start.61 = (bf16[512,1024]{1,0:T(8,128)(2,1)S(1)}, bf16[512,1024]{1,0:T(8,128)(2,1)S(1)}, u32[]{:S(2)}, u32[]{:S(2)}) collective-permute-start(bf16[512,1024]{1,0:T(8,128)(2,1)S(1)} %copy-done.89), channel_id=1, source_target_pairs={{0,16},{8,24},{16,0},{24,8},{1,17},{9,25},{17,1},{25,9},{2,18},{10... | collective-permute-start | bytes 3145736 | tf_op jit(solution)/shard_map/ppermute | solution.py:645
  859.9 53.0 %collective-permute-start.71 = (bf16[256,2048]{1,0:T(8,128)(2,1)S(1)}, bf16[256,2048]{1,0:T(8,128)(2,1)S(1)}, u32[]{:S(2)}, u32[]{:S(2)}) collective-permute-start(bf16[256,2048]{1,0:T(8,128)(2,1)S(1)} %add_convert_fusion.2), channel_id=1, source_target_pairs={{0,16},{8,24},{16,0},{24,8},{1,17},{9,25},{17,1},{25,9},{2,18},{10... | collective-permute-start | bytes 3145736 | tf_op jit(solution)/shard_map/ppermute | solution.py:645
  878.6 37.6 %collective-permute-start.74 = (bf16[256,2048]{1,0:T(8,128)(2,1)S(1)}, bf16[256,2048]{1,0:T(8,128)(2,1)S(1)}, u32[]{:S(2)}, u32[]{:S(2)}) collective-permute-start(bf16[256,2048]{1,0:T(8,128)(2,1)S(1)} %add_convert_fusion.1), channel_id=1, source_target_pairs={{0,8},{8,0},{16,24},{24,16},{1,9},{9,1},{17,25},{25,17},{2,10},{10... | collective-permute-start | bytes 3145736 | tf_op jit(solution)/shard_map/ppermute | solution.py:645
  890.4 36.7 %collective-permute-start.63 = (bf16[512,1024]{1,0:T(8,128)(2,1)S(1)}, bf16[512,1024]{1,0:T(8,128)(2,1)S(1)}, u32[]{:S(2)}, u32[]{:S(2)}) collective-permute-start(bf16[512,1024]{1,0:T(8,128)(2,1)S(1)} %copy-done.88), channel_id=1, source_target_pairs={{0,8},{8,0},{16,24},{24,16},{1,9},{9,1},{17,25},{25,17},{2,10},{10... | collective-permute-start | bytes 3145736 | tf_op jit(solution)/shard_map/ppermute | solution.py:645
  892.4 66.6 %collective-permute-start.66 = (bf16[512,1024]{1,0:T(8,128)(2,1)S(1)}, bf16[512,1024]{1,0:T(8,128)(2,1)S(1)}, u32[]{:S(2)}, u32[]{:S(2)}) collective-permute-start(bf16[512,1024]{1,0:T(8,128)(2,1)S(1)} %copy-done.87), channel_id=1, source_target_pairs={{0,16},{8,24},{16,0},{24,8},{1,17},{9,25},{17,1},{25,9},{2,18},{10... | collective-permute-start | bytes 3145736 | tf_op jit(solution)/shard_map/ppermute | solution.py:645
  893.0 64.9 %collective-permute-start.65 = (bf16[512,1024]{1,0:T(8,128)(2,1)S(1)}, bf16[512,1024]{1,0:T(8,128)(2,1)S(1)}, u32[]{:S(2)}, u32[]{:S(2)}) collective-permute-start(bf16[512,1024]{1,0:T(8,128)(2,1)S(1)} %add_convert_fusion.4), channel_id=1, source_target_pairs={{0,16},{8,24},{16,0},{24,8},{1,17},{9,25},{17,1},{25,9},{2,18},{10... | collective-permute-start | bytes 3145736 | tf_op jit(solution)/shard_map/ppermute | solution.py:645
  912.9 47.6 %collective-permute-start.68 = (bf16[512,1024]{1,0:T(8,128)(2,1)S(1)}, bf16[512,1024]{1,0:T(8,128)(2,1)S(1)}, u32[]{:S(2)}, u32[]{:S(2)}) collective-permute-start(bf16[512,1024]{1,0:T(8,128)(2,1)S(1)} %add_convert_fusion.3), channel_id=1, source_target_pairs={{0,8},{8,0},{16,24},{24,16},{1,9},{9,1},{17,25},{25,17},{2,10},{10... | collective-permute-start | bytes 3145736 | tf_op jit(solution)/shard_map/ppermute | solution.py:645
  916.2 55.9 %collective-permute-start.57 = (bf16[512,1024]{1,0:T(8,128)(2,1)S(1)}, bf16[512,1024]{1,0:T(8,128)(2,1)S(1)}, u32[]{:S(2)}, u32[]{:S(2)}) collective-permute-start(bf16[512,1024]{1,0:T(8,128)(2,1)S(1)} %copy-done.86), channel_id=1, source_target_pairs={{0,8},{8,0},{16,24},{24,16},{1,9},{9,1},{17,25},{25,17},{2,10},{10... | collective-permute-start | bytes 3145736 | tf_op jit(solution)/shard_map/ppermute | solution.py:645
  927.1 71.9 %collective-permute-start.60 = (bf16[512,1024]{1,0:T(8,128)(2,1)S(1)}, bf16[512,1024]{1,0:T(8,128)(2,1)S(1)}, u32[]{:S(2)}, u32[]{:S(2)}) collective-permute-start(bf16[512,1024]{1,0:T(8,128)(2,1)S(1)} %copy-done.85), channel_id=1, source_target_pairs={{0,16},{8,24},{16,0},{24,8},{1,17},{9,25},{17,1},{25,9},{2,18},{10... | collective-permute-start | bytes 3145736 | tf_op jit(solution)/shard_map/ppermute | solution.py:645
  957.9 39.2 %collective-permute-start.59 = (bf16[512,1024]{1,0:T(8,128)(2,1)S(1)}, bf16[512,1024]{1,0:T(8,128)(2,1)S(1)}, u32[]{:S(2)}, u32[]{:S(2)}) collective-permute-start(bf16[512,1024]{1,0:T(8,128)(2,1)S(1)} %add_convert_fusion.6), channel_id=1, source_target_pairs={{0,16},{8,24},{16,0},{24,8},{1,17},{9,25},{17,1},{25,9},{2,18},{10... | collective-permute-start | bytes 3145736 | tf_op jit(solution)/shard_map/ppermute | solution.py:645
  959.0 40.0 %collective-permute-start.62 = (bf16[512,1024]{1,0:T(8,128)(2,1)S(1)}, bf16[512,1024]{1,0:T(8,128)(2,1)S(1)}, u32[]{:S(2)}, u32[]{:S(2)}) collective-permute-start(bf16[512,1024]{1,0:T(8,128)(2,1)S(1)} %add_convert_fusion.5), channel_id=1, source_target_pairs={{0,8},{8,0},{16,24},{24,16},{1,9},{9,1},{17,25},{25,17},{2,10},{10... | collective-permute-start | bytes 3145736 | tf_op jit(solution)/shard_map/ppermute | solution.py:645
  (136 other events, 2935.0 us)
Sparse Core Ops, SparseCore 0:
  24.2 47.8 all-gather.9
  74.3 27.8 all-gather.7
  104.5 81.4 all-gather.11
  187.4 27.5 all-gather.13
  216.5 46.2 all-gather.17
  264.8 45.6 all-gather.15
  565.2 48.2 reduce-scatter.8
  663.0 96.6 reduce-scatter.10
  762.0 34.3 reduce-scatter.12
  798.5 34.5 reduce-scatter.16
  835.4 48.6 reduce-scatter.14
  886.3 48.3 reduce-scatter.6

commit v5 on v4

--- a/solution.py
+++ b/solution.py
@@ -761,13 +761,18 @@
         )
     ]
     slices = head_turn(slices)
-    output_rows = lax.all_gather(output_weight, "blk", axis=0, tiled=True)
     token_pieces = head_pieces(tokens)
     rows_here = jnp.stack(absolute(slices)).reshape(heads_axis * part, 3 * columns)
     pair_full = lax.all_gather(rows_here[:, : 2 * columns], "blk", axis=0, tiled=True)
     pair_full = move_rows(pair_full, blocks, heads_axis, part)
-    query_full = lax.all_gather(rows_here[:, 2 * columns :], "blk", axis=0, tiled=True)
-    query_full = move_rows(query_full, blocks, heads_axis, part)
+    query_output = jnp.concatenate(
+        [rows_here[:, 2 * columns :], output_weight.reshape(heads_axis * part, columns)], axis=0
+    )
+    query_output = lax.all_gather(query_output, "blk", axis=0, tiled=False)
+    query_full = move_rows(
+        query_output[:, : heads_axis * part].reshape(width, columns), blocks, heads_axis, part
+    )
+    output_rows = query_output[:, heads_axis * part :].reshape(columns, width)
     cot_all = lax.all_gather(cotangent, "blk", axis=0, tiled=True)
 
     small = jnp.concatenate(

time: 1090 us -> 1090 us (level)
  transfers between devices with their start and end apart: 89 -> 88, of which waited for: 40 -> 38; matrix products, arithmetic and copies ran while one was open for 19% -> 19% of each run, Pallas kernels for 5% -> 5%
where the time goes in v5:
time: 1090 us; the launch traced here: 1080 us
  waiting for transfers between devices  577 us (53%)
  Pallas kernels  145 us (13%)
  starting transfers between devices  94.8 us (9%)
  other arithmetic  83.5 us (8%)
  matrix products  79.6 us (7%)
  local copies, waits for them, and re-layouts  67.6 us (6%)
  between operations  15.8 us (1%)
  blocking collectives  14.8 us (1%)
    ppermute x75, waiting for transfers between devices, exchange(): lax.ppermute(array, 'head', [(at, at ^ offset) for at in range(count)])  383 us
    ppermute x75, starting transfers between devices, exchange(): lax.ppermute(array, 'head', [(at, at ^ offset) for at in range(count)])  81.2 us
    reduce_scatter x1, waiting for transfers between devices, layer(): lax.psum_scatter(pairs_back, 'blk', scatter_dimension=0, tiled=True)  73.7 us
    all_gather x1, waiting for transfers between devices, layer(): pairs_all = lax.all_gather(pairs, 'blk', axis=0, tiled=True)  63.5 us
    pallas_call x2, Pallas kernels, run_expert(): pl.pallas_call(expert_kernel, grid_spec=pltpu.PrefetchScalarGridSpec(num_...  56.9 us
    dot_general x24, matrix products, pieces_of(): jnp.dot(left[:, offset * size:(offset + 1) * size].T, right, preferred_el...  47.2 us
    reduce_scatter x1, waiting for transfers between devices, layer(): lax.psum_scatter(incoming.reshape(blocks * rows, width), 'blk', scatter_d...  36.6 us
    concatenate x6, other arithmetic, layer(): jnp.concatenate(pieces, axis=0)  31 us
  transfers between devices with their start and end apart: 88, of which 38 were waited for; matrix products, arithmetic and copies ran while one was open for 19% of the time, Pallas kernels for 5%

profile of v5, /device:TPU:0, one launch (start us, length us, event | category | flops | bytes accessed | tf_op | source)
XLA Modules:
  0.0 1077.5 jit_solution(10542938852128188789)
XLA Ops:
  14.1 5.0 collective-permute-done.6
  28.8 14.8 %all-gather.1 = bf16[8,1,3328]{2,1,0:T(2,128)(2,1)S(1)} all-gather(bf16[1,1,3328]{2,1,0:T(2,128)(2,1)S(1)} %maximum_bitcast_fusion), channel_id=1, replica_groups=mesh['head'=4,'blk'=8] {'blk'}, dimensions={0}, use_global_device_ids=true | all-gather | bytes 59904 | tf_op jit(solution)/shard_map/all_gather | solution.py:790
  57.5 4.4 collective-permute-done.refs_1_
  62.0 11.0 %collective-permute-done.1.refs_2_ = bf16[128,2048]{1,0:T(8,128)(2,1)S(1)} collective-permute-done((bf16[128,2048]{1,0:T(8,128)(2,1)S(1)}, bf16[128,2048]{1,0:T(8,128)(2,1)S(1)}, u32[]{:S(2)}, u32[]{:S(2)}) %collective-permute-start.1) | collective-permute-done | bytes 524320 | tf_op jit(solution)/shard_map/ppermute | solution.py:645
  77.6 4.9 copy.119
  82.6 4.6 shard_map.292
  106.8 13.5 %all-gather.16.cloned.1.call-done = bf16[4096,512]{1,0:T(8,128)(2,1)} async-done(((bf16[512,512]{1,0:T(8,128)(2,1)}), bf16[4096,512]{1,0:T(8,128)(2,1)}) %all-gather.16.cloned.1.call-update) | async-done | bytes 4194320 | tf_op jit(solution)/shard_map/all_gather | solution.py:771
  140.0 63.5 %all-gather.10.cloned.1.call-done.pairs = bf16[4096,1024]{1,0:T(8,128)(2,1)} async-done(((bf16[512,1024]{1,0:T(8,128)(2,1)}), bf16[4096,1024]{1,0:T(8,128)(2,1)}) %all-gather.10.cloned.1.call-update) | async-done | bytes 8388624 | tf_op jit(solution)/shard_map/all_gather | solution.py:835
  203.4 11.5 %attend_forward.1 = (f32[512,512]{1,0:T(8,128)}, bf16[512,512]{1,0:T(8,128)(2,1)}, f32[512,512]{1,0:T(8,128)}) custom-call(s32[2,16]{1,0:T(2,128)} %select_reduce_fusion.2.listed, s32[2]{0:T(128)} %get-tuple-element.206.counts, bf16[512,512]{1,0:T(8,128)(2,1)} %get-tuple-element.61.query, bf16[4096,1024]{1,0:T(8,128)(2,1)} %all-gather.10.cloned.1.call-done.pairs, ...), custom_call_target="tpu_custom_call" | custom-call | tf_op jit(solution)/shard_map/attend_forward/pallas_call | solution.py:299
  221.0 11.3 %collective-permute-done.15 = bf16[128,2048]{1,0:T(8,128)(2,1)S(1)} collective-permute-done((bf16[128,2048]{1,0:T(8,128)(2,1)S(1)}, bf16[128,2048]{1,0:T(8,128)(2,1)S(1)}, u32[]{:S(2)}, u32[]{:S(2)}) %collective-permute-start.15) | collective-permute-done | bytes 524320 | tf_op jit(solution)/shard_map/ppermute | solution.py:645
  232.3 11.7 %collective-permute-done.16 = bf16[128,2048]{1,0:T(8,128)(2,1)S(1)} collective-permute-done((bf16[128,2048]{1,0:T(8,128)(2,1)S(1)}, bf16[128,2048]{1,0:T(8,128)(2,1)S(1)}, u32[]{:S(2)}, u32[]{:S(2)}) %collective-permute-start.16) | collective-permute-done | bytes 524320 | tf_op jit(solution)/shard_map/ppermute | solution.py:645
  255.7 18.3 %collective-permute-done.18 = bf16[512,1024]{1,0:T(8,128)(2,1)} collective-permute-done((bf16[512,1024]{1,0:T(8,128)(2,1)S(1)}, bf16[512,1024]{1,0:T(8,128)(2,1)}, u32[]{:S(2)}, u32[]{:S(2)}) %collective-permute-start.18) | collective-permute-done | bytes 1048608 | tf_op jit(solution)/shard_map/ppermute | solution.py:645
  276.0 20.3 %collective-permute-done.21 = bf16[512,1024]{1,0:T(8,128)(2,1)S(1)} collective-permute-done((bf16[512,1024]{1,0:T(8,128)(2,1)S(1)}, bf16[512,1024]{1,0:T(8,128)(2,1)S(1)}, u32[]{:S(2)}, u32[]{:S(2)}) %collective-permute-start.21) | collective-permute-done | bytes 1048608 | tf_op jit(solution)/shard_map/ppermute | solution.py:645
  299.7 19.1 %collective-permute-done.24 = bf16[256,2048]{1,0:T(8,128)(2,1)} collective-permute-done((bf16[256,2048]{1,0:T(8,128)(2,1)}, bf16[256,2048]{1,0:T(8,128)(2,1)}, u32[]{:S(2)}, u32[]{:S(2)}) %collective-permute-start.24) | collective-permute-done | bytes 1048608 | tf_op jit(solution)/shard_map/ppermute | solution.py:645
  321.9 20.6 %collective-permute-done.28 = bf16[512,1024]{1,0:T(8,128)(2,1)} collective-permute-done((bf16[512,1024]{1,0:T(8,128)(2,1)S(1)}, bf16[512,1024]{1,0:T(8,128)(2,1)}, u32[]{:S(2)}, u32[]{:S(2)}) %collective-permute-start.28) | collective-permute-done | bytes 1048608 | tf_op jit(solution)/shard_map/ppermute | solution.py:645
  352.3 12.7 %collective-permute-done.20 = bf16[512,1024]{1,0:T(8,128)(2,1)} collective-permute-done((bf16[512,1024]{1,0:T(8,128)(2,1)}, bf16[512,1024]{1,0:T(8,128)(2,1)}, u32[]{:S(2)}, u32[]{:S(2)}) %collective-permute-start.20) | collective-permute-done | bytes 1048608 | tf_op jit(solution)/shard_map/ppermute | solution.py:645
  370.0 17.5 %collective-permute-done.31 = bf16[512,1024]{1,0:T(8,128)(2,1)} collective-permute-done((bf16[512,1024]{1,0:T(8,128)(2,1)}, bf16[512,1024]{1,0:T(8,128)(2,1)}, u32[]{:S(2)}, u32[]{:S(2)}) %collective-permute-start.31) | collective-permute-done | bytes 1048608 | tf_op jit(solution)/shard_map/ppermute | solution.py:645
  388.3 21.6 %collective-permute-done.23 = bf16[512,1024]{1,0:T(8,128)(2,1)} collective-permute-done((bf16[512,1024]{1,0:T(8,128)(2,1)}, bf16[512,1024]{1,0:T(8,128)(2,1)}, u32[]{:S(2)}, u32[]{:S(2)}) %collective-permute-start.23) | collective-permute-done | bytes 1048608 | tf_op jit(solution)/shard_map/ppermute | solution.py:645
  414.1 18.3 %collective-permute-done.34 = bf16[256,2048]{1,0:T(8,128)(2,1)} collective-permute-done((bf16[256,2048]{1,0:T(8,128)(2,1)}, bf16[256,2048]{1,0:T(8,128)(2,1)}, u32[]{:S(2)}, u32[]{:S(2)}) %collective-permute-start.34) | collective-permute-done | bytes 1048608 | tf_op jit(solution)/shard_map/ppermute | solution.py:645
  433.3 19.9 %collective-permute-done.26 = bf16[256,2048]{1,0:T(8,128)(2,1)} collective-permute-done((bf16[256,2048]{1,0:T(8,128)(2,1)}, bf16[256,2048]{1,0:T(8,128)(2,1)}, u32[]{:S(2)}, u32[]{:S(2)}) %collective-permute-start.26) | collective-permute-done | bytes 1048608 | tf_op jit(solution)/shard_map/ppermute | solution.py:645
  460.9 8.9 pad_maximum_fusion.4.up_weight
  469.8 7.0 collective-permute-done.35
  476.8 7.5 pad_maximum_fusion.5.down_weight
  484.9 6.3 shard_map.295
  495.3 6.3 shard_map.294
  501.6 28.4 %run_expert.2 = (bf16[640,1024]{1,0:T(8,128)(2,1)}, bf16[640,1024]{1,0:T(8,128)(2,1)}, bf16[640,1024]{1,0:T(8,128)(2,1)}, bf16[640,2048]{1,0:T(8,128)(2,1)}, f32...) custom-call(s32[4]{0:T(128)} %iota_xor_fusion.perm, ...), custom_call_target="tpu_custom_call" | custom-call | tf_op jit(solution)/shard_map/run_expert/pallas_call | solution.py:523
  530.0 28.5 %run_expert.3 = (bf16[640,1024]{1,0:T(8,128)(2,1)}, bf16[640,1024]{1,0:T(8,128)(2,1)}, bf16[640,1024]{1,0:T(8,128)(2,1)}, bf16[640,2048]{1,0:T(8,128)(2,1)}, f32...) custom-call(s32[4]{0:T(128)} %iota_xor_fusion.perm, ...), custom_call_target="tpu_custom_call" | custom-call | tf_op jit(solution)/shard_map/run_expert/pallas_call | solution.py:523
  558.6 5.8 shard_map.297
  567.4 5.6 all-to-all-start
  573.1 5.8 all-to-all-done
  578.9 36.6 %reduce-scatter.9.cloned.1.call-done = bf16[128,2048]{1,0:T(8,128)(2,1)} async-done(((bf16[1024,2048]{1,0:T(8,128)(2,1)}), bf16[128,2048]{1,0:T(8,128)(2,1)}) %reduce-scatter.9.cloned.1.call-update) | async-done | bytes 524304 | tf_op jit(solution)/shard_map/reduce_scatter | solution.py:916
  622.3 11.3 %collective-permute-done.36 = bf16[128,2048]{1,0:T(8,128)(2,1)S(1)} collective-permute-done((bf16[128,2048]{1,0:T(8,128)(2,1)S(1)}, bf16[128,2048]{1,0:T(8,128)(2,1)S(1)}, u32[]{:S(2)}, u32[]{:S(2)}) %collective-permute-start.36) | collective-permute-done | bytes 524320 | tf_op jit(solution)/shard_map/ppermute | solution.py:645
  633.6 9.4 collective-permute-done.37
  645.2 19.7 %attend_backward.1 = (bf16[512,512]{1,0:T(8,128)(2,1)}, bf16[4096,1024]{1,0:T(8,128)(2,1)}) custom-call(s32[2,16]{1,0:T(2,128)} %copy-done.56, bf16[512,512]{1,0:T(8,128)(2,1)} %get-tuple-element.61.query, bf16[4096,1024]{1,0:T(8,128)(2,1)} %all-gather.10.cloned.1.call-done.pairs, bf16[512,512]{1,0:T(8,128)(2,1)} %convolution_convert_fusion.28.grad, ...), custom_call_target="tpu_custom_call" | custom-call | tf_op jit(solution)/shard_map/attend_backward/pallas_call | solution.py:409
  688.0 73.7 %reduce-scatter.11.cloned.1.call-done.back.refs_7_ = bf16[512,1024]{1,0:T(8,128)(2,1)} async-done(((bf16[4096,1024]{1,0:T(8,128)(2,1)}), bf16[512,1024]{1,0:T(8,128)(2,1)}) %reduce-scatter.11.cloned.1.call-update) | async-done | bytes 1048592 | tf_op jit(solution)/shard_map/reduce_scatter | solution.py:980
  776.7 5.5 convolution_convert_fusion
  837.4 6.1 shard_map.296
  846.2 11.2 %collective-permute-done.64 = bf16[512,1024]{1,0:T(8,128)(2,1)} collective-permute-done((bf16[512,1024]{1,0:T(8,128)(2,1)}, bf16[512,1024]{1,0:T(8,128)(2,1)}, u32[]{:S(2)}, u32[]{:S(2)}) %collective-permute-start.64) | collective-permute-done | bytes 1048608 | tf_op jit(solution)/shard_map/ppermute | solution.py:645
  865.1 15.6 %collective-permute-done.58 = bf16[512,1024]{1,0:T(8,128)(2,1)S(1)} collective-permute-done((bf16[512,1024]{1,0:T(8,128)(2,1)S(1)}, bf16[512,1024]{1,0:T(8,128)(2,1)S(1)}, u32[]{:S(2)}, u32[]{:S(2)}) %collective-permute-start.58) | collective-permute-done | bytes 1048608 | tf_op jit(solution)/shard_map/ppermute | solution.py:645
  881.6 10.9 %collective-permute-done.61 = bf16[512,1024]{1,0:T(8,128)(2,1)S(1)} collective-permute-done((bf16[512,1024]{1,0:T(8,128)(2,1)S(1)}, bf16[512,1024]{1,0:T(8,128)(2,1)S(1)}, u32[]{:S(2)}, u32[]{:S(2)}) %collective-permute-start.61) | collective-permute-done | bytes 1048608 | tf_op jit(solution)/shard_map/ppermute | solution.py:645
  896.5 18.4 %collective-permute-done.71 = bf16[256,2048]{1,0:T(8,128)(2,1)S(1)} collective-permute-done((bf16[256,2048]{1,0:T(8,128)(2,1)S(1)}, bf16[256,2048]{1,0:T(8,128)(2,1)S(1)}, u32[]{:S(2)}, u32[]{:S(2)}) %collective-permute-start.71) | collective-permute-done | bytes 1048608 | tf_op jit(solution)/shard_map/ppermute | solution.py:645
  919.4 9.8 collective-permute-done.63
  929.7 30.2 %collective-permute-done.65 = bf16[512,1024]{1,0:T(8,128)(2,1)S(1)} collective-permute-done((bf16[512,1024]{1,0:T(8,128)(2,1)S(1)}, bf16[512,1024]{1,0:T(8,128)(2,1)S(1)}, u32[]{:S(2)}, u32[]{:S(2)}) %collective-permute-start.65) | collective-permute-done | bytes 1048608 | tf_op jit(solution)/shard_map/ppermute | solution.py:645
  967.8 6.3 collective-permute-done.57
  974.1 25.0 %collective-permute-done.59 = bf16[512,1024]{1,0:T(8,128)(2,1)S(1)} collective-permute-done((bf16[512,1024]{1,0:T(8,128)(2,1)S(1)}, bf16[512,1024]{1,0:T(8,128)(2,1)S(1)}, u32[]{:S(2)}, u32[]{:S(2)}) %collective-permute-start.59) | collective-permute-done | bytes 1048608 | tf_op jit(solution)/shard_map/ppermute | solution.py:645
  1007.5 4.6 fusion.69
  1028.9 5.5 collective-permute-done.46
  1048.2 6.8 all-to-all-start.1
  (543 shorter events, 320.4 us)
Async XLA Ops:
  7.2 70.5 %all-gather.8.cloned.1.call-start = ((), (), s32[]{:S(2)}) async-start(), calls=%async_computation.8 | async-start | bytes 4718592 | tf_op jit(solution)/shard_map/all_gather | solution.py:766
  24.1 96.3 %all-gather.16.cloned.1.call-start = ((), (), s32[]{:S(2)}) async-start(), calls=%async_computation.18 | async-start | bytes 4718592 | tf_op jit(solution)/shard_map/all_gather | solution.py:771
  25.2 178.2 %all-gather.10.cloned.1.call-start = ((), (), s32[]{:S(2)}) async-start(), calls=%async_computation.9 | async-start | bytes 9437184 | tf_op jit(solution)/shard_map/all_gather | solution.py:835
  48.7 24.3 %collective-permute-start.1 = (bf16[128,2048]{1,0:T(8,128)(2,1)S(1)}, bf16[128,2048]{1,0:T(8,128)(2,1)S(1)}, u32[]{:S(2)}, u32[]{:S(2)}) collective-permute-start(bf16[128,2048]{1,0:T(8,128)(2,1)S(1)} %copy-done.9), channel_id=1, source_target_pairs={{0,16},{8,24},{16,0},{24,8},{1,17},{9,25},{17,1},{25,9},{2,18},{10... | collective-permute-start | bytes 1572872 | tf_op jit(solution)/shard_map/ppermute | solution.py:645
  98.2 386.1 %all-gather.14.cloned.1.call-start = ((), (), s32[]{:S(2)}) async-start(), calls=%async_computation.11 | async-start | bytes 4718592 | tf_op jit(solution)/shard_map/all_gather | solution.py:776
  98.8 392.5 %all-gather.12.cloned.1.call-start = ((), (), s32[]{:S(2)}) async-start(), calls=%async_computation.10 | async-start | bytes 4718592 | tf_op jit(solution)/shard_map/all_gather | solution.py:844
  219.0 25.0 %collective-permute-start.16 = (bf16[128,2048]{1,0:T(8,128)(2,1)S(1)}, bf16[128,2048]{1,0:T(8,128)(2,1)S(1)}, u32[]{:S(2)}, u32[]{:S(2)}) collective-permute-start(bf16[128,2048]{1,0:T(8,128)(2,1)S(1)} %get-tuple-element.221), channel_id=1, source_target_pairs={{0,16},{8,24},{16,0},{24,8},{1,17},{9,25},{17,1},{25,9},{2,18},{10... | collective-permute-start | bytes 1572872 | tf_op jit(solution)/shard_map/ppermute | solution.py:645
  245.8 369.7 %reduce-scatter.9.cloned.1.call-start = ((), (), s32[]{:S(2)}) async-start(), calls=%async_computation.13 | async-start | bytes 4718592 | tf_op jit(solution)/shard_map/reduce_scatter | solution.py:916
  247.7 26.2 %collective-permute-start.18 = (bf16[512,1024]{1,0:T(8,128)(2,1)S(1)}, bf16[512,1024]{1,0:T(8,128)(2,1)}, u32[]{:S(2)}, u32[]{:S(2)}) collective-permute-start(bf16[512,1024]{1,0:T(8,128)(2,1)S(1)} %get-tuple-element.218), channel_id=1, source_target_pairs={{0,8},{8,0},{16,24},{24,16},{1,9},{9,1},{17,25},{25,17},{2,10},{10... | collective-permute-start | bytes 3145736 | tf_op jit(solution)/shard_map/ppermute | solution.py:645
  249.0 26.4 %collective-permute-start.19 = (bf16[512,1024]{1,0:T(8,128)(2,1)S(1)}, bf16[512,1024]{1,0:T(8,128)(2,1)S(1)}, u32[]{:S(2)}, u32[]{:S(2)}) collective-permute-start(bf16[512,1024]{1,0:T(8,128)(2,1)S(1)} %get-tuple-element.218), channel_id=1, source_target_pairs={{0,16},{8,24},{16,0},{24,8},{1,17},{9,25},{17,1},{25,9},{2,18},{10... | collective-permute-start | bytes 3145736 | tf_op jit(solution)/shard_map/ppermute | solution.py:645
  251.0 45.3 %collective-permute-start.21 = (bf16[512,1024]{1,0:T(8,128)(2,1)S(1)}, bf16[512,1024]{1,0:T(8,128)(2,1)S(1)}, u32[]{:S(2)}, u32[]{:S(2)}) collective-permute-start(bf16[512,1024]{1,0:T(8,128)(2,1)S(1)} %get-tuple-element.216), channel_id=1, source_target_pairs={{0,8},{8,0},{16,24},{24,16},{1,9},{9,1},{17,25},{25,17},{2,10},{10... | collective-permute-start | bytes 3145736 | tf_op jit(solution)/shard_map/ppermute | solution.py:645
  252.5 45.0 %collective-permute-start.22 = (bf16[512,1024]{1,0:T(8,128)(2,1)S(1)}, bf16[512,1024]{1,0:T(8,128)(2,1)S(1)}, u32[]{:S(2)}, u32[]{:S(2)}) collective-permute-start(bf16[512,1024]{1,0:T(8,128)(2,1)S(1)} %get-tuple-element.216), channel_id=1, source_target_pairs={{0,16},{8,24},{16,0},{24,8},{1,17},{9,25},{17,1},{25,9},{2,18},{10... | collective-permute-start | bytes 3145736 | tf_op jit(solution)/shard_map/ppermute | solution.py:645
  254.5 64.4 %collective-permute-start.24 = (bf16[256,2048]{1,0:T(8,128)(2,1)}, bf16[256,2048]{1,0:T(8,128)(2,1)}, u32[]{:S(2)}, u32[]{:S(2)}) collective-permute-start(bf16[256,2048]{1,0:T(8,128)(2,1)} %get-tuple-element.214), channel_id=1, source_target_pairs={{0,8},{8,0},{16,24},{24,16},{1,9},{9,1},{17,25},{25,17},{2,10},{10... | collective-permute-start | bytes 3145736 | tf_op jit(solution)/shard_map/ppermute | solution.py:645
  273.9 46.4 %collective-permute-start.25 = (bf16[256,2048]{1,0:T(8,128)(2,1)}, bf16[256,2048]{1,0:T(8,128)(2,1)}, u32[]{:S(2)}, u32[]{:S(2)}) collective-permute-start(bf16[256,2048]{1,0:T(8,128)(2,1)} %get-tuple-element.214), channel_id=1, source_target_pairs={{0,16},{8,24},{16,0},{24,8},{1,17},{9,25},{17,1},{25,9},{2,18},{10... | collective-permute-start | bytes 3145736 | tf_op jit(solution)/shard_map/ppermute | solution.py:645
  275.4 67.1 %collective-permute-start.28 = (bf16[512,1024]{1,0:T(8,128)(2,1)S(1)}, bf16[512,1024]{1,0:T(8,128)(2,1)}, u32[]{:S(2)}, u32[]{:S(2)}) collective-permute-start(bf16[512,1024]{1,0:T(8,128)(2,1)S(1)} %get-tuple-element.217), channel_id=1, source_target_pairs={{0,16},{8,24},{16,0},{24,8},{1,17},{9,25},{17,1},{25,9},{2,18},{10... | collective-permute-start | bytes 3145736 | tf_op jit(solution)/shard_map/ppermute | solution.py:645
  296.3 47.1 %collective-permute-start.27 = (bf16[512,1024]{1,0:T(8,128)(2,1)S(1)}, bf16[512,1024]{1,0:T(8,128)(2,1)}, u32[]{:S(2)}, u32[]{:S(2)}) collective-permute-start(bf16[512,1024]{1,0:T(8,128)(2,1)S(1)} %get-tuple-element.217), channel_id=1, source_target_pairs={{0,8},{8,0},{16,24},{24,16},{1,9},{9,1},{17,25},{25,17},{2,10},{10... | collective-permute-start | bytes 3145736 | tf_op jit(solution)/shard_map/ppermute | solution.py:645
  298.5 66.5 %collective-permute-start.20 = (bf16[512,1024]{1,0:T(8,128)(2,1)}, bf16[512,1024]{1,0:T(8,128)(2,1)}, u32[]{:S(2)}, u32[]{:S(2)}) collective-permute-start(bf16[512,1024]{1,0:T(8,128)(2,1)} %collective-permute-done.18), channel_id=1, source_target_pairs={{0,16},{8,24},{16,0},{24,8},{1,17},{9,25},{17,1},{25,9},{2,18},{10... | collective-permute-start | bytes 3145736 | tf_op jit(solution)/shard_map/ppermute | solution.py:645
  318.9 68.6 %collective-permute-start.31 = (bf16[512,1024]{1,0:T(8,128)(2,1)}, bf16[512,1024]{1,0:T(8,128)(2,1)}, u32[]{:S(2)}, u32[]{:S(2)}) collective-permute-start(bf16[512,1024]{1,0:T(8,128)(2,1)} %get-tuple-element.215), channel_id=1, source_target_pairs={{0,16},{8,24},{16,0},{24,8},{1,17},{9,25},{17,1},{25,9},{2,18},{10... | collective-permute-start | bytes 3145736 | tf_op jit(solution)/shard_map/ppermute | solution.py:645
  320.4 89.6 %collective-permute-start.23 = (bf16[512,1024]{1,0:T(8,128)(2,1)}, bf16[512,1024]{1,0:T(8,128)(2,1)}, u32[]{:S(2)}, u32[]{:S(2)}) collective-permute-start(bf16[512,1024]{1,0:T(8,128)(2,1)} %copy-done.39), channel_id=1, source_target_pairs={{0,16},{8,24},{16,0},{24,8},{1,17},{9,25},{17,1},{25,9},{2,18},{10... | collective-permute-start | bytes 3145736 | tf_op jit(solution)/shard_map/ppermute | solution.py:645
  342.5 89.9 %collective-permute-start.34 = (bf16[256,2048]{1,0:T(8,128)(2,1)}, bf16[256,2048]{1,0:T(8,128)(2,1)}, u32[]{:S(2)}, u32[]{:S(2)}) collective-permute-start(bf16[256,2048]{1,0:T(8,128)(2,1)} %get-tuple-element.213), channel_id=1, source_target_pairs={{0,16},{8,24},{16,0},{24,8},{1,17},{9,25},{17,1},{25,9},{2,18},{10... | collective-permute-start | bytes 3145736 | tf_op jit(solution)/shard_map/ppermute | solution.py:645
  343.4 109.8 %collective-permute-start.26 = (bf16[256,2048]{1,0:T(8,128)(2,1)}, bf16[256,2048]{1,0:T(8,128)(2,1)}, u32[]{:S(2)}, u32[]{:S(2)}) collective-permute-start(bf16[256,2048]{1,0:T(8,128)(2,1)} %collective-permute-done.24), channel_id=1, source_target_pairs={{0,16},{8,24},{16,0},{24,8},{1,17},{9,25},{17,1},{25,9},{2,18},{10... | collective-permute-start | bytes 3145736 | tf_op jit(solution)/shard_map/ppermute | solution.py:645
  365.0 92.5 %collective-permute-start.29 = (bf16[512,1024]{1,0:T(8,128)(2,1)}, bf16[512,1024]{1,0:T(8,128)(2,1)S(1)}, u32[]{:S(2)}, u32[]{:S(2)}) collective-permute-start(bf16[512,1024]{1,0:T(8,128)(2,1)} %collective-permute-done.28), channel_id=1, source_target_pairs={{0,8},{8,0},{16,24},{24,16},{1,9},{9,1},{17,25},{25,17},{2,10},{10... | collective-permute-start | bytes 3145736 | tf_op jit(solution)/shard_map/ppermute | solution.py:645
  387.5 73.4 %collective-permute-start.30 = (bf16[512,1024]{1,0:T(8,128)(2,1)S(1)}, bf16[512,1024]{1,0:T(8,128)(2,1)S(1)}, u32[]{:S(2)}, u32[]{:S(2)}) collective-permute-start(bf16[512,1024]{1,0:T(8,128)(2,1)S(1)} %copy-done.15), channel_id=1, source_target_pairs={{0,8},{8,0},{16,24},{24,16},{1,9},{9,1},{17,25},{25,17},{2,10},{10... | collective-permute-start | bytes 3145736 | tf_op jit(solution)/shard_map/ppermute | solution.py:645
  409.9 51.0 %collective-permute-start.32 = (bf16[512,1024]{1,0:T(8,128)(2,1)}, bf16[512,1024]{1,0:T(8,128)(2,1)S(1)}, u32[]{:S(2)}, u32[]{:S(2)}) collective-permute-start(bf16[512,1024]{1,0:T(8,128)(2,1)} %collective-permute-done.31), channel_id=1, source_target_pairs={{0,8},{8,0},{16,24},{24,16},{1,9},{9,1},{17,25},{25,17},{2,10},{10... | collective-permute-start | bytes 3145736 | tf_op jit(solution)/shard_map/ppermute | solution.py:645
  432.4 37.4 %collective-permute-start.33 = (bf16[256,2048]{1,0:T(8,128)(2,1)S(1)}, bf16[256,2048]{1,0:T(8,128)(2,1)S(1)}, u32[]{:S(2)}, u32[]{:S(2)}) collective-permute-start(bf16[256,2048]{1,0:T(8,128)(2,1)S(1)} %copy-done.16), channel_id=1, source_target_pairs={{0,8},{8,0},{16,24},{24,16},{1,9},{9,1},{17,25},{25,17},{2,10},{10... | collective-permute-start | bytes 3145736 | tf_op jit(solution)/shard_map/ppermute | solution.py:645
  453.1 23.6 %collective-permute-start.35 = (bf16[256,2048]{1,0:T(8,128)(2,1)}, bf16[256,2048]{1,0:T(8,128)(2,1)S(1)}, u32[]{:S(2)}, u32[]{:S(2)}) collective-permute-start(bf16[256,2048]{1,0:T(8,128)(2,1)} %collective-permute-done.34), channel_id=1, source_target_pairs={{0,8},{8,0},{16,24},{24,16},{1,9},{9,1},{17,25},{25,17},{2,10},{10... | collective-permute-start | bytes 3145736 | tf_op jit(solution)/shard_map/ppermute | solution.py:645
  573.0 188.7 %reduce-scatter.11.cloned.1.call-start = ((), (), s32[]{:S(2)}) async-start(), calls=%async_computation.14 | async-start | bytes 9437184 | tf_op jit(solution)/shard_map/reduce_scatter | solution.py:980
  664.9 338.2 %reduce-scatter.13.cloned.1.call-start = ((), (), s32[]{:S(2)}) async-start(), calls=%async_computation.15 | async-start | bytes 2359296 | tf_op jit(solution)/shard_map/reduce_scatter | solution.py:987
  683.8 339.8 %reduce-scatter.17.cloned.1.call-start = ((), (), s32[]{:S(2)}) async-start(), calls=%async_computation.17 | async-start | bytes 2359296 | tf_op jit(solution)/shard_map/reduce_scatter | solution.py:976
  688.0 367.0 %reduce-scatter.15.cloned.1.call-start = ((), (), s32[]{:S(2)}) async-start(), calls=%async_computation.16 | async-start | bytes 4718592 | tf_op jit(solution)/shard_map/reduce_scatter | solution.py:995
  782.2 278.0 %reduce-scatter.7.cloned.1.call-start = ((), (), s32[]{:S(2)}) async-start(), calls=%async_computation.12 | async-start | bytes 4718592 | tf_op jit(solution)/shard_map/reduce_scatter | solution.py:922
  789.0 105.4 %collective-permute-start.69 = (bf16[256,2048]{1,0:T(8,128)(2,1)}, bf16[256,2048]{1,0:T(8,128)(2,1)}, u32[]{:S(2)}, u32[]{:S(2)}) collective-permute-start(bf16[256,2048]{1,0:T(8,128)(2,1)} %convolution_convert_fusion.10), channel_id=1, source_target_pairs={{0,8},{8,0},{16,24},{24,16},{1,9},{9,1},{17,25},{25,17},{2,10},{10... | collective-permute-start | bytes 3145736 | tf_op jit(solution)/shard_map/ppermute | solution.py:645
  793.5 50.3 %collective-permute-start.70 = (bf16[256,2048]{1,0:T(8,128)(2,1)}, bf16[256,2048]{1,0:T(8,128)(2,1)}, u32[]{:S(2)}, u32[]{:S(2)}) collective-permute-start(bf16[256,2048]{1,0:T(8,128)(2,1)} %convolution_convert_fusion.8), channel_id=1, source_target_pairs={{0,8},{8,0},{16,24},{24,16},{1,9},{9,1},{17,25},{25,17},{2,10},{10... | collective-permute-start | bytes 3145736 | tf_op jit(solution)/shard_map/ppermute | solution.py:645
  797.0 64.9 %collective-permute-start.73 = (bf16[256,2048]{1,0:T(8,128)(2,1)}, bf16[256,2048]{1,0:T(8,128)(2,1)}, u32[]{:S(2)}, u32[]{:S(2)}) collective-permute-start(bf16[256,2048]{1,0:T(8,128)(2,1)} %convolution_convert_fusion.4), channel_id=1, source_target_pairs={{0,16},{8,24},{16,0},{24,8},{1,17},{9,25},{17,1},{25,9},{2,18},{10... | collective-permute-start | bytes 3145736 | tf_op jit(solution)/shard_map/ppermute | solution.py:645
  804.6 52.9 %collective-permute-start.64 = (bf16[512,1024]{1,0:T(8,128)(2,1)}, bf16[512,1024]{1,0:T(8,128)(2,1)}, u32[]{:S(2)}, u32[]{:S(2)}) collective-permute-start(bf16[512,1024]{1,0:T(8,128)(2,1)} %convolution_convert_fusion.16), channel_id=1, source_target_pairs={{0,8},{8,0},{16,24},{24,16},{1,9},{9,1},{17,25},{25,17},{2,10},{10... | collective-permute-start | bytes 3145736 | tf_op jit(solution)/shard_map/ppermute | solution.py:645
  813.6 46.0 %collective-permute-start.67 = (bf16[512,1024]{1,0:T(8,128)(2,1)}, bf16[512,1024]{1,0:T(8,128)(2,1)}, u32[]{:S(2)}, u32[]{:S(2)}) collective-permute-start(bf16[512,1024]{1,0:T(8,128)(2,1)} %convolution_convert_fusion.12), channel_id=1, source_target_pairs={{0,16},{8,24},{16,0},{24,8},{1,17},{9,25},{17,1},{25,9},{2,18},{10... | collective-permute-start | bytes 3145736 | tf_op jit(solution)/shard_map/ppermute | solution.py:645
  843.7 51.3 %collective-permute-start.72 = (bf16[256,2048]{1,0:T(8,128)(2,1)}, bf16[256,2048]{1,0:T(8,128)(2,1)S(1)}, u32[]{:S(2)}, u32[]{:S(2)}) collective-permute-start(bf16[256,2048]{1,0:T(8,128)(2,1)} %convolution_convert_fusion.6), channel_id=1, source_target_pairs={{0,16},{8,24},{16,0},{24,8},{1,17},{9,25},{17,1},{25,9},{2,18},{10... | collective-permute-start | bytes 3145736 | tf_op jit(solution)/shard_map/ppermute | solution.py:645
  859.6 32.8 %collective-permute-start.61 = (bf16[512,1024]{1,0:T(8,128)(2,1)S(1)}, bf16[512,1024]{1,0:T(8,128)(2,1)S(1)}, u32[]{:S(2)}, u32[]{:S(2)}) collective-permute-start(bf16[512,1024]{1,0:T(8,128)(2,1)S(1)} %copy-done.91), channel_id=1, source_target_pairs={{0,16},{8,24},{16,0},{24,8},{1,17},{9,25},{17,1},{25,9},{2,18},{10... | collective-permute-start | bytes 3145736 | tf_op jit(solution)/shard_map/ppermute | solution.py:645
  861.9 53.1 %collective-permute-start.71 = (bf16[256,2048]{1,0:T(8,128)(2,1)S(1)}, bf16[256,2048]{1,0:T(8,128)(2,1)S(1)}, u32[]{:S(2)}, u32[]{:S(2)}) collective-permute-start(bf16[256,2048]{1,0:T(8,128)(2,1)S(1)} %add_convert_fusion.2), channel_id=1, source_target_pairs={{0,16},{8,24},{16,0},{24,8},{1,17},{9,25},{17,1},{25,9},{2,18},{10... | collective-permute-start | bytes 3145736 | tf_op jit(solution)/shard_map/ppermute | solution.py:645
  880.7 37.6 %collective-permute-start.74 = (bf16[256,2048]{1,0:T(8,128)(2,1)S(1)}, bf16[256,2048]{1,0:T(8,128)(2,1)S(1)}, u32[]{:S(2)}, u32[]{:S(2)}) collective-permute-start(bf16[256,2048]{1,0:T(8,128)(2,1)S(1)} %add_convert_fusion.1), channel_id=1, source_target_pairs={{0,8},{8,0},{16,24},{24,16},{1,9},{9,1},{17,25},{25,17},{2,10},{10... | collective-permute-start | bytes 3145736 | tf_op jit(solution)/shard_map/ppermute | solution.py:645
  892.5 36.7 %collective-permute-start.63 = (bf16[512,1024]{1,0:T(8,128)(2,1)S(1)}, bf16[512,1024]{1,0:T(8,128)(2,1)S(1)}, u32[]{:S(2)}, u32[]{:S(2)}) collective-permute-start(bf16[512,1024]{1,0:T(8,128)(2,1)S(1)} %copy-done.90), channel_id=1, source_target_pairs={{0,8},{8,0},{16,24},{24,16},{1,9},{9,1},{17,25},{25,17},{2,10},{10... | collective-permute-start | bytes 3145736 | tf_op jit(solution)/shard_map/ppermute | solution.py:645
  894.4 66.6 %collective-permute-start.66 = (bf16[512,1024]{1,0:T(8,128)(2,1)S(1)}, bf16[512,1024]{1,0:T(8,128)(2,1)S(1)}, u32[]{:S(2)}, u32[]{:S(2)}) collective-permute-start(bf16[512,1024]{1,0:T(8,128)(2,1)S(1)} %copy-done.89), channel_id=1, source_target_pairs={{0,16},{8,24},{16,0},{24,8},{1,17},{9,25},{17,1},{25,9},{2,18},{10... | collective-permute-start | bytes 3145736 | tf_op jit(solution)/shard_map/ppermute | solution.py:645
  895.0 64.9 %collective-permute-start.65 = (bf16[512,1024]{1,0:T(8,128)(2,1)S(1)}, bf16[512,1024]{1,0:T(8,128)(2,1)S(1)}, u32[]{:S(2)}, u32[]{:S(2)}) collective-permute-start(bf16[512,1024]{1,0:T(8,128)(2,1)S(1)} %add_convert_fusion.4), channel_id=1, source_target_pairs={{0,16},{8,24},{16,0},{24,8},{1,17},{9,25},{17,1},{25,9},{2,18},{10... | collective-permute-start | bytes 3145736 | tf_op jit(solution)/shard_map/ppermute | solution.py:645
  915.0 47.6 %collective-permute-start.68 = (bf16[512,1024]{1,0:T(8,128)(2,1)S(1)}, bf16[512,1024]{1,0:T(8,128)(2,1)S(1)}, u32[]{:S(2)}, u32[]{:S(2)}) collective-permute-start(bf16[512,1024]{1,0:T(8,128)(2,1)S(1)} %add_convert_fusion.3), channel_id=1, source_target_pairs={{0,8},{8,0},{16,24},{24,16},{1,9},{9,1},{17,25},{25,17},{2,10},{10... | collective-permute-start | bytes 3145736 | tf_op jit(solution)/shard_map/ppermute | solution.py:645
  918.3 55.9 %collective-permute-start.57 = (bf16[512,1024]{1,0:T(8,128)(2,1)S(1)}, bf16[512,1024]{1,0:T(8,128)(2,1)S(1)}, u32[]{:S(2)}, u32[]{:S(2)}) collective-permute-start(bf16[512,1024]{1,0:T(8,128)(2,1)S(1)} %copy-done.88), channel_id=1, source_target_pairs={{0,8},{8,0},{16,24},{24,16},{1,9},{9,1},{17,25},{25,17},{2,10},{10... | collective-permute-start | bytes 3145736 | tf_op jit(solution)/shard_map/ppermute | solution.py:645
  929.2 71.9 %collective-permute-start.60 = (bf16[512,1024]{1,0:T(8,128)(2,1)S(1)}, bf16[512,1024]{1,0:T(8,128)(2,1)S(1)}, u32[]{:S(2)}, u32[]{:S(2)}) collective-permute-start(bf16[512,1024]{1,0:T(8,128)(2,1)S(1)} %copy-done.87), channel_id=1, source_target_pairs={{0,16},{8,24},{16,0},{24,8},{1,17},{9,25},{17,1},{25,9},{2,18},{10... | collective-permute-start | bytes 3145736 | tf_op jit(solution)/shard_map/ppermute | solution.py:645
  959.9 39.2 %collective-permute-start.59 = (bf16[512,1024]{1,0:T(8,128)(2,1)S(1)}, bf16[512,1024]{1,0:T(8,128)(2,1)S(1)}, u32[]{:S(2)}, u32[]{:S(2)}) collective-permute-start(bf16[512,1024]{1,0:T(8,128)(2,1)S(1)} %add_convert_fusion.6), channel_id=1, source_target_pairs={{0,16},{8,24},{16,0},{24,8},{1,17},{9,25},{17,1},{25,9},{2,18},{10... | collective-permute-start | bytes 3145736 | tf_op jit(solution)/shard_map/ppermute | solution.py:645
  961.0 40.1 %collective-permute-start.62 = (bf16[512,1024]{1,0:T(8,128)(2,1)S(1)}, bf16[512,1024]{1,0:T(8,128)(2,1)S(1)}, u32[]{:S(2)}, u32[]{:S(2)}) collective-permute-start(bf16[512,1024]{1,0:T(8,128)(2,1)S(1)} %add_convert_fusion.5), channel_id=1, source_target_pairs={{0,8},{8,0},{16,24},{24,16},{1,9},{9,1},{17,25},{25,17},{2,10},{10... | collective-permute-start | bytes 3145736 | tf_op jit(solution)/shard_map/ppermute | solution.py:645
  (137 other events, 2950.9 us)
Sparse Core Ops, SparseCore 0:
  24.2 47.8 all-gather.7
  74.3 46.0 all-gather.15
  122.6 80.8 all-gather.9
  204.9 45.3 all-gather.13
  252.3 45.6 all-gather.11
  564.5 50.9 reduce-scatter.8
  665.0 96.6 reduce-scatter.10
  764.0 34.3 reduce-scatter.12
  800.7 34.8 reduce-scatter.16
  837.8 48.5 reduce-scatter.14
  888.7 48.3 reduce-scatter.6

commit v6 on v5

--- a/solution.py
+++ b/solution.py
@@ -973,7 +973,6 @@
     branch_grad = jnp.concatenate(branch_grad, axis=0)
     context_grad = jnp.dot(branch_grad, output_rows.T, preferred_element_type=f32).astype(bf16)
     output_sum = jnp.dot(context.T, branch_grad, preferred_element_type=f32).astype(bf16)
-    output_out = lax.psum_scatter(output_sum, "blk", scatter_dimension=0, tiled=True)
     query_back, pairs_back = attend_backward(
         query_heads, pairs_all, context_grad, attended, totals, marks, tables, TILE
     )
@@ -984,7 +983,16 @@
     query_inner = head_pieces(query_inner)
     query_raw_grad = raw_backward(query_inner, query_scaled, query_raw, query_factor, None, width)
     query_sum = jnp.dot(normed_moved.T, query_raw_grad, preferred_element_type=f32).astype(bf16)
-    query_sum = lax.psum_scatter(query_sum, "blk", scatter_dimension=0, tiled=True)
+    query_output_sum = jnp.concatenate(
+        [
+            query_sum.reshape(blocks, heads_axis * part, columns),
+            output_sum.reshape(blocks, heads_axis * part, columns),
+        ],
+        axis=1,
+    ).reshape(blocks * 2 * heads_axis * part, columns)
+    query_output_sum = lax.psum_scatter(query_output_sum, "blk", scatter_dimension=0, tiled=True)
+    query_sum = query_output_sum[: heads_axis * part]
+    output_out = query_output_sum[heads_axis * part :].reshape(part, width)
     normed_part = jnp.dot(query_raw_grad, query_full.T, preferred_element_type=f32)
     key_scaled, key_inner, keynorm_sum = rope_backward(
         pairs_back, key_raw, key_factor, key_scale, cosine, sine_part, 2

time: 1090 us -> 1090 us (level)
  transfers between devices with their start and end apart: 88 -> 87, of which waited for: 38 -> 39; matrix products, arithmetic and copies ran while one was open for 19% -> 20% of each run, Pallas kernels for 5% -> 5%
where the time goes in v6:
time: 1090 us; the launch traced here: 1080 us
  waiting for transfers between devices  572 us (52%)
  Pallas kernels  144 us (13%)
  starting transfers between devices  93.9 us (9%)
  other arithmetic  86.2 us (8%)
  matrix products  77.6 us (7%)
  local copies, waits for them, and re-layouts  73.4 us (7%)
  between operations  16.1 us (1%)
  blocking collectives  14.8 us (1%)
    ppermute x75, waiting for transfers between devices, exchange(): lax.ppermute(array, 'head', [(at, at ^ offset) for at in range(count)])  384 us
    ppermute x75, starting transfers between devices, exchange(): lax.ppermute(array, 'head', [(at, at ^ offset) for at in range(count)])  81 us
    reduce_scatter x1, waiting for transfers between devices, layer(): lax.psum_scatter(pairs_back, 'blk', scatter_dimension=0, tiled=True)  68 us
    all_gather x1, waiting for transfers between devices, layer(): pairs_all = lax.all_gather(pairs, 'blk', axis=0, tiled=True)  63.6 us
    pallas_call x2, Pallas kernels, run_expert(): pl.pallas_call(expert_kernel, grid_spec=pltpu.PrefetchScalarGridSpec(num_...  56.9 us
    dot_general x24, matrix products, pieces_of(): jnp.dot(left[:, offset * size:(offset + 1) * size].T, right, preferred_el...  47.3 us
    reduce_scatter x1, waiting for transfers between devices, layer(): lax.psum_scatter(incoming.reshape(blocks * rows, width), 'blk', scatter_d...  36.6 us
    concatenate x6, other arithmetic, layer(): jnp.concatenate(pieces, axis=0)  30.9 us
  transfers between devices with their start and end apart: 87, of which 39 were waited for; matrix products, arithmetic and copies ran while one was open for 20% of the time, Pallas kernels for 5%

profile of v6, /device:TPU:0, one launch (start us, length us, event | category | flops | bytes accessed | tf_op | source)
XLA Modules:
  0.0 1078.2 jit_solution(11207012566988222061)
XLA Ops:
  14.1 5.0 collective-permute-done.6
  28.8 14.8 %all-gather.1 = bf16[8,1,3328]{2,1,0:T(2,128)(2,1)S(1)} all-gather(bf16[1,1,3328]{2,1,0:T(2,128)(2,1)S(1)} %maximum_bitcast_fusion), channel_id=1, replica_groups=mesh['head'=4,'blk'=8] {'blk'}, dimensions={0}, use_global_device_ids=true | all-gather | bytes 59904 | tf_op jit(solution)/shard_map/all_gather | solution.py:790
  57.5 4.5 collective-permute-done.refs_1_
  62.0 11.0 %collective-permute-done.1.refs_2_ = bf16[128,2048]{1,0:T(8,128)(2,1)S(1)} collective-permute-done((bf16[128,2048]{1,0:T(8,128)(2,1)S(1)}, bf16[128,2048]{1,0:T(8,128)(2,1)S(1)}, u32[]{:S(2)}, u32[]{:S(2)}) %collective-permute-start.1) | collective-permute-done | bytes 524320 | tf_op jit(solution)/shard_map/ppermute | solution.py:645
  77.6 4.9 copy.119
  82.5 4.6 shard_map.292
  106.7 13.7 %all-gather.16.cloned.1.call-done = bf16[4096,512]{1,0:T(8,128)(2,1)} async-done(((bf16[512,512]{1,0:T(8,128)(2,1)}), bf16[4096,512]{1,0:T(8,128)(2,1)}) %all-gather.16.cloned.1.call-update) | async-done | bytes 4194320 | tf_op jit(solution)/shard_map/all_gather | solution.py:771
  139.9 63.6 %all-gather.10.cloned.1.call-done.pairs = bf16[4096,1024]{1,0:T(8,128)(2,1)} async-done(((bf16[512,1024]{1,0:T(8,128)(2,1)}), bf16[4096,1024]{1,0:T(8,128)(2,1)}) %all-gather.10.cloned.1.call-update) | async-done | bytes 8388624 | tf_op jit(solution)/shard_map/all_gather | solution.py:835
  203.4 11.5 %attend_forward.1 = (f32[512,512]{1,0:T(8,128)}, bf16[512,512]{1,0:T(8,128)(2,1)}, f32[512,512]{1,0:T(8,128)}) custom-call(s32[2,16]{1,0:T(2,128)} %select_reduce_fusion.2.listed, s32[2]{0:T(128)} %get-tuple-element.206.counts, bf16[512,512]{1,0:T(8,128)(2,1)} %get-tuple-element.61.query, bf16[4096,1024]{1,0:T(8,128)(2,1)} %all-gather.10.cloned.1.call-done.pairs, ...), custom_call_target="tpu_custom_call" | custom-call | tf_op jit(solution)/shard_map/attend_forward/pallas_call | solution.py:299
  221.0 11.3 %collective-permute-done.15 = bf16[128,2048]{1,0:T(8,128)(2,1)S(1)} collective-permute-done((bf16[128,2048]{1,0:T(8,128)(2,1)S(1)}, bf16[128,2048]{1,0:T(8,128)(2,1)S(1)}, u32[]{:S(2)}, u32[]{:S(2)}) %collective-permute-start.15) | collective-permute-done | bytes 524320 | tf_op jit(solution)/shard_map/ppermute | solution.py:645
  232.3 11.7 %collective-permute-done.16 = bf16[128,2048]{1,0:T(8,128)(2,1)S(1)} collective-permute-done((bf16[128,2048]{1,0:T(8,128)(2,1)S(1)}, bf16[128,2048]{1,0:T(8,128)(2,1)S(1)}, u32[]{:S(2)}, u32[]{:S(2)}) %collective-permute-start.16) | collective-permute-done | bytes 524320 | tf_op jit(solution)/shard_map/ppermute | solution.py:645
  255.7 18.3 %collective-permute-done.18 = bf16[512,1024]{1,0:T(8,128)(2,1)} collective-permute-done((bf16[512,1024]{1,0:T(8,128)(2,1)S(1)}, bf16[512,1024]{1,0:T(8,128)(2,1)}, u32[]{:S(2)}, u32[]{:S(2)}) %collective-permute-start.18) | collective-permute-done | bytes 1048608 | tf_op jit(solution)/shard_map/ppermute | solution.py:645
  276.0 20.3 %collective-permute-done.21 = bf16[512,1024]{1,0:T(8,128)(2,1)S(1)} collective-permute-done((bf16[512,1024]{1,0:T(8,128)(2,1)S(1)}, bf16[512,1024]{1,0:T(8,128)(2,1)S(1)}, u32[]{:S(2)}, u32[]{:S(2)}) %collective-permute-start.21) | collective-permute-done | bytes 1048608 | tf_op jit(solution)/shard_map/ppermute | solution.py:645
  299.7 19.1 %collective-permute-done.24 = bf16[256,2048]{1,0:T(8,128)(2,1)} collective-permute-done((bf16[256,2048]{1,0:T(8,128)(2,1)}, bf16[256,2048]{1,0:T(8,128)(2,1)}, u32[]{:S(2)}, u32[]{:S(2)}) %collective-permute-start.24) | collective-permute-done | bytes 1048608 | tf_op jit(solution)/shard_map/ppermute | solution.py:645
  321.9 20.6 %collective-permute-done.28 = bf16[512,1024]{1,0:T(8,128)(2,1)} collective-permute-done((bf16[512,1024]{1,0:T(8,128)(2,1)S(1)}, bf16[512,1024]{1,0:T(8,128)(2,1)}, u32[]{:S(2)}, u32[]{:S(2)}) %collective-permute-start.28) | collective-permute-done | bytes 1048608 | tf_op jit(solution)/shard_map/ppermute | solution.py:645
  352.3 12.7 %collective-permute-done.20 = bf16[512,1024]{1,0:T(8,128)(2,1)} collective-permute-done((bf16[512,1024]{1,0:T(8,128)(2,1)}, bf16[512,1024]{1,0:T(8,128)(2,1)}, u32[]{:S(2)}, u32[]{:S(2)}) %collective-permute-start.20) | collective-permute-done | bytes 1048608 | tf_op jit(solution)/shard_map/ppermute | solution.py:645
  369.9 17.5 %collective-permute-done.31 = bf16[512,1024]{1,0:T(8,128)(2,1)} collective-permute-done((bf16[512,1024]{1,0:T(8,128)(2,1)}, bf16[512,1024]{1,0:T(8,128)(2,1)}, u32[]{:S(2)}, u32[]{:S(2)}) %collective-permute-start.31) | collective-permute-done | bytes 1048608 | tf_op jit(solution)/shard_map/ppermute | solution.py:645
  388.3 21.6 %collective-permute-done.23 = bf16[512,1024]{1,0:T(8,128)(2,1)} collective-permute-done((bf16[512,1024]{1,0:T(8,128)(2,1)}, bf16[512,1024]{1,0:T(8,128)(2,1)}, u32[]{:S(2)}, u32[]{:S(2)}) %collective-permute-start.23) | collective-permute-done | bytes 1048608 | tf_op jit(solution)/shard_map/ppermute | solution.py:645
  414.1 18.3 %collective-permute-done.34 = bf16[256,2048]{1,0:T(8,128)(2,1)} collective-permute-done((bf16[256,2048]{1,0:T(8,128)(2,1)}, bf16[256,2048]{1,0:T(8,128)(2,1)}, u32[]{:S(2)}, u32[]{:S(2)}) %collective-permute-start.34) | collective-permute-done | bytes 1048608 | tf_op jit(solution)/shard_map/ppermute | solution.py:645
  433.3 19.9 %collective-permute-done.26 = bf16[256,2048]{1,0:T(8,128)(2,1)} collective-permute-done((bf16[256,2048]{1,0:T(8,128)(2,1)}, bf16[256,2048]{1,0:T(8,128)(2,1)}, u32[]{:S(2)}, u32[]{:S(2)}) %collective-permute-start.26) | collective-permute-done | bytes 1048608 | tf_op jit(solution)/shard_map/ppermute | solution.py:645
  460.9 8.9 pad_maximum_fusion.4.up_weight
  469.8 7.0 collective-permute-done.35
  476.8 7.5 pad_maximum_fusion.5.down_weight
  484.9 6.3 shard_map.295
  495.3 6.3 shard_map.294
  501.6 28.4 %run_expert.2 = (bf16[640,1024]{1,0:T(8,128)(2,1)}, bf16[640,1024]{1,0:T(8,128)(2,1)}, bf16[640,1024]{1,0:T(8,128)(2,1)}, bf16[640,2048]{1,0:T(8,128)(2,1)}, f32...) custom-call(s32[4]{0:T(128)} %iota_xor_fusion.perm, ...), custom_call_target="tpu_custom_call" | custom-call | tf_op jit(solution)/shard_map/run_expert/pallas_call | solution.py:523
  530.0 28.5 %run_expert.3 = (bf16[640,1024]{1,0:T(8,128)(2,1)}, bf16[640,1024]{1,0:T(8,128)(2,1)}, bf16[640,1024]{1,0:T(8,128)(2,1)}, bf16[640,2048]{1,0:T(8,128)(2,1)}, f32...) custom-call(s32[4]{0:T(128)} %iota_xor_fusion.perm, ...), custom_call_target="tpu_custom_call" | custom-call | tf_op jit(solution)/shard_map/run_expert/pallas_call | solution.py:523
  558.5 5.8 shard_map.297
  567.4 5.6 all-to-all-start
  573.0 5.8 all-to-all-done
  578.8 36.6 %reduce-scatter.8.cloned.1.call-done = bf16[128,2048]{1,0:T(8,128)(2,1)} async-done(((bf16[1024,2048]{1,0:T(8,128)(2,1)}), bf16[128,2048]{1,0:T(8,128)(2,1)}) %reduce-scatter.8.cloned.1.call-update) | async-done | bytes 524304 | tf_op jit(solution)/shard_map/reduce_scatter | solution.py:916
  622.3 11.3 %collective-permute-done.36 = bf16[128,2048]{1,0:T(8,128)(2,1)S(1)} collective-permute-done((bf16[128,2048]{1,0:T(8,128)(2,1)S(1)}, bf16[128,2048]{1,0:T(8,128)(2,1)S(1)}, u32[]{:S(2)}, u32[]{:S(2)}) %collective-permute-start.36) | collective-permute-done | bytes 524320 | tf_op jit(solution)/shard_map/ppermute | solution.py:645
  633.6 9.4 collective-permute-done.37
  645.2 19.7 %attend_backward.1 = (bf16[512,512]{1,0:T(8,128)(2,1)}, bf16[4096,1024]{1,0:T(8,128)(2,1)}) custom-call(s32[2,16]{1,0:T(2,128)} %copy-done.57, bf16[512,512]{1,0:T(8,128)(2,1)} %get-tuple-element.61.query, bf16[4096,1024]{1,0:T(8,128)(2,1)} %all-gather.10.cloned.1.call-done.pairs, bf16[512,512]{1,0:T(8,128)(2,1)} %convolution_convert_fusion.28.grad, ...), custom_call_target="tpu_custom_call" | custom-call | tf_op jit(solution)/shard_map/attend_backward/pallas_call | solution.py:409
  693.7 68.0 %reduce-scatter.10.cloned.1.call-done.back.refs_7_ = bf16[512,1024]{1,0:T(8,128)(2,1)} async-done(((bf16[4096,1024]{1,0:T(8,128)(2,1)}), bf16[512,1024]{1,0:T(8,128)(2,1)}) %reduce-scatter.10.cloned.1.call-update) | async-done | bytes 1048592 | tf_op jit(solution)/shard_map/reduce_scatter | solution.py:979
  776.7 5.6 convolution_convert_fusion
  837.7 6.1 shard_map.296
  846.5 11.0 %collective-permute-done.64 = bf16[512,1024]{1,0:T(8,128)(2,1)} collective-permute-done((bf16[512,1024]{1,0:T(8,128)(2,1)}, bf16[512,1024]{1,0:T(8,128)(2,1)}, u32[]{:S(2)}, u32[]{:S(2)}) %collective-permute-start.64) | collective-permute-done | bytes 1048608 | tf_op jit(solution)/shard_map/ppermute | solution.py:645
  865.1 15.7 %collective-permute-done.58 = bf16[512,1024]{1,0:T(8,128)(2,1)S(1)} collective-permute-done((bf16[512,1024]{1,0:T(8,128)(2,1)S(1)}, bf16[512,1024]{1,0:T(8,128)(2,1)S(1)}, u32[]{:S(2)}, u32[]{:S(2)}) %collective-permute-start.58) | collective-permute-done | bytes 1048608 | tf_op jit(solution)/shard_map/ppermute | solution.py:645
  881.7 11.0 %collective-permute-done.61 = bf16[512,1024]{1,0:T(8,128)(2,1)S(1)} collective-permute-done((bf16[512,1024]{1,0:T(8,128)(2,1)S(1)}, bf16[512,1024]{1,0:T(8,128)(2,1)S(1)}, u32[]{:S(2)}, u32[]{:S(2)}) %collective-permute-start.61) | collective-permute-done | bytes 1048608 | tf_op jit(solution)/shard_map/ppermute | solution.py:645
  896.8 18.4 %collective-permute-done.71 = bf16[256,2048]{1,0:T(8,128)(2,1)S(1)} collective-permute-done((bf16[256,2048]{1,0:T(8,128)(2,1)S(1)}, bf16[256,2048]{1,0:T(8,128)(2,1)S(1)}, u32[]{:S(2)}, u32[]{:S(2)}) %collective-permute-start.71) | collective-permute-done | bytes 1048608 | tf_op jit(solution)/shard_map/ppermute | solution.py:645
  919.6 9.7 collective-permute-done.63
  929.8 30.3 %collective-permute-done.65 = bf16[512,1024]{1,0:T(8,128)(2,1)S(1)} collective-permute-done((bf16[512,1024]{1,0:T(8,128)(2,1)S(1)}, bf16[512,1024]{1,0:T(8,128)(2,1)S(1)}, u32[]{:S(2)}, u32[]{:S(2)}) %collective-permute-start.65) | collective-permute-done | bytes 1048608 | tf_op jit(solution)/shard_map/ppermute | solution.py:645
  968.0 6.3 collective-permute-done.57
  974.3 25.0 %collective-permute-done.59 = bf16[512,1024]{1,0:T(8,128)(2,1)S(1)} collective-permute-done((bf16[512,1024]{1,0:T(8,128)(2,1)S(1)}, bf16[512,1024]{1,0:T(8,128)(2,1)S(1)}, u32[]{:S(2)}, u32[]{:S(2)}) %collective-permute-start.59) | collective-permute-done | bytes 1048608 | tf_op jit(solution)/shard_map/ppermute | solution.py:645
  1008.4 4.6 fusion.69
  1029.0 6.3 collective-permute-done.46
  1048.8 6.5 all-to-all-start.1
  (555 shorter events, 325.5 us)
Async XLA Ops:
  7.2 70.4 %all-gather.8.cloned.1.call-start = ((), (), s32[]{:S(2)}) async-start(), calls=%async_computation.7 | async-start | bytes 4718592 | tf_op jit(solution)/shard_map/all_gather | solution.py:766
  24.1 96.3 %all-gather.16.cloned.1.call-start = ((), (), s32[]{:S(2)}) async-start(), calls=%async_computation.16 | async-start | bytes 4718592 | tf_op jit(solution)/shard_map/all_gather | solution.py:771
  25.2 178.2 %all-gather.10.cloned.1.call-start = ((), (), s32[]{:S(2)}) async-start(), calls=%async_computation.8 | async-start | bytes 9437184 | tf_op jit(solution)/shard_map/all_gather | solution.py:835
  48.7 24.3 %collective-permute-start.1 = (bf16[128,2048]{1,0:T(8,128)(2,1)S(1)}, bf16[128,2048]{1,0:T(8,128)(2,1)S(1)}, u32[]{:S(2)}, u32[]{:S(2)}) collective-permute-start(bf16[128,2048]{1,0:T(8,128)(2,1)S(1)} %copy-done.9), channel_id=1, source_target_pairs={{0,16},{8,24},{16,0},{24,8},{1,17},{9,25},{17,1},{25,9},{2,18},{10... | collective-permute-start | bytes 1572872 | tf_op jit(solution)/shard_map/ppermute | solution.py:645
  98.1 386.1 %all-gather.14.cloned.1.call-start = ((), (), s32[]{:S(2)}) async-start(), calls=%async_computation.10 | async-start | bytes 4718592 | tf_op jit(solution)/shard_map/all_gather | solution.py:776
  98.7 392.5 %all-gather.12.cloned.1.call-start = ((), (), s32[]{:S(2)}) async-start(), calls=%async_computation.9 | async-start | bytes 4718592 | tf_op jit(solution)/shard_map/all_gather | solution.py:844
  219.0 25.0 %collective-permute-start.16 = (bf16[128,2048]{1,0:T(8,128)(2,1)S(1)}, bf16[128,2048]{1,0:T(8,128)(2,1)S(1)}, u32[]{:S(2)}, u32[]{:S(2)}) collective-permute-start(bf16[128,2048]{1,0:T(8,128)(2,1)S(1)} %get-tuple-element.221), channel_id=1, source_target_pairs={{0,16},{8,24},{16,0},{24,8},{1,17},{9,25},{17,1},{25,9},{2,18},{10... | collective-permute-start | bytes 1572872 | tf_op jit(solution)/shard_map/ppermute | solution.py:645
  220.5 23.6 %collective-permute-start.17 = (bf16[128,2048]{1,0:T(8,128)(2,1)S(1)}, bf16[128,2048]{1,0:T(8,128)(2,1)S(1)}, u32[]{:S(2)}, u32[]{:S(2)}) collective-permute-start(bf16[128,2048]{1,0:T(8,128)(2,1)S(1)} %get-tuple-element.220), channel_id=1, source_target_pairs={{0,24},{8,16},{16,8},{24,0},{1,25},{9,17},{17,9},{25,1},{2,26},{10... | collective-permute-start | bytes 1572872 | tf_op jit(solution)/shard_map/ppermute | solution.py:645
  245.8 369.7 %reduce-scatter.8.cloned.1.call-start = ((), (), s32[]{:S(2)}) async-start(), calls=%async_computation.12 | async-start | bytes 4718592 | tf_op jit(solution)/shard_map/reduce_scatter | solution.py:916
  247.7 26.2 %collective-permute-start.18 = (bf16[512,1024]{1,0:T(8,128)(2,1)S(1)}, bf16[512,1024]{1,0:T(8,128)(2,1)}, u32[]{:S(2)}, u32[]{:S(2)}) collective-permute-start(bf16[512,1024]{1,0:T(8,128)(2,1)S(1)} %get-tuple-element.218), channel_id=1, source_target_pairs={{0,8},{8,0},{16,24},{24,16},{1,9},{9,1},{17,25},{25,17},{2,10},{10... | collective-permute-start | bytes 3145736 | tf_op jit(solution)/shard_map/ppermute | solution.py:645
  249.0 26.4 %collective-permute-start.19 = (bf16[512,1024]{1,0:T(8,128)(2,1)S(1)}, bf16[512,1024]{1,0:T(8,128)(2,1)S(1)}, u32[]{:S(2)}, u32[]{:S(2)}) collective-permute-start(bf16[512,1024]{1,0:T(8,128)(2,1)S(1)} %get-tuple-element.218), channel_id=1, source_target_pairs={{0,16},{8,24},{16,0},{24,8},{1,17},{9,25},{17,1},{25,9},{2,18},{10... | collective-permute-start | bytes 3145736 | tf_op jit(solution)/shard_map/ppermute | solution.py:645
  251.0 45.3 %collective-permute-start.21 = (bf16[512,1024]{1,0:T(8,128)(2,1)S(1)}, bf16[512,1024]{1,0:T(8,128)(2,1)S(1)}, u32[]{:S(2)}, u32[]{:S(2)}) collective-permute-start(bf16[512,1024]{1,0:T(8,128)(2,1)S(1)} %get-tuple-element.216), channel_id=1, source_target_pairs={{0,8},{8,0},{16,24},{24,16},{1,9},{9,1},{17,25},{25,17},{2,10},{10... | collective-permute-start | bytes 3145736 | tf_op jit(solution)/shard_map/ppermute | solution.py:645
  252.5 45.0 %collective-permute-start.22 = (bf16[512,1024]{1,0:T(8,128)(2,1)S(1)}, bf16[512,1024]{1,0:T(8,128)(2,1)S(1)}, u32[]{:S(2)}, u32[]{:S(2)}) collective-permute-start(bf16[512,1024]{1,0:T(8,128)(2,1)S(1)} %get-tuple-element.216), channel_id=1, source_target_pairs={{0,16},{8,24},{16,0},{24,8},{1,17},{9,25},{17,1},{25,9},{2,18},{10... | collective-permute-start | bytes 3145736 | tf_op jit(solution)/shard_map/ppermute | solution.py:645
  254.5 64.4 %collective-permute-start.24 = (bf16[256,2048]{1,0:T(8,128)(2,1)}, bf16[256,2048]{1,0:T(8,128)(2,1)}, u32[]{:S(2)}, u32[]{:S(2)}) collective-permute-start(bf16[256,2048]{1,0:T(8,128)(2,1)} %get-tuple-element.214), channel_id=1, source_target_pairs={{0,8},{8,0},{16,24},{24,16},{1,9},{9,1},{17,25},{25,17},{2,10},{10... | collective-permute-start | bytes 3145736 | tf_op jit(solution)/shard_map/ppermute | solution.py:645
  273.9 46.4 %collective-permute-start.25 = (bf16[256,2048]{1,0:T(8,128)(2,1)}, bf16[256,2048]{1,0:T(8,128)(2,1)}, u32[]{:S(2)}, u32[]{:S(2)}) collective-permute-start(bf16[256,2048]{1,0:T(8,128)(2,1)} %get-tuple-element.214), channel_id=1, source_target_pairs={{0,16},{8,24},{16,0},{24,8},{1,17},{9,25},{17,1},{25,9},{2,18},{10... | collective-permute-start | bytes 3145736 | tf_op jit(solution)/shard_map/ppermute | solution.py:645
  275.4 67.1 %collective-permute-start.28 = (bf16[512,1024]{1,0:T(8,128)(2,1)S(1)}, bf16[512,1024]{1,0:T(8,128)(2,1)}, u32[]{:S(2)}, u32[]{:S(2)}) collective-permute-start(bf16[512,1024]{1,0:T(8,128)(2,1)S(1)} %get-tuple-element.217), channel_id=1, source_target_pairs={{0,16},{8,24},{16,0},{24,8},{1,17},{9,25},{17,1},{25,9},{2,18},{10... | collective-permute-start | bytes 3145736 | tf_op jit(solution)/shard_map/ppermute | solution.py:645
  296.3 47.1 %collective-permute-start.27 = (bf16[512,1024]{1,0:T(8,128)(2,1)S(1)}, bf16[512,1024]{1,0:T(8,128)(2,1)}, u32[]{:S(2)}, u32[]{:S(2)}) collective-permute-start(bf16[512,1024]{1,0:T(8,128)(2,1)S(1)} %get-tuple-element.217), channel_id=1, source_target_pairs={{0,8},{8,0},{16,24},{24,16},{1,9},{9,1},{17,25},{25,17},{2,10},{10... | collective-permute-start | bytes 3145736 | tf_op jit(solution)/shard_map/ppermute | solution.py:645
  298.5 66.5 %collective-permute-start.20 = (bf16[512,1024]{1,0:T(8,128)(2,1)}, bf16[512,1024]{1,0:T(8,128)(2,1)}, u32[]{:S(2)}, u32[]{:S(2)}) collective-permute-start(bf16[512,1024]{1,0:T(8,128)(2,1)} %collective-permute-done.18), channel_id=1, source_target_pairs={{0,16},{8,24},{16,0},{24,8},{1,17},{9,25},{17,1},{25,9},{2,18},{10... | collective-permute-start | bytes 3145736 | tf_op jit(solution)/shard_map/ppermute | solution.py:645
  318.9 68.6 %collective-permute-start.31 = (bf16[512,1024]{1,0:T(8,128)(2,1)}, bf16[512,1024]{1,0:T(8,128)(2,1)}, u32[]{:S(2)}, u32[]{:S(2)}) collective-permute-start(bf16[512,1024]{1,0:T(8,128)(2,1)} %get-tuple-element.215), channel_id=1, source_target_pairs={{0,16},{8,24},{16,0},{24,8},{1,17},{9,25},{17,1},{25,9},{2,18},{10... | collective-permute-start | bytes 3145736 | tf_op jit(solution)/shard_map/ppermute | solution.py:645
  320.4 89.6 %collective-permute-start.23 = (bf16[512,1024]{1,0:T(8,128)(2,1)}, bf16[512,1024]{1,0:T(8,128)(2,1)}, u32[]{:S(2)}, u32[]{:S(2)}) collective-permute-start(bf16[512,1024]{1,0:T(8,128)(2,1)} %copy-done.39), channel_id=1, source_target_pairs={{0,16},{8,24},{16,0},{24,8},{1,17},{9,25},{17,1},{25,9},{2,18},{10... | collective-permute-start | bytes 3145736 | tf_op jit(solution)/shard_map/ppermute | solution.py:645
  342.5 89.9 %collective-permute-start.34 = (bf16[256,2048]{1,0:T(8,128)(2,1)}, bf16[256,2048]{1,0:T(8,128)(2,1)}, u32[]{:S(2)}, u32[]{:S(2)}) collective-permute-start(bf16[256,2048]{1,0:T(8,128)(2,1)} %get-tuple-element.213), channel_id=1, source_target_pairs={{0,16},{8,24},{16,0},{24,8},{1,17},{9,25},{17,1},{25,9},{2,18},{10... | collective-permute-start | bytes 3145736 | tf_op jit(solution)/shard_map/ppermute | solution.py:645
  343.4 109.8 %collective-permute-start.26 = (bf16[256,2048]{1,0:T(8,128)(2,1)}, bf16[256,2048]{1,0:T(8,128)(2,1)}, u32[]{:S(2)}, u32[]{:S(2)}) collective-permute-start(bf16[256,2048]{1,0:T(8,128)(2,1)} %collective-permute-done.24), channel_id=1, source_target_pairs={{0,16},{8,24},{16,0},{24,8},{1,17},{9,25},{17,1},{25,9},{2,18},{10... | collective-permute-start | bytes 3145736 | tf_op jit(solution)/shard_map/ppermute | solution.py:645
  365.0 92.4 %collective-permute-start.29 = (bf16[512,1024]{1,0:T(8,128)(2,1)}, bf16[512,1024]{1,0:T(8,128)(2,1)S(1)}, u32[]{:S(2)}, u32[]{:S(2)}) collective-permute-start(bf16[512,1024]{1,0:T(8,128)(2,1)} %collective-permute-done.28), channel_id=1, source_target_pairs={{0,8},{8,0},{16,24},{24,16},{1,9},{9,1},{17,25},{25,17},{2,10},{10... | collective-permute-start | bytes 3145736 | tf_op jit(solution)/shard_map/ppermute | solution.py:645
  387.5 73.4 %collective-permute-start.30 = (bf16[512,1024]{1,0:T(8,128)(2,1)S(1)}, bf16[512,1024]{1,0:T(8,128)(2,1)S(1)}, u32[]{:S(2)}, u32[]{:S(2)}) collective-permute-start(bf16[512,1024]{1,0:T(8,128)(2,1)S(1)} %copy-done.15), channel_id=1, source_target_pairs={{0,8},{8,0},{16,24},{24,16},{1,9},{9,1},{17,25},{25,17},{2,10},{10... | collective-permute-start | bytes 3145736 | tf_op jit(solution)/shard_map/ppermute | solution.py:645
  409.9 50.9 %collective-permute-start.32 = (bf16[512,1024]{1,0:T(8,128)(2,1)}, bf16[512,1024]{1,0:T(8,128)(2,1)S(1)}, u32[]{:S(2)}, u32[]{:S(2)}) collective-permute-start(bf16[512,1024]{1,0:T(8,128)(2,1)} %collective-permute-done.31), channel_id=1, source_target_pairs={{0,8},{8,0},{16,24},{24,16},{1,9},{9,1},{17,25},{25,17},{2,10},{10... | collective-permute-start | bytes 3145736 | tf_op jit(solution)/shard_map/ppermute | solution.py:645
  432.4 37.4 %collective-permute-start.33 = (bf16[256,2048]{1,0:T(8,128)(2,1)S(1)}, bf16[256,2048]{1,0:T(8,128)(2,1)S(1)}, u32[]{:S(2)}, u32[]{:S(2)}) collective-permute-start(bf16[256,2048]{1,0:T(8,128)(2,1)S(1)} %copy-done.16), channel_id=1, source_target_pairs={{0,8},{8,0},{16,24},{24,16},{1,9},{9,1},{17,25},{25,17},{2,10},{10... | collective-permute-start | bytes 3145736 | tf_op jit(solution)/shard_map/ppermute | solution.py:645
  453.1 23.6 %collective-permute-start.35 = (bf16[256,2048]{1,0:T(8,128)(2,1)}, bf16[256,2048]{1,0:T(8,128)(2,1)S(1)}, u32[]{:S(2)}, u32[]{:S(2)}) collective-permute-start(bf16[256,2048]{1,0:T(8,128)(2,1)} %collective-permute-done.34), channel_id=1, source_target_pairs={{0,8},{8,0},{16,24},{24,16},{1,9},{9,1},{17,25},{25,17},{2,10},{10... | collective-permute-start | bytes 3145736 | tf_op jit(solution)/shard_map/ppermute | solution.py:645
  573.0 188.7 %reduce-scatter.10.cloned.1.call-start = ((), (), s32[]{:S(2)}) async-start(), calls=%async_computation.13 | async-start | bytes 9437184 | tf_op jit(solution)/shard_map/reduce_scatter | solution.py:979
  664.8 338.2 %reduce-scatter.12.cloned.1.call-start = ((), (), s32[]{:S(2)}) async-start(), calls=%async_computation.14 | async-start | bytes 4718592 | tf_op jit(solution)/shard_map/reduce_scatter | solution.py:993
  693.6 361.8 %reduce-scatter.14.cloned.1.call-start = ((), (), s32[]{:S(2)}) async-start(), calls=%async_computation.15 | async-start | bytes 4718592 | tf_op jit(solution)/shard_map/reduce_scatter | solution.py:1003
  782.3 278.4 %reduce-scatter.6.cloned.1.call-start = ((), (), s32[]{:S(2)}) async-start(), calls=%async_computation.11 | async-start | bytes 4718592 | tf_op jit(solution)/shard_map/reduce_scatter | solution.py:922
  789.0 105.7 %collective-permute-start.69 = (bf16[256,2048]{1,0:T(8,128)(2,1)}, bf16[256,2048]{1,0:T(8,128)(2,1)}, u32[]{:S(2)}, u32[]{:S(2)}) collective-permute-start(bf16[256,2048]{1,0:T(8,128)(2,1)} %convolution_convert_fusion.10), channel_id=1, source_target_pairs={{0,8},{8,0},{16,24},{24,16},{1,9},{9,1},{17,25},{25,17},{2,10},{10... | collective-permute-start | bytes 3145736 | tf_op jit(solution)/shard_map/ppermute | solution.py:645
  793.6 50.4 %collective-permute-start.70 = (bf16[256,2048]{1,0:T(8,128)(2,1)}, bf16[256,2048]{1,0:T(8,128)(2,1)}, u32[]{:S(2)}, u32[]{:S(2)}) collective-permute-start(bf16[256,2048]{1,0:T(8,128)(2,1)} %convolution_convert_fusion.8), channel_id=1, source_target_pairs={{0,8},{8,0},{16,24},{24,16},{1,9},{9,1},{17,25},{25,17},{2,10},{10... | collective-permute-start | bytes 3145736 | tf_op jit(solution)/shard_map/ppermute | solution.py:645
  797.1 64.8 %collective-permute-start.73 = (bf16[256,2048]{1,0:T(8,128)(2,1)}, bf16[256,2048]{1,0:T(8,128)(2,1)}, u32[]{:S(2)}, u32[]{:S(2)}) collective-permute-start(bf16[256,2048]{1,0:T(8,128)(2,1)} %convolution_convert_fusion.4), channel_id=1, source_target_pairs={{0,16},{8,24},{16,0},{24,8},{1,17},{9,25},{17,1},{25,9},{2,18},{10... | collective-permute-start | bytes 3145736 | tf_op jit(solution)/shard_map/ppermute | solution.py:645
  804.7 52.8 %collective-permute-start.64 = (bf16[512,1024]{1,0:T(8,128)(2,1)}, bf16[512,1024]{1,0:T(8,128)(2,1)}, u32[]{:S(2)}, u32[]{:S(2)}) collective-permute-start(bf16[512,1024]{1,0:T(8,128)(2,1)} %convolution_convert_fusion.16), channel_id=1, source_target_pairs={{0,8},{8,0},{16,24},{24,16},{1,9},{9,1},{17,25},{25,17},{2,10},{10... | collective-permute-start | bytes 3145736 | tf_op jit(solution)/shard_map/ppermute | solution.py:645
  813.8 45.8 %collective-permute-start.67 = (bf16[512,1024]{1,0:T(8,128)(2,1)}, bf16[512,1024]{1,0:T(8,128)(2,1)}, u32[]{:S(2)}, u32[]{:S(2)}) collective-permute-start(bf16[512,1024]{1,0:T(8,128)(2,1)} %convolution_convert_fusion.12), channel_id=1, source_target_pairs={{0,16},{8,24},{16,0},{24,8},{1,17},{9,25},{17,1},{25,9},{2,18},{10... | collective-permute-start | bytes 3145736 | tf_op jit(solution)/shard_map/ppermute | solution.py:645
  844.0 51.2 %collective-permute-start.72 = (bf16[256,2048]{1,0:T(8,128)(2,1)}, bf16[256,2048]{1,0:T(8,128)(2,1)S(1)}, u32[]{:S(2)}, u32[]{:S(2)}) collective-permute-start(bf16[256,2048]{1,0:T(8,128)(2,1)} %convolution_convert_fusion.6), channel_id=1, source_target_pairs={{0,16},{8,24},{16,0},{24,8},{1,17},{9,25},{17,1},{25,9},{2,18},{10... | collective-permute-start | bytes 3145736 | tf_op jit(solution)/shard_map/ppermute | solution.py:645
  859.7 33.1 %collective-permute-start.61 = (bf16[512,1024]{1,0:T(8,128)(2,1)S(1)}, bf16[512,1024]{1,0:T(8,128)(2,1)S(1)}, u32[]{:S(2)}, u32[]{:S(2)}) collective-permute-start(bf16[512,1024]{1,0:T(8,128)(2,1)S(1)} %copy-done.93), channel_id=1, source_target_pairs={{0,16},{8,24},{16,0},{24,8},{1,17},{9,25},{17,1},{25,9},{2,18},{10... | collective-permute-start | bytes 3145736 | tf_op jit(solution)/shard_map/ppermute | solution.py:645
  861.9 53.3 %collective-permute-start.71 = (bf16[256,2048]{1,0:T(8,128)(2,1)S(1)}, bf16[256,2048]{1,0:T(8,128)(2,1)S(1)}, u32[]{:S(2)}, u32[]{:S(2)}) collective-permute-start(bf16[256,2048]{1,0:T(8,128)(2,1)S(1)} %add_convert_fusion.2), channel_id=1, source_target_pairs={{0,16},{8,24},{16,0},{24,8},{1,17},{9,25},{17,1},{25,9},{2,18},{10... | collective-permute-start | bytes 3145736 | tf_op jit(solution)/shard_map/ppermute | solution.py:645
  880.8 37.7 %collective-permute-start.74 = (bf16[256,2048]{1,0:T(8,128)(2,1)S(1)}, bf16[256,2048]{1,0:T(8,128)(2,1)S(1)}, u32[]{:S(2)}, u32[]{:S(2)}) collective-permute-start(bf16[256,2048]{1,0:T(8,128)(2,1)S(1)} %add_convert_fusion.1), channel_id=1, source_target_pairs={{0,8},{8,0},{16,24},{24,16},{1,9},{9,1},{17,25},{25,17},{2,10},{10... | collective-permute-start | bytes 3145736 | tf_op jit(solution)/shard_map/ppermute | solution.py:645
  892.8 36.6 %collective-permute-start.63 = (bf16[512,1024]{1,0:T(8,128)(2,1)S(1)}, bf16[512,1024]{1,0:T(8,128)(2,1)S(1)}, u32[]{:S(2)}, u32[]{:S(2)}) collective-permute-start(bf16[512,1024]{1,0:T(8,128)(2,1)S(1)} %copy-done.92), channel_id=1, source_target_pairs={{0,8},{8,0},{16,24},{24,16},{1,9},{9,1},{17,25},{25,17},{2,10},{10... | collective-permute-start | bytes 3145736 | tf_op jit(solution)/shard_map/ppermute | solution.py:645
  894.7 66.5 %collective-permute-start.66 = (bf16[512,1024]{1,0:T(8,128)(2,1)S(1)}, bf16[512,1024]{1,0:T(8,128)(2,1)S(1)}, u32[]{:S(2)}, u32[]{:S(2)}) collective-permute-start(bf16[512,1024]{1,0:T(8,128)(2,1)S(1)} %copy-done.91), channel_id=1, source_target_pairs={{0,16},{8,24},{16,0},{24,8},{1,17},{9,25},{17,1},{25,9},{2,18},{10... | collective-permute-start | bytes 3145736 | tf_op jit(solution)/shard_map/ppermute | solution.py:645
  895.2 64.9 %collective-permute-start.65 = (bf16[512,1024]{1,0:T(8,128)(2,1)S(1)}, bf16[512,1024]{1,0:T(8,128)(2,1)S(1)}, u32[]{:S(2)}, u32[]{:S(2)}) collective-permute-start(bf16[512,1024]{1,0:T(8,128)(2,1)S(1)} %add_convert_fusion.4), channel_id=1, source_target_pairs={{0,16},{8,24},{16,0},{24,8},{1,17},{9,25},{17,1},{25,9},{2,18},{10... | collective-permute-start | bytes 3145736 | tf_op jit(solution)/shard_map/ppermute | solution.py:645
  915.2 47.6 %collective-permute-start.68 = (bf16[512,1024]{1,0:T(8,128)(2,1)S(1)}, bf16[512,1024]{1,0:T(8,128)(2,1)S(1)}, u32[]{:S(2)}, u32[]{:S(2)}) collective-permute-start(bf16[512,1024]{1,0:T(8,128)(2,1)S(1)} %add_convert_fusion.3), channel_id=1, source_target_pairs={{0,8},{8,0},{16,24},{24,16},{1,9},{9,1},{17,25},{25,17},{2,10},{10... | collective-permute-start | bytes 3145736 | tf_op jit(solution)/shard_map/ppermute | solution.py:645
  918.5 55.8 %collective-permute-start.57 = (bf16[512,1024]{1,0:T(8,128)(2,1)S(1)}, bf16[512,1024]{1,0:T(8,128)(2,1)S(1)}, u32[]{:S(2)}, u32[]{:S(2)}) collective-permute-start(bf16[512,1024]{1,0:T(8,128)(2,1)S(1)} %copy-done.90), channel_id=1, source_target_pairs={{0,8},{8,0},{16,24},{24,16},{1,9},{9,1},{17,25},{25,17},{2,10},{10... | collective-permute-start | bytes 3145736 | tf_op jit(solution)/shard_map/ppermute | solution.py:645
  929.3 71.8 %collective-permute-start.60 = (bf16[512,1024]{1,0:T(8,128)(2,1)S(1)}, bf16[512,1024]{1,0:T(8,128)(2,1)S(1)}, u32[]{:S(2)}, u32[]{:S(2)}) collective-permute-start(bf16[512,1024]{1,0:T(8,128)(2,1)S(1)} %copy-done.89), channel_id=1, source_target_pairs={{0,16},{8,24},{16,0},{24,8},{1,17},{9,25},{17,1},{25,9},{2,18},{10... | collective-permute-start | bytes 3145736 | tf_op jit(solution)/shard_map/ppermute | solution.py:645
  960.2 39.1 %collective-permute-start.59 = (bf16[512,1024]{1,0:T(8,128)(2,1)S(1)}, bf16[512,1024]{1,0:T(8,128)(2,1)S(1)}, u32[]{:S(2)}, u32[]{:S(2)}) collective-permute-start(bf16[512,1024]{1,0:T(8,128)(2,1)S(1)} %add_convert_fusion.6), channel_id=1, source_target_pairs={{0,16},{8,24},{16,0},{24,8},{1,17},{9,25},{17,1},{25,9},{2,18},{10... | collective-permute-start | bytes 3145736 | tf_op jit(solution)/shard_map/ppermute | solution.py:645
  961.3 39.9 %collective-permute-start.62 = (bf16[512,1024]{1,0:T(8,128)(2,1)S(1)}, bf16[512,1024]{1,0:T(8,128)(2,1)S(1)}, u32[]{:S(2)}, u32[]{:S(2)}) collective-permute-start(bf16[512,1024]{1,0:T(8,128)(2,1)S(1)} %add_convert_fusion.5), channel_id=1, source_target_pairs={{0,8},{8,0},{16,24},{24,16},{1,9},{9,1},{17,25},{25,17},{2,10},{10... | collective-permute-start | bytes 3145736 | tf_op jit(solution)/shard_map/ppermute | solution.py:645
  (142 other events, 2970.1 us)
Sparse Core Ops, SparseCore 0:
  24.2 47.8 all-gather.7
  74.3 46.0 all-gather.15
  122.6 80.8 all-gather.9
  204.9 45.3 all-gather.13
  252.3 45.6 all-gather.11
  564.5 50.9 reduce-scatter.7
  665.0 96.6 reduce-scatter.9
  764.0 48.3 reduce-scatter.11
  814.7 48.3 reduce-scatter.13
  865.2 48.3 reduce-scatter.5

commit v7 on v6

--- a/solution.py
+++ b/solution.py
@@ -950,7 +950,7 @@
             [
                 scatter_pieces(pieces_of(store[left], store[right]), item)
                 for item, store in enumerate(stores)
-            ]
+            ],
         )
         for left, right in ((2, 1), (0, 3), (0, 4))
     )
@@ -1010,8 +1010,8 @@
     own_factor = rms_factor(jnp.sum(own_tokens * own_tokens, axis=-1, keepdims=True), width)
     scaled = normed_grad * mixing_scale
     inner = jnp.mean(scaled * own_tokens, axis=-1, keepdims=True)
+    mixing_sum = jnp.sum(normed_grad * own_tokens * own_factor, axis=0)
     tokens_grad = middle_grad + own_factor * scaled - own_tokens * (own_factor**3 * inner)
-    mixing_sum = jnp.sum(normed_grad * own_tokens * own_factor, axis=0)
 
     def turned_back(array):
         return jnp.stack(
@@ -1042,7 +1042,8 @@
         ],
         axis=1,
     ).reshape(heads_axis, -1)
-    lines = add_all(head_turn(xor_order(lines, 0)))
+    lines = xor_order(lines, 0)
+    lines = add_all(head_turn(lines))
     lines = lax.all_to_all(lines.reshape(blocks, -1), "blk", 0, 0, tiled=True)
     lines = jnp.sum(lines, axis=0).reshape(part, 4 + experts)
     return (

time: 1090 us -> 1090 us (level)
  no operation moved by 1% of the time
where the time goes in v7:
time: 1090 us; the launch traced here: 1080 us
  waiting for transfers between devices  572 us (52%)
  Pallas kernels  144 us (13%)
  starting transfers between devices  93.9 us (9%)
  other arithmetic  86.2 us (8%)
  matrix products  77.6 us (7%)
  local copies, waits for them, and re-layouts  73.4 us (7%)
  between operations  16.1 us (1%)
  blocking collectives  14.8 us (1%)
    ppermute x75, waiting for transfers between devices, exchange(): lax.ppermute(array, 'head', [(at, at ^ offset) for at in range(count)])  384 us
    ppermute x75, starting transfers between devices, exchange(): lax.ppermute(array, 'head', [(at, at ^ offset) for at in range(count)])  81 us
    reduce_scatter x1, waiting for transfers between devices, layer(): lax.psum_scatter(pairs_back, 'blk', scatter_dimension=0, tiled=True)  68 us
    all_gather x1, waiting for transfers between devices, layer(): pairs_all = lax.all_gather(pairs, 'blk', axis=0, tiled=True)  63.6 us
    pallas_call x2, Pallas kernels, run_expert(): pl.pallas_call(expert_kernel, grid_spec=pltpu.PrefetchScalarGridSpec(num_...  56.9 us
    dot_general x24, matrix products, pieces_of(): jnp.dot(left[:, offset * size:(offset + 1) * size].T, right, preferred_el...  47.3 us
    reduce_scatter x1, waiting for transfers between devices, layer(): lax.psum_scatter(incoming.reshape(blocks * rows, width), 'blk', scatter_d...  36.6 us
    concatenate x6, other arithmetic, layer(): jnp.concatenate(pieces, axis=0)  30.9 us
  transfers between devices with their start and end apart: 87, of which 39 were waited for; matrix products, arithmetic and copies ran while one was open for 20% of the time, Pallas kernels for 5%

profile of v7, /device:TPU:0, one launch (start us, length us, event | category | flops | bytes accessed | tf_op | source)
XLA Modules:
  0.0 1078.2 jit_solution(11207012566988222061)
XLA Ops:
  14.1 5.0 collective-permute-done.6
  28.8 14.8 %all-gather.1 = bf16[8,1,3328]{2,1,0:T(2,128)(2,1)S(1)} all-gather(bf16[1,1,3328]{2,1,0:T(2,128)(2,1)S(1)} %maximum_bitcast_fusion), channel_id=1, replica_groups=mesh['head'=4,'blk'=8] {'blk'}, dimensions={0}, use_global_device_ids=true | all-gather | bytes 59904 | tf_op jit(solution)/shard_map/all_gather | solution.py:790
  57.5 4.5 collective-permute-done.refs_1_
  62.0 11.0 %collective-permute-done.1.refs_2_ = bf16[128,2048]{1,0:T(8,128)(2,1)S(1)} collective-permute-done((bf16[128,2048]{1,0:T(8,128)(2,1)S(1)}, bf16[128,2048]{1,0:T(8,128)(2,1)S(1)}, u32[]{:S(2)}, u32[]{:S(2)}) %collective-permute-start.1) | collective-permute-done | bytes 524320 | tf_op jit(solution)/shard_map/ppermute | solution.py:645
  77.6 4.9 copy.119
  82.5 4.6 shard_map.292
  106.7 13.7 %all-gather.16.cloned.1.call-done = bf16[4096,512]{1,0:T(8,128)(2,1)} async-done(((bf16[512,512]{1,0:T(8,128)(2,1)}), bf16[4096,512]{1,0:T(8,128)(2,1)}) %all-gather.16.cloned.1.call-update) | async-done | bytes 4194320 | tf_op jit(solution)/shard_map/all_gather | solution.py:771
  139.9 63.6 %all-gather.10.cloned.1.call-done.pairs = bf16[4096,1024]{1,0:T(8,128)(2,1)} async-done(((bf16[512,1024]{1,0:T(8,128)(2,1)}), bf16[4096,1024]{1,0:T(8,128)(2,1)}) %all-gather.10.cloned.1.call-update) | async-done | bytes 8388624 | tf_op jit(solution)/shard_map/all_gather | solution.py:835
  203.4 11.5 %attend_forward.1 = (f32[512,512]{1,0:T(8,128)}, bf16[512,512]{1,0:T(8,128)(2,1)}, f32[512,512]{1,0:T(8,128)}) custom-call(s32[2,16]{1,0:T(2,128)} %select_reduce_fusion.2.listed, s32[2]{0:T(128)} %get-tuple-element.206.counts, bf16[512,512]{1,0:T(8,128)(2,1)} %get-tuple-element.61.query, bf16[4096,1024]{1,0:T(8,128)(2,1)} %all-gather.10.cloned.1.call-done.pairs, ...), custom_call_target="tpu_custom_call" | custom-call | tf_op jit(solution)/shard_map/attend_forward/pallas_call | solution.py:299
  221.0 11.3 %collective-permute-done.15 = bf16[128,2048]{1,0:T(8,128)(2,1)S(1)} collective-permute-done((bf16[128,2048]{1,0:T(8,128)(2,1)S(1)}, bf16[128,2048]{1,0:T(8,128)(2,1)S(1)}, u32[]{:S(2)}, u32[]{:S(2)}) %collective-permute-start.15) | collective-permute-done | bytes 524320 | tf_op jit(solution)/shard_map/ppermute | solution.py:645
  232.3 11.7 %collective-permute-done.16 = bf16[128,2048]{1,0:T(8,128)(2,1)S(1)} collective-permute-done((bf16[128,2048]{1,0:T(8,128)(2,1)S(1)}, bf16[128,2048]{1,0:T(8,128)(2,1)S(1)}, u32[]{:S(2)}, u32[]{:S(2)}) %collective-permute-start.16) | collective-permute-done | bytes 524320 | tf_op jit(solution)/shard_map/ppermute | solution.py:645
  255.7 18.3 %collective-permute-done.18 = bf16[512,1024]{1,0:T(8,128)(2,1)} collective-permute-done((bf16[512,1024]{1,0:T(8,128)(2,1)S(1)}, bf16[512,1024]{1,0:T(8,128)(2,1)}, u32[]{:S(2)}, u32[]{:S(2)}) %collective-permute-start.18) | collective-permute-done | bytes 1048608 | tf_op jit(solution)/shard_map/ppermute | solution.py:645
  276.0 20.3 %collective-permute-done.21 = bf16[512,1024]{1,0:T(8,128)(2,1)S(1)} collective-permute-done((bf16[512,1024]{1,0:T(8,128)(2,1)S(1)}, bf16[512,1024]{1,0:T(8,128)(2,1)S(1)}, u32[]{:S(2)}, u32[]{:S(2)}) %collective-permute-start.21) | collective-permute-done | bytes 1048608 | tf_op jit(solution)/shard_map/ppermute | solution.py:645
  299.7 19.1 %collective-permute-done.24 = bf16[256,2048]{1,0:T(8,128)(2,1)} collective-permute-done((bf16[256,2048]{1,0:T(8,128)(2,1)}, bf16[256,2048]{1,0:T(8,128)(2,1)}, u32[]{:S(2)}, u32[]{:S(2)}) %collective-permute-start.24) | collective-permute-done | bytes 1048608 | tf_op jit(solution)/shard_map/ppermute | solution.py:645
  321.9 20.6 %collective-permute-done.28 = bf16[512,1024]{1,0:T(8,128)(2,1)} collective-permute-done((bf16[512,1024]{1,0:T(8,128)(2,1)S(1)}, bf16[512,1024]{1,0:T(8,128)(2,1)}, u32[]{:S(2)}, u32[]{:S(2)}) %collective-permute-start.28) | collective-permute-done | bytes 1048608 | tf_op jit(solution)/shard_map/ppermute | solution.py:645
  352.3 12.7 %collective-permute-done.20 = bf16[512,1024]{1,0:T(8,128)(2,1)} collective-permute-done((bf16[512,1024]{1,0:T(8,128)(2,1)}, bf16[512,1024]{1,0:T(8,128)(2,1)}, u32[]{:S(2)}, u32[]{:S(2)}) %collective-permute-start.20) | collective-permute-done | bytes 1048608 | tf_op jit(solution)/shard_map/ppermute | solution.py:645
  369.9 17.5 %collective-permute-done.31 = bf16[512,1024]{1,0:T(8,128)(2,1)} collective-permute-done((bf16[512,1024]{1,0:T(8,128)(2,1)}, bf16[512,1024]{1,0:T(8,128)(2,1)}, u32[]{:S(2)}, u32[]{:S(2)}) %collective-permute-start.31) | collective-permute-done | bytes 1048608 | tf_op jit(solution)/shard_map/ppermute | solution.py:645
  388.3 21.6 %collective-permute-done.23 = bf16[512,1024]{1,0:T(8,128)(2,1)} collective-permute-done((bf16[512,1024]{1,0:T(8,128)(2,1)}, bf16[512,1024]{1,0:T(8,128)(2,1)}, u32[]{:S(2)}, u32[]{:S(2)}) %collective-permute-start.23) | collective-permute-done | bytes 1048608 | tf_op jit(solution)/shard_map/ppermute | solution.py:645
  414.1 18.3 %collective-permute-done.34 = bf16[256,2048]{1,0:T(8,128)(2,1)} collective-permute-done((bf16[256,2048]{1,0:T(8,128)(2,1)}, bf16[256,2048]{1,0:T(8,128)(2,1)}, u32[]{:S(2)}, u32[]{:S(2)}) %collective-permute-start.34) | collective-permute-done | bytes 1048608 | tf_op jit(solution)/shard_map/ppermute | solution.py:645
  433.3 19.9 %collective-permute-done.26 = bf16[256,2048]{1,0:T(8,128)(2,1)} collective-permute-done((bf16[256,2048]{1,0:T(8,128)(2,1)}, bf16[256,2048]{1,0:T(8,128)(2,1)}, u32[]{:S(2)}, u32[]{:S(2)}) %collective-permute-start.26) | collective-permute-done | bytes 1048608 | tf_op jit(solution)/shard_map/ppermute | solution.py:645
  460.9 8.9 pad_maximum_fusion.4.up_weight
  469.8 7.0 collective-permute-done.35
  476.8 7.5 pad_maximum_fusion.5.down_weight
  484.9 6.3 shard_map.295
  495.3 6.3 shard_map.294
  501.6 28.4 %run_expert.2 = (bf16[640,1024]{1,0:T(8,128)(2,1)}, bf16[640,1024]{1,0:T(8,128)(2,1)}, bf16[640,1024]{1,0:T(8,128)(2,1)}, bf16[640,2048]{1,0:T(8,128)(2,1)}, f32...) custom-call(s32[4]{0:T(128)} %iota_xor_fusion.perm, ...), custom_call_target="tpu_custom_call" | custom-call | tf_op jit(solution)/shard_map/run_expert/pallas_call | solution.py:523
  530.0 28.5 %run_expert.3 = (bf16[640,1024]{1,0:T(8,128)(2,1)}, bf16[640,1024]{1,0:T(8,128)(2,1)}, bf16[640,1024]{1,0:T(8,128)(2,1)}, bf16[640,2048]{1,0:T(8,128)(2,1)}, f32...) custom-call(s32[4]{0:T(128)} %iota_xor_fusion.perm, ...), custom_call_target="tpu_custom_call" | custom-call | tf_op jit(solution)/shard_map/run_expert/pallas_call | solution.py:523
  558.5 5.8 shard_map.297
  567.4 5.6 all-to-all-start
  573.0 5.8 all-to-all-done
  578.8 36.6 %reduce-scatter.8.cloned.1.call-done = bf16[128,2048]{1,0:T(8,128)(2,1)} async-done(((bf16[1024,2048]{1,0:T(8,128)(2,1)}), bf16[128,2048]{1,0:T(8,128)(2,1)}) %reduce-scatter.8.cloned.1.call-update) | async-done | bytes 524304 | tf_op jit(solution)/shard_map/reduce_scatter | solution.py:916
  622.3 11.3 %collective-permute-done.36 = bf16[128,2048]{1,0:T(8,128)(2,1)S(1)} collective-permute-done((bf16[128,2048]{1,0:T(8,128)(2,1)S(1)}, bf16[128,2048]{1,0:T(8,128)(2,1)S(1)}, u32[]{:S(2)}, u32[]{:S(2)}) %collective-permute-start.36) | collective-permute-done | bytes 524320 | tf_op jit(solution)/shard_map/ppermute | solution.py:645
  633.6 9.4 collective-permute-done.37
  645.2 19.7 %attend_backward.1 = (bf16[512,512]{1,0:T(8,128)(2,1)}, bf16[4096,1024]{1,0:T(8,128)(2,1)}) custom-call(s32[2,16]{1,0:T(2,128)} %copy-done.57, bf16[512,512]{1,0:T(8,128)(2,1)} %get-tuple-element.61.query, bf16[4096,1024]{1,0:T(8,128)(2,1)} %all-gather.10.cloned.1.call-done.pairs, bf16[512,512]{1,0:T(8,128)(2,1)} %convolution_convert_fusion.28.grad, ...), custom_call_target="tpu_custom_call" | custom-call | tf_op jit(solution)/shard_map/attend_backward/pallas_call | solution.py:409
  693.7 68.0 %reduce-scatter.10.cloned.1.call-done.back.refs_7_ = bf16[512,1024]{1,0:T(8,128)(2,1)} async-done(((bf16[4096,1024]{1,0:T(8,128)(2,1)}), bf16[512,1024]{1,0:T(8,128)(2,1)}) %reduce-scatter.10.cloned.1.call-update) | async-done | bytes 1048592 | tf_op jit(solution)/shard_map/reduce_scatter | solution.py:979
  776.7 5.6 convolution_convert_fusion
  837.7 6.1 shard_map.296
  846.5 11.0 %collective-permute-done.64 = bf16[512,1024]{1,0:T(8,128)(2,1)} collective-permute-done((bf16[512,1024]{1,0:T(8,128)(2,1)}, bf16[512,1024]{1,0:T(8,128)(2,1)}, u32[]{:S(2)}, u32[]{:S(2)}) %collective-permute-start.64) | collective-permute-done | bytes 1048608 | tf_op jit(solution)/shard_map/ppermute | solution.py:645
  865.1 15.7 %collective-permute-done.58 = bf16[512,1024]{1,0:T(8,128)(2,1)S(1)} collective-permute-done((bf16[512,1024]{1,0:T(8,128)(2,1)S(1)}, bf16[512,1024]{1,0:T(8,128)(2,1)S(1)}, u32[]{:S(2)}, u32[]{:S(2)}) %collective-permute-start.58) | collective-permute-done | bytes 1048608 | tf_op jit(solution)/shard_map/ppermute | solution.py:645
  881.7 11.0 %collective-permute-done.61 = bf16[512,1024]{1,0:T(8,128)(2,1)S(1)} collective-permute-done((bf16[512,1024]{1,0:T(8,128)(2,1)S(1)}, bf16[512,1024]{1,0:T(8,128)(2,1)S(1)}, u32[]{:S(2)}, u32[]{:S(2)}) %collective-permute-start.61) | collective-permute-done | bytes 1048608 | tf_op jit(solution)/shard_map/ppermute | solution.py:645
  896.8 18.4 %collective-permute-done.71 = bf16[256,2048]{1,0:T(8,128)(2,1)S(1)} collective-permute-done((bf16[256,2048]{1,0:T(8,128)(2,1)S(1)}, bf16[256,2048]{1,0:T(8,128)(2,1)S(1)}, u32[]{:S(2)}, u32[]{:S(2)}) %collective-permute-start.71) | collective-permute-done | bytes 1048608 | tf_op jit(solution)/shard_map/ppermute | solution.py:645
  919.6 9.7 collective-permute-done.63
  929.8 30.3 %collective-permute-done.65 = bf16[512,1024]{1,0:T(8,128)(2,1)S(1)} collective-permute-done((bf16[512,1024]{1,0:T(8,128)(2,1)S(1)}, bf16[512,1024]{1,0:T(8,128)(2,1)S(1)}, u32[]{:S(2)}, u32[]{:S(2)}) %collective-permute-start.65) | collective-permute-done | bytes 1048608 | tf_op jit(solution)/shard_map/ppermute | solution.py:645
  968.0 6.3 collective-permute-done.57
  974.3 25.0 %collective-permute-done.59 = bf16[512,1024]{1,0:T(8,128)(2,1)S(1)} collective-permute-done((bf16[512,1024]{1,0:T(8,128)(2,1)S(1)}, bf16[512,1024]{1,0:T(8,128)(2,1)S(1)}, u32[]{:S(2)}, u32[]{:S(2)}) %collective-permute-start.59) | collective-permute-done | bytes 1048608 | tf_op jit(solution)/shard_map/ppermute | solution.py:645
  1008.4 4.6 fusion.69
  1029.0 6.3 collective-permute-done.46
  1048.8 6.5 all-to-all-start.1
  (555 shorter events, 325.5 us)
Async XLA Ops:
  7.2 70.4 %all-gather.8.cloned.1.call-start = ((), (), s32[]{:S(2)}) async-start(), calls=%async_computation.7 | async-start | bytes 4718592 | tf_op jit(solution)/shard_map/all_gather | solution.py:766
  24.1 96.3 %all-gather.16.cloned.1.call-start = ((), (), s32[]{:S(2)}) async-start(), calls=%async_computation.16 | async-start | bytes 4718592 | tf_op jit(solution)/shard_map/all_gather | solution.py:771
  25.2 178.2 %all-gather.10.cloned.1.call-start = ((), (), s32[]{:S(2)}) async-start(), calls=%async_computation.8 | async-start | bytes 9437184 | tf_op jit(solution)/shard_map/all_gather | solution.py:835
  48.7 24.3 %collective-permute-start.1 = (bf16[128,2048]{1,0:T(8,128)(2,1)S(1)}, bf16[128,2048]{1,0:T(8,128)(2,1)S(1)}, u32[]{:S(2)}, u32[]{:S(2)}) collective-permute-start(bf16[128,2048]{1,0:T(8,128)(2,1)S(1)} %copy-done.9), channel_id=1, source_target_pairs={{0,16},{8,24},{16,0},{24,8},{1,17},{9,25},{17,1},{25,9},{2,18},{10... | collective-permute-start | bytes 1572872 | tf_op jit(solution)/shard_map/ppermute | solution.py:645
  98.1 386.1 %all-gather.14.cloned.1.call-start = ((), (), s32[]{:S(2)}) async-start(), calls=%async_computation.10 | async-start | bytes 4718592 | tf_op jit(solution)/shard_map/all_gather | solution.py:776
  98.7 392.5 %all-gather.12.cloned.1.call-start = ((), (), s32[]{:S(2)}) async-start(), calls=%async_computation.9 | async-start | bytes 4718592 | tf_op jit(solution)/shard_map/all_gather | solution.py:844
  219.0 25.0 %collective-permute-start.16 = (bf16[128,2048]{1,0:T(8,128)(2,1)S(1)}, bf16[128,2048]{1,0:T(8,128)(2,1)S(1)}, u32[]{:S(2)}, u32[]{:S(2)}) collective-permute-start(bf16[128,2048]{1,0:T(8,128)(2,1)S(1)} %get-tuple-element.221), channel_id=1, source_target_pairs={{0,16},{8,24},{16,0},{24,8},{1,17},{9,25},{17,1},{25,9},{2,18},{10... | collective-permute-start | bytes 1572872 | tf_op jit(solution)/shard_map/ppermute | solution.py:645
  220.5 23.6 %collective-permute-start.17 = (bf16[128,2048]{1,0:T(8,128)(2,1)S(1)}, bf16[128,2048]{1,0:T(8,128)(2,1)S(1)}, u32[]{:S(2)}, u32[]{:S(2)}) collective-permute-start(bf16[128,2048]{1,0:T(8,128)(2,1)S(1)} %get-tuple-element.220), channel_id=1, source_target_pairs={{0,24},{8,16},{16,8},{24,0},{1,25},{9,17},{17,9},{25,1},{2,26},{10... | collective-permute-start | bytes 1572872 | tf_op jit(solution)/shard_map/ppermute | solution.py:645
  245.8 369.7 %reduce-scatter.8.cloned.1.call-start = ((), (), s32[]{:S(2)}) async-start(), calls=%async_computation.12 | async-start | bytes 4718592 | tf_op jit(solution)/shard_map/reduce_scatter | solution.py:916
  247.7 26.2 %collective-permute-start.18 = (bf16[512,1024]{1,0:T(8,128)(2,1)S(1)}, bf16[512,1024]{1,0:T(8,128)(2,1)}, u32[]{:S(2)}, u32[]{:S(2)}) collective-permute-start(bf16[512,1024]{1,0:T(8,128)(2,1)S(1)} %get-tuple-element.218), channel_id=1, source_target_pairs={{0,8},{8,0},{16,24},{24,16},{1,9},{9,1},{17,25},{25,17},{2,10},{10... | collective-permute-start | bytes 3145736 | tf_op jit(solution)/shard_map/ppermute | solution.py:645
  249.0 26.4 %collective-permute-start.19 = (bf16[512,1024]{1,0:T(8,128)(2,1)S(1)}, bf16[512,1024]{1,0:T(8,128)(2,1)S(1)}, u32[]{:S(2)}, u32[]{:S(2)}) collective-permute-start(bf16[512,1024]{1,0:T(8,128)(2,1)S(1)} %get-tuple-element.218), channel_id=1, source_target_pairs={{0,16},{8,24},{16,0},{24,8},{1,17},{9,25},{17,1},{25,9},{2,18},{10... | collective-permute-start | bytes 3145736 | tf_op jit(solution)/shard_map/ppermute | solution.py:645
  251.0 45.3 %collective-permute-start.21 = (bf16[512,1024]{1,0:T(8,128)(2,1)S(1)}, bf16[512,1024]{1,0:T(8,128)(2,1)S(1)}, u32[]{:S(2)}, u32[]{:S(2)}) collective-permute-start(bf16[512,1024]{1,0:T(8,128)(2,1)S(1)} %get-tuple-element.216), channel_id=1, source_target_pairs={{0,8},{8,0},{16,24},{24,16},{1,9},{9,1},{17,25},{25,17},{2,10},{10... | collective-permute-start | bytes 3145736 | tf_op jit(solution)/shard_map/ppermute | solution.py:645
  252.5 45.0 %collective-permute-start.22 = (bf16[512,1024]{1,0:T(8,128)(2,1)S(1)}, bf16[512,1024]{1,0:T(8,128)(2,1)S(1)}, u32[]{:S(2)}, u32[]{:S(2)}) collective-permute-start(bf16[512,1024]{1,0:T(8,128)(2,1)S(1)} %get-tuple-element.216), channel_id=1, source_target_pairs={{0,16},{8,24},{16,0},{24,8},{1,17},{9,25},{17,1},{25,9},{2,18},{10... | collective-permute-start | bytes 3145736 | tf_op jit(solution)/shard_map/ppermute | solution.py:645
  254.5 64.4 %collective-permute-start.24 = (bf16[256,2048]{1,0:T(8,128)(2,1)}, bf16[256,2048]{1,0:T(8,128)(2,1)}, u32[]{:S(2)}, u32[]{:S(2)}) collective-permute-start(bf16[256,2048]{1,0:T(8,128)(2,1)} %get-tuple-element.214), channel_id=1, source_target_pairs={{0,8},{8,0},{16,24},{24,16},{1,9},{9,1},{17,25},{25,17},{2,10},{10... | collective-permute-start | bytes 3145736 | tf_op jit(solution)/shard_map/ppermute | solution.py:645
  273.9 46.4 %collective-permute-start.25 = (bf16[256,2048]{1,0:T(8,128)(2,1)}, bf16[256,2048]{1,0:T(8,128)(2,1)}, u32[]{:S(2)}, u32[]{:S(2)}) collective-permute-start(bf16[256,2048]{1,0:T(8,128)(2,1)} %get-tuple-element.214), channel_id=1, source_target_pairs={{0,16},{8,24},{16,0},{24,8},{1,17},{9,25},{17,1},{25,9},{2,18},{10... | collective-permute-start | bytes 3145736 | tf_op jit(solution)/shard_map/ppermute | solution.py:645
  275.4 67.1 %collective-permute-start.28 = (bf16[512,1024]{1,0:T(8,128)(2,1)S(1)}, bf16[512,1024]{1,0:T(8,128)(2,1)}, u32[]{:S(2)}, u32[]{:S(2)}) collective-permute-start(bf16[512,1024]{1,0:T(8,128)(2,1)S(1)} %get-tuple-element.217), channel_id=1, source_target_pairs={{0,16},{8,24},{16,0},{24,8},{1,17},{9,25},{17,1},{25,9},{2,18},{10... | collective-permute-start | bytes 3145736 | tf_op jit(solution)/shard_map/ppermute | solution.py:645
  296.3 47.1 %collective-permute-start.27 = (bf16[512,1024]{1,0:T(8,128)(2,1)S(1)}, bf16[512,1024]{1,0:T(8,128)(2,1)}, u32[]{:S(2)}, u32[]{:S(2)}) collective-permute-start(bf16[512,1024]{1,0:T(8,128)(2,1)S(1)} %get-tuple-element.217), channel_id=1, source_target_pairs={{0,8},{8,0},{16,24},{24,16},{1,9},{9,1},{17,25},{25,17},{2,10},{10... | collective-permute-start | bytes 3145736 | tf_op jit(solution)/shard_map/ppermute | solution.py:645
  298.5 66.5 %collective-permute-start.20 = (bf16[512,1024]{1,0:T(8,128)(2,1)}, bf16[512,1024]{1,0:T(8,128)(2,1)}, u32[]{:S(2)}, u32[]{:S(2)}) collective-permute-start(bf16[512,1024]{1,0:T(8,128)(2,1)} %collective-permute-done.18), channel_id=1, source_target_pairs={{0,16},{8,24},{16,0},{24,8},{1,17},{9,25},{17,1},{25,9},{2,18},{10... | collective-permute-start | bytes 3145736 | tf_op jit(solution)/shard_map/ppermute | solution.py:645
  318.9 68.6 %collective-permute-start.31 = (bf16[512,1024]{1,0:T(8,128)(2,1)}, bf16[512,1024]{1,0:T(8,128)(2,1)}, u32[]{:S(2)}, u32[]{:S(2)}) collective-permute-start(bf16[512,1024]{1,0:T(8,128)(2,1)} %get-tuple-element.215), channel_id=1, source_target_pairs={{0,16},{8,24},{16,0},{24,8},{1,17},{9,25},{17,1},{25,9},{2,18},{10... | collective-permute-start | bytes 3145736 | tf_op jit(solution)/shard_map/ppermute | solution.py:645
  320.4 89.6 %collective-permute-start.23 = (bf16[512,1024]{1,0:T(8,128)(2,1)}, bf16[512,1024]{1,0:T(8,128)(2,1)}, u32[]{:S(2)}, u32[]{:S(2)}) collective-permute-start(bf16[512,1024]{1,0:T(8,128)(2,1)} %copy-done.39), channel_id=1, source_target_pairs={{0,16},{8,24},{16,0},{24,8},{1,17},{9,25},{17,1},{25,9},{2,18},{10... | collective-permute-start | bytes 3145736 | tf_op jit(solution)/shard_map/ppermute | solution.py:645
  342.5 89.9 %collective-permute-start.34 = (bf16[256,2048]{1,0:T(8,128)(2,1)}, bf16[256,2048]{1,0:T(8,128)(2,1)}, u32[]{:S(2)}, u32[]{:S(2)}) collective-permute-start(bf16[256,2048]{1,0:T(8,128)(2,1)} %get-tuple-element.213), channel_id=1, source_target_pairs={{0,16},{8,24},{16,0},{24,8},{1,17},{9,25},{17,1},{25,9},{2,18},{10... | collective-permute-start | bytes 3145736 | tf_op jit(solution)/shard_map/ppermute | solution.py:645
  343.4 109.8 %collective-permute-start.26 = (bf16[256,2048]{1,0:T(8,128)(2,1)}, bf16[256,2048]{1,0:T(8,128)(2,1)}, u32[]{:S(2)}, u32[]{:S(2)}) collective-permute-start(bf16[256,2048]{1,0:T(8,128)(2,1)} %collective-permute-done.24), channel_id=1, source_target_pairs={{0,16},{8,24},{16,0},{24,8},{1,17},{9,25},{17,1},{25,9},{2,18},{10... | collective-permute-start | bytes 3145736 | tf_op jit(solution)/shard_map/ppermute | solution.py:645
  365.0 92.4 %collective-permute-start.29 = (bf16[512,1024]{1,0:T(8,128)(2,1)}, bf16[512,1024]{1,0:T(8,128)(2,1)S(1)}, u32[]{:S(2)}, u32[]{:S(2)}) collective-permute-start(bf16[512,1024]{1,0:T(8,128)(2,1)} %collective-permute-done.28), channel_id=1, source_target_pairs={{0,8},{8,0},{16,24},{24,16},{1,9},{9,1},{17,25},{25,17},{2,10},{10... | collective-permute-start | bytes 3145736 | tf_op jit(solution)/shard_map/ppermute | solution.py:645
  387.5 73.4 %collective-permute-start.30 = (bf16[512,1024]{1,0:T(8,128)(2,1)S(1)}, bf16[512,1024]{1,0:T(8,128)(2,1)S(1)}, u32[]{:S(2)}, u32[]{:S(2)}) collective-permute-start(bf16[512,1024]{1,0:T(8,128)(2,1)S(1)} %copy-done.15), channel_id=1, source_target_pairs={{0,8},{8,0},{16,24},{24,16},{1,9},{9,1},{17,25},{25,17},{2,10},{10... | collective-permute-start | bytes 3145736 | tf_op jit(solution)/shard_map/ppermute | solution.py:645
  409.9 50.9 %collective-permute-start.32 = (bf16[512,1024]{1,0:T(8,128)(2,1)}, bf16[512,1024]{1,0:T(8,128)(2,1)S(1)}, u32[]{:S(2)}, u32[]{:S(2)}) collective-permute-start(bf16[512,1024]{1,0:T(8,128)(2,1)} %collective-permute-done.31), channel_id=1, source_target_pairs={{0,8},{8,0},{16,24},{24,16},{1,9},{9,1},{17,25},{25,17},{2,10},{10... | collective-permute-start | bytes 3145736 | tf_op jit(solution)/shard_map/ppermute | solution.py:645
  432.4 37.4 %collective-permute-start.33 = (bf16[256,2048]{1,0:T(8,128)(2,1)S(1)}, bf16[256,2048]{1,0:T(8,128)(2,1)S(1)}, u32[]{:S(2)}, u32[]{:S(2)}) collective-permute-start(bf16[256,2048]{1,0:T(8,128)(2,1)S(1)} %copy-done.16), channel_id=1, source_target_pairs={{0,8},{8,0},{16,24},{24,16},{1,9},{9,1},{17,25},{25,17},{2,10},{10... | collective-permute-start | bytes 3145736 | tf_op jit(solution)/shard_map/ppermute | solution.py:645
  453.1 23.6 %collective-permute-start.35 = (bf16[256,2048]{1,0:T(8,128)(2,1)}, bf16[256,2048]{1,0:T(8,128)(2,1)S(1)}, u32[]{:S(2)}, u32[]{:S(2)}) collective-permute-start(bf16[256,2048]{1,0:T(8,128)(2,1)} %collective-permute-done.34), channel_id=1, source_target_pairs={{0,8},{8,0},{16,24},{24,16},{1,9},{9,1},{17,25},{25,17},{2,10},{10... | collective-permute-start | bytes 3145736 | tf_op jit(solution)/shard_map/ppermute | solution.py:645
  573.0 188.7 %reduce-scatter.10.cloned.1.call-start = ((), (), s32[]{:S(2)}) async-start(), calls=%async_computation.13 | async-start | bytes 9437184 | tf_op jit(solution)/shard_map/reduce_scatter | solution.py:979
  664.8 338.2 %reduce-scatter.12.cloned.1.call-start = ((), (), s32[]{:S(2)}) async-start(), calls=%async_computation.14 | async-start | bytes 4718592 | tf_op jit(solution)/shard_map/reduce_scatter | solution.py:993
  693.6 361.8 %reduce-scatter.14.cloned.1.call-start = ((), (), s32[]{:S(2)}) async-start(), calls=%async_computation.15 | async-start | bytes 4718592 | tf_op jit(solution)/shard_map/reduce_scatter | solution.py:1003
  782.3 278.4 %reduce-scatter.6.cloned.1.call-start = ((), (), s32[]{:S(2)}) async-start(), calls=%async_computation.11 | async-start | bytes 4718592 | tf_op jit(solution)/shard_map/reduce_scatter | solution.py:922
  789.0 105.7 %collective-permute-start.69 = (bf16[256,2048]{1,0:T(8,128)(2,1)}, bf16[256,2048]{1,0:T(8,128)(2,1)}, u32[]{:S(2)}, u32[]{:S(2)}) collective-permute-start(bf16[256,2048]{1,0:T(8,128)(2,1)} %convolution_convert_fusion.10), channel_id=1, source_target_pairs={{0,8},{8,0},{16,24},{24,16},{1,9},{9,1},{17,25},{25,17},{2,10},{10... | collective-permute-start | bytes 3145736 | tf_op jit(solution)/shard_map/ppermute | solution.py:645
  793.6 50.4 %collective-permute-start.70 = (bf16[256,2048]{1,0:T(8,128)(2,1)}, bf16[256,2048]{1,0:T(8,128)(2,1)}, u32[]{:S(2)}, u32[]{:S(2)}) collective-permute-start(bf16[256,2048]{1,0:T(8,128)(2,1)} %convolution_convert_fusion.8), channel_id=1, source_target_pairs={{0,8},{8,0},{16,24},{24,16},{1,9},{9,1},{17,25},{25,17},{2,10},{10... | collective-permute-start | bytes 3145736 | tf_op jit(solution)/shard_map/ppermute | solution.py:645
  797.1 64.8 %collective-permute-start.73 = (bf16[256,2048]{1,0:T(8,128)(2,1)}, bf16[256,2048]{1,0:T(8,128)(2,1)}, u32[]{:S(2)}, u32[]{:S(2)}) collective-permute-start(bf16[256,2048]{1,0:T(8,128)(2,1)} %convolution_convert_fusion.4), channel_id=1, source_target_pairs={{0,16},{8,24},{16,0},{24,8},{1,17},{9,25},{17,1},{25,9},{2,18},{10... | collective-permute-start | bytes 3145736 | tf_op jit(solution)/shard_map/ppermute | solution.py:645
  804.7 52.8 %collective-permute-start.64 = (bf16[512,1024]{1,0:T(8,128)(2,1)}, bf16[512,1024]{1,0:T(8,128)(2,1)}, u32[]{:S(2)}, u32[]{:S(2)}) collective-permute-start(bf16[512,1024]{1,0:T(8,128)(2,1)} %convolution_convert_fusion.16), channel_id=1, source_target_pairs={{0,8},{8,0},{16,24},{24,16},{1,9},{9,1},{17,25},{25,17},{2,10},{10... | collective-permute-start | bytes 3145736 | tf_op jit(solution)/shard_map/ppermute | solution.py:645
  813.8 45.8 %collective-permute-start.67 = (bf16[512,1024]{1,0:T(8,128)(2,1)}, bf16[512,1024]{1,0:T(8,128)(2,1)}, u32[]{:S(2)}, u32[]{:S(2)}) collective-permute-start(bf16[512,1024]{1,0:T(8,128)(2,1)} %convolution_convert_fusion.12), channel_id=1, source_target_pairs={{0,16},{8,24},{16,0},{24,8},{1,17},{9,25},{17,1},{25,9},{2,18},{10... | collective-permute-start | bytes 3145736 | tf_op jit(solution)/shard_map/ppermute | solution.py:645
  844.0 51.2 %collective-permute-start.72 = (bf16[256,2048]{1,0:T(8,128)(2,1)}, bf16[256,2048]{1,0:T(8,128)(2,1)S(1)}, u32[]{:S(2)}, u32[]{:S(2)}) collective-permute-start(bf16[256,2048]{1,0:T(8,128)(2,1)} %convolution_convert_fusion.6), channel_id=1, source_target_pairs={{0,16},{8,24},{16,0},{24,8},{1,17},{9,25},{17,1},{25,9},{2,18},{10... | collective-permute-start | bytes 3145736 | tf_op jit(solution)/shard_map/ppermute | solution.py:645
  859.7 33.1 %collective-permute-start.61 = (bf16[512,1024]{1,0:T(8,128)(2,1)S(1)}, bf16[512,1024]{1,0:T(8,128)(2,1)S(1)}, u32[]{:S(2)}, u32[]{:S(2)}) collective-permute-start(bf16[512,1024]{1,0:T(8,128)(2,1)S(1)} %copy-done.93), channel_id=1, source_target_pairs={{0,16},{8,24},{16,0},{24,8},{1,17},{9,25},{17,1},{25,9},{2,18},{10... | collective-permute-start | bytes 3145736 | tf_op jit(solution)/shard_map/ppermute | solution.py:645
  861.9 53.3 %collective-permute-start.71 = (bf16[256,2048]{1,0:T(8,128)(2,1)S(1)}, bf16[256,2048]{1,0:T(8,128)(2,1)S(1)}, u32[]{:S(2)}, u32[]{:S(2)}) collective-permute-start(bf16[256,2048]{1,0:T(8,128)(2,1)S(1)} %add_convert_fusion.2), channel_id=1, source_target_pairs={{0,16},{8,24},{16,0},{24,8},{1,17},{9,25},{17,1},{25,9},{2,18},{10... | collective-permute-start | bytes 3145736 | tf_op jit(solution)/shard_map/ppermute | solution.py:645
  880.8 37.7 %collective-permute-start.74 = (bf16[256,2048]{1,0:T(8,128)(2,1)S(1)}, bf16[256,2048]{1,0:T(8,128)(2,1)S(1)}, u32[]{:S(2)}, u32[]{:S(2)}) collective-permute-start(bf16[256,2048]{1,0:T(8,128)(2,1)S(1)} %add_convert_fusion.1), channel_id=1, source_target_pairs={{0,8},{8,0},{16,24},{24,16},{1,9},{9,1},{17,25},{25,17},{2,10},{10... | collective-permute-start | bytes 3145736 | tf_op jit(solution)/shard_map/ppermute | solution.py:645
  892.8 36.6 %collective-permute-start.63 = (bf16[512,1024]{1,0:T(8,128)(2,1)S(1)}, bf16[512,1024]{1,0:T(8,128)(2,1)S(1)}, u32[]{:S(2)}, u32[]{:S(2)}) collective-permute-start(bf16[512,1024]{1,0:T(8,128)(2,1)S(1)} %copy-done.92), channel_id=1, source_target_pairs={{0,8},{8,0},{16,24},{24,16},{1,9},{9,1},{17,25},{25,17},{2,10},{10... | collective-permute-start | bytes 3145736 | tf_op jit(solution)/shard_map/ppermute | solution.py:645
  894.7 66.5 %collective-permute-start.66 = (bf16[512,1024]{1,0:T(8,128)(2,1)S(1)}, bf16[512,1024]{1,0:T(8,128)(2,1)S(1)}, u32[]{:S(2)}, u32[]{:S(2)}) collective-permute-start(bf16[512,1024]{1,0:T(8,128)(2,1)S(1)} %copy-done.91), channel_id=1, source_target_pairs={{0,16},{8,24},{16,0},{24,8},{1,17},{9,25},{17,1},{25,9},{2,18},{10... | collective-permute-start | bytes 3145736 | tf_op jit(solution)/shard_map/ppermute | solution.py:645
  895.2 64.9 %collective-permute-start.65 = (bf16[512,1024]{1,0:T(8,128)(2,1)S(1)}, bf16[512,1024]{1,0:T(8,128)(2,1)S(1)}, u32[]{:S(2)}, u32[]{:S(2)}) collective-permute-start(bf16[512,1024]{1,0:T(8,128)(2,1)S(1)} %add_convert_fusion.4), channel_id=1, source_target_pairs={{0,16},{8,24},{16,0},{24,8},{1,17},{9,25},{17,1},{25,9},{2,18},{10... | collective-permute-start | bytes 3145736 | tf_op jit(solution)/shard_map/ppermute | solution.py:645
  915.2 47.6 %collective-permute-start.68 = (bf16[512,1024]{1,0:T(8,128)(2,1)S(1)}, bf16[512,1024]{1,0:T(8,128)(2,1)S(1)}, u32[]{:S(2)}, u32[]{:S(2)}) collective-permute-start(bf16[512,1024]{1,0:T(8,128)(2,1)S(1)} %add_convert_fusion.3), channel_id=1, source_target_pairs={{0,8},{8,0},{16,24},{24,16},{1,9},{9,1},{17,25},{25,17},{2,10},{10... | collective-permute-start | bytes 3145736 | tf_op jit(solution)/shard_map/ppermute | solution.py:645
  918.5 55.8 %collective-permute-start.57 = (bf16[512,1024]{1,0:T(8,128)(2,1)S(1)}, bf16[512,1024]{1,0:T(8,128)(2,1)S(1)}, u32[]{:S(2)}, u32[]{:S(2)}) collective-permute-start(bf16[512,1024]{1,0:T(8,128)(2,1)S(1)} %copy-done.90), channel_id=1, source_target_pairs={{0,8},{8,0},{16,24},{24,16},{1,9},{9,1},{17,25},{25,17},{2,10},{10... | collective-permute-start | bytes 3145736 | tf_op jit(solution)/shard_map/ppermute | solution.py:645
  929.3 71.8 %collective-permute-start.60 = (bf16[512,1024]{1,0:T(8,128)(2,1)S(1)}, bf16[512,1024]{1,0:T(8,128)(2,1)S(1)}, u32[]{:S(2)}, u32[]{:S(2)}) collective-permute-start(bf16[512,1024]{1,0:T(8,128)(2,1)S(1)} %copy-done.89), channel_id=1, source_target_pairs={{0,16},{8,24},{16,0},{24,8},{1,17},{9,25},{17,1},{25,9},{2,18},{10... | collective-permute-start | bytes 3145736 | tf_op jit(solution)/shard_map/ppermute | solution.py:645
  960.2 39.1 %collective-permute-start.59 = (bf16[512,1024]{1,0:T(8,128)(2,1)S(1)}, bf16[512,1024]{1,0:T(8,128)(2,1)S(1)}, u32[]{:S(2)}, u32[]{:S(2)}) collective-permute-start(bf16[512,1024]{1,0:T(8,128)(2,1)S(1)} %add_convert_fusion.6), channel_id=1, source_target_pairs={{0,16},{8,24},{16,0},{24,8},{1,17},{9,25},{17,1},{25,9},{2,18},{10... | collective-permute-start | bytes 3145736 | tf_op jit(solution)/shard_map/ppermute | solution.py:645
  961.3 39.9 %collective-permute-start.62 = (bf16[512,1024]{1,0:T(8,128)(2,1)S(1)}, bf16[512,1024]{1,0:T(8,128)(2,1)S(1)}, u32[]{:S(2)}, u32[]{:S(2)}) collective-permute-start(bf16[512,1024]{1,0:T(8,128)(2,1)S(1)} %add_convert_fusion.5), channel_id=1, source_target_pairs={{0,8},{8,0},{16,24},{24,16},{1,9},{9,1},{17,25},{25,17},{2,10},{10... | collective-permute-start | bytes 3145736 | tf_op jit(solution)/shard_map/ppermute | solution.py:645
  (142 other events, 2970.1 us)
Sparse Core Ops, SparseCore 0:
  24.2 47.8 all-gather.7
  74.3 46.0 all-gather.15
  122.6 80.8 all-gather.9
  204.9 45.3 all-gather.13
  252.3 45.6 all-gather.11
  564.5 50.9 reduce-scatter.7
  665.0 96.6 reduce-scatter.9
  764.0 48.3 reduce-scatter.11
  814.7 48.3 reduce-scatter.13
  865.2 48.3 reduce-scatter.5
